TPU v7x, 256 devices: a whole 4x4x8 slice. The times are simulated.
256 devices in a mesh: cfg: 8 (over y, core), node: 32 (over z, x).
Axes of the slice: x: 4, y: 4, z: 8, core: 2. Of those that a mesh axis runs over, the one named last changes fastest.
Arguments:
- node_feats: bfloat16 [1048576, 256], P(('cfg', 'node')), may hold values from -6 to 6
- neighbors: int32 [1048576, 4], P(('cfg', 'node')), may hold values from 0 to 5119
- self_weight: bfloat16 [256, 256], replicated, may hold values from -0.375 to 0.375
- neighbor_weight: bfloat16 [256, 256], replicated, may hold values from -0.375 to 0.375
- sage_bias: float32 [256], replicated, may hold values from -3 to 3
- conf_index: int32 [32768], P(('cfg', 'node')), may hold values from 0 to 4095
- layout_ids: int32 [128, 32768], P('cfg', 'node'), may hold values from 0 to 127
- join_weight: bfloat16 [256, 256], replicated, may hold values from -0.375 to 0.375
- layout_table: bfloat16 [128, 256], replicated, may hold values from -6 to 6
- join_bias: float32 [256], replicated, may hold values from -3 to 3
- mid_weight: bfloat16 [256, 256], replicated, may hold values from -0.375 to 0.375
- mid_bias: float32 [256], replicated, may hold values from -3 to 3
- score_weight: float32 [256], replicated, may hold values from -0.375 to 0.375
- config_pairs: int32 [512, 2], replicated, may hold values from 0 to 127
Outputs:
- node_embed: bfloat16 [1048576, 256], P(('cfg', 'node'))
- pair_loss: float32 [], replicated
- conf_grad: float32 [32768, 256], P(('cfg', 'node'))
All inputs are finite; a program needn't handle non-finite values.
Results may differ from a plain program's by a relative error of at most 0.028.
Values may be sent and summed in bfloat16 or wider, within the bound.
No kernel may reach another device: no remote copies, remote signals or barrier semaphores. Data moves between devices by JAX's collectives and lax.ppermute only.
A program may use at most 64 MiB of HBM per device.

v0:
```python
import math

import jax
import jax.numpy as jnp
from jax import lax
from jax.sharding import PartitionSpec as P

HALO = 512


def with_halo(value, sides, width):
    for axis, dim in sides:
        size, length = (lax.axis_size(axis), value.shape[dim])
        up = [(i, (i + 1) % size) for i in range(size - 1)]
        down = [(j, i) for i, j in up]
        last = lax.slice_in_dim(value, length - width, length, axis=dim)
        leading = lax.slice_in_dim(value, 0, width, axis=dim)
        before = lax.ppermute(last, axis, up)
        after = lax.ppermute(leading, axis, down)
        value = jnp.concatenate([before, value, after], axis=dim)
    return value


def silu_slope(value):
    sigma = jax.nn.sigmoid(value)
    return sigma * (1.0 + value * (1.0 - sigma))


def pair_terms(config_score, config_pairs):
    config_total_count = config_score.shape[0]
    pair_first = config_pairs[:, 0]
    pair_second = config_pairs[:, 1]
    score_gap = jnp.take(config_score, pair_second) - jnp.take(config_score, pair_first)
    pair_loss = jnp.mean(jax.nn.softplus(score_gap))
    pair_slope = jax.nn.sigmoid(score_gap) / config_pairs.shape[0]
    columns = jnp.arange(config_total_count, dtype=jnp.int32)
    signed = (pair_second[:, None] == columns[None, :]).astype(jnp.float32) - (
        pair_first[:, None] == columns[None, :]
    ).astype(jnp.float32)
    score_grad = 65536.0 * jnp.dot(pair_slope, signed, precision=lax.Precision.HIGHEST)
    return (pair_loss, score_grad)


def shards(
    node_feats,
    neighbors,
    self_weight,
    neighbor_weight,
    sage_bias,
    conf_index,
    layout_ids,
    join_weight,
    layout_table,
    join_bias,
    mid_weight,
    mid_bias,
    score_weight,
    config_pairs,
):
    node_rows = node_feats.shape[0]
    feat_width = node_feats.shape[1]
    hidden_width = join_weight.shape[1]
    padded = with_halo(node_feats, ((("cfg", "node"), 0),), HALO)
    summed = jnp.zeros((node_rows, feat_width), jnp.float32)
    for neighbor in range(neighbors.shape[1]):
        summed = summed + jnp.take(padded, neighbors[:, neighbor], axis=0).astype(jnp.float32)
    neighbour_mean = (summed / neighbors.shape[1]).astype(jnp.bfloat16)
    pre_act = (
        jnp.dot(node_feats, self_weight, preferred_element_type=jnp.float32)
        + jnp.dot(neighbour_mean, neighbor_weight, preferred_element_type=jnp.float32)
        + sage_bias
    )
    node_embed = jax.nn.silu(pre_act).astype(jnp.bfloat16)
    conf_src = jnp.take(node_embed, conf_index, axis=0)
    node_count = lax.axis_size("node")
    group_count = lax.axis_size("cfg")
    local_conf = conf_index.shape[0]
    per_peer = local_conf // node_count
    local_configs = layout_ids.shape[0]
    norm_scale = 1.0 / math.sqrt(layout_ids.shape[1] * node_count)
    table_ids = jnp.arange(layout_table.shape[0], dtype=jnp.int32)

    def hidden_rows(base_rows, row_ids):
        picks = (row_ids[:, None] == table_ids[None, :]).astype(jnp.bfloat16)
        inner_pre = (
            base_rows + jnp.dot(picks, layout_table, preferred_element_type=jnp.float32) + join_bias
        )
        inner_act = jax.nn.silu(inner_pre).astype(jnp.bfloat16)
        outer_pre = jnp.dot(inner_act, mid_weight, preferred_element_type=jnp.float32) + mid_bias
        return (inner_pre, outer_pre)

    grouped = lax.all_gather(conf_src, "cfg", axis=0, tiled=True)
    spread = lax.all_to_all(
        grouped.reshape(group_count, node_count, per_peer, feat_width),
        "node",
        split_axis=1,
        concat_axis=1,
        tiled=True,
    )
    conf_rows = spread.reshape(-1, feat_width)
    row_count = conf_rows.shape[0]
    base = jnp.dot(conf_rows, join_weight, preferred_element_type=jnp.float32)

    def config_total(row_ids):
        inner_pre, outer_pre = hidden_rows(base, row_ids)
        scores = jnp.dot(jax.nn.silu(outer_pre), score_weight, precision=lax.Precision.HIGHEST)
        return jnp.sum(scores)

    partial_sums = lax.map(config_total, layout_ids)
    local_score = lax.psum(partial_sums, "node") * norm_scale
    config_score = lax.all_gather(local_score, "cfg", axis=0, tiled=True)
    pair_loss, score_grad = pair_terms(config_score, config_pairs)
    local_grads = lax.dynamic_slice_in_dim(
        score_grad, lax.axis_index("cfg") * local_configs, local_configs, 0
    )

    def config_step(carried, inputs):
        row_ids, config_grad = inputs
        inner_pre, outer_pre = hidden_rows(base, row_ids)
        outer_grad = (config_grad * norm_scale * score_weight * silu_slope(outer_pre)).astype(
            jnp.bfloat16
        )
        inner_grad = lax.dot_general(
            outer_grad, mid_weight, (((1,), (1,)), ((), ())), preferred_element_type=jnp.float32
        ) * silu_slope(inner_pre)
        return (carried + inner_grad, None)

    zero_rows = jnp.zeros((row_count, hidden_width), jnp.float32)
    group_part, unused = lax.scan(config_step, zero_rows, (layout_ids, local_grads))
    row_sum = lax.psum_scatter(
        group_part.astype(jnp.bfloat16), "cfg", scatter_dimension=0, tiled=True
    )
    local_grad = lax.dot_general(
        row_sum, join_weight, (((1,), (1,)), ((), ())), preferred_element_type=jnp.float32
    )
    returned = lax.all_to_all(
        local_grad.reshape(node_count, per_peer, feat_width).astype(jnp.bfloat16),
        "node",
        split_axis=0,
        concat_axis=0,
        tiled=True,
    ).astype(jnp.float32)
    conf_grad = returned.reshape(-1, feat_width)
    return (node_embed, pair_loss, conf_grad)


def solution(mesh):
    placed = (
        P(("cfg", "node"), None),
        P(("cfg", "node"), None),
        P(),
        P(),
        P(),
        P(("cfg", "node")),
        P("cfg", "node"),
        P(),
        P(),
        P(),
        P(),
        P(),
        P(),
        P(),
    )
    return jax.shard_map(
        shards,
        mesh=mesh,
        in_specs=placed,
        out_specs=(P(("cfg", "node"), None), P(), P(("cfg", "node"), None)),
        check_vma=False,
    )
```

profile of v0, /device:TPU:2, one launch (start us, length us, event | category | flops | bytes accessed | tf_op | source)
XLA Modules:
  0.0 480.4 jit_solution(4784900319033597347)
XLA Ops:
  8.3 3.4 collective-permute-start
  11.7 2.5 collective-permute-start.1
  16.6 4.4 fusion.62
  21.4 17.0 %gather_fusion.4 = bf16[4096,256]{1,0:T(8,128)(2,1)} fusion(bf16[5120,256]{1,0:T(8,128)(2,1)S(1)} %constant_dynamic-update-slice_fusion, s32[4096]{0:T(1024)S(1)} %fusion.55), kind=kCustom, calls=%fused_computation.4.clone | custom fusion | bytes 4210688 | tf_op jit(solution)/shard_map/jit(_take)/gather | solution.py:66
  38.4 16.9 %gather_fusion.1 = bf16[4096,256]{1,0:T(8,128)(2,1)} fusion(bf16[5120,256]{1,0:T(8,128)(2,1)S(1)} %constant_dynamic-update-slice_fusion, s32[4096]{0:T(1024)S(1)} %fusion.52), kind=kCustom, calls=%fused_computation.clone | custom fusion | bytes 4210688 | tf_op jit(solution)/shard_map/jit(_take)/gather | solution.py:66
  55.3 16.9 %gather_fusion.2 = bf16[4096,256]{1,0:T(8,128)(2,1)} fusion(bf16[5120,256]{1,0:T(8,128)(2,1)S(1)} %constant_dynamic-update-slice_fusion, s32[4096]{0:T(1024)S(1)} %fusion.53), kind=kCustom, calls=%fused_computation.2.clone | custom fusion | bytes 4210688 | tf_op jit(solution)/shard_map/jit(_take)/gather | solution.py:66
  72.2 16.9 %gather_fusion.3 = bf16[4096,256]{1,0:T(8,128)(2,1)} fusion(bf16[5120,256]{1,0:T(8,128)(2,1)S(1)} %constant_dynamic-update-slice_fusion, s32[4096]{0:T(1024)S(1)} %fusion.54), kind=kCustom, calls=%fused_computation.3.clone | custom fusion | bytes 4210688 | tf_op jit(solution)/shard_map/jit(_take)/gather | solution.py:66
  89.1 8.0 %multiply_convert_fusion.5 = bf16[4096,256]{1,0:T(8,128)(2,1)S(1)} fusion(f32[4096,256]{1,0:T(8,128)} %fusion.62, bf16[256,256]{1,0:T(8,128)(2,1)S(1)} %copy-done.8, bf16[4096,256]{1,0:T(8,128)(2,1)} %gather_fusion.4, bf16[4096,256]{1,0:T(8,128)(2,1)} %gather_fusion.3, bf16[4096,256]{1,0:T(8,128)(2,1)} %gather_fusion.2, ...), kind=kOutput, calls=%fused_computation.48 | convolution fusion | flops 557842432 | bytes 14828544 | tf_op jit(solution)/shard_map/dot_general | solution.py:70
  98.6 13.6 %all_gather.6 = bf16[1024,256]{1,0:T(8,128)(2,1)S(1)} all-gather(bf16[128,256]{1,0:T(8,128)(2,1)S(1)} %broadcast_select_fusion), channel_id=1, replica_groups=mesh['cfg'=8,'node'=32] {'cfg'}, dimensions={0}, use_global_device_ids=true | all-gather | bytes 589824 | tf_op jit(solution)/shard_map/all_gather | solution.py:92
  113.4 13.7 %all-to-all-start = ((bf16[8,32,4,256]{3,2,0,1:T(4,128)(2,1)}), bf16[8,32,4,256]{3,2,0,1:T(4,128)(2,1)S(1)}, u32[]{:S(2)}, u32[]{:S(2)}) async-start(bf16[8,32,4,256]{3,2,0,1:T(4,128)(2,1)} %copy.18), calls=%async_computation | async-start | bytes 1048576 | tf_op jit(solution)/shard_map/all_to_all | solution.py:93
  128.5 15.9 %all-to-all-done = bf16[8,32,4,256]{3,2,0,1:T(4,128)(2,1)S(1)} async-done(((bf16[8,32,4,256]{3,2,0,1:T(4,128)(2,1)}), bf16[8,32,4,256]{3,2,0,1:T(4,128)(2,1)S(1)}, u32[]{:S(2)}, u32[]{:S(2)}) %all-to-all-start) | async-done | bytes 524320 | tf_op jit(solution)/shard_map/all_to_all | solution.py:93
  145.1 113.5 %while.22 = (s32[]{:T(128)}, f32[16]{0:T(128)S(1)}, s32[16,1024]{1,0:T(8,128)}, bf16[128,256]{1,0:T(8,128)(2,1)S(1)}, f32[1024,256]{1,0:T(8,128)S(1)}, /*index=5...) while((s32[]{:T(128)}, f32[16]{0:T(128)S(1)}, ...), condition=%wide.region_2.4_spmd.clone, body=%wide.region_0.3_spmd.clone.sunk | while | flops 207750144 | bytes 3366021 | solution.py:109
  145.9 2.5 convolution_add_fusion.6
  148.4 2.4 fusion.92
  153.0 2.5 convolution_add_fusion.6
  155.5 2.4 fusion.92
  160.1 2.5 convolution_add_fusion.6
  162.6 2.4 fusion.92
  167.2 2.5 convolution_add_fusion.6
  169.7 2.4 fusion.92
  174.3 2.5 convolution_add_fusion.6
  176.8 2.4 fusion.92
  181.4 2.5 convolution_add_fusion.6
  188.5 2.5 convolution_add_fusion.6
  191.0 2.4 fusion.92
  195.6 2.5 convolution_add_fusion.6
  198.1 2.4 fusion.92
  202.7 2.5 convolution_add_fusion.6
  205.2 2.4 fusion.92
  209.8 2.5 convolution_add_fusion.6
  216.8 2.5 convolution_add_fusion.6
  219.3 2.4 fusion.92
  223.9 2.5 convolution_add_fusion.6
  226.4 2.4 fusion.92
  231.0 2.5 convolution_add_fusion.6
  238.1 2.5 convolution_add_fusion.6
  245.2 2.5 convolution_add_fusion.6
  247.7 2.4 fusion.92
  252.3 2.5 convolution_add_fusion.6
  254.8 2.4 fusion.92
  258.7 70.7 %psum.7 = f32[16]{0:T(128)S(1)} all-reduce(f32[16]{0:T(128)S(1)} %get-tuple-element.114), channel_id=1, replica_groups=mesh['cfg'=8,'node'=32] {'node'}, use_global_device_ids=true, to_apply=%region_3.5 | all-reduce | flops 16 | bytes 128 | tf_op jit(solution)/shard_map/psum | solution.py:110
  329.5 12.4 %all-reduce = f32[128]{0:T(128)S(1)} all-reduce(f32[128]{0:T(128)S(1)} %multiply_dynamic-update-slice_fusion), channel_id=1, replica_groups=mesh['cfg'=8,'node'=32] {'cfg'}, use_global_device_ids=true, to_apply=%add | all-reduce | flops 128 | bytes 1024
  341.9 3.3 gather_fusion.5
  345.2 3.3 gather_fusion.6
  349.1 72.5 %while.23 = (s32[]{:T(128)}, f32[1024,256]{1,0:T(8,128)S(1)}, f32[16]{0:T(128)S(1)}, f32[256]{0:T(256)S(1)}, s32[16,1024]{1,0:T(8,128)}, /*index=5*/bf16[128,256...) while((s32[]{:T(128)}, f32[1024,256]{1,0:T(8,128)S(1)}, ...), condition=%wide.region_6.9_spmd.clone, body=%wide.region_5.8_spmd.clone.sunk | while | flops 342753536 | bytes 5457063 | solution.py:129
  422.4 28.7 %reduce-scatter.2.cloned.1.call-done = bf16[128,256]{1,0:T(8,128)(2,1)} async-done(((bf16[1024,256]{1,0:T(8,128)(2,1)}), bf16[128,256]{1,0:T(8,128)(2,1)}) %reduce-scatter.2.cloned.1.call-update) | async-done | bytes 65552 | tf_op jit(solution)/shard_map/reduce_scatter | solution.py:130
  452.8 10.2 %all-to-all-start.1 = ((bf16[32,4,256]{2,1,0:T(4,128)(2,1)}), bf16[32,4,256]{2,1,0:T(4,128)(2,1)S(1)}, u32[]{:S(2)}, u32[]{:S(2)}) async-start(bf16[32,4,256]{2,1,0:T(4,128)(2,1)} %convert_element_type.55), calls=%async_computation.2 | async-start | bytes 131072 | tf_op jit(solution)/shard_map/all_to_all | solution.py:136
  464.3 7.4 %all-to-all-done.1 = bf16[32,4,256]{2,1,0:T(4,128)(2,1)S(1)} async-done(((bf16[32,4,256]{2,1,0:T(4,128)(2,1)}), bf16[32,4,256]{2,1,0:T(4,128)(2,1)S(1)}, u32[]{:S(2)}, u32[]{:S(2)}) %all-to-all-start.1) | async-done | bytes 65568 | tf_op jit(solution)/shard_map/all_to_all | solution.py:136
  (198 shorter events, 117.9 us)
Async XLA Ops:
  7.2 9.4 %copy-start = (bf16[256,256]{1,0:T(8,128)(2,1)S(1)}, bf16[256,256]{1,0:T(8,128)(2,1)}, u32[]{:S(2)}) copy-start(bf16[256,256]{1,0:T(8,128)(2,1)} %param.24) | copy-start | bytes 393220
  8.3 12.8 %collective-permute-start = (bf16[512,256]{1,0:T(8,128)(2,1)S(1)}, bf16[512,256]{1,0:T(8,128)(2,1)S(1)}, u32[]{:S(2)}, u32[]{:S(2)}) collective-permute-start(bf16[512,256]{1,0:T(8,128)(2,1)S(1)} %get-tuple-element.212), channel_id=1, source_target_pairs={{0,1},{1,2},{2,3},{3,4},{4,5},{5,6},{6,7},{7,8},{8,9},{9,10},{10,1... | collective-permute-start | bytes 786440 | tf_op jit(solution)/shard_map/ppermute | solution.py:18
  11.7 9.7 %collective-permute-start.1 = (bf16[512,256]{1,0:T(8,128)(2,1)S(1)}, bf16[512,256]{1,0:T(8,128)(2,1)S(1)}, u32[]{:S(2)}, u32[]{:S(2)}) collective-permute-start(bf16[512,256]{1,0:T(8,128)(2,1)S(1)} %get-tuple-element.211), channel_id=1, source_target_pairs={{1,0},{2,1},{3,2},{4,3},{5,4},{6,5},{7,6},{8,7},{9,8},{10,9},{11,1... | collective-permute-start | bytes 786440 | tf_op jit(solution)/shard_map/ppermute | solution.py:19
  16.6 4.5 copy-start.1
  72.2 16.9 %copy-start.8 = (bf16[256,256]{1,0:T(8,128)(2,1)S(1)}, bf16[256,256]{1,0:T(8,128)(2,1)}, u32[]{:S(2)}) copy-start(bf16[256,256]{1,0:T(8,128)(2,1)} %param.25) | copy-start | bytes 393220
  72.2 16.9 %copy-start.9 = (f32[256]{0:T(256)S(1)}, f32[256]{0:T(256)}, u32[]{:S(2)}) copy-start(f32[256]{0:T(256)} %param.26) | copy-start | bytes 3076
  97.2 1.3 copy-start.4
  97.2 30.0 %copy-start.11 = (u32[256]{0:T(256)S(1)}, u32[256]{0:T(256)}, u32[]{:S(2)}) copy-start(u32[256]{0:T(256)} %constant.97) | copy-start | bytes 3076
  98.5 30.0 %copy-start.7 = (s32[512,2]{0,1:T(2,128)S(1)}, s32[512,2]{0,1:T(2,128)}, u32[]{:S(2)}) copy-start(s32[512,2]{0,1:T(2,128)} %param.35) | copy-start | bytes 12292
  112.4 32.4 %copy-start.3 = (bf16[256,256]{1,0:T(8,128)(2,1)S(1)}, bf16[256,256]{1,0:T(8,128)(2,1)}, u32[]{:S(2)}) copy-start(bf16[256,256]{1,0:T(8,128)(2,1)} %param.29) | copy-start | bytes 393220
  113.4 31.0 %all-to-all-start = ((bf16[8,32,4,256]{3,2,0,1:T(4,128)(2,1)}), bf16[8,32,4,256]{3,2,0,1:T(4,128)(2,1)S(1)}, u32[]{:S(2)}, u32[]{:S(2)}) async-start(bf16[8,32,4,256]{3,2,0,1:T(4,128)(2,1)} %copy.18), calls=%async_computation | async-start | bytes 1048576 | tf_op jit(solution)/shard_map/all_to_all | solution.py:93
  127.1 18.0 %copy-start.2 = (bf16[128,256]{1,0:T(8,128)(2,1)S(1)}, bf16[128,256]{1,0:T(8,128)(2,1)}, u32[]{:S(2)}) copy-start(bf16[128,256]{1,0:T(8,128)(2,1)} %param.30) | copy-start | bytes 196612
  127.1 18.0 %copy-start.5 = (f32[256]{0:T(256)S(1)}, f32[256]{0:T(256)}, u32[]{:S(2)}) copy-start(f32[256]{0:T(256)} %param.31) | copy-start | bytes 3076
  127.1 18.0 %copy-start.6 = (f32[256]{0:T(256)S(1)}, f32[256]{0:T(256)}, u32[]{:S(2)}) copy-start(f32[256]{0:T(256)} %param.34) | copy-start | bytes 3076
  127.1 18.0 %copy-start.10 = (f32[256]{0:T(256)S(1)}, f32[256]{0:T(256)}, u32[]{:S(2)}) copy-start(f32[256]{0:T(256)} %param.33) | copy-start | bytes 3076
  127.2 324.0 %reduce-scatter.2.cloned.1.call-start = ((), (), s32[]{:S(2)}) async-start(), calls=%async_computation.3 | async-start | bytes 589824 | tf_op jit(solution)/shard_map/reduce_scatter | solution.py:130
  452.8 18.9 %all-to-all-start.1 = ((bf16[32,4,256]{2,1,0:T(4,128)(2,1)}), bf16[32,4,256]{2,1,0:T(4,128)(2,1)S(1)}, u32[]{:S(2)}, u32[]{:S(2)}) async-start(bf16[32,4,256]{2,1,0:T(4,128)(2,1)} %convert_element_type.55), calls=%async_computation.2 | async-start | bytes 131072 | tf_op jit(solution)/shard_map/all_to_all | solution.py:136
Sparse Core Ops, SparseCore 0:
  422.5 28.5 reduce-scatter.1
where the time goes:
time: 485 us; the launch traced here: 480 us
  matrix products  132 us (27%)
  local copies, waits for them, and re-layouts  127 us (26%)
  blocking collectives  96.7 us (20%)
  waiting for transfers between devices  52.2 us (11%)
  starting transfers between devices  29.8 us (6%)
  between operations  16.9 us (3%)
  other arithmetic  14 us (3%)
  loops' own time  11.2 us (2%)
    psum x1, blocking collectives, shards(): local_score = lax.psum(partial_sums, 'node') * norm_scale  70.7 us
    gather x4, local copies, waits for them, and re-layouts, shards(): jnp.take(padded, neighbors[:, neighbor], axis=0).astype(jnp.float32)  67.7 us
    dot_general x16, matrix products, hidden_rows(): jnp.dot(inner_act, mid_weight, preferred_element_type=jnp.float32)  40 us
    dot_general x16, matrix products, config_total(): jnp.dot(jax.nn.silu(outer_pre), score_weight, precision=lax.Precision.HIG...  38.7 us
    dot_general x16, matrix products, config_step(): lax.dot_general(outer_grad, mid_weight, (((1,), (1,)), ((), ())), preferr...  33.9 us
    reduce_scatter x1, waiting for transfers between devices, shards(): lax.psum_scatter(group_part.astype(jnp.bfloat16), 'cfg', scatter_dimensio...  28.7 us
    dynamic_slice x32, local copies, waits for them, and re-layouts, shards(): partial_sums = lax.map(config_total, layout_ids)  24.5 us
    all_to_all x1, waiting for transfers between devices, shards(): lax.all_to_all(grouped.reshape(group_count, node_count, per_peer, feat_wi...  15.9 us
  transfers between devices with their start and end apart: 5, of which 4 were waited for; matrix products, arithmetic and copies ran while one was open for 2% of the time, Pallas kernels for 0%

commit v1 on v0

v1 whole, which is shorter than its diff:
```python
import functools
import math

import jax
import jax.numpy as jnp
from jax import lax
from jax.experimental import pallas as pl
from jax.experimental.pallas import tpu as pltpu
from jax.sharding import PartitionSpec as P

HALO = 512
f32 = jnp.float32
bf16 = jnp.bfloat16
VMEM = pl.BlockSpec(memory_space=pltpu.VMEM)
SMEM = pl.BlockSpec(memory_space=pltpu.SMEM)


def half_silu(half):
    tanh = jnp.tanh(half)
    scaled = half * tanh
    return half + scaled, tanh, scaled


def twice_slope(half, tanh, scaled):
    inner = 1.0 + half - scaled
    return inner + tanh * inner


def build_table(table, before, feats, after):
    offset = 0
    for source in (before, feats, after):
        rows = source.shape[0]
        step = min(rows, 512)
        for start in range(0, rows, step):
            value = source[start : start + step, :].astype(f32)
            table[pl.ds(2 * (offset + start), step, stride=2), :] = value[:, :128]
            table[pl.ds(2 * (offset + start) + 1, step, stride=2), :] = value[:, 128:]
        offset += rows


def conf_kernel(nodes, nbrs, picks, before, feats, after, sw, nw, bias, out, table, own, acc):
    build_table(table, before, feats, after)
    count = picks.shape[0]
    rows = table.reshape(table.shape[0] // 2, 2, 128)
    own3 = own.reshape(count, 2, 128)
    acc3 = acc.reshape(count, 2, 128)

    def body(block, carry):
        values = []
        for j in range(8):
            g = picks[block * 8 + j]
            near = [rows[nbrs[k * nodes + g]] for k in range(4)]
            values.append((rows[HALO + g], (near[0] + near[1]) + (near[2] + near[3])))
        for j in range(8):
            own3[block * 8 + j], acc3[block * 8 + j] = values[j]
        return carry

    lax.fori_loop(0, count // 8, body, 0)
    halves = [ref[pl.ds(side, count, stride=2), :] for ref in (own, acc) for side in (0, 1)]
    out[...] = layer_rows(
        halves[0].astype(bf16),
        halves[1].astype(bf16),
        (halves[2] * 0.25).astype(bf16),
        (halves[3] * 0.25).astype(bf16),
        sw,
        nw,
        bias,
    )


def layer_rows(own_left, own_right, left, right, sw, nw, bias):
    pre = jnp.dot(own_left, sw[:128, :], preferred_element_type=f32)
    pre += jnp.dot(own_right, sw[128:, :], preferred_element_type=f32)
    pre += jnp.dot(left, nw[:128, :], preferred_element_type=f32)
    pre += jnp.dot(right, nw[128:, :], preferred_element_type=f32)
    return half_silu(0.5 * (pre + bias[...]))[0].astype(bf16)


def conf_rows_of(nbrs, picks, before, feats, after, sw, nw, bias):
    nodes, width = feats.shape
    count = picks.shape[0]
    window = nodes + 2 * HALO
    return pl.pallas_call(
        functools.partial(conf_kernel, nodes),
        out_shape=jax.ShapeDtypeStruct((count, width), bf16),
        in_specs=[SMEM, SMEM] + [VMEM] * 6,
        out_specs=VMEM,
        scratch_shapes=[
            pltpu.VMEM((2 * window, 128), f32),
            pltpu.VMEM((2 * count, 128), f32),
            pltpu.VMEM((2 * count, 128), f32),
        ],
        cost_estimate=pl.CostEstimate(
            flops=4 * count * width * width, transcendentals=0, bytes_accessed=6 << 20
        ),
        compiler_params=pltpu.CompilerParams(vmem_limit_bytes=24 << 20),
        name="conf_rows",
    )(nbrs, picks, before, feats, after, sw, nw, bias)


def layer_kernel(tile, nodes, nbrs, before, feats, after, sw, nw, bias, out, table, acc):
    step = pl.program_id(0)

    @pl.when(step == 0)
    def _():
        build_table(table, before, feats, after)

    rows = table.reshape(table.shape[0] // 2, 2, 128)
    acc3 = acc.reshape(tile, 2, 128)
    unroll = 16

    def body(block, carry):
        values = []
        for j in range(unroll):
            g = step * tile + block * unroll + j
            near = [rows[nbrs[k * nodes + g]] for k in range(4)]
            values.append((near[0] + near[1]) + (near[2] + near[3]))
        for j in range(unroll):
            acc3[block * unroll + j] = values[j]
        return carry

    lax.fori_loop(0, tile // unroll, body, 0)
    own = feats[pl.ds(pl.multiple_of(step * tile, tile), tile), :]
    out[...] = layer_rows(
        own[:, :128],
        own[:, 128:],
        (acc[pl.ds(0, tile, stride=2), :] * 0.25).astype(bf16),
        (acc[pl.ds(1, tile, stride=2), :] * 0.25).astype(bf16),
        sw,
        nw,
        bias,
    )


def layer_of(nbrs, before, feats, after, sw, nw, bias):
    nodes, width = feats.shape
    tile = 512
    window = nodes + 2 * HALO
    return pl.pallas_call(
        functools.partial(layer_kernel, tile, nodes),
        out_shape=jax.ShapeDtypeStruct((nodes, width), bf16),
        grid=(nodes // tile,),
        in_specs=[SMEM] + [VMEM] * 6,
        out_specs=pl.BlockSpec((tile, width), lambda i: (i, 0)),
        scratch_shapes=[
            pltpu.VMEM((2 * window, 128), f32),
            pltpu.VMEM((2 * tile, 128), f32),
        ],
        cost_estimate=pl.CostEstimate(
            flops=4 * nodes * width * width, transcendentals=0, bytes_accessed=64 << 20
        ),
        compiler_params=pltpu.CompilerParams(vmem_limit_bytes=24 << 20),
        name="graph_layer",
    )(nbrs, before, feats, after, sw, nw, bias)


def scorer_kernel(groups, order, where, *refs):
    xs, refs = refs[:groups], refs[groups:]
    ids, join, table, jbias, mid, mbias, weight, grads, sent = refs[:9]
    base, tabh, midh, back, total = refs[9:]
    step = pl.program_id(0)
    chunk = xs[0].shape[0]
    configs = ids.shape[0]
    layouts = table.shape[0]

    @pl.when(step == 0)
    def _():
        for i in range(groups):
            base[i] = 0.5 * (
                jnp.dot(xs[i][...], join[...], preferred_element_type=f32) + jbias[...]
            )
        tabh[...] = (table[...].astype(f32) * 0.5).astype(bf16)
        middle = mid[...].astype(f32)
        midh[...] = (middle * 0.5).astype(bf16)
        back[...] = jnp.transpose(middle * (weight[...] * 0.25)).astype(bf16)
        total[...] = jnp.zeros_like(total)

    columns = jnp.transpose(ids[...].astype(f32))
    lanes = lax.broadcasted_iota(jnp.int32, (chunk, layouts), 1).astype(f32)
    rows = base[step]
    some = 4
    for first in range(0, configs, some):
        picks = jnp.concatenate(
            [
                jnp.where(columns[:, k : k + 1] == lanes, 1.0, 0.0).astype(bf16)
                for k in range(first, first + some)
            ],
            axis=0,
        )
        half = jnp.dot(picks, tabh[...], preferred_element_type=f32)
        half = half + jnp.concatenate([rows] * some, axis=0)
        act, tanh, scaled = half_silu(half)
        outer = jnp.dot(act.astype(bf16), midh[...], preferred_element_type=f32)
        outer = outer + 0.5 * mbias[...]
        act2, tanh2, scaled2 = half_silu(outer)
        for q in range(some):
            part = act2[q * chunk : (q + 1) * chunk, :]
            total[first + q : first + q + 1, :] += jnp.sum(part, axis=0, keepdims=True)
        slope2 = twice_slope(outer, tanh2, scaled2).astype(bf16)
        grad = jnp.dot(slope2, back[...], preferred_element_type=f32)
        grad = grad * twice_slope(half, tanh, scaled)
        for q in range(some):
            grads[0, first + q] = grad[q * chunk : (q + 1) * chunk, :].astype(bf16)

    @pl.when(step == groups - 1)
    def _():
        scores = jnp.sum(total[...] * weight[...], axis=1, keepdims=True)
        lane = lax.broadcasted_iota(jnp.int32, (configs, 128), 1)
        sub = lax.broadcasted_iota(jnp.int32, (configs, 128), 0)
        spread = jnp.where(lane == sub + where[0] * configs, scores, 0.0)
        sent[...] = jnp.broadcast_to(jnp.sum(spread, axis=0, keepdims=True), sent.shape)


def scorer_of(order, where, xs, ids, join, table, jbias, mid, mbias, weight, devices):
    groups = len(xs)
    configs = ids.shape[0]
    chunk, width = xs[0].shape
    whole = lambda i, *_: (0, 0)
    hidden = join.shape[1]
    return pl.pallas_call(
        functools.partial(scorer_kernel, groups),
        out_shape=(
            jax.ShapeDtypeStruct((groups, configs, chunk, hidden), bf16),
            jax.ShapeDtypeStruct((devices, 128), f32),
        ),
        grid_spec=pltpu.PrefetchScalarGridSpec(
            num_scalar_prefetch=2,
            grid=(groups,),
            in_specs=[VMEM] * groups
            + [pl.BlockSpec((configs, chunk), lambda i, order, where: (0, order[i]))]
            + [VMEM] * 6,
            out_specs=(
                pl.BlockSpec((1, configs, chunk, hidden), lambda i, *_: (i, 0, 0, 0)),
                pl.BlockSpec((devices, 128), whole),
            ),
            scratch_shapes=[
                pltpu.VMEM((groups, chunk, hidden), f32),
                pltpu.VMEM(table.shape, bf16),
                pltpu.VMEM(mid.shape, bf16),
                pltpu.VMEM(mid.shape, bf16),
                pltpu.VMEM((configs, hidden), f32),
            ],
        ),
        cost_estimate=pl.CostEstimate(
            flops=6 * groups * configs * chunk * width * width,
            transcendentals=2 * groups * configs * chunk * width,
            bytes_accessed=10 << 20,
        ),
        compiler_params=pltpu.CompilerParams(vmem_limit_bytes=24 << 20),
        name="scorer",
    )(order, where, *xs, ids, join, table, jbias, mid, mbias, weight)


def weighted(coef, grads, configs):
    rows = grads[0, 0].astype(f32) * coef[0:1, :]
    for k in range(1, configs):
        rows = rows + grads[0, k].astype(f32) * coef[k : k + 1, :]
    return rows


def ranking_kernel(scale, where, got, pairs, grads, loss, coef, out):
    configs = coef.shape[0]

    @pl.when(pl.program_id(0) == 0)
    def _():
        score = jnp.sum(got[...], axis=0, keepdims=True) * scale
        count = pairs.shape[0]
        lane = lax.broadcasted_iota(jnp.int32, (count, 128), 1)
        second = jnp.where(pairs[:, 1:2] == lane, 1.0, 0.0)
        signed = second - jnp.where(pairs[:, 0:1] == lane, 1.0, 0.0)
        gap = jnp.sum(signed * score, axis=1, keepdims=True)
        fade = jnp.exp(-jnp.abs(gap))
        soft = jnp.maximum(gap, 0.0) + jnp.log1p(fade)
        loss[...] = jnp.sum(soft, axis=0, keepdims=True) * (1.0 / count)
        slope = jnp.where(gap >= 0.0, 1.0, fade) / (1.0 + fade)
        grad = jnp.sum(slope * signed, axis=0, keepdims=True) * (65536.0 / count)
        lanes = lax.broadcasted_iota(jnp.int32, (configs, 128), 1)
        subs = lax.broadcasted_iota(jnp.int32, (configs, 128), 0)
        mine = jnp.where(lanes == subs + where[0] * configs, grad * scale, 0.0)
        own = jnp.sum(mine, axis=1, keepdims=True)
        coef[...] = jnp.broadcast_to(own, coef.shape)

    out[0] = weighted(coef, grads, configs).astype(bf16)


def ranking_of(scale, where, got, pairs, grads, first):
    groups, configs, chunk, hidden = grads.shape
    half = groups // 2
    return pl.pallas_call(
        functools.partial(ranking_kernel, scale),
        out_shape=(
            jax.ShapeDtypeStruct((1, 1), f32),
            jax.ShapeDtypeStruct((configs, hidden), f32),
            jax.ShapeDtypeStruct((half, chunk, hidden), bf16),
        ),
        grid=(half,),
        in_specs=[
            SMEM,
            VMEM,
            VMEM,
            pl.BlockSpec(
                (1, configs, chunk, hidden), lambda d: (first + (half - d) % half, 0, 0, 0)
            ),
        ],
        out_specs=(
            pl.BlockSpec((1, 1), lambda d: (0, 0)),
            pl.BlockSpec((configs, hidden), lambda d: (0, 0)),
            pl.BlockSpec((1, chunk, hidden), lambda d: (d, 0, 0)),
        ),
        cost_estimate=pl.CostEstimate(flops=1 << 24, transcendentals=0, bytes_accessed=6 << 20),
        name="ranking",
    )(where, got, pairs, grads)


def rest_kernel(coef, grads, out):
    out[0] = weighted(coef, grads, coef.shape[0]).astype(bf16)


def rest_of(coef, grads, first):
    groups, configs, chunk, hidden = grads.shape
    half = groups // 2
    return pl.pallas_call(
        rest_kernel,
        out_shape=jax.ShapeDtypeStruct((half, chunk, hidden), bf16),
        grid=(half,),
        in_specs=[
            VMEM,
            pl.BlockSpec(
                (1, configs, chunk, hidden), lambda d: (first + (half - d) % half, 0, 0, 0)
            ),
        ],
        out_specs=pl.BlockSpec((1, chunk, hidden), lambda d: (d, 0, 0)),
        cost_estimate=pl.CostEstimate(flops=1 << 24, transcendentals=0, bytes_accessed=6 << 20),
        name="rest",
    )(coef, grads)


def shards(
    node_feats,
    neighbors,
    self_weight,
    neighbor_weight,
    sage_bias,
    conf_index,
    layout_ids,
    join_weight,
    layout_table,
    join_bias,
    mid_weight,
    mid_bias,
    score_weight,
    config_pairs,
):
    both = ("cfg", "node")
    devices = lax.axis_size(both)
    node_count = lax.axis_size("node")
    group_count = lax.axis_size("cfg")
    rings = group_count // 2
    local_conf = conf_index.shape[0]
    width = node_feats.shape[1]
    per_peer = local_conf // node_count
    scale = 1.0 / math.sqrt(layout_ids.shape[1] * node_count)
    group = lax.axis_index("cfg")

    up = [(i, i + 1) for i in range(devices - 1)]
    down = [(i + 1, i) for i in range(devices - 1)]
    before = lax.ppermute(node_feats[-HALO:], both, up)
    after = lax.ppermute(node_feats[:HALO], both, down)
    nbrs = neighbors.T.reshape(-1)
    bias = sage_bias.reshape(1, -1)

    conf_src = conf_rows_of(
        nbrs, conf_index, before, node_feats, after, self_weight, neighbor_weight, bias
    )
    node_embed = layer_of(nbrs, before, node_feats, after, self_weight, neighbor_weight, bias)

    swap = [(i, i ^ 1) for i in range(group_count)]

    def shift(value, by):
        perm = [(i, (i // 2 + by) % rings * 2 + i % 2) for i in range(group_count)]
        return lax.ppermute(value, "cfg", perm)

    mine = lax.all_to_all(
        conf_src.reshape(node_count, per_peer, width), "node", 0, 0, tiled=True
    ).reshape(local_conf, width)
    xs = [mine] + [shift(mine, by) for by in range(1, rings)]
    xs = xs + [lax.ppermute(x, "cfg", swap) for x in xs]
    ring, core = group // 2, group % 2
    turns = jnp.arange(group_count, dtype=jnp.int32)
    order = (ring + rings - turns % rings) % rings * 2 + (core + turns // rings) % 2
    where = group.reshape(1)

    grads, sent = scorer_of(
        order,
        where,
        xs,
        layout_ids,
        join_weight,
        layout_table,
        join_bias.reshape(1, -1),
        mid_weight,
        mid_bias.reshape(1, -1),
        score_weight.reshape(1, -1),
        devices,
    )
    got = lax.all_to_all(sent.reshape(devices, 1, 128), both, 0, 0, tiled=True)
    loss, coef, away = ranking_of(
        scale, where, got.reshape(devices, 128), config_pairs, grads, rings
    )
    came = lax.ppermute(away, "cfg", swap)
    kept = rest_of(coef, grads, 0)
    sums = [kept[d].astype(f32) + came[d].astype(f32) for d in range(rings)]
    arrived = [shift(sums[d].astype(bf16), d) for d in range(1, rings)]
    row_grad = sums[0]
    for part in arrived:
        row_grad = row_grad + part.astype(f32)
    local_grad = lax.dot_general(
        row_grad.astype(bf16),
        join_weight,
        (((1,), (1,)), ((), ())),
        preferred_element_type=f32,
    )
    conf_grad = lax.all_to_all(
        local_grad.astype(bf16).reshape(node_count, per_peer, width), "node", 0, 0, tiled=True
    )
    conf_grad = conf_grad.astype(f32).reshape(local_conf, width)
    return (node_embed, loss.reshape(()), conf_grad)


def solution(mesh):
    split = P(("cfg", "node"), None)
    placed = (split, split, P(), P(), P(), P(("cfg", "node")), P("cfg", "node")) + (P(),) * 7
    return jax.shard_map(
        shards,
        mesh=mesh,
        in_specs=placed,
        out_specs=(split, P(), split),
        check_vma=False,
    )
```

time: 485 us -> 145 us (0.30)
  matrix products: 132 us -> 1.03 us
  local copies, waits for them, and re-layouts: 127 us -> 12.9 us
  blocking collectives: 96.7 us -> 22.1 us
  Pallas kernels: 0 us -> 53.7 us
  waiting for transfers between devices: 52.2 us -> 23.5 us
  between operations: 16.9 us -> 0.88 us
  other arithmetic: 14 us -> 0.97 us
  loops' own time: 11.2 us -> 0 us
    dot_general x69 -> x1, matrix products: 132 us -> 1.03 us  [shards(): lax.dot_general(row_grad.astype(bf16), join_weight, (((1,), (1,)), ((), (...]
    gather x7 -> x0, local copies, waits for them, and re-layouts: 75.3 us -> none  [the longest x4 67.7 us: shards(): jnp.take(padded, neighbors[:, neighbor], axis=0).astype(jnp.float32)]
    psum x1 -> x0, blocking collectives: 70.7 us -> none  [shards(): local_score = lax.psum(partial_sums, 'node') * norm_scale]
    pallas_call x0 -> x5, Pallas kernels: none -> 53.7 us  [the longest x1 25.4 us: layer_of(): pl.pallas_call(functools.partial(layer_kernel, tile, nodes), out_shape=ja...]
    dynamic_slice x49 -> x0, local copies, waits for them, and re-layouts: 34 us -> none  [the longest x32 24.5 us: shards(): partial_sums = lax.map(config_total, layout_ids)]
    reduce_scatter x1 -> x0, waiting for transfers between devices: 28.7 us -> none  [shards(): lax.psum_scatter(group_part.astype(jnp.bfloat16), 'cfg', scatter_dimensio...]
    all_to_all x0 -> x1, blocking collectives: none -> 22.1 us  [shards(): lax.all_to_all(conf_src.reshape(node_count, per_peer, width), 'node', 0,...]
    all_gather x1 -> x0, blocking collectives: 13.6 us -> none  [shards(): grouped = lax.all_gather(conf_src, 'cfg', axis=0, tiled=True)]
  transfers between devices with their start and end apart: 5 -> 15, of which waited for: 4 -> 8; matrix products, arithmetic and copies ran while one was open for 2% -> 1% of each run, Pallas kernels for 0% -> 21%
where the time goes in v1:
time: 145 us
  Pallas kernels  53.7 us (37%)
  starting transfers between devices  29.6 us (20%)
  waiting for transfers between devices  23.5 us (16%)
  blocking collectives  22.1 us (15%)
  local copies, waits for them, and re-layouts  12.9 us (9%)
    pallas_call x1, Pallas kernels, layer_of(): pl.pallas_call(functools.partial(layer_kernel, tile, nodes), out_shape=ja...  25.4 us
    all_to_all x1, blocking collectives, shards(): lax.all_to_all(conf_src.reshape(node_count, per_peer, width), 'node', 0,...  22.1 us
    pallas_call x1, Pallas kernels, scorer_of(): pl.pallas_call(functools.partial(scorer_kernel, groups), out_shape=(jax.S...  16.1 us
    all_to_all x1, waiting for transfers between devices, shards(): got = lax.all_to_all(sent.reshape(devices, 1, 128), both, 0, 0, tiled=True)  10.6 us
    ppermute x6, starting transfers between devices, shift(): return lax.ppermute(value, 'cfg', perm)  10.5 us
    unnamed x40, local copies, waits for them, and re-layouts  10.4 us
    all_to_all x1, starting transfers between devices, shards(): got = lax.all_to_all(sent.reshape(devices, 1, 128), both, 0, 0, tiled=True)  7.02 us
    all_to_all x1, starting transfers between devices, shards(): lax.all_to_all(local_grad.astype(bf16).reshape(node_count, per_peer, widt...  5.55 us
  transfers between devices with their start and end apart: 15, of which 8 were waited for; matrix products, arithmetic and copies ran while one was open for 1% of the time, Pallas kernels for 21%

profile of v1, /device:TPU:2, one launch (start us, length us, event | category | flops | bytes accessed | tf_op | source)
XLA Modules:
  0.0 144.8 jit_solution(3781553641219242307)
XLA Ops:
  0.7 1.1 fusion.15
  1.8 3.4 %collective-permute-start = (bf16[512,256]{1,0:T(8,128)(2,1)S(1)}, bf16[512,256]{1,0:T(8,128)(2,1)S(1)}, u32[]{:S(2)}, u32[]{:S(2)}) collective-permute-start(bf16[512,256]{1,0:T(8,128)(2,1)S(1)} %get-tuple-element.14), channel_id=1, source_target_pairs={{0,1},{1,2},{2,3},{3,4},{4,5},{5,6},{6,7},{7,8},{8,9},{9,10},{10,1... | collective-permute-start | bytes 786440 | tf_op jit(solution)/shard_map/ppermute | solution.py:367
  5.3 2.5 %collective-permute-start.1 = (bf16[512,256]{1,0:T(8,128)(2,1)S(1)}, bf16[512,256]{1,0:T(8,128)(2,1)S(1)}, u32[]{:S(2)}, u32[]{:S(2)}) collective-permute-start(bf16[512,256]{1,0:T(8,128)(2,1)S(1)} %get-tuple-element.13), channel_id=1, source_target_pairs={{1,0},{2,1},{3,2},{4,3},{5,4},{6,5},{7,6},{8,7},{9,8},{10,9},{11,1... | collective-permute-start | bytes 786440 | tf_op jit(solution)/shard_map/ppermute | solution.py:368
  7.7 0.8 copy.20
  8.6 3.2 %collective-permute-done.before = bf16[512,256]{1,0:T(8,128)(2,1)S(1)} collective-permute-done((bf16[512,256]{1,0:T(8,128)(2,1)S(1)}, bf16[512,256]{1,0:T(8,128)(2,1)S(1)}, u32[]{:S(2)}, u32[]{:S(2)}) %collective-permute-start) | collective-permute-done | bytes 262176 | tf_op jit(solution)/shard_map/ppermute | solution.py:367
  11.8 3.1 %collective-permute-done.1.after = bf16[512,256]{1,0:T(8,128)(2,1)S(1)} collective-permute-done((bf16[512,256]{1,0:T(8,128)(2,1)S(1)}, bf16[512,256]{1,0:T(8,128)(2,1)S(1)}, u32[]{:S(2)}, u32[]{:S(2)}) %collective-permute-start.1) | collective-permute-done | bytes 262176 | tf_op jit(solution)/shard_map/ppermute | solution.py:368
  14.9 1.6 %copy-done.1 = bf16[4096,256]{1,0:T(8,128)(2,1)S(1)} copy-done((bf16[4096,256]{1,0:T(8,128)(2,1)S(1)}, bf16[4096,256]{1,0:T(8,128)(2,1)}, u32[]{:S(2)}) %copy-start.1) | copy-done | bytes 2097176
  16.5 0.9 copy-done.3
  17.4 0.9 copy-done.5
  18.3 0.7 copy-done.8
  19.0 0.7 copy-done.10
  19.7 2.9 %conf_rows.1 = bf16[128,256]{1,0:T(8,128)(2,1)S(1)} custom-call(s32[16384]{0:T(1024)S(1)} %bitcast.29, s32[128]{0:T(128)S(1)} %copy-done.10, bf16[512,256]{1,0:T(8,128)(2,1)S(1)} %collective-permute-done.before, bf16[4096,256]{1,0:T(8,128)(2,1)S(1)} %copy-done.1, bf16[512,256]{1,0:T(8,128)(2,1)S(1)} %collective-permute-done.1.after, ...), custom_call_target="tpu_custom_call" | custom-call | flops 33554432 | bytes 6291456 | tf_op jit(solution)/shard_map/conf_rows/pallas_call | solution.py:83
  22.6 22.1 %all_to_all.15 = bf16[32,4,256]{2,1,0:T(4,128)(2,1)S(1)} all-to-all(bf16[32,4,256]{2,1,0:T(4,128)(2,1)S(1)} %reshape.66), channel_id=1, replica_groups=mesh['cfg'=8,'node'=32] {'node'}, dimensions={0} | all-to-all | bytes 131072 | tf_op jit(solution)/shard_map/all_to_all | solution.py:383
  44.8 1.6 %collective-permute-start.2 = (bf16[128,256]{1,0:T(8,128)(2,1)S(1)}, bf16[128,256]{1,0:T(8,128)(2,1)S(1)}, u32[]{:S(2)}, u32[]{:S(2)}) collective-permute-start(bf16[128,256]{1,0:T(8,128)(2,1)S(1)} %reshape.67.refs_0_), channel_id=1, source_target_pairs={{0,64},{32,96},{64,128},{96,160},{128,192},{160,224},{192,0},{224,... | collective-permute-start | bytes 196616 | tf_op jit(solution)/shard_map/ppermute | solution.py:381
  46.5 2.9 %collective-permute-start.3 = (bf16[128,256]{1,0:T(8,128)(2,1)S(1)}, bf16[128,256]{1,0:T(8,128)(2,1)S(1)}, u32[]{:S(2)}, u32[]{:S(2)}) collective-permute-start(bf16[128,256]{1,0:T(8,128)(2,1)S(1)} %reshape.67.refs_0_), channel_id=1, source_target_pairs={{0,128},{32,160},{64,192},{96,224},{128,0},{160,32},{192,64},{224,... | collective-permute-start | bytes 196616 | tf_op jit(solution)/shard_map/ppermute | solution.py:381
  49.4 1.3 collective-permute-start.4
  50.7 0.0 collective-permute-start.5
  50.7 0.0 collective-permute-done.2.refs_1_
  50.7 0.5 collective-permute-start.6
  51.2 1.1 collective-permute-done.3.refs_2_
  52.3 0.0 collective-permute-start.7
  52.3 1.3 collective-permute-done.4.refs_3_
  53.6 0.0 collective-permute-start.8
  53.6 0.0 collective-permute-done.5.refs_4_
  53.7 1.2 collective-permute-done.8.refs_7_
  54.9 0.0 copy-start.18
  54.9 16.1 %scorer.1 = (bf16[8,16,128,256]{3,2,1,0:T(8,128)(2,1)S(1)}, f32[256,128]{1,0:T(8,128)}) custom-call(s32[8]{0:T(128)S(1)} %fusion.9.order, s32[1]{0:T(128)} %bitcast.2.where, bf16[128,256]{1,0:T(8,128)(2,1)S(1)} %reshape.67.refs_0_, bf16[128,256]{1,0:T(8,128)(2,1)S(1)} %collective-permute-done.2.refs_1_, bf16[128,256]{1,0:T(8,128)(2,1)S(1)} %collective-permute-done.3.refs_2_, ...), custom_call_target="tpu_custom_call" | custom-call | flops 6442450944 | bytes 10485760 | tf_op jit(solution)/shard_map/scorer/pallas_call | solution.py:220
  71.0 3.3 %copy-done = bf16[8,16,128,256]{3,2,1,0:T(8,128)(2,1)} copy-done((bf16[8,16,128,256]{3,2,1,0:T(8,128)(2,1)}, bf16[8,16,128,256]{3,2,1,0:T(8,128)(2,1)S(1)}, u32[]{:S(2)}) %copy-start) | copy-done | bytes 8388632
  74.3 7.0 %all-to-all-start.1 = ((f32[256,1,128]{2,1,0:T(1,128)}), f32[256,1,128]{2,1,0:T(1,128)S(1)}, u32[]{:S(2)}, u32[]{:S(2)}) async-start(f32[256,1,128]{2,1,0:T(1,128)} %bitcast.7), calls=%async_computation.1 | async-start | bytes 262144 | tf_op jit(solution)/shard_map/all_to_all | solution.py:406
  81.4 0.9 copy.19.pairs
  82.2 10.6 %all-to-all-done.1 = f32[256,1,128]{2,1,0:T(1,128)S(1)} async-done(((f32[256,1,128]{2,1,0:T(1,128)}), f32[256,1,128]{2,1,0:T(1,128)S(1)}, u32[]{:S(2)}, u32[]{:S(2)}) %all-to-all-start.1) | async-done | bytes 131104 | tf_op jit(solution)/shard_map/all_to_all | solution.py:406
  92.8 0.7 copy-done.17
  93.4 4.9 %ranking.1 = (f32[1,1]{1,0:T(1,128)}, f32[16,256]{1,0:T(8,128)}, bf16[4,128,256]{2,1,0:T(8,128)(2,1)}) custom-call(s32[1]{0:T(128)} %bitcast.2.where, f32[256,128]{1,0:T(8,128)} %bitcast.36, s32[512,2]{1,0:T(8,128)} %copy.19.pairs, bf16[8,16,128,256]{3,2,1,0:T(8,128)(2,1)} %copy-done), custom_call_target="tpu_custom_call" | custom-call | flops 16777216 | bytes 6291456 | tf_op jit(solution)/shard_map/ranking/pallas_call | solution.py:289
  98.3 0.2 collective-permute-start.9
  98.6 4.4 %rest.1 = bf16[4,128,256]{2,1,0:T(8,128)(2,1)} custom-call(f32[16,256]{1,0:T(8,128)} %get-tuple-element.11.coef, bf16[8,16,128,256]{3,2,1,0:T(8,128)(2,1)} %copy-done), custom_call_target="tpu_custom_call" | custom-call | flops 16777216 | bytes 6291456 | tf_op jit(solution)/shard_map/rest/pallas_call | solution.py:322
  102.9 1.0 fusion.3
  103.9 0.7 collective-permute-start.10
  104.6 1.8 %collective-permute-start.11 = (bf16[128,256]{1,0:T(8,128)(2,1)S(1)}, bf16[128,256]{1,0:T(8,128)(2,1)S(1)}, u32[]{:S(2)}, u32[]{:S(2)}) collective-permute-start(bf16[128,256]{1,0:T(8,128)(2,1)S(1)} %get-tuple-element.17), channel_id=1, source_target_pairs={{0,128},{32,160},{64,192},{96,224},{128,0},{160,32},{192,64},{224,... | collective-permute-start | bytes 196616 | tf_op jit(solution)/shard_map/ppermute | solution.py:381
  106.4 2.1 %collective-permute-start.12 = (bf16[128,256]{1,0:T(8,128)(2,1)S(1)}, bf16[128,256]{1,0:T(8,128)(2,1)S(1)}, u32[]{:S(2)}, u32[]{:S(2)}) collective-permute-start(bf16[128,256]{1,0:T(8,128)(2,1)S(1)} %get-tuple-element.16), channel_id=1, source_target_pairs={{0,192},{32,224},{64,0},{96,32},{128,64},{160,96},{192,128},{224,1... | collective-permute-start | bytes 196616 | tf_op jit(solution)/shard_map/ppermute | solution.py:381
  108.5 2.4 %collective-permute-done.10 = bf16[128,256]{1,0:T(8,128)(2,1)S(1)} collective-permute-done((bf16[128,256]{1,0:T(8,128)(2,1)S(1)}, bf16[128,256]{1,0:T(8,128)(2,1)S(1)}, u32[]{:S(2)}, u32[]{:S(2)}) %collective-permute-start.10) | collective-permute-done | bytes 65568 | tf_op jit(solution)/shard_map/ppermute | solution.py:381
  110.9 0.0 collective-permute-done.11
  110.9 0.6 collective-permute-done.12
  111.5 1.0 convolution_convert_fusion
  112.5 0.7 reshape.74
  113.2 5.5 %all-to-all-start.2 = ((bf16[32,4,256]{2,1,0:T(4,128)(2,1)}), bf16[32,4,256]{2,1,0:T(4,128)(2,1)S(1)}, u32[]{:S(2)}, u32[]{:S(2)}) async-start(bf16[32,4,256]{2,1,0:T(4,128)(2,1)} %reshape.74), calls=%async_computation.2 | async-start | bytes 131072 | tf_op jit(solution)/shard_map/all_to_all | solution.py:423
  118.8 25.4 %graph_layer.1 = bf16[4096,256]{1,0:T(8,128)(2,1)} custom-call(s32[16384]{0:T(1024)S(1)} %bitcast.30, bf16[512,256]{1,0:T(8,128)(2,1)S(1)} %collective-permute-done.before, bf16[4096,256]{1,0:T(8,128)(2,1)S(1)} %copy-done.2, bf16[512,256]{1,0:T(8,128)(2,1)S(1)} %collective-permute-done.1.after, bf16[256,256]{1,0:T(8,128)(2,1)S(1)} %copy-done.4, ...), custom_call_target="tpu_custom_call" | custom-call | flops 1073741824 | bytes 67108864 | tf_op jit(solution)/shard_map/graph_layer/pallas_call | solution.py:139
  144.1 0.0 all-to-all-done.2
  144.1 0.7 reshape.78
  (36 shorter events, 0.1 us)
Async XLA Ops:
  0.6 54.3 %copy-start.14 = (f32[256]{0:T(256)S(1)}, f32[256]{0:T(256)}, u32[]{:S(2)}) copy-start(f32[256]{0:T(256)} %param.23) | copy-start | bytes 3076
  0.6 54.2 %copy-start.15 = (f32[256]{0:T(256)S(1)}, f32[256]{0:T(256)}, u32[]{:S(2)}) copy-start(f32[256]{0:T(256)} %param.25) | copy-start | bytes 3076
  0.7 54.2 %copy-start.16 = (f32[256]{0:T(256)S(1)}, f32[256]{0:T(256)}, u32[]{:S(2)}) copy-start(f32[256]{0:T(256)} %param.26) | copy-start | bytes 3076
  0.7 54.2 %copy-start.12 = (s32[16,1024]{1,0:T(8,128)S(1)}, s32[16,1024]{1,0:T(8,128)}, u32[]{:S(2)}) copy-start(s32[16,1024]{1,0:T(8,128)} %refs_8_.1) | copy-start | bytes 196612
  0.7 54.2 %copy-start.7 = (bf16[256,256]{1,0:T(8,128)(2,1)S(1)}, bf16[256,256]{1,0:T(8,128)(2,1)}, u32[]{:S(2)}) copy-start(bf16[256,256]{1,0:T(8,128)(2,1)} %refs_9_.1) | copy-start | bytes 393220
  0.7 54.2 %copy-start.13 = (bf16[128,256]{1,0:T(8,128)(2,1)S(1)}, bf16[128,256]{1,0:T(8,128)(2,1)}, u32[]{:S(2)}) copy-start(bf16[128,256]{1,0:T(8,128)(2,1)} %refs_10_.1) | copy-start | bytes 196612
  0.7 54.2 %copy-start.11 = (bf16[256,256]{1,0:T(8,128)(2,1)S(1)}, bf16[256,256]{1,0:T(8,128)(2,1)}, u32[]{:S(2)}) copy-start(bf16[256,256]{1,0:T(8,128)(2,1)} %refs_12_.1) | copy-start | bytes 393220
  1.8 9.9 %collective-permute-start = (bf16[512,256]{1,0:T(8,128)(2,1)S(1)}, bf16[512,256]{1,0:T(8,128)(2,1)S(1)}, u32[]{:S(2)}, u32[]{:S(2)}) collective-permute-start(bf16[512,256]{1,0:T(8,128)(2,1)S(1)} %get-tuple-element.14), channel_id=1, source_target_pairs={{0,1},{1,2},{2,3},{3,4},{4,5},{5,6},{6,7},{7,8},{8,9},{9,10},{10,1... | collective-permute-start | bytes 786440 | tf_op jit(solution)/shard_map/ppermute | solution.py:367
  5.3 9.7 %collective-permute-start.1 = (bf16[512,256]{1,0:T(8,128)(2,1)S(1)}, bf16[512,256]{1,0:T(8,128)(2,1)S(1)}, u32[]{:S(2)}, u32[]{:S(2)}) collective-permute-start(bf16[512,256]{1,0:T(8,128)(2,1)S(1)} %get-tuple-element.13), channel_id=1, source_target_pairs={{1,0},{2,1},{3,2},{4,3},{5,4},{6,5},{7,6},{8,7},{9,8},{10,9},{11,1... | collective-permute-start | bytes 786440 | tf_op jit(solution)/shard_map/ppermute | solution.py:368
  14.9 1.6 %copy-start.1 = (bf16[4096,256]{1,0:T(8,128)(2,1)S(1)}, bf16[4096,256]{1,0:T(8,128)(2,1)}, u32[]{:S(2)}) copy-start(bf16[4096,256]{1,0:T(8,128)(2,1)} %feats.3) | copy-start | bytes 6291460
  16.5 0.9 copy-start.3
  17.4 0.9 copy-start.5
  18.3 0.7 copy-start.8
  19.0 0.7 copy-start.10
  44.8 5.9 %collective-permute-start.2 = (bf16[128,256]{1,0:T(8,128)(2,1)S(1)}, bf16[128,256]{1,0:T(8,128)(2,1)S(1)}, u32[]{:S(2)}, u32[]{:S(2)}) collective-permute-start(bf16[128,256]{1,0:T(8,128)(2,1)S(1)} %reshape.67.refs_0_), channel_id=1, source_target_pairs={{0,64},{32,96},{64,128},{96,160},{128,192},{160,224},{192,0},{224,... | collective-permute-start | bytes 196616 | tf_op jit(solution)/shard_map/ppermute | solution.py:381
  46.5 5.9 %collective-permute-start.3 = (bf16[128,256]{1,0:T(8,128)(2,1)S(1)}, bf16[128,256]{1,0:T(8,128)(2,1)S(1)}, u32[]{:S(2)}, u32[]{:S(2)}) collective-permute-start(bf16[128,256]{1,0:T(8,128)(2,1)S(1)} %reshape.67.refs_0_), channel_id=1, source_target_pairs={{0,128},{32,160},{64,192},{96,224},{128,0},{160,32},{192,64},{224,... | collective-permute-start | bytes 196616 | tf_op jit(solution)/shard_map/ppermute | solution.py:381
  49.4 4.3 %collective-permute-start.4 = (bf16[128,256]{1,0:T(8,128)(2,1)S(1)}, bf16[128,256]{1,0:T(8,128)(2,1)S(1)}, u32[]{:S(2)}, u32[]{:S(2)}) collective-permute-start(bf16[128,256]{1,0:T(8,128)(2,1)S(1)} %reshape.67.refs_0_), channel_id=1, source_target_pairs={{0,192},{32,224},{64,0},{96,32},{128,64},{160,96},{192,128},{224,1... | collective-permute-start | bytes 196616 | tf_op jit(solution)/shard_map/ppermute | solution.py:381
  50.7 2.9 %collective-permute-start.5 = (bf16[128,256]{1,0:T(8,128)(2,1)S(1)}, bf16[128,256]{1,0:T(8,128)(2,1)S(1)}, u32[]{:S(2)}, u32[]{:S(2)}) collective-permute-start(bf16[128,256]{1,0:T(8,128)(2,1)S(1)} %reshape.67.refs_0_), channel_id=1, source_target_pairs={{0,32},{32,0},{64,96},{96,64},{128,160},{160,128},{192,224},{224,1... | collective-permute-start | bytes 196616 | tf_op jit(solution)/shard_map/ppermute | solution.py:387
  50.7 3.0 %collective-permute-start.6 = (bf16[128,256]{1,0:T(8,128)(2,1)S(1)}, bf16[128,256]{1,0:T(8,128)(2,1)S(1)}, u32[]{:S(2)}, u32[]{:S(2)}) collective-permute-start(bf16[128,256]{1,0:T(8,128)(2,1)S(1)} %collective-permute-done.2.refs_1_), channel_id=1, source_target_pairs={{0,32},{32,0},{64,96},{96,64},{128,160},{160,128},{192,224},{224,1... | collective-permute-start | bytes 196616 | tf_op jit(solution)/shard_map/ppermute | solution.py:387
  52.3 1.4 collective-permute-start.7
  53.6 1.3 collective-permute-start.8
  54.9 26.4 %copy-start.18 = (s32[512,2]{0,1:T(2,128)S(1)}, s32[512,2]{0,1:T(2,128)}, u32[]{:S(2)}) copy-start(s32[512,2]{0,1:T(2,128)} %param.27) | copy-start | bytes 12292
  71.0 3.3 %copy-start = (bf16[8,16,128,256]{3,2,1,0:T(8,128)(2,1)}, bf16[8,16,128,256]{3,2,1,0:T(8,128)(2,1)S(1)}, u32[]{:S(2)}) copy-start(bf16[8,16,128,256]{3,2,1,0:T(8,128)(2,1)S(1)} %get-tuple-element.9.grads) | copy-start | bytes 25165828
  74.3 18.5 %all-to-all-start.1 = ((f32[256,1,128]{2,1,0:T(1,128)}), f32[256,1,128]{2,1,0:T(1,128)S(1)}, u32[]{:S(2)}, u32[]{:S(2)}) async-start(f32[256,1,128]{2,1,0:T(1,128)} %bitcast.7), calls=%async_computation.1 | async-start | bytes 262144 | tf_op jit(solution)/shard_map/all_to_all | solution.py:406
  92.8 0.7 copy-start.17
  98.3 4.6 %collective-permute-start.9 = (bf16[4,128,256]{2,1,0:T(8,128)(2,1)}, bf16[4,128,256]{2,1,0:T(8,128)(2,1)S(1)}, u32[]{:S(2)}, u32[]{:S(2)}) collective-permute-start(bf16[4,128,256]{2,1,0:T(8,128)(2,1)} %get-tuple-element.12), channel_id=1, source_target_pairs={{0,32},{32,0},{64,96},{96,64},{128,160},{160,128},{192,224},{224,1... | collective-permute-start | bytes 786440 | tf_op jit(solution)/shard_map/ppermute | solution.py:410
  98.5 20.2 %copy-start.2 = (bf16[4096,256]{1,0:T(8,128)(2,1)S(1)}, bf16[4096,256]{1,0:T(8,128)(2,1)}, u32[]{:S(2)}) copy-start(bf16[4096,256]{1,0:T(8,128)(2,1)} %feats.3) | copy-start | bytes 6291460
  98.5 20.2 %copy-start.4 = (bf16[256,256]{1,0:T(8,128)(2,1)S(1)}, bf16[256,256]{1,0:T(8,128)(2,1)}, u32[]{:S(2)}) copy-start(bf16[256,256]{1,0:T(8,128)(2,1)} %sw.3) | copy-start | bytes 393220
  98.5 20.2 %copy-start.6 = (bf16[256,256]{1,0:T(8,128)(2,1)S(1)}, bf16[256,256]{1,0:T(8,128)(2,1)}, u32[]{:S(2)}) copy-start(bf16[256,256]{1,0:T(8,128)(2,1)} %nw.3) | copy-start | bytes 393220
  98.6 20.2 %copy-start.9 = (f32[256]{0:T(256)S(1)}, f32[256]{0:T(256)}, u32[]{:S(2)}) copy-start(f32[256]{0:T(256)} %param.18) | copy-start | bytes 3076
  103.9 7.0 %collective-permute-start.10 = (bf16[128,256]{1,0:T(8,128)(2,1)S(1)}, bf16[128,256]{1,0:T(8,128)(2,1)S(1)}, u32[]{:S(2)}, u32[]{:S(2)}) collective-permute-start(bf16[128,256]{1,0:T(8,128)(2,1)S(1)} %get-tuple-element.15), channel_id=1, source_target_pairs={{0,64},{32,96},{64,128},{96,160},{128,192},{160,224},{192,0},{224,... | collective-permute-start | bytes 196616 | tf_op jit(solution)/shard_map/ppermute | solution.py:381
  104.6 6.3 %collective-permute-start.11 = (bf16[128,256]{1,0:T(8,128)(2,1)S(1)}, bf16[128,256]{1,0:T(8,128)(2,1)S(1)}, u32[]{:S(2)}, u32[]{:S(2)}) collective-permute-start(bf16[128,256]{1,0:T(8,128)(2,1)S(1)} %get-tuple-element.17), channel_id=1, source_target_pairs={{0,128},{32,160},{64,192},{96,224},{128,0},{160,32},{192,64},{224,... | collective-permute-start | bytes 196616 | tf_op jit(solution)/shard_map/ppermute | solution.py:381
  106.4 5.1 %collective-permute-start.12 = (bf16[128,256]{1,0:T(8,128)(2,1)S(1)}, bf16[128,256]{1,0:T(8,128)(2,1)S(1)}, u32[]{:S(2)}, u32[]{:S(2)}) collective-permute-start(bf16[128,256]{1,0:T(8,128)(2,1)S(1)} %get-tuple-element.16), channel_id=1, source_target_pairs={{0,192},{32,224},{64,0},{96,32},{128,64},{160,96},{192,128},{224,1... | collective-permute-start | bytes 196616 | tf_op jit(solution)/shard_map/ppermute | solution.py:381
  113.2 31.0 %all-to-all-start.2 = ((bf16[32,4,256]{2,1,0:T(4,128)(2,1)}), bf16[32,4,256]{2,1,0:T(4,128)(2,1)S(1)}, u32[]{:S(2)}, u32[]{:S(2)}) async-start(bf16[32,4,256]{2,1,0:T(4,128)(2,1)} %reshape.74), calls=%async_computation.2 | async-start | bytes 131072 | tf_op jit(solution)/shard_map/all_to_all | solution.py:423

commit v2 on v1

v2 whole, which is shorter than its diff:
```python
import functools
import math

import jax
import jax.numpy as jnp
from jax import lax
from jax.experimental import pallas as pl
from jax.experimental.pallas import tpu as pltpu
from jax.sharding import PartitionSpec as P

HALO = 512
f32 = jnp.float32
bf16 = jnp.bfloat16
VMEM = pl.BlockSpec(memory_space=pltpu.VMEM)
SMEM = pl.BlockSpec(memory_space=pltpu.SMEM)
HBM = pl.BlockSpec(memory_space=pltpu.HBM)


def in_hbm(value):
    return pltpu.with_memory_space_constraint(value, pltpu.HBM)


def half_silu(half):
    tanh = jnp.tanh(half)
    scaled = half * tanh
    return half + scaled, tanh, scaled


def twice_slope(half, tanh, scaled):
    inner = 1.0 + half - scaled
    return inner + tanh * inner


def put_rows(table, first, source):
    rows = source.shape[0]
    value = source[...].astype(f32)
    table[pl.ds(2 * first, rows, stride=2), :] = value[:, :128]
    table[pl.ds(2 * first + 1, rows, stride=2), :] = value[:, 128:]


def pair_at(table, at):
    return table[pl.ds(pl.multiple_of(at, 2), 2), :]


def table_kernel(feats, table):
    rows = feats.shape[0]
    put_rows(table, HALO + pl.multiple_of(pl.program_id(0) * rows, rows), feats)


def table_of(feats):
    nodes, width = feats.shape
    tile = 512
    return pl.pallas_call(
        table_kernel,
        out_shape=jax.ShapeDtypeStruct((2 * (nodes + 2 * HALO), 128), f32),
        grid=(nodes // tile,),
        in_specs=[pl.BlockSpec((tile, width), lambda i: (i, 0))],
        out_specs=VMEM,
        cost_estimate=pl.CostEstimate(flops=1 << 20, transcendentals=0, bytes_accessed=6 << 20),
        compiler_params=pltpu.CompilerParams(vmem_limit_bytes=16 << 20),
        name="window_rows",
    )(feats)


def layer_rows(own_left, own_right, left, right, sw, nw, bias):
    pre = jnp.dot(own_left, sw[:128, :], preferred_element_type=f32)
    pre += jnp.dot(own_right, sw[128:, :], preferred_element_type=f32)
    pre += jnp.dot(left, nw[:128, :], preferred_element_type=f32)
    pre += jnp.dot(right, nw[128:, :], preferred_element_type=f32)
    return half_silu(0.5 * (pre + bias[...]))[0].astype(bf16)


def conf_kernel(
    nbrs, picks, before, after, sw_hbm, nw_hbm, bias_hbm, given, out, table, own, acc, sw, nw, bias, sems
):
    copies = [
        pltpu.make_async_copy(source, target, sems.at[i])
        for i, (source, target) in enumerate(((sw_hbm, sw), (nw_hbm, nw), (bias_hbm, bias)))
    ]
    for copy in copies:
        copy.start()
    window = table.shape[0] // 2
    put_rows(table, 0, before)
    put_rows(table, window - HALO, after)
    count = picks.shape[0]
    own3 = own.reshape(count, 2, 128)
    acc3 = acc.reshape(count, 2, 128)

    def body(block, carry):
        values = []
        for j in range(8):
            g = picks[block * 8 + j]
            at = (g >> 7) * 512 + (g & 127)
            near = [pair_at(table, nbrs[at + 128 * k]) for k in range(4)]
            values.append((pair_at(table, 2 * (HALO + g)), (near[0] + near[1]) + (near[2] + near[3])))
        for j in range(8):
            own3[block * 8 + j], acc3[block * 8 + j] = values[j]
        return carry

    lax.fori_loop(0, count // 8, body, 0)
    halves = [ref[pl.ds(side, count, stride=2), :] for ref in (own, acc) for side in (0, 1)]
    for copy in copies:
        copy.wait()
    out[...] = layer_rows(
        halves[0].astype(bf16),
        halves[1].astype(bf16),
        (halves[2] * 0.25).astype(bf16),
        (halves[3] * 0.25).astype(bf16),
        sw,
        nw,
        bias,
    )


def conf_rows_of(nbrs, picks, before, after, sw, nw, bias, table):
    count = picks.shape[0]
    width = before.shape[1]
    return pl.pallas_call(
        conf_kernel,
        out_shape=(
            jax.ShapeDtypeStruct((count, width), bf16),
            jax.ShapeDtypeStruct(table.shape, f32),
        ),
        in_specs=[SMEM, SMEM, VMEM, VMEM] + [HBM] * 3 + [VMEM],
        out_specs=(VMEM, VMEM),
        input_output_aliases={7: 1},
        scratch_shapes=[
            pltpu.VMEM((2 * count, 128), f32),
            pltpu.VMEM((2 * count, 128), f32),
            pltpu.VMEM(sw.shape, bf16),
            pltpu.VMEM(nw.shape, bf16),
            pltpu.VMEM(bias.shape, f32),
            pltpu.SemaphoreType.DMA((3,)),
        ],
        cost_estimate=pl.CostEstimate(
            flops=4 * count * width * width, transcendentals=0, bytes_accessed=6 << 20
        ),
        compiler_params=pltpu.CompilerParams(vmem_limit_bytes=16 << 20),
        name="conf_rows",
    )(nbrs, picks, before, after, in_hbm(sw), in_hbm(nw), in_hbm(bias), table)


def layer_kernel(nbrs, before, feats, after, own, sw, nw, bias, *refs):
    out, table, acc = refs[-3:]
    tile = own.shape[0]
    nodes = feats.shape[0]

    @pl.when(pl.program_id(0) == 0)
    def _():
        put_rows(table, 0, before)
        for start in range(0, nodes, 512):
            put_rows(table, HALO + start, feats.at[start : start + 512, :])
        put_rows(table, HALO + nodes, after)

    acc3 = acc.reshape(tile, 2, 128)

    def body(block, carry):
        values = []
        for j in range(128):
            near = [pair_at(table, nbrs[block * 512 + (128 * k + j)]) for k in range(4)]
            values.append((near[0] + near[1]) + (near[2] + near[3]))
        for j in range(128):
            acc3[block * 128 + j] = values[j]
        return carry

    lax.fori_loop(0, tile // 128, body, 0)
    rows = own[...]
    out[...] = layer_rows(
        rows[:, :128],
        rows[:, 128:],
        (acc[pl.ds(0, tile, stride=2), :] * 0.25).astype(bf16),
        (acc[pl.ds(1, tile, stride=2), :] * 0.25).astype(bf16),
        sw,
        nw,
        bias,
    )


def layer_of(first, steps, nbrs, before, feats, after, sw, nw, bias, given):
    nodes, width = feats.shape
    tile = 1024
    ahead = [] if given is None else [given]
    return pl.pallas_call(
        layer_kernel,
        out_shape=jax.ShapeDtypeStruct((nodes, width), bf16),
        grid=(steps,),
        in_specs=[
            pl.BlockSpec((4 * tile,), lambda i: (first + i,), memory_space=pltpu.SMEM),
            VMEM,
            VMEM,
            VMEM,
            pl.BlockSpec((tile, width), lambda i: (first + i, 0)),
            VMEM,
            VMEM,
            VMEM,
        ]
        + [HBM] * len(ahead),
        out_specs=pl.BlockSpec((tile, width), lambda i: (first + i, 0)),
        input_output_aliases={8: 0} if ahead else {},
        scratch_shapes=[
            pltpu.VMEM((2 * (nodes + 2 * HALO), 128), f32),
            pltpu.VMEM((2 * tile, 128), f32),
        ],
        cost_estimate=pl.CostEstimate(
            flops=steps * 4 * tile * width * width, transcendentals=0, bytes_accessed=steps << 23
        ),
        compiler_params=pltpu.CompilerParams(vmem_limit_bytes=24 << 20),
        name="graph_layer",
    )(nbrs, before, feats, after, feats, sw, nw, bias, *ahead)


def place_of(group, turn):
    return (((group >> 1) + 4 - (turn & 3)) & 3) * 2 + ((group ^ (turn >> 2)) & 1)


def scorer_kernel(groups, where, *refs):
    xs, refs = refs[:groups], refs[groups:]
    ids, join, table, jbias, mid, mbias, weight, grads_hbm, sent = refs[:9]
    base, tabh, midh, back, total, grads, sems = refs[9:]
    step = pl.program_id(0)
    slot = step & 1
    chunk = xs[0].shape[0]
    configs = ids.shape[0]
    layouts = table.shape[0]
    one = jnp.asarray(1.0, bf16)

    @pl.when(step == 0)
    def _():
        for i in range(groups):
            base[i] = 0.5 * (
                jnp.dot(xs[i][...], join[...], preferred_element_type=f32) + jbias[...]
            )
        tabh[...] = (table[...].astype(f32) * 0.5).astype(bf16)
        middle = mid[...].astype(f32)
        midh[...] = (middle * 0.5).astype(bf16)
        back[...] = jnp.transpose(middle * (weight[...] * 0.25)).astype(bf16)
        total[...] = jnp.zeros_like(total)

    def copy_of(turn, place):
        return pltpu.make_async_copy(grads.at[place], grads_hbm.at[turn], sems.at[place])

    @pl.when(step >= 2)
    def _():
        copy_of(step - 2, slot).wait()

    columns = jnp.transpose(ids[...].astype(f32))
    lanes = lax.broadcasted_iota(jnp.int32, (chunk, layouts), 1).astype(f32)
    rows = base[step]
    some = 8
    for first in range(0, configs, some):
        picks = jnp.concatenate(
            [
                jnp.where(columns[:, k : k + 1] == lanes, 1.0, 0.0).astype(bf16)
                for k in range(first, first + some)
            ],
            axis=0,
        )
        half = jnp.dot(picks, tabh[...], preferred_element_type=f32)
        half = (half + jnp.concatenate([rows] * some, axis=0)).astype(bf16)
        tanh = jnp.tanh(half)
        act = half + half * tanh
        slope = (one + tanh) * (one + half * (one - tanh))
        outer = jnp.dot(act, midh[...], preferred_element_type=f32)
        outer = (outer + 0.5 * mbias[...]).astype(bf16)
        tanh2 = jnp.tanh(outer)
        act2 = (outer + outer * tanh2).astype(f32)
        slope2 = (one + tanh2) * (one + outer * (one - tanh2))
        for q in range(some):
            part = act2[q * chunk : (q + 1) * chunk, :]
            total[first + q : first + q + 1, :] += jnp.sum(part, axis=0, keepdims=True)
        grad = jnp.dot(slope2, back[...], preferred_element_type=f32).astype(bf16) * slope
        for q in range(some):
            grads[slot, first + q] = grad[q * chunk : (q + 1) * chunk, :]

    copy_of(step, slot).start()

    @pl.when(step == groups - 1)
    def _():
        scores = jnp.sum(total[...] * weight[...], axis=1, keepdims=True)
        lane = lax.broadcasted_iota(jnp.int32, (configs, 128), 1)
        sub = lax.broadcasted_iota(jnp.int32, (configs, 128), 0)
        spread = jnp.where(lane == sub + where[0] * configs, scores, 0.0)
        sent[...] = jnp.broadcast_to(jnp.sum(spread, axis=0, keepdims=True), sent.shape)
        copy_of(step - 1, 1 - slot).wait()
        copy_of(step, slot).wait()


def scorer_of(where, xs, ids, join, table, jbias, mid, mbias, weight, devices):
    groups = len(xs)
    configs = ids.shape[0]
    chunk, width = xs[0].shape
    hidden = join.shape[1]
    return pl.pallas_call(
        functools.partial(scorer_kernel, groups),
        out_shape=(
            pltpu.HBM((groups, configs, chunk, hidden), bf16),
            jax.ShapeDtypeStruct((devices, 128), f32),
        ),
        grid_spec=pltpu.PrefetchScalarGridSpec(
            num_scalar_prefetch=1,
            grid=(groups,),
            in_specs=[VMEM] * groups
            + [pl.BlockSpec((configs, chunk), lambda i, where: (0, place_of(where[0], i)))]
            + [VMEM] * 6,
            out_specs=(HBM, VMEM),
            scratch_shapes=[
                pltpu.VMEM((groups, chunk, hidden), f32),
                pltpu.VMEM(table.shape, bf16),
                pltpu.VMEM(mid.shape, bf16),
                pltpu.VMEM(mid.shape, bf16),
                pltpu.VMEM((configs, hidden), f32),
                pltpu.VMEM((2, configs, chunk, hidden), bf16),
                pltpu.SemaphoreType.DMA((2,)),
            ],
        ),
        cost_estimate=pl.CostEstimate(
            flops=6 * groups * configs * chunk * width * width,
            transcendentals=2 * groups * configs * chunk * width,
            bytes_accessed=10 << 20,
        ),
        compiler_params=pltpu.CompilerParams(vmem_limit_bytes=30 << 20),
        name="scorer",
    )(where, *xs, ids, join, table, jbias, mid, mbias, weight)


def weighted(coef, grads, out):
    configs, chunk, hidden = grads.shape
    some = 32
    for start in range(0, chunk, some):
        rows = grads[0, start : start + some, :].astype(f32) * coef[0:1, :]
        for k in range(1, configs):
            rows = rows + grads[k, start : start + some, :].astype(f32) * coef[k : k + 1, :]
        out[start : start + some, :] = rows.astype(bf16)


def fetches(grads_hbm, grads, sems, first):
    half = grads.shape[0]
    return [
        pltpu.make_async_copy(
            grads_hbm.at[first + (half - d) % half], grads.at[d], sems.at[d]
        )
        for d in range(half)
    ]


def ranking_kernel(scale, where, got, pairs, grads_hbm, loss, coef, out, column, grads, sems):
    half, configs, chunk, hidden = grads.shape
    copies = fetches(grads_hbm, grads, sems, half)
    for copy in copies:
        copy.start()
    score = jnp.sum(got[...], axis=0, keepdims=True) * scale
    lane = lax.broadcasted_iota(jnp.int32, (128, 128), 1)
    sub = lax.broadcasted_iota(jnp.int32, (128, 128), 0)
    score = jnp.sum(jnp.where(lane == sub, score, 0.0), axis=1, keepdims=True)
    count = pairs.shape[1]
    ids = lax.broadcasted_iota(jnp.int32, (128, count), 0)
    second = jnp.where(pairs[1:2, :] == ids, 1.0, 0.0)
    signed = second - jnp.where(pairs[0:1, :] == ids, 1.0, 0.0)
    gap = jnp.sum(signed * score, axis=0, keepdims=True)
    fade = jnp.exp(-jnp.abs(gap))
    soft = jnp.maximum(gap, 0.0) + jnp.log1p(fade)
    loss[...] = jnp.sum(soft, axis=1, keepdims=True) * (1.0 / count)
    slope = jnp.where(gap >= 0.0, 1.0, fade) / (1.0 + fade)
    grad = jnp.sum(slope * signed, axis=1, keepdims=True) * (65536.0 * scale / count)
    column[...] = jnp.broadcast_to(grad, column.shape)
    coef[...] = column[pl.ds(pl.multiple_of(where[0] * configs, configs), configs), :]
    for d in range(half):
        copies[d].wait()
        weighted(coef, grads.at[d], out.at[d])


def ranking_of(scale, where, got, pairs, grads):
    groups, configs, chunk, hidden = grads.shape
    half = groups // 2
    return pl.pallas_call(
        functools.partial(ranking_kernel, scale),
        out_shape=(
            jax.ShapeDtypeStruct((1, 1), f32),
            jax.ShapeDtypeStruct((configs, hidden), f32),
            jax.ShapeDtypeStruct((half, chunk, hidden), bf16),
        ),
        in_specs=[SMEM, VMEM, VMEM, HBM],
        out_specs=(VMEM, VMEM, VMEM),
        scratch_shapes=[
            pltpu.VMEM((128, hidden), f32),
            pltpu.VMEM((half, configs, chunk, hidden), bf16),
            pltpu.SemaphoreType.DMA((half,)),
        ],
        cost_estimate=pl.CostEstimate(flops=1 << 24, transcendentals=0, bytes_accessed=6 << 20),
        compiler_params=pltpu.CompilerParams(vmem_limit_bytes=16 << 20),
        name="ranking",
    )(where, got, pairs, in_hbm(grads))


def rest_kernel(coef, grads_hbm, out, grads, sems):
    copies = fetches(grads_hbm, grads, sems, 0)
    for copy in copies:
        copy.start()
    for d, copy in enumerate(copies):
        copy.wait()
        weighted(coef, grads.at[d], out.at[d])


def rest_of(coef, grads):
    groups, configs, chunk, hidden = grads.shape
    half = groups // 2
    return pl.pallas_call(
        rest_kernel,
        out_shape=jax.ShapeDtypeStruct((half, chunk, hidden), bf16),
        in_specs=[VMEM, HBM],
        out_specs=VMEM,
        scratch_shapes=[
            pltpu.VMEM((half, configs, chunk, hidden), bf16),
            pltpu.SemaphoreType.DMA((half,)),
        ],
        cost_estimate=pl.CostEstimate(flops=1 << 24, transcendentals=0, bytes_accessed=6 << 20),
        compiler_params=pltpu.CompilerParams(vmem_limit_bytes=16 << 20),
        name="rest",
    )(coef, in_hbm(grads))


def shards(
    node_feats,
    neighbors,
    self_weight,
    neighbor_weight,
    sage_bias,
    conf_index,
    layout_ids,
    join_weight,
    layout_table,
    join_bias,
    mid_weight,
    mid_bias,
    score_weight,
    config_pairs,
):
    both = ("cfg", "node")
    devices = lax.axis_size(both)
    node_count = lax.axis_size("node")
    group_count = lax.axis_size("cfg")
    rings = group_count // 2
    local_conf = conf_index.shape[0]
    width = node_feats.shape[1]
    per_peer = local_conf // node_count
    scale = 1.0 / math.sqrt(layout_ids.shape[1] * node_count)
    group = lax.axis_index("cfg")

    up = [(i, i + 1) for i in range(devices - 1)]
    down = [(i + 1, i) for i in range(devices - 1)]
    before = lax.ppermute(node_feats[-HALO:], both, up)
    after = lax.ppermute(node_feats[:HALO], both, down)
    nodes, near = neighbors.shape
    nbrs = (2 * neighbors).T.reshape(near, nodes // 128, 128).transpose(1, 0, 2).reshape(-1)
    bias = sage_bias.reshape(1, -1)
    hold = lax.optimization_barrier

    table = table_of(node_feats)
    conf_src, _ = conf_rows_of(
        nbrs, conf_index, before, after, self_weight, neighbor_weight, bias, table
    )

    def layer(first, steps, given):
        return layer_of(
            first,
            steps,
            nbrs,
            before,
            node_feats,
            after,
            self_weight,
            neighbor_weight,
            bias,
            given,
        )

    swap = [(i, i ^ 1) for i in range(group_count)]

    def shift(value, by):
        perm = [(i, (i // 2 + by) % rings * 2 + i % 2) for i in range(group_count)]
        return lax.ppermute(value, "cfg", perm)

    mine = lax.all_to_all(
        conf_src.reshape(node_count, per_peer, width), "node", 0, 0, tiled=True
    )
    embed = layer(0, 1, None)
    mine, embed = hold((mine, embed))
    mine = mine.reshape(local_conf, width)
    xs = [mine] + [shift(mine, by) for by in range(1, rings)]
    xs = xs + [lax.ppermute(x, "cfg", swap) for x in xs]
    where = group.reshape(1)

    grads, sent = scorer_of(
        where,
        xs,
        layout_ids,
        join_weight,
        layout_table,
        join_bias.reshape(1, -1),
        mid_weight,
        mid_bias.reshape(1, -1),
        score_weight.reshape(1, -1),
        devices,
    )
    sent, embed = hold((sent, embed))
    got = lax.all_to_all(sent.reshape(devices, 1, 128), both, 0, 0, tiled=True)
    embed = layer(1, 1, embed)
    got, embed = hold((got, embed))
    loss, coef, away = ranking_of(scale, where, got.reshape(devices, 128), config_pairs.T, grads)
    came = lax.ppermute(away, "cfg", swap)
    kept = rest_of(coef, grads)
    sums = [kept[d].astype(f32) + came[d].astype(f32) for d in range(rings)]
    arrived = [shift(sums[d].astype(bf16), d) for d in range(1, rings)]
    row_grad = sums[0]
    for part in arrived:
        row_grad = row_grad + part.astype(f32)
    local_grad = lax.dot_general(
        row_grad.astype(bf16),
        join_weight,
        (((1,), (1,)), ((), ())),
        preferred_element_type=f32,
    )
    local_grad, embed = hold((local_grad.astype(bf16), embed))
    conf_grad = lax.all_to_all(
        local_grad.reshape(node_count, per_peer, width), "node", 0, 0, tiled=True
    )
    embed = layer(2, 2, embed)
    conf_grad = conf_grad.astype(f32).reshape(local_conf, width)
    return (embed, loss.reshape(()), conf_grad)


def solution(mesh):
    split = P(("cfg", "node"), None)
    placed = (split, split, P(), P(), P(), P(("cfg", "node")), P("cfg", "node")) + (P(),) * 7
    return jax.shard_map(
        shards,
        mesh=mesh,
        in_specs=placed,
        out_specs=(split, P(), split),
        check_vma=False,
    )
```

time: 145 us -> 120 us (0.83)
  blocking collectives: 22.1 us -> 0 us
  starting transfers between devices: 29.6 us -> 44.4 us
  Pallas kernels: 53.7 us -> 45.1 us
  local copies, waits for them, and re-layouts: 12.9 us -> 4.72 us
    all_to_all x1 -> x0, blocking collectives: 22.1 us -> none  [shards(): lax.all_to_all(conf_src.reshape(node_count, per_peer, width), 'node', 0,...]
    all_to_all x1 -> x2, starting transfers between devices: 5.55 us -> 19.3 us  [the longest x1 13.9 us: shards(): lax.all_to_all(conf_src.reshape(node_count, per_peer, width), 'node', 0,...]
    unnamed x40 -> x28, local copies, waits for them, and re-layouts: 10.4 us -> 1.66 us
    all_to_all x1, waiting for transfers between devices: 10.6 us -> 5.45 us  [shards(): got = lax.all_to_all(sent.reshape(devices, 1, 128), both, 0, 0, tiled=True)]
    ppermute x6, waiting for transfers between devices: 5.38 us -> 10.4 us  [shift(): return lax.ppermute(value, 'cfg', perm)]
    pallas_call x3 -> x6, Pallas kernels: 44.4 us -> 40 us  [the longest x3 21.9 us: layer_of(): pl.pallas_call(layer_kernel, out_shape=jax.ShapeDtypeStruct((nodes, width...]
    all_to_all x1 -> x2, waiting for transfers between devices: 0.01 us -> 2.64 us  [the longest x1 2.64 us: shards(): lax.all_to_all(conf_src.reshape(node_count, per_peer, width), 'node', 0,...]
    pallas_call x1, Pallas kernels: 4.91 us -> 2.73 us  [ranking_of(): pl.pallas_call(functools.partial(ranking_kernel, scale), out_shape=(jax.S...]
  transfers between devices with their start and end apart: 15 -> 16, of which waited for: 8 -> 12; matrix products, arithmetic and copies ran while one was open for 1% -> 1% of each run, Pallas kernels for 21% -> 21%
where the time goes in v2:
time: 120 us
  Pallas kernels  45.1 us (38%)
  starting transfers between devices  44.4 us (37%)
  waiting for transfers between devices  23.6 us (20%)
  local copies, waits for them, and re-layouts  4.72 us (4%)
    pallas_call x3, Pallas kernels, layer_of(): pl.pallas_call(layer_kernel, out_shape=jax.ShapeDtypeStruct((nodes, width...  21.9 us
    pallas_call x1, Pallas kernels, scorer_of(): pl.pallas_call(functools.partial(scorer_kernel, groups), out_shape=(pltpu...  14.9 us
    all_to_all x1, starting transfers between devices, shards(): lax.all_to_all(conf_src.reshape(node_count, per_peer, width), 'node', 0,...  13.9 us
    ppermute x6, waiting for transfers between devices, shift(): return lax.ppermute(value, 'cfg', perm)  10.4 us
    ppermute x6, starting transfers between devices, shift(): return lax.ppermute(value, 'cfg', perm)  10.4 us
    all_to_all x1, starting transfers between devices, shards(): got = lax.all_to_all(sent.reshape(devices, 1, 128), both, 0, 0, tiled=True)  8.36 us
    all_to_all x1, waiting for transfers between devices, shards(): got = lax.all_to_all(sent.reshape(devices, 1, 128), both, 0, 0, tiled=True)  5.45 us
    all_to_all x1, starting transfers between devices, shards(): lax.all_to_all(local_grad.reshape(node_count, per_peer, width), 'node', 0...  5.36 us
  transfers between devices with their start and end apart: 16, of which 12 were waited for; matrix products, arithmetic and copies ran while one was open for 1% of the time, Pallas kernels for 21%

profile of v2, /device:TPU:2, one launch (start us, length us, event | category | flops | bytes accessed | tf_op | source)
XLA Modules:
  0.0 119.9 jit_solution(16789312243462183804)
XLA Ops:
  0.6 1.1 fusion.9
  1.7 4.2 %collective-permute-start.1 = (bf16[512,256]{1,0:T(8,128)(2,1)S(1)}, bf16[512,256]{1,0:T(8,128)(2,1)S(1)}, u32[]{:S(2)}, u32[]{:S(2)}) collective-permute-start(bf16[512,256]{1,0:T(8,128)(2,1)S(1)} %get-tuple-element.31), channel_id=1, source_target_pairs={{1,0},{2,1},{3,2},{4,3},{5,4},{6,5},{7,6},{8,7},{9,8},{10,9},{11,1... | collective-permute-start | bytes 786440 | tf_op jit(solution)/shard_map/ppermute | solution.py:452
  5.9 1.9 %collective-permute-start = (bf16[512,256]{1,0:T(8,128)(2,1)S(1)}, bf16[512,256]{1,0:T(8,128)(2,1)S(1)}, u32[]{:S(2)}, u32[]{:S(2)}) collective-permute-start(bf16[512,256]{1,0:T(8,128)(2,1)S(1)} %get-tuple-element.32), channel_id=1, source_target_pairs={{0,1},{1,2},{2,3},{3,4},{4,5},{5,6},{6,7},{7,8},{8,9},{9,10},{10,1... | collective-permute-start | bytes 786440 | tf_op jit(solution)/shard_map/ppermute | solution.py:451
  7.8 0.9 broadcast_multiply_fusion
  8.7 0.0 copy-start
  8.7 1.6 %copy-done = bf16[4096,256]{1,0:T(8,128)(2,1)S(1)} copy-done((bf16[4096,256]{1,0:T(8,128)(2,1)S(1)}, bf16[4096,256]{1,0:T(8,128)(2,1)}, u32[]{:S(2)}) %copy-start) | copy-done | bytes 2097176
  10.3 0.4 window_rows.1.given
  10.7 1.0 collective-permute-done.1.after
  11.6 2.5 %collective-permute-done.before = bf16[512,256]{1,0:T(8,128)(2,1)S(1)} collective-permute-done((bf16[512,256]{1,0:T(8,128)(2,1)S(1)}, bf16[512,256]{1,0:T(8,128)(2,1)S(1)}, u32[]{:S(2)}, u32[]{:S(2)}) %collective-permute-start) | collective-permute-done | bytes 262176 | tf_op jit(solution)/shard_map/ppermute | solution.py:451
  14.2 0.0 copy-start.5
  14.2 2.8 %conf_rows.1 = (bf16[128,256]{1,0:T(8,128)(2,1)S(1)}, f32[10240,128]{1,0:T(8,128)S(1)}) custom-call(s32[16384]{0:T(1024)S(1)} %bitcast.34, s32[128]{0:T(128)S(1)} %copy-done.7, bf16[512,256]{1,0:T(8,128)(2,1)S(1)} %collective-permute-done.before, bf16[512,256]{1,0:T(8,128)(2,1)S(1)} %collective-permute-done.1.after, ...), custom_call_target="tpu_custom_call", output_to_operand_aliasing={{1}: (7, {})} | custom-call | flops 33554432 | bytes 6291456 | tf_op jit(solution)/shard_map/conf_rows/pallas_call | solution.py:118
  17.0 0.7 reshape.70
  17.7 13.9 %all-to-all-start = ((bf16[32,4,256]{2,1,0:T(4,128)(2,1)}), bf16[32,4,256]{2,1,0:T(4,128)(2,1)S(1)}, u32[]{:S(2)}, u32[]{:S(2)}) async-start(bf16[32,4,256]{2,1,0:T(4,128)(2,1)} %reshape.70), calls=%async_computation | async-start | bytes 131072 | tf_op jit(solution)/shard_map/all_to_all | solution.py:483
  31.6 0.0 copy-start.4
  31.6 0.0 copy-start.8
  31.6 0.0 copy-start.9
  31.7 0.0 copy-start.10
  31.7 0.0 copy-start.13
  31.7 6.0 %graph_layer.3.refs_0_ = bf16[4096,256]{1,0:T(8,128)(2,1)} custom-call(s32[16384]{0:T(1024)S(1)} %bitcast.35, bf16[512,256]{1,0:T(8,128)(2,1)S(1)} %collective-permute-done.before, bf16[4096,256]{1,0:T(8,128)(2,1)S(1)} %copy-done.1, bf16[512,256]{1,0:T(8,128)(2,1)S(1)} %collective-permute-done.1.after, bf16[4096,256]{1,0:T(8,128)(2,1)S(1)} %copy-done.1, ...), custom_call_target="tpu_custom_call" | custom-call | flops 268435456 | bytes 8388608 | tf_op jit(solution)/shard_map/graph_layer/pallas_call | solution.py:183
  37.7 2.6 %all-to-all-done = bf16[32,4,256]{2,1,0:T(4,128)(2,1)S(1)} async-done(((bf16[32,4,256]{2,1,0:T(4,128)(2,1)}), bf16[32,4,256]{2,1,0:T(4,128)(2,1)S(1)}, u32[]{:S(2)}, u32[]{:S(2)}) %all-to-all-start) | async-done | bytes 65568 | tf_op jit(solution)/shard_map/all_to_all | solution.py:483
  40.3 5.2 %collective-permute-start.4 = (bf16[128,256]{1,0:T(8,128)(2,1)S(1)}, bf16[128,256]{1,0:T(8,128)(2,1)S(1)}, u32[]{:S(2)}, u32[]{:S(2)}) collective-permute-start(bf16[128,256]{1,0:T(8,128)(2,1)S(1)} %reshape.71.refs_0_), channel_id=1, source_target_pairs={{0,192},{32,224},{64,0},{96,32},{128,64},{160,96},{192,128},{224,1... | collective-permute-start | bytes 196616 | tf_op jit(solution)/shard_map/ppermute | solution.py:481
  45.5 0.3 collective-permute-start.3
  45.8 1.0 collective-permute-start.2
  46.7 0.6 collective-permute-done.4.refs_3_
  47.4 3.9 %collective-permute-done.3.refs_2_ = bf16[128,256]{1,0:T(8,128)(2,1)S(1)} collective-permute-done((bf16[128,256]{1,0:T(8,128)(2,1)S(1)}, bf16[128,256]{1,0:T(8,128)(2,1)S(1)}, u32[]{:S(2)}, u32[]{:S(2)}) %collective-permute-start.3) | collective-permute-done | bytes 65568 | tf_op jit(solution)/shard_map/ppermute | solution.py:481
  51.3 0.7 collective-permute-done.2.refs_1_
  52.1 0.6 collective-permute-done.7.refs_6_
  52.7 0.9 collective-permute-done.6.refs_5_
  53.7 14.9 %scorer.1 = (bf16[8,16,128,256]{3,2,1,0:T(8,128)(2,1)}, f32[256,128]{1,0:T(8,128)}) custom-call(s32[1]{0:T(128)} %bitcast.5.where, bf16[128,256]{1,0:T(8,128)(2,1)S(1)} %reshape.71.refs_0_, bf16[128,256]{1,0:T(8,128)(2,1)} %collective-permute-done.2.refs_1_, bf16[128,256]{1,0:T(8,128)(2,1)S(1)} %collective-permute-done.3.refs_2_, ...), custom_call_target="tpu_custom_call" | custom-call | flops 6442450944 | bytes 10485760 | tf_op jit(solution)/shard_map/scorer/pallas_call | solution.py:293
  68.6 8.4 %all-to-all-start.1 = ((f32[256,1,128]{2,1,0:T(1,128)}), f32[256,1,128]{2,1,0:T(1,128)S(1)}, u32[]{:S(2)}, u32[]{:S(2)}) async-start(f32[256,1,128]{2,1,0:T(1,128)} %bitcast.13), calls=%async_computation.1 | async-start | bytes 262144 | tf_op jit(solution)/shard_map/all_to_all | solution.py:506
  76.9 0.0 copy-start.6
  77.0 6.0 %graph_layer.4.refs_0_ = bf16[4096,256]{1,0:T(8,128)(2,1)} custom-call(s32[16384]{0:T(1024)S(1)} %bitcast.36, bf16[512,256]{1,0:T(8,128)(2,1)S(1)} %collective-permute-done.before, bf16[4096,256]{1,0:T(8,128)(2,1)S(1)} %copy-done.1, bf16[512,256]{1,0:T(8,128)(2,1)S(1)} %collective-permute-done.1.after, ...), custom_call_target="tpu_custom_call", output_to_operand_aliasing={{}: (8, {})} | custom-call | flops 268435456 | bytes 8388608 | tf_op jit(solution)/shard_map/graph_layer/pallas_call | solution.py:183
  82.9 5.5 %all-to-all-done.1 = f32[256,1,128]{2,1,0:T(1,128)S(1)} async-done(((f32[256,1,128]{2,1,0:T(1,128)}), f32[256,1,128]{2,1,0:T(1,128)S(1)}, u32[]{:S(2)}, u32[]{:S(2)}) %all-to-all-start.1) | async-done | bytes 131104 | tf_op jit(solution)/shard_map/all_to_all | solution.py:506
  88.4 2.7 %ranking.1 = (f32[1,1]{1,0:T(1,128)}, f32[16,256]{1,0:T(8,128)S(1)}, bf16[4,128,256]{2,1,0:T(8,128)(2,1)S(1)}) custom-call(s32[1]{0:T(128)} %bitcast.5.where, f32[256,128]{1,0:T(8,128)S(1)} %bitcast.38, s32[2,512]{1,0:T(2,128)S(1)} %bitcast.43, bf16[8,16,128,256]{3,2,1,0:T(8,128)(2,1)} %get-tuple-element.24.grads_hbm), custom_call_target="tpu_custom_call" | custom-call | flops 16777216 | bytes 6291456 | tf_op jit(solution)/shard_map/ranking/pallas_call | solution.py:375
  91.1 0.3 collective-permute-start.9
  91.4 2.4 %rest.1 = bf16[4,128,256]{2,1,0:T(8,128)(2,1)S(1)} custom-call(f32[16,256]{1,0:T(8,128)S(1)} %get-tuple-element.25.coef, bf16[8,16,128,256]{3,2,1,0:T(8,128)(2,1)} %get-tuple-element.24.grads_hbm), custom_call_target="tpu_custom_call" | custom-call | flops 16777216 | bytes 6291456 | tf_op jit(solution)/shard_map/rest/pallas_call | solution.py:407
  93.8 0.1 fusion.3
  93.9 0.7 collective-permute-start.10
  94.6 2.6 %collective-permute-start.12 = (bf16[128,256]{1,0:T(8,128)(2,1)S(1)}, bf16[128,256]{1,0:T(8,128)(2,1)S(1)}, u32[]{:S(2)}, u32[]{:S(2)}) collective-permute-start(bf16[128,256]{1,0:T(8,128)(2,1)S(1)} %get-tuple-element.34), channel_id=1, source_target_pairs={{0,192},{32,224},{64,0},{96,32},{128,64},{160,96},{192,128},{224,1... | collective-permute-start | bytes 196616 | tf_op jit(solution)/shard_map/ppermute | solution.py:481
  97.2 0.7 collective-permute-start.11
  97.9 1.6 %collective-permute-done.10 = bf16[128,256]{1,0:T(8,128)(2,1)S(1)} collective-permute-done((bf16[128,256]{1,0:T(8,128)(2,1)S(1)}, bf16[128,256]{1,0:T(8,128)(2,1)S(1)}, u32[]{:S(2)}, u32[]{:S(2)}) %collective-permute-start.10) | collective-permute-done | bytes 65568 | tf_op jit(solution)/shard_map/ppermute | solution.py:481
  99.5 0.7 collective-permute-done.12
  100.2 2.8 %collective-permute-done.11 = bf16[128,256]{1,0:T(8,128)(2,1)S(1)} collective-permute-done((bf16[128,256]{1,0:T(8,128)(2,1)S(1)}, bf16[128,256]{1,0:T(8,128)(2,1)S(1)}, u32[]{:S(2)}, u32[]{:S(2)}) %collective-permute-start.11) | collective-permute-done | bytes 65568 | tf_op jit(solution)/shard_map/ppermute | solution.py:481
  103.0 0.2 convolution_convert_fusion
  103.2 0.7 reshape.78
  103.8 5.4 %all-to-all-start.2 = ((bf16[32,4,256]{2,1,0:T(4,128)(2,1)}), bf16[32,4,256]{2,1,0:T(4,128)(2,1)S(1)}, u32[]{:S(2)}, u32[]{:S(2)}) async-start(bf16[32,4,256]{2,1,0:T(4,128)(2,1)} %reshape.78), calls=%async_computation.2 | async-start | bytes 131072 | tf_op jit(solution)/shard_map/all_to_all | solution.py:524
  109.2 10.0 %graph_layer.5 = bf16[4096,256]{1,0:T(8,128)(2,1)} custom-call(s32[16384]{0:T(1024)S(1)} %bitcast.37, bf16[512,256]{1,0:T(8,128)(2,1)S(1)} %collective-permute-done.before, bf16[4096,256]{1,0:T(8,128)(2,1)S(1)} %copy-done.1, bf16[512,256]{1,0:T(8,128)(2,1)S(1)} %collective-permute-done.1.after, ...), custom_call_target="tpu_custom_call", output_to_operand_aliasing={{}: (8, {})} | custom-call | flops 536870912 | bytes 16777216 | tf_op jit(solution)/shard_map/graph_layer/pallas_call | solution.py:183
  119.2 0.7 reshape.82
  (28 shorter events, 0.1 us)
Async XLA Ops:
  1.7 9.9 %collective-permute-start.1 = (bf16[512,256]{1,0:T(8,128)(2,1)S(1)}, bf16[512,256]{1,0:T(8,128)(2,1)S(1)}, u32[]{:S(2)}, u32[]{:S(2)}) collective-permute-start(bf16[512,256]{1,0:T(8,128)(2,1)S(1)} %get-tuple-element.31), channel_id=1, source_target_pairs={{1,0},{2,1},{3,2},{4,3},{5,4},{6,5},{7,6},{8,7},{9,8},{10,9},{11,1... | collective-permute-start | bytes 786440 | tf_op jit(solution)/shard_map/ppermute | solution.py:452
  5.9 8.3 %collective-permute-start = (bf16[512,256]{1,0:T(8,128)(2,1)S(1)}, bf16[512,256]{1,0:T(8,128)(2,1)S(1)}, u32[]{:S(2)}, u32[]{:S(2)}) collective-permute-start(bf16[512,256]{1,0:T(8,128)(2,1)S(1)} %get-tuple-element.32), channel_id=1, source_target_pairs={{0,1},{1,2},{2,3},{3,4},{4,5},{5,6},{6,7},{7,8},{8,9},{9,10},{10,1... | collective-permute-start | bytes 786440 | tf_op jit(solution)/shard_map/ppermute | solution.py:451
  8.7 1.6 %copy-start = (bf16[4096,256]{1,0:T(8,128)(2,1)S(1)}, bf16[4096,256]{1,0:T(8,128)(2,1)}, u32[]{:S(2)}) copy-start(bf16[4096,256]{1,0:T(8,128)(2,1)} %own.5) | copy-start | bytes 6291460
  10.3 3.9 %copy-start.7 = (s32[128]{0:T(128)S(1)}, s32[128]{0:T(128)}, u32[]{:S(2)}) copy-start(s32[128]{0:T(128)} %picks.1) | copy-start | bytes 1540
  14.2 17.4 %copy-start.1 = (bf16[4096,256]{1,0:T(8,128)(2,1)S(1)}, bf16[4096,256]{1,0:T(8,128)(2,1)}, u32[]{:S(2)}) copy-start(bf16[4096,256]{1,0:T(8,128)(2,1)} %own.5) | copy-start | bytes 6291460
  14.2 17.4 %copy-start.2 = (bf16[256,256]{1,0:T(8,128)(2,1)S(1)}, bf16[256,256]{1,0:T(8,128)(2,1)}, u32[]{:S(2)}) copy-start(bf16[256,256]{1,0:T(8,128)(2,1)} %sw.5) | copy-start | bytes 393220
  14.2 17.4 %copy-start.3 = (bf16[256,256]{1,0:T(8,128)(2,1)S(1)}, bf16[256,256]{1,0:T(8,128)(2,1)}, u32[]{:S(2)}) copy-start(bf16[256,256]{1,0:T(8,128)(2,1)} %nw.5) | copy-start | bytes 393220
  14.2 17.4 %copy-start.5 = (f32[256]{0:T(256)S(1)}, f32[256]{0:T(256)}, u32[]{:S(2)}) copy-start(f32[256]{0:T(256)} %param.18) | copy-start | bytes 3076
  17.7 22.6 %all-to-all-start = ((bf16[32,4,256]{2,1,0:T(4,128)(2,1)}), bf16[32,4,256]{2,1,0:T(4,128)(2,1)S(1)}, u32[]{:S(2)}, u32[]{:S(2)}) async-start(bf16[32,4,256]{2,1,0:T(4,128)(2,1)} %reshape.70), calls=%async_computation | async-start | bytes 131072 | tf_op jit(solution)/shard_map/all_to_all | solution.py:483
  31.6 22.0 %copy-start.4 = (bf16[256,256]{1,0:T(8,128)(2,1)S(1)}, bf16[256,256]{1,0:T(8,128)(2,1)}, u32[]{:S(2)}) copy-start(bf16[256,256]{1,0:T(8,128)(2,1)} %refs_9_.1) | copy-start | bytes 393220
  31.6 22.0 %copy-start.8 = (bf16[256,256]{1,0:T(8,128)(2,1)S(1)}, bf16[256,256]{1,0:T(8,128)(2,1)}, u32[]{:S(2)}) copy-start(bf16[256,256]{1,0:T(8,128)(2,1)} %refs_12_.1) | copy-start | bytes 393220
  31.6 22.0 %copy-start.9 = (s32[16,1024]{1,0:T(8,128)S(1)}, s32[16,1024]{1,0:T(8,128)}, u32[]{:S(2)}) copy-start(s32[16,1024]{1,0:T(8,128)} %refs_8_.1) | copy-start | bytes 196612
  31.7 22.0 %copy-start.10 = (bf16[128,256]{1,0:T(8,128)(2,1)S(1)}, bf16[128,256]{1,0:T(8,128)(2,1)}, u32[]{:S(2)}) copy-start(bf16[128,256]{1,0:T(8,128)(2,1)} %refs_10_.1) | copy-start | bytes 196612
  31.7 22.0 %copy-start.11 = (f32[256]{0:T(256)S(1)}, f32[256]{0:T(256)}, u32[]{:S(2)}) copy-start(f32[256]{0:T(256)} %param.23) | copy-start | bytes 3076
  31.7 22.0 %copy-start.12 = (f32[256]{0:T(256)S(1)}, f32[256]{0:T(256)}, u32[]{:S(2)}) copy-start(f32[256]{0:T(256)} %param.25) | copy-start | bytes 3076
  31.7 22.0 %copy-start.13 = (f32[256]{0:T(256)S(1)}, f32[256]{0:T(256)}, u32[]{:S(2)}) copy-start(f32[256]{0:T(256)} %param.26) | copy-start | bytes 3076
  40.3 7.1 %collective-permute-start.4 = (bf16[128,256]{1,0:T(8,128)(2,1)S(1)}, bf16[128,256]{1,0:T(8,128)(2,1)S(1)}, u32[]{:S(2)}, u32[]{:S(2)}) collective-permute-start(bf16[128,256]{1,0:T(8,128)(2,1)S(1)} %reshape.71.refs_0_), channel_id=1, source_target_pairs={{0,192},{32,224},{64,0},{96,32},{128,64},{160,96},{192,128},{224,1... | collective-permute-start | bytes 196616 | tf_op jit(solution)/shard_map/ppermute | solution.py:481
  45.5 5.8 %collective-permute-start.3 = (bf16[128,256]{1,0:T(8,128)(2,1)S(1)}, bf16[128,256]{1,0:T(8,128)(2,1)S(1)}, u32[]{:S(2)}, u32[]{:S(2)}) collective-permute-start(bf16[128,256]{1,0:T(8,128)(2,1)S(1)} %reshape.71.refs_0_), channel_id=1, source_target_pairs={{0,128},{32,160},{64,192},{96,224},{128,0},{160,32},{192,64},{224,... | collective-permute-start | bytes 196616 | tf_op jit(solution)/shard_map/ppermute | solution.py:481
  45.8 6.3 %collective-permute-start.2 = (bf16[128,256]{1,0:T(8,128)(2,1)S(1)}, bf16[128,256]{1,0:T(8,128)(2,1)}, u32[]{:S(2)}, u32[]{:S(2)}) collective-permute-start(bf16[128,256]{1,0:T(8,128)(2,1)S(1)} %reshape.71.refs_0_), channel_id=1, source_target_pairs={{0,64},{32,96},{64,128},{96,160},{128,192},{160,224},{192,0},{224,... | collective-permute-start | bytes 196616 | tf_op jit(solution)/shard_map/ppermute | solution.py:481
  46.7 5.3 %collective-permute-start.5 = (bf16[128,256]{1,0:T(8,128)(2,1)S(1)}, bf16[128,256]{1,0:T(8,128)(2,1)}, u32[]{:S(2)}, u32[]{:S(2)}) collective-permute-start(bf16[128,256]{1,0:T(8,128)(2,1)S(1)} %reshape.71.refs_0_), channel_id=1, source_target_pairs={{0,32},{32,0},{64,96},{96,64},{128,160},{160,128},{192,224},{224,1... | collective-permute-start | bytes 196616 | tf_op jit(solution)/shard_map/ppermute | solution.py:490
  47.4 4.7 %collective-permute-start.8 = (bf16[128,256]{1,0:T(8,128)(2,1)S(1)}, bf16[128,256]{1,0:T(8,128)(2,1)}, u32[]{:S(2)}, u32[]{:S(2)}) collective-permute-start(bf16[128,256]{1,0:T(8,128)(2,1)S(1)} %collective-permute-done.4.refs_3_), channel_id=1, source_target_pairs={{0,32},{32,0},{64,96},{96,64},{128,160},{160,128},{192,224},{224,1... | collective-permute-start | bytes 196616 | tf_op jit(solution)/shard_map/ppermute | solution.py:490
  51.3 1.4 %collective-permute-start.7 = (bf16[128,256]{1,0:T(8,128)(2,1)S(1)}, bf16[128,256]{1,0:T(8,128)(2,1)}, u32[]{:S(2)}, u32[]{:S(2)}) collective-permute-start(bf16[128,256]{1,0:T(8,128)(2,1)S(1)} %collective-permute-done.3.refs_2_), channel_id=1, source_target_pairs={{0,32},{32,0},{64,96},{96,64},{128,160},{160,128},{192,224},{224,1... | collective-permute-start | bytes 196616 | tf_op jit(solution)/shard_map/ppermute | solution.py:490
  52.0 1.6 %collective-permute-start.6 = (bf16[128,256]{1,0:T(8,128)(2,1)}, bf16[128,256]{1,0:T(8,128)(2,1)}, u32[]{:S(2)}, u32[]{:S(2)}) collective-permute-start(bf16[128,256]{1,0:T(8,128)(2,1)} %collective-permute-done.2.refs_1_), channel_id=1, source_target_pairs={{0,32},{32,0},{64,96},{96,64},{128,160},{160,128},{192,224},{224,1... | collective-permute-start | bytes 196616 | tf_op jit(solution)/shard_map/ppermute | solution.py:490
  68.6 19.8 %all-to-all-start.1 = ((f32[256,1,128]{2,1,0:T(1,128)}), f32[256,1,128]{2,1,0:T(1,128)S(1)}, u32[]{:S(2)}, u32[]{:S(2)}) async-start(f32[256,1,128]{2,1,0:T(1,128)} %bitcast.13), calls=%async_computation.1 | async-start | bytes 262144 | tf_op jit(solution)/shard_map/all_to_all | solution.py:506
  76.9 11.4 %copy-start.6 = (s32[512,2]{0,1:T(2,128)S(1)}, s32[512,2]{0,1:T(2,128)}, u32[]{:S(2)}) copy-start(s32[512,2]{0,1:T(2,128)} %param.27) | copy-start | bytes 12292
  91.1 2.7 %collective-permute-start.9 = (bf16[4,128,256]{2,1,0:T(8,128)(2,1)S(1)}, bf16[4,128,256]{2,1,0:T(8,128)(2,1)S(1)}, u32[]{:S(2)}, u32[]{:S(2)}) collective-permute-start(bf16[4,128,256]{2,1,0:T(8,128)(2,1)S(1)} %get-tuple-element.26), channel_id=1, source_target_pairs={{0,32},{32,0},{64,96},{96,64},{128,160},{160,128},{192,224},{224,1... | collective-permute-start | bytes 786440 | tf_op jit(solution)/shard_map/ppermute | solution.py:510
  93.9 5.6 %collective-permute-start.10 = (bf16[128,256]{1,0:T(8,128)(2,1)S(1)}, bf16[128,256]{1,0:T(8,128)(2,1)S(1)}, u32[]{:S(2)}, u32[]{:S(2)}) collective-permute-start(bf16[128,256]{1,0:T(8,128)(2,1)S(1)} %get-tuple-element.33), channel_id=1, source_target_pairs={{0,64},{32,96},{64,128},{96,160},{128,192},{160,224},{192,0},{224,... | collective-permute-start | bytes 196616 | tf_op jit(solution)/shard_map/ppermute | solution.py:481
  94.6 5.6 %collective-permute-start.12 = (bf16[128,256]{1,0:T(8,128)(2,1)S(1)}, bf16[128,256]{1,0:T(8,128)(2,1)S(1)}, u32[]{:S(2)}, u32[]{:S(2)}) collective-permute-start(bf16[128,256]{1,0:T(8,128)(2,1)S(1)} %get-tuple-element.34), channel_id=1, source_target_pairs={{0,192},{32,224},{64,0},{96,32},{128,64},{160,96},{192,128},{224,1... | collective-permute-start | bytes 196616 | tf_op jit(solution)/shard_map/ppermute | solution.py:481
  97.2 5.8 %collective-permute-start.11 = (bf16[128,256]{1,0:T(8,128)(2,1)S(1)}, bf16[128,256]{1,0:T(8,128)(2,1)S(1)}, u32[]{:S(2)}, u32[]{:S(2)}) collective-permute-start(bf16[128,256]{1,0:T(8,128)(2,1)S(1)} %get-tuple-element.35), channel_id=1, source_target_pairs={{0,128},{32,160},{64,192},{96,224},{128,0},{160,32},{192,64},{224,... | collective-permute-start | bytes 196616 | tf_op jit(solution)/shard_map/ppermute | solution.py:481
  103.8 15.4 %all-to-all-start.2 = ((bf16[32,4,256]{2,1,0:T(4,128)(2,1)}), bf16[32,4,256]{2,1,0:T(4,128)(2,1)S(1)}, u32[]{:S(2)}, u32[]{:S(2)}) async-start(bf16[32,4,256]{2,1,0:T(4,128)(2,1)} %reshape.78), calls=%async_computation.2 | async-start | bytes 131072 | tf_op jit(solution)/shard_map/all_to_all | solution.py:524

commit v3 on v2

--- a/solution.py
+++ b/solution.py
@@ -36,6 +36,28 @@
     value = source[...].astype(f32)
     table[pl.ds(2 * first, rows, stride=2), :] = value[:, :128]
     table[pl.ds(2 * first + 1, rows, stride=2), :] = value[:, 128:]
+
+
+def put_halo(table, spot, peers, near, far):
+    before, after = near
+    first, last = far
+    end = table.shape[0] // 2 - HALO
+
+    @pl.when(spot[0] == 0)
+    def _():
+        put_rows(table, 0, first)
+
+    @pl.when(spot[0] != 0)
+    def _():
+        put_rows(table, 0, before)
+
+    @pl.when(spot[0] == peers - 1)
+    def _():
+        put_rows(table, end, last)
+
+    @pl.when(spot[0] != peers - 1)
+    def _():
+        put_rows(table, end, after)
 
 
 def pair_at(table, at):
@@ -70,18 +92,16 @@
     return half_silu(0.5 * (pre + bias[...]))[0].astype(bf16)
 
 
-def conf_kernel(
-    nbrs, picks, before, after, sw_hbm, nw_hbm, bias_hbm, given, out, table, own, acc, sw, nw, bias, sems
-):
+def conf_kernel(peers, spot, nbrs, picks, *refs):
+    near, far, refs = refs[:2], refs[2:4], refs[4:]
+    sw_hbm, nw_hbm, bias_hbm, given, out, table, own, acc, sw, nw, bias, sems = refs
     copies = [
         pltpu.make_async_copy(source, target, sems.at[i])
         for i, (source, target) in enumerate(((sw_hbm, sw), (nw_hbm, nw), (bias_hbm, bias)))
     ]
     for copy in copies:
         copy.start()
-    window = table.shape[0] // 2
-    put_rows(table, 0, before)
-    put_rows(table, window - HALO, after)
+    put_halo(table, spot, peers, near, far)
     count = picks.shape[0]
     own3 = own.reshape(count, 2, 128)
     acc3 = acc.reshape(count, 2, 128)
@@ -112,18 +132,18 @@
     )
 
 
-def conf_rows_of(nbrs, picks, before, after, sw, nw, bias, table):
+def conf_rows_of(peers, spot, nbrs, picks, rims, sw, nw, bias, table):
     count = picks.shape[0]
-    width = before.shape[1]
+    width = sw.shape[0]
     return pl.pallas_call(
-        conf_kernel,
+        functools.partial(conf_kernel, peers),
         out_shape=(
             jax.ShapeDtypeStruct((count, width), bf16),
             jax.ShapeDtypeStruct(table.shape, f32),
         ),
-        in_specs=[SMEM, SMEM, VMEM, VMEM] + [HBM] * 3 + [VMEM],
+        in_specs=[SMEM] * 3 + [VMEM] * 4 + [HBM] * 3 + [VMEM],
         out_specs=(VMEM, VMEM),
-        input_output_aliases={7: 1},
+        input_output_aliases={10: 1},
         scratch_shapes=[
             pltpu.VMEM((2 * count, 128), f32),
             pltpu.VMEM((2 * count, 128), f32),
@@ -137,20 +157,20 @@
         ),
         compiler_params=pltpu.CompilerParams(vmem_limit_bytes=16 << 20),
         name="conf_rows",
-    )(nbrs, picks, before, after, in_hbm(sw), in_hbm(nw), in_hbm(bias), table)
-
-
-def layer_kernel(nbrs, before, feats, after, own, sw, nw, bias, *refs):
+    )(spot, nbrs, picks, *rims, in_hbm(sw), in_hbm(nw), in_hbm(bias), table)
+
+
+def layer_kernel(peers, spot, nbrs, *refs):
+    near, far, (feats, own, sw, nw, bias) = refs[:2], refs[2:4], refs[4:9]
     out, table, acc = refs[-3:]
     tile = own.shape[0]
     nodes = feats.shape[0]
 
     @pl.when(pl.program_id(0) == 0)
     def _():
-        put_rows(table, 0, before)
+        put_halo(table, spot, peers, near, far)
         for start in range(0, nodes, 512):
             put_rows(table, HALO + start, feats.at[start : start + 512, :])
-        put_rows(table, HALO + nodes, after)
 
     acc3 = acc.reshape(tile, 2, 128)
 
@@ -176,19 +196,20 @@
     )
 
 
-def layer_of(first, steps, nbrs, before, feats, after, sw, nw, bias, given):
+def layer_of(first, steps, peers, spot, nbrs, rims, feats, sw, nw, bias, given):
     nodes, width = feats.shape
     tile = 1024
     ahead = [] if given is None else [given]
     return pl.pallas_call(
-        layer_kernel,
+        functools.partial(layer_kernel, peers),
         out_shape=jax.ShapeDtypeStruct((nodes, width), bf16),
         grid=(steps,),
         in_specs=[
+            SMEM,
             pl.BlockSpec((4 * tile,), lambda i: (first + i,), memory_space=pltpu.SMEM),
-            VMEM,
-            VMEM,
-            VMEM,
+        ]
+        + [VMEM] * 5
+        + [
             pl.BlockSpec((tile, width), lambda i: (first + i, 0)),
             VMEM,
             VMEM,
@@ -196,7 +217,7 @@
         ]
         + [HBM] * len(ahead),
         out_specs=pl.BlockSpec((tile, width), lambda i: (first + i, 0)),
-        input_output_aliases={8: 0} if ahead else {},
+        input_output_aliases={11: 0} if ahead else {},
         scratch_shapes=[
             pltpu.VMEM((2 * (nodes + 2 * HALO), 128), f32),
             pltpu.VMEM((2 * tile, 128), f32),
@@ -206,7 +227,7 @@
         ),
         compiler_params=pltpu.CompilerParams(vmem_limit_bytes=24 << 20),
         name="graph_layer",
-    )(nbrs, before, feats, after, feats, sw, nw, bias, *ahead)
+    )(spot, nbrs, *rims, feats, feats, sw, nw, bias, *ahead)
 
 
 def place_of(group, turn):
@@ -446,10 +467,16 @@
     scale = 1.0 / math.sqrt(layout_ids.shape[1] * node_count)
     group = lax.axis_index("cfg")
 
-    up = [(i, i + 1) for i in range(devices - 1)]
-    down = [(i + 1, i) for i in range(devices - 1)]
-    before = lax.ppermute(node_feats[-HALO:], both, up)
-    after = lax.ppermute(node_feats[:HALO], both, down)
+    up = [(i, (i + 1) % node_count) for i in range(node_count)]
+    down = [(i, j) for j, i in up]
+    before = lax.ppermute(node_feats[-HALO:], "node", up)
+    after = lax.ppermute(node_feats[:HALO], "node", down)
+    starts = [c * node_count for c in range(group_count)]
+    first = lax.ppermute(before, both, list(zip(starts[:-1], starts[1:])))
+    ends = [start + node_count - 1 for start in starts]
+    last = lax.ppermute(after, both, list(zip(ends[1:], ends[:-1])))
+    rims = (before, after, first, last)
+    spot = lax.axis_index("node").reshape(1)
     nodes, near = neighbors.shape
     nbrs = (2 * neighbors).T.reshape(near, nodes // 128, 128).transpose(1, 0, 2).reshape(-1)
     bias = sage_bias.reshape(1, -1)
@@ -457,17 +484,18 @@
 
     table = table_of(node_feats)
     conf_src, _ = conf_rows_of(
-        nbrs, conf_index, before, after, self_weight, neighbor_weight, bias, table
+        node_count, spot, nbrs, conf_index, rims, self_weight, neighbor_weight, bias, table
     )
 
     def layer(first, steps, given):
         return layer_of(
             first,
             steps,
+            node_count,
+            spot,
             nbrs,
-            before,
+            rims,
             node_feats,
-            after,
             self_weight,
             neighbor_weight,
             bias,

time: 120 us -> 130 us (1.083)
  waiting for transfers between devices: 23.6 us -> 30.8 us
  local copies, waits for them, and re-layouts: 4.72 us -> 9.91 us
  starting transfers between devices: 44.4 us -> 41 us
    ppermute x2 -> x4, waiting for transfers between devices: 3.5 us -> 11.7 us  [the longest x1 5.89 us: shards(): before = lax.ppermute(node_feats[-HALO:], 'node', up)]
    unnamed x28 -> x32, local copies, waits for them, and re-layouts: 1.66 us -> 6.02 us
    all_to_all x1, starting transfers between devices: 13.9 us -> 9.82 us  [shards(): lax.all_to_all(conf_src.reshape(node_count, per_peer, width), 'node', 0,...]
    ppermute x2 -> x4, starting transfers between devices: 6.1 us -> 3.68 us  [the longest x1 2.35 us: shards(): after = lax.ppermute(node_feats[:HALO], 'node', down)]
    ppermute x6, starting transfers between devices: 10.4 us -> 11.9 us  [shift(): return lax.ppermute(value, 'cfg', perm)]
  transfers between devices with their start and end apart: 16 -> 18, of which waited for: 12 -> 12; matrix products, arithmetic and copies ran while one was open for 1% -> 1% of each run, Pallas kernels for 21% -> 19%
where the time goes in v3:
time: 130 us
  Pallas kernels  45.9 us (35%)
  starting transfers between devices  41 us (32%)
  waiting for transfers between devices  30.8 us (24%)
  local copies, waits for them, and re-layouts  9.91 us (8%)
    pallas_call x3, Pallas kernels, layer_of(): pl.pallas_call(functools.partial(layer_kernel, peers), out_shape=jax.Shap...  22.1 us
    pallas_call x1, Pallas kernels, scorer_of(): pl.pallas_call(functools.partial(scorer_kernel, groups), out_shape=(pltpu...  14.5 us
    ppermute x6, starting transfers between devices, shift(): return lax.ppermute(value, 'cfg', perm)  11.9 us
    ppermute x6, waiting for transfers between devices, shift(): return lax.ppermute(value, 'cfg', perm)  9.91 us
    all_to_all x1, starting transfers between devices, shards(): lax.all_to_all(conf_src.reshape(node_count, per_peer, width), 'node', 0,...  9.82 us
    all_to_all x1, starting transfers between devices, shards(): got = lax.all_to_all(sent.reshape(devices, 1, 128), both, 0, 0, tiled=True)  9.26 us
    all_to_all x1, starting transfers between devices, shards(): lax.all_to_all(local_grad.reshape(node_count, per_peer, width), 'node', 0...  6.06 us
    unnamed x32, local copies, waits for them, and re-layouts  6.02 us
  transfers between devices with their start and end apart: 18, of which 12 were waited for; matrix products, arithmetic and copies ran while one was open for 1% of the time, Pallas kernels for 19%

profile of v3, /device:TPU:2, one launch (start us, length us, event | category | flops | bytes accessed | tf_op | source)
XLA Modules:
  0.0 129.7 jit_solution(10596237207361698315)
XLA Ops:
  0.6 1.1 fusion.9
  1.7 2.3 %collective-permute-start.1 = (bf16[512,256]{1,0:T(8,128)(2,1)S(1)}, bf16[512,256]{1,0:T(8,128)(2,1)S(1)}, u32[]{:S(2)}, u32[]{:S(2)}) collective-permute-start(bf16[512,256]{1,0:T(8,128)(2,1)S(1)} %get-tuple-element.31), channel_id=1, source_target_pairs={{1,0},{2,1},{3,2},{4,3},{5,4},{6,5},{7,6},{8,7},{9,8},{10,9},{11,1... | collective-permute-start | bytes 786440 | tf_op jit(solution)/shard_map/ppermute | solution.py:473
  4.0 5.8 %collective-permute-done.1.refs_1_ = bf16[512,256]{1,0:T(8,128)(2,1)S(1)} collective-permute-done((bf16[512,256]{1,0:T(8,128)(2,1)S(1)}, bf16[512,256]{1,0:T(8,128)(2,1)S(1)}, u32[]{:S(2)}, u32[]{:S(2)}) %collective-permute-start.1) | collective-permute-done | bytes 262176 | tf_op jit(solution)/shard_map/ppermute | solution.py:473
  9.8 0.7 collective-permute-start.3
  10.5 5.9 %collective-permute-done.refs_0_ = bf16[512,256]{1,0:T(8,128)(2,1)S(1)} collective-permute-done((bf16[512,256]{1,0:T(8,128)(2,1)S(1)}, bf16[512,256]{1,0:T(8,128)(2,1)S(1)}, u32[]{:S(2)}, u32[]{:S(2)}) %collective-permute-start) | collective-permute-done | bytes 262176 | tf_op jit(solution)/shard_map/ppermute | solution.py:472
  16.4 0.7 collective-permute-start.2
  17.1 0.9 broadcast_multiply_fusion
  17.9 1.6 %copy-done = bf16[4096,256]{1,0:T(8,128)(2,1)S(1)} copy-done((bf16[4096,256]{1,0:T(8,128)(2,1)S(1)}, bf16[4096,256]{1,0:T(8,128)(2,1)}, u32[]{:S(2)}) %copy-start) | copy-done | bytes 2097176
  19.5 0.4 window_rows.1.refs_7_
  19.9 0.3 copy-done.9
  20.2 2.8 %conf_rows.1 = (bf16[128,256]{1,0:T(8,128)(2,1)S(1)}, f32[10240,128]{1,0:T(8,128)S(1)}) custom-call(s32[1]{0:T(128)} %bitcast.spot, s32[16384]{0:T(1024)S(1)} %bitcast.35, s32[128]{0:T(128)S(1)} %copy-done.9, bf16[512,256]{1,0:T(8,128)(2,1)S(1)} %collective-permute-done.refs_0_, ...), custom_call_target="tpu_custom_call", output_to_operand_aliasing={{1}: (10, {})} | custom-call | flops 33554432 | bytes 6291456 | tf_op jit(solution)/shard_map/conf_rows/pallas_call | solution.py:138
  23.0 0.7 reshape.74
  23.7 9.8 %all-to-all-start = ((bf16[32,4,256]{2,1,0:T(4,128)(2,1)}), bf16[32,4,256]{2,1,0:T(4,128)(2,1)}, u32[]{:S(2)}, u32[]{:S(2)}) async-start(bf16[32,4,256]{2,1,0:T(4,128)(2,1)} %reshape.74), calls=%async_computation | async-start | bytes 131072 | tf_op jit(solution)/shard_map/all_to_all | solution.py:511
  33.6 6.0 %graph_layer.3.refs_9_ = bf16[4096,256]{1,0:T(8,128)(2,1)} custom-call(s32[1]{0:T(128)} %bitcast.spot, s32[16384]{0:T(1024)S(1)} %bitcast.36, bf16[512,256]{1,0:T(8,128)(2,1)S(1)} %collective-permute-done.refs_0_, bf16[512,256]{1,0:T(8,128)(2,1)S(1)} %collective-permute-done.1.refs_1_, bf16[512,256]{1,0:T(8,128)(2,1)S(1)} %collective-permute-done.2.refs_2_, ...), custom_call_target="tpu_custom_call" | custom-call | flops 268435456 | bytes 8388608 | tf_op jit(solution)/shard_map/graph_layer/pallas_call | solution.py:203
  39.6 2.8 %all-to-all-done = bf16[32,4,256]{2,1,0:T(4,128)(2,1)} async-done(((bf16[32,4,256]{2,1,0:T(4,128)(2,1)}), bf16[32,4,256]{2,1,0:T(4,128)(2,1)}, u32[]{:S(2)}, u32[]{:S(2)}) %all-to-all-start) | async-done | bytes 65568 | tf_op jit(solution)/shard_map/all_to_all | solution.py:511
  42.4 0.9 reshape.75.refs_0_
  43.2 6.4 %collective-permute-start.6 = (bf16[128,256]{1,0:T(8,128)(2,1)S(1)}, bf16[128,256]{1,0:T(8,128)(2,1)}, u32[]{:S(2)}, u32[]{:S(2)}) collective-permute-start(bf16[128,256]{1,0:T(8,128)(2,1)S(1)} %reshape.75.refs_0_), channel_id=1, source_target_pairs={{0,192},{32,224},{64,0},{96,32},{128,64},{160,96},{192,128},{224,1... | collective-permute-start | bytes 196616 | tf_op jit(solution)/shard_map/ppermute | solution.py:509
  49.6 0.6 collective-permute-start.5
  50.2 1.0 collective-permute-start.4
  51.2 0.3 collective-permute-done.6.refs_3_
  51.5 0.2 collective-permute-start.10
  51.7 3.8 %collective-permute-done.5.refs_2_ = bf16[128,256]{1,0:T(8,128)(2,1)} collective-permute-done((bf16[128,256]{1,0:T(8,128)(2,1)S(1)}, bf16[128,256]{1,0:T(8,128)(2,1)}, u32[]{:S(2)}, u32[]{:S(2)}) %collective-permute-start.5) | collective-permute-done | bytes 65568 | tf_op jit(solution)/shard_map/ppermute | solution.py:509
  55.5 0.7 collective-permute-done.4.refs_1_
  56.2 0.9 collective-permute-done.9.refs_6_
  57.1 0.7 collective-permute-done.8.refs_5_
  57.8 0.9 copy-done.5
  58.7 0.9 copy-done.10
  59.6 0.8 copy-done.11
  60.5 0.8 copy-done.12
  61.3 14.5 %scorer.1 = (bf16[8,16,128,256]{3,2,1,0:T(8,128)(2,1)}, f32[256,128]{1,0:T(8,128)S(1)}) custom-call(s32[1]{0:T(128)} %bitcast.6.where, bf16[128,256]{1,0:T(8,128)(2,1)S(1)} %reshape.75.refs_0_, bf16[128,256]{1,0:T(8,128)(2,1)} %collective-permute-done.4.refs_1_, bf16[128,256]{1,0:T(8,128)(2,1)} %collective-permute-done.5.refs_2_, ...), custom_call_target="tpu_custom_call" | custom-call | flops 6442450944 | bytes 10485760 | tf_op jit(solution)/shard_map/scorer/pallas_call | solution.py:314
  75.8 0.6 copy-done.4
  76.4 9.3 %all-to-all-start.1 = ((f32[256,1,128]{2,1,0:T(1,128)}), f32[256,1,128]{2,1,0:T(1,128)}, u32[]{:S(2)}, u32[]{:S(2)}) async-start(f32[256,1,128]{2,1,0:T(1,128)} %bitcast.39), calls=%async_computation.1 | async-start | bytes 262144 | tf_op jit(solution)/shard_map/all_to_all | solution.py:534
  85.7 6.2 %graph_layer.4.refs_9_ = bf16[4096,256]{1,0:T(8,128)(2,1)} custom-call(s32[1]{0:T(128)} %bitcast.spot, s32[16384]{0:T(1024)S(1)} %bitcast.37, bf16[512,256]{1,0:T(8,128)(2,1)S(1)} %collective-permute-done.refs_0_, bf16[512,256]{1,0:T(8,128)(2,1)S(1)} %collective-permute-done.1.refs_1_, ...), custom_call_target="tpu_custom_call", output_to_operand_aliasing={{}: (11, {})} | custom-call | flops 268435456 | bytes 8388608 | tf_op jit(solution)/shard_map/graph_layer/pallas_call | solution.py:203
  91.9 4.8 %all-to-all-done.1 = f32[256,1,128]{2,1,0:T(1,128)} async-done(((f32[256,1,128]{2,1,0:T(1,128)}), f32[256,1,128]{2,1,0:T(1,128)}, u32[]{:S(2)}, u32[]{:S(2)}) %all-to-all-start.1) | async-done | bytes 131104 | tf_op jit(solution)/shard_map/all_to_all | solution.py:534
  96.7 3.6 %ranking.1 = (f32[1,1]{1,0:T(1,128)}, f32[16,256]{1,0:T(8,128)S(1)}, bf16[4,128,256]{2,1,0:T(8,128)(2,1)S(1)}) custom-call(s32[1]{0:T(128)} %bitcast.6.where, f32[256,128]{1,0:T(8,128)} %bitcast.15.got, s32[2,512]{1,0:T(2,128)S(1)} %bitcast.44, bf16[8,16,128,256]{3,2,1,0:T(8,128)(2,1)} %get-tuple-element.24.grads_hbm), custom_call_target="tpu_custom_call" | custom-call | flops 16777216 | bytes 6291456 | tf_op jit(solution)/shard_map/ranking/pallas_call | solution.py:396
  100.3 0.1 collective-permute-start.11
  100.5 2.5 %rest.1 = bf16[4,128,256]{2,1,0:T(8,128)(2,1)S(1)} custom-call(f32[16,256]{1,0:T(8,128)S(1)} %get-tuple-element.25.coef, bf16[8,16,128,256]{3,2,1,0:T(8,128)(2,1)} %get-tuple-element.24.grads_hbm), custom_call_target="tpu_custom_call" | custom-call | flops 16777216 | bytes 6291456 | tf_op jit(solution)/shard_map/rest/pallas_call | solution.py:428
  103.0 0.6 collective-permute-start.12
  103.6 2.7 %collective-permute-start.14 = (bf16[128,256]{1,0:T(8,128)(2,1)S(1)}, bf16[128,256]{1,0:T(8,128)(2,1)S(1)}, u32[]{:S(2)}, u32[]{:S(2)}) collective-permute-start(bf16[128,256]{1,0:T(8,128)(2,1)S(1)} %get-tuple-element.34), channel_id=1, source_target_pairs={{0,192},{32,224},{64,0},{96,32},{128,64},{160,96},{192,128},{224,1... | collective-permute-start | bytes 196616 | tf_op jit(solution)/shard_map/ppermute | solution.py:509
  106.3 0.6 collective-permute-start.13
  106.9 1.8 %collective-permute-done.12 = bf16[128,256]{1,0:T(8,128)(2,1)S(1)} collective-permute-done((bf16[128,256]{1,0:T(8,128)(2,1)S(1)}, bf16[128,256]{1,0:T(8,128)(2,1)S(1)}, u32[]{:S(2)}, u32[]{:S(2)}) %collective-permute-start.12) | collective-permute-done | bytes 65568 | tf_op jit(solution)/shard_map/ppermute | solution.py:509
  108.8 0.7 collective-permute-done.14
  109.5 2.6 %collective-permute-done.13 = bf16[128,256]{1,0:T(8,128)(2,1)S(1)} collective-permute-done((bf16[128,256]{1,0:T(8,128)(2,1)S(1)}, bf16[128,256]{1,0:T(8,128)(2,1)S(1)}, u32[]{:S(2)}, u32[]{:S(2)}) %collective-permute-start.13) | collective-permute-done | bytes 65568 | tf_op jit(solution)/shard_map/ppermute | solution.py:509
  112.1 0.2 convolution_convert_fusion
  112.3 0.7 reshape.82
  112.9 6.1 %all-to-all-start.2 = ((bf16[32,4,256]{2,1,0:T(4,128)(2,1)}), bf16[32,4,256]{2,1,0:T(4,128)(2,1)S(1)}, u32[]{:S(2)}, u32[]{:S(2)}) async-start(bf16[32,4,256]{2,1,0:T(4,128)(2,1)} %reshape.82), calls=%async_computation.2 | async-start | bytes 131072 | tf_op jit(solution)/shard_map/all_to_all | solution.py:552
  119.0 10.0 %graph_layer.5 = bf16[4096,256]{1,0:T(8,128)(2,1)} custom-call(s32[1]{0:T(128)} %bitcast.spot, s32[16384]{0:T(1024)S(1)} %bitcast.38, bf16[512,256]{1,0:T(8,128)(2,1)S(1)} %collective-permute-done.refs_0_, bf16[512,256]{1,0:T(8,128)(2,1)S(1)} %collective-permute-done.1.refs_1_, ...), custom_call_target="tpu_custom_call", output_to_operand_aliasing={{}: (11, {})} | custom-call | flops 536870912 | bytes 16777216 | tf_op jit(solution)/shard_map/graph_layer/pallas_call | solution.py:203
  129.0 0.7 reshape.86
  (36 shorter events, 0.1 us)
Async XLA Ops:
  1.7 8.1 %collective-permute-start.1 = (bf16[512,256]{1,0:T(8,128)(2,1)S(1)}, bf16[512,256]{1,0:T(8,128)(2,1)S(1)}, u32[]{:S(2)}, u32[]{:S(2)}) collective-permute-start(bf16[512,256]{1,0:T(8,128)(2,1)S(1)} %get-tuple-element.31), channel_id=1, source_target_pairs={{1,0},{2,1},{3,2},{4,3},{5,4},{6,5},{7,6},{8,7},{9,8},{10,9},{11,1... | collective-permute-start | bytes 786440 | tf_op jit(solution)/shard_map/ppermute | solution.py:473
  4.0 12.3 %collective-permute-start = (bf16[512,256]{1,0:T(8,128)(2,1)S(1)}, bf16[512,256]{1,0:T(8,128)(2,1)S(1)}, u32[]{:S(2)}, u32[]{:S(2)}) collective-permute-start(bf16[512,256]{1,0:T(8,128)(2,1)S(1)} %get-tuple-element.32), channel_id=1, source_target_pairs={{0,1},{1,2},{2,3},{3,4},{4,5},{5,6},{6,7},{7,8},{8,9},{9,10},{10,1... | collective-permute-start | bytes 786440 | tf_op jit(solution)/shard_map/ppermute | solution.py:472
  9.8 10.1 %collective-permute-start.3 = (bf16[512,256]{1,0:T(8,128)(2,1)S(1)}, bf16[512,256]{1,0:T(8,128)(2,1)S(1)}, u32[]{:S(2)}, u32[]{:S(2)}) collective-permute-start(bf16[512,256]{1,0:T(8,128)(2,1)S(1)} %collective-permute-done.1.refs_1_), channel_id=1, source_target_pairs={{63,31},{95,63},{127,95},{159,127},{191,159},{223,191},{255,223}} | collective-permute-start | bytes 786440 | tf_op jit(solution)/shard_map/ppermute | solution.py:477
  16.4 3.5 %collective-permute-start.2 = (bf16[512,256]{1,0:T(8,128)(2,1)S(1)}, bf16[512,256]{1,0:T(8,128)(2,1)S(1)}, u32[]{:S(2)}, u32[]{:S(2)}) collective-permute-start(bf16[512,256]{1,0:T(8,128)(2,1)S(1)} %collective-permute-done.refs_0_), channel_id=1, source_target_pairs={{0,32},{32,64},{64,96},{96,128},{128,160},{160,192},{192,224}} | collective-permute-start | bytes 786440 | tf_op jit(solution)/shard_map/ppermute | solution.py:475
  17.9 1.6 %copy-start = (bf16[4096,256]{1,0:T(8,128)(2,1)S(1)}, bf16[4096,256]{1,0:T(8,128)(2,1)}, u32[]{:S(2)}) copy-start(bf16[4096,256]{1,0:T(8,128)(2,1)} %refs_5_.7) | copy-start | bytes 6291460
  19.5 0.7 copy-start.9
  20.2 13.3 %copy-start.1 = (bf16[4096,256]{1,0:T(8,128)(2,1)S(1)}, bf16[4096,256]{1,0:T(8,128)(2,1)}, u32[]{:S(2)}) copy-start(bf16[4096,256]{1,0:T(8,128)(2,1)} %refs_5_.7) | copy-start | bytes 6291460
  20.2 13.3 %copy-start.2 = (bf16[256,256]{1,0:T(8,128)(2,1)S(1)}, bf16[256,256]{1,0:T(8,128)(2,1)}, u32[]{:S(2)}) copy-start(bf16[256,256]{1,0:T(8,128)(2,1)} %refs_6_.5) | copy-start | bytes 393220
  20.2 13.3 %copy-start.3 = (bf16[256,256]{1,0:T(8,128)(2,1)S(1)}, bf16[256,256]{1,0:T(8,128)(2,1)}, u32[]{:S(2)}) copy-start(bf16[256,256]{1,0:T(8,128)(2,1)} %refs_7_.5) | copy-start | bytes 393220
  20.2 13.4 %copy-start.7 = (f32[256]{0:T(256)S(1)}, f32[256]{0:T(256)}, u32[]{:S(2)}) copy-start(f32[256]{0:T(256)} %param.18) | copy-start | bytes 3076
  23.7 18.7 %all-to-all-start = ((bf16[32,4,256]{2,1,0:T(4,128)(2,1)}), bf16[32,4,256]{2,1,0:T(4,128)(2,1)}, u32[]{:S(2)}, u32[]{:S(2)}) async-start(bf16[32,4,256]{2,1,0:T(4,128)(2,1)} %reshape.74), calls=%async_computation | async-start | bytes 131072 | tf_op jit(solution)/shard_map/all_to_all | solution.py:511
  33.5 24.2 %copy-start.13 = (f32[256]{0:T(256)S(1)}, f32[256]{0:T(256)}, u32[]{:S(2)}) copy-start(f32[256]{0:T(256)} %param.23) | copy-start | bytes 3076
  33.6 24.2 %copy-start.14 = (f32[256]{0:T(256)S(1)}, f32[256]{0:T(256)}, u32[]{:S(2)}) copy-start(f32[256]{0:T(256)} %param.25) | copy-start | bytes 3076
  33.6 24.2 %copy-start.15 = (f32[256]{0:T(256)S(1)}, f32[256]{0:T(256)}, u32[]{:S(2)}) copy-start(f32[256]{0:T(256)} %param.26) | copy-start | bytes 3076
  43.2 8.3 %collective-permute-start.6 = (bf16[128,256]{1,0:T(8,128)(2,1)S(1)}, bf16[128,256]{1,0:T(8,128)(2,1)}, u32[]{:S(2)}, u32[]{:S(2)}) collective-permute-start(bf16[128,256]{1,0:T(8,128)(2,1)S(1)} %reshape.75.refs_0_), channel_id=1, source_target_pairs={{0,192},{32,224},{64,0},{96,32},{128,64},{160,96},{192,128},{224,1... | collective-permute-start | bytes 196616 | tf_op jit(solution)/shard_map/ppermute | solution.py:509
  49.6 5.9 %collective-permute-start.5 = (bf16[128,256]{1,0:T(8,128)(2,1)S(1)}, bf16[128,256]{1,0:T(8,128)(2,1)}, u32[]{:S(2)}, u32[]{:S(2)}) collective-permute-start(bf16[128,256]{1,0:T(8,128)(2,1)S(1)} %reshape.75.refs_0_), channel_id=1, source_target_pairs={{0,128},{32,160},{64,192},{96,224},{128,0},{160,32},{192,64},{224,... | collective-permute-start | bytes 196616 | tf_op jit(solution)/shard_map/ppermute | solution.py:509
  50.2 5.9 %collective-permute-start.4 = (bf16[128,256]{1,0:T(8,128)(2,1)S(1)}, bf16[128,256]{1,0:T(8,128)(2,1)}, u32[]{:S(2)}, u32[]{:S(2)}) collective-permute-start(bf16[128,256]{1,0:T(8,128)(2,1)S(1)} %reshape.75.refs_0_), channel_id=1, source_target_pairs={{0,64},{32,96},{64,128},{96,160},{128,192},{160,224},{192,0},{224,... | collective-permute-start | bytes 196616 | tf_op jit(solution)/shard_map/ppermute | solution.py:509
  51.2 5.0 %collective-permute-start.7 = (bf16[128,256]{1,0:T(8,128)(2,1)S(1)}, bf16[128,256]{1,0:T(8,128)(2,1)}, u32[]{:S(2)}, u32[]{:S(2)}) collective-permute-start(bf16[128,256]{1,0:T(8,128)(2,1)S(1)} %reshape.75.refs_0_), channel_id=1, source_target_pairs={{0,32},{32,0},{64,96},{96,64},{128,160},{160,128},{192,224},{224,1... | collective-permute-start | bytes 196616 | tf_op jit(solution)/shard_map/ppermute | solution.py:518
  51.5 4.7 %collective-permute-start.10 = (bf16[128,256]{1,0:T(8,128)(2,1)}, bf16[128,256]{1,0:T(8,128)(2,1)}, u32[]{:S(2)}, u32[]{:S(2)}) collective-permute-start(bf16[128,256]{1,0:T(8,128)(2,1)} %collective-permute-done.6.refs_3_), channel_id=1, source_target_pairs={{0,32},{32,0},{64,96},{96,64},{128,160},{160,128},{192,224},{224,1... | collective-permute-start | bytes 196616 | tf_op jit(solution)/shard_map/ppermute | solution.py:518
  55.5 1.6 %collective-permute-start.9 = (bf16[128,256]{1,0:T(8,128)(2,1)}, bf16[128,256]{1,0:T(8,128)(2,1)}, u32[]{:S(2)}, u32[]{:S(2)}) collective-permute-start(bf16[128,256]{1,0:T(8,128)(2,1)} %collective-permute-done.5.refs_2_), channel_id=1, source_target_pairs={{0,32},{32,0},{64,96},{96,64},{128,160},{160,128},{192,224},{224,1... | collective-permute-start | bytes 196616 | tf_op jit(solution)/shard_map/ppermute | solution.py:518
  56.2 1.6 %collective-permute-start.8 = (bf16[128,256]{1,0:T(8,128)(2,1)}, bf16[128,256]{1,0:T(8,128)(2,1)}, u32[]{:S(2)}, u32[]{:S(2)}) collective-permute-start(bf16[128,256]{1,0:T(8,128)(2,1)} %collective-permute-done.4.refs_1_), channel_id=1, source_target_pairs={{0,32},{32,0},{64,96},{96,64},{128,160},{160,128},{192,224},{224,1... | collective-permute-start | bytes 196616 | tf_op jit(solution)/shard_map/ppermute | solution.py:518
  57.8 0.9 copy-start.5
  58.7 0.9 copy-start.10
  59.6 0.8 copy-start.11
  60.5 0.8 copy-start.12
  75.8 0.7 copy-start.4
  76.4 20.3 %all-to-all-start.1 = ((f32[256,1,128]{2,1,0:T(1,128)}), f32[256,1,128]{2,1,0:T(1,128)}, u32[]{:S(2)}, u32[]{:S(2)}) async-start(f32[256,1,128]{2,1,0:T(1,128)} %bitcast.39), calls=%async_computation.1 | async-start | bytes 262144 | tf_op jit(solution)/shard_map/all_to_all | solution.py:534
  85.7 11.0 %copy-start.8 = (s32[512,2]{0,1:T(2,128)S(1)}, s32[512,2]{0,1:T(2,128)}, u32[]{:S(2)}) copy-start(s32[512,2]{0,1:T(2,128)} %param.27) | copy-start | bytes 12292
  100.3 2.6 %collective-permute-start.11 = (bf16[4,128,256]{2,1,0:T(8,128)(2,1)S(1)}, bf16[4,128,256]{2,1,0:T(8,128)(2,1)S(1)}, u32[]{:S(2)}, u32[]{:S(2)}) collective-permute-start(bf16[4,128,256]{2,1,0:T(8,128)(2,1)S(1)} %get-tuple-element.26), channel_id=1, source_target_pairs={{0,32},{32,0},{64,96},{96,64},{128,160},{160,128},{192,224},{224,1... | collective-permute-start | bytes 786440 | tf_op jit(solution)/shard_map/ppermute | solution.py:538
  100.4 11.6 %copy-start.6 = (bf16[256,256]{1,0:T(8,128)(2,1)S(1)}, bf16[256,256]{1,0:T(8,128)(2,1)}, u32[]{:S(2)}) copy-start(bf16[256,256]{1,0:T(8,128)(2,1)} %refs_9_.1) | copy-start | bytes 393220
  103.0 5.8 %collective-permute-start.12 = (bf16[128,256]{1,0:T(8,128)(2,1)S(1)}, bf16[128,256]{1,0:T(8,128)(2,1)S(1)}, u32[]{:S(2)}, u32[]{:S(2)}) collective-permute-start(bf16[128,256]{1,0:T(8,128)(2,1)S(1)} %get-tuple-element.33), channel_id=1, source_target_pairs={{0,64},{32,96},{64,128},{96,160},{128,192},{160,224},{192,0},{224,... | collective-permute-start | bytes 196616 | tf_op jit(solution)/shard_map/ppermute | solution.py:509
  103.6 5.8 %collective-permute-start.14 = (bf16[128,256]{1,0:T(8,128)(2,1)S(1)}, bf16[128,256]{1,0:T(8,128)(2,1)S(1)}, u32[]{:S(2)}, u32[]{:S(2)}) collective-permute-start(bf16[128,256]{1,0:T(8,128)(2,1)S(1)} %get-tuple-element.34), channel_id=1, source_target_pairs={{0,192},{32,224},{64,0},{96,32},{128,64},{160,96},{192,128},{224,1... | collective-permute-start | bytes 196616 | tf_op jit(solution)/shard_map/ppermute | solution.py:509
  106.3 5.8 %collective-permute-start.13 = (bf16[128,256]{1,0:T(8,128)(2,1)S(1)}, bf16[128,256]{1,0:T(8,128)(2,1)S(1)}, u32[]{:S(2)}, u32[]{:S(2)}) collective-permute-start(bf16[128,256]{1,0:T(8,128)(2,1)S(1)} %get-tuple-element.35), channel_id=1, source_target_pairs={{0,128},{32,160},{64,192},{96,224},{128,0},{160,32},{192,64},{224,... | collective-permute-start | bytes 196616 | tf_op jit(solution)/shard_map/ppermute | solution.py:509
  112.9 16.1 %all-to-all-start.2 = ((bf16[32,4,256]{2,1,0:T(4,128)(2,1)}), bf16[32,4,256]{2,1,0:T(4,128)(2,1)S(1)}, u32[]{:S(2)}, u32[]{:S(2)}) async-start(bf16[32,4,256]{2,1,0:T(4,128)(2,1)} %reshape.82), calls=%async_computation.2 | async-start | bytes 131072 | tf_op jit(solution)/shard_map/all_to_all | solution.py:552

commit v4 on v2

--- a/solution.py
+++ b/solution.py
@@ -36,6 +36,12 @@
     value = source[...].astype(f32)
     table[pl.ds(2 * first, rows, stride=2), :] = value[:, :128]
     table[pl.ds(2 * first + 1, rows, stride=2), :] = value[:, 128:]
+
+
+def put_rims(table, flip, inner, outer):
+    end = table.shape[0] // 2 - HALO
+    put_rows(table, pl.multiple_of((1 - flip[0]) * end, HALO), inner)
+    put_rows(table, pl.multiple_of(flip[0] * end, HALO), outer)
 
 
 def pair_at(table, at):
@@ -70,18 +76,15 @@
     return half_silu(0.5 * (pre + bias[...]))[0].astype(bf16)
 
 
-def conf_kernel(
-    nbrs, picks, before, after, sw_hbm, nw_hbm, bias_hbm, given, out, table, own, acc, sw, nw, bias, sems
-):
+def conf_kernel(flip, nbrs, picks, inner, outer, *refs):
+    sw_hbm, nw_hbm, bias_hbm, given, out, table, own, acc, sw, nw, bias, sems = refs
     copies = [
         pltpu.make_async_copy(source, target, sems.at[i])
         for i, (source, target) in enumerate(((sw_hbm, sw), (nw_hbm, nw), (bias_hbm, bias)))
     ]
     for copy in copies:
         copy.start()
-    window = table.shape[0] // 2
-    put_rows(table, 0, before)
-    put_rows(table, window - HALO, after)
+    put_rims(table, flip, inner, outer)
     count = picks.shape[0]
     own3 = own.reshape(count, 2, 128)
     acc3 = acc.reshape(count, 2, 128)
@@ -112,18 +115,18 @@
     )
 
 
-def conf_rows_of(nbrs, picks, before, after, sw, nw, bias, table):
+def conf_rows_of(flip, nbrs, picks, inner, outer, sw, nw, bias, table):
     count = picks.shape[0]
-    width = before.shape[1]
+    width = sw.shape[0]
     return pl.pallas_call(
         conf_kernel,
         out_shape=(
             jax.ShapeDtypeStruct((count, width), bf16),
             jax.ShapeDtypeStruct(table.shape, f32),
         ),
-        in_specs=[SMEM, SMEM, VMEM, VMEM] + [HBM] * 3 + [VMEM],
+        in_specs=[SMEM] * 3 + [VMEM] * 2 + [HBM] * 3 + [VMEM],
         out_specs=(VMEM, VMEM),
-        input_output_aliases={7: 1},
+        input_output_aliases={8: 1},
         scratch_shapes=[
             pltpu.VMEM((2 * count, 128), f32),
             pltpu.VMEM((2 * count, 128), f32),
@@ -137,20 +140,19 @@
         ),
         compiler_params=pltpu.CompilerParams(vmem_limit_bytes=16 << 20),
         name="conf_rows",
-    )(nbrs, picks, before, after, in_hbm(sw), in_hbm(nw), in_hbm(bias), table)
-
-
-def layer_kernel(nbrs, before, feats, after, own, sw, nw, bias, *refs):
+    )(flip, nbrs, picks, inner, outer, in_hbm(sw), in_hbm(nw), in_hbm(bias), table)
+
+
+def layer_kernel(flip, nbrs, inner, outer, feats, own, sw, nw, bias, *refs):
     out, table, acc = refs[-3:]
     tile = own.shape[0]
     nodes = feats.shape[0]
 
     @pl.when(pl.program_id(0) == 0)
     def _():
-        put_rows(table, 0, before)
+        put_rims(table, flip, inner, outer)
         for start in range(0, nodes, 512):
             put_rows(table, HALO + start, feats.at[start : start + 512, :])
-        put_rows(table, HALO + nodes, after)
 
     acc3 = acc.reshape(tile, 2, 128)
 
@@ -176,7 +178,7 @@
     )
 
 
-def layer_of(first, steps, nbrs, before, feats, after, sw, nw, bias, given):
+def layer_of(first, steps, flip, nbrs, inner, outer, feats, sw, nw, bias, given):
     nodes, width = feats.shape
     tile = 1024
     ahead = [] if given is None else [given]
@@ -185,6 +187,7 @@
         out_shape=jax.ShapeDtypeStruct((nodes, width), bf16),
         grid=(steps,),
         in_specs=[
+            SMEM,
             pl.BlockSpec((4 * tile,), lambda i: (first + i,), memory_space=pltpu.SMEM),
             VMEM,
             VMEM,
@@ -196,7 +199,7 @@
         ]
         + [HBM] * len(ahead),
         out_specs=pl.BlockSpec((tile, width), lambda i: (first + i, 0)),
-        input_output_aliases={8: 0} if ahead else {},
+        input_output_aliases={9: 0} if ahead else {},
         scratch_shapes=[
             pltpu.VMEM((2 * (nodes + 2 * HALO), 128), f32),
             pltpu.VMEM((2 * tile, 128), f32),
@@ -206,11 +209,11 @@
         ),
         compiler_params=pltpu.CompilerParams(vmem_limit_bytes=24 << 20),
         name="graph_layer",
-    )(nbrs, before, feats, after, feats, sw, nw, bias, *ahead)
+    )(flip, nbrs, inner, outer, feats, feats, sw, nw, bias, *ahead)
 
 
 def place_of(group, turn):
-    return (((group >> 1) + 4 - (turn & 3)) & 3) * 2 + ((group ^ (turn >> 2)) & 1)
+    return group ^ (2 * (turn & 3) + (turn >> 2))
 
 
 def scorer_kernel(groups, where, *refs):
@@ -336,9 +339,7 @@
 def fetches(grads_hbm, grads, sems, first):
     half = grads.shape[0]
     return [
-        pltpu.make_async_copy(
-            grads_hbm.at[first + (half - d) % half], grads.at[d], sems.at[d]
-        )
+        pltpu.make_async_copy(grads_hbm.at[first + d], grads.at[d], sems.at[d])
         for d in range(half)
     ]
 
@@ -446,28 +447,35 @@
     scale = 1.0 / math.sqrt(layout_ids.shape[1] * node_count)
     group = lax.axis_index("cfg")
 
-    up = [(i, i + 1) for i in range(devices - 1)]
-    down = [(i + 1, i) for i in range(devices - 1)]
-    before = lax.ppermute(node_feats[-HALO:], both, up)
-    after = lax.ppermute(node_feats[:HALO], both, down)
     nodes, near = neighbors.shape
+    spot = lax.axis_index("node")
+    flip = (spot & 1).reshape(1)
+
+    def trade(odd, partner):
+        rows = lax.dynamic_slice_in_dim(node_feats, odd * (nodes - HALO), HALO, 0)
+        pairs = [(i, partner(i)) for i in range(devices) if 0 <= partner(i) < devices]
+        return lax.ppermute(rows, both, pairs)
+
+    outer = trade(spot & 1, lambda i: i + 1 if i % 2 else i - 1)
+    inner = trade(1 - (spot & 1), lambda i: i ^ 1)
     nbrs = (2 * neighbors).T.reshape(near, nodes // 128, 128).transpose(1, 0, 2).reshape(-1)
     bias = sage_bias.reshape(1, -1)
     hold = lax.optimization_barrier
 
     table = table_of(node_feats)
     conf_src, _ = conf_rows_of(
-        nbrs, conf_index, before, after, self_weight, neighbor_weight, bias, table
+        flip, nbrs, conf_index, inner, outer, self_weight, neighbor_weight, bias, table
     )
 
     def layer(first, steps, given):
         return layer_of(
             first,
             steps,
+            flip,
             nbrs,
-            before,
+            inner,
+            outer,
             node_feats,
-            after,
             self_weight,
             neighbor_weight,
             bias,
@@ -477,8 +485,7 @@
     swap = [(i, i ^ 1) for i in range(group_count)]
 
     def shift(value, by):
-        perm = [(i, (i // 2 + by) % rings * 2 + i % 2) for i in range(group_count)]
-        return lax.ppermute(value, "cfg", perm)
+        return lax.ppermute(value, "cfg", [(i, i ^ (2 * by)) for i in range(group_count)])
 
     mine = lax.all_to_all(
         conf_src.reshape(node_count, per_peer, width), "node", 0, 0, tiled=True

time: 120 us -> 116 us (0.967)
  starting transfers between devices: 44.4 us -> 41.7 us
  waiting for transfers between devices: 23.6 us -> 21.9 us
    ppermute x8, starting transfers between devices: 16.5 us -> 11.9 us  [the longest x6 8.36 us: shift(): lax.ppermute(value, 'cfg', [(i, i ^ 2 * by) for i in range(group_count)])]
    ppermute x8, waiting for transfers between devices: 13.9 us -> 12.5 us  [the longest x6 8.86 us: shift(): lax.ppermute(value, 'cfg', [(i, i ^ 2 * by) for i in range(group_count)])]
  transfers between devices with their start and end apart: 16 -> 16, of which waited for: 12 -> 10; matrix products, arithmetic and copies ran while one was open for 1% -> 1% of each run, Pallas kernels for 21% -> 21%
where the time goes in v4:
time: 116 us; the launch traced here: 115 us
  Pallas kernels  45.1 us (39%)
  starting transfers between devices  41.7 us (36%)
  waiting for transfers between devices  21.9 us (19%)
  local copies, waits for them, and re-layouts  4.73 us (4%)
    pallas_call x3, Pallas kernels, layer_of(): pl.pallas_call(layer_kernel, out_shape=jax.ShapeDtypeStruct((nodes, width...  21.9 us
    pallas_call x1, Pallas kernels, scorer_of(): pl.pallas_call(functools.partial(scorer_kernel, groups), out_shape=(pltpu...  14.8 us
    all_to_all x1, starting transfers between devices, shards(): lax.all_to_all(conf_src.reshape(node_count, per_peer, width), 'node', 0,...  13.5 us
    all_to_all x1, starting transfers between devices, shards(): got = lax.all_to_all(sent.reshape(devices, 1, 128), both, 0, 0, tiled=True)  9.1 us
    ppermute x6, waiting for transfers between devices, shift(): lax.ppermute(value, 'cfg', [(i, i ^ 2 * by) for i in range(group_count)])  8.86 us
    ppermute x6, starting transfers between devices, shift(): lax.ppermute(value, 'cfg', [(i, i ^ 2 * by) for i in range(group_count)])  8.36 us
    all_to_all x1, starting transfers between devices, shards(): lax.all_to_all(local_grad.reshape(node_count, per_peer, width), 'node', 0...  6.47 us
    all_to_all x1, waiting for transfers between devices, shards(): got = lax.all_to_all(sent.reshape(devices, 1, 128), both, 0, 0, tiled=True)  5.46 us
  transfers between devices with their start and end apart: 16, of which 10 were waited for; matrix products, arithmetic and copies ran while one was open for 1% of the time, Pallas kernels for 21%

profile of v4, /device:TPU:2, one launch (start us, length us, event | category | flops | bytes accessed | tf_op | source)
XLA Modules:
  0.0 115.5 jit_solution(15905548340014795428)
XLA Ops:
  0.6 1.1 constant_dynamic-slice_fusion
  1.7 3.4 %collective-permute-start.1 = (bf16[512,256]{1,0:T(8,128)(2,1)S(1)}, bf16[512,256]{1,0:T(8,128)(2,1)S(1)}, u32[]{:S(2)}, u32[]{:S(2)}) collective-permute-start(bf16[512,256]{1,0:T(8,128)(2,1)S(1)} %get-tuple-element.31), channel_id=1, source_target_pairs={{1,2},{2,1},{3,4},{4,3},{5,6},{6,5},{7,8},{8,7},{9,10},{10,9},{11,... | collective-permute-start | bytes 786440 | tf_op jit(solution)/shard_map/ppermute | solution.py:457
  5.1 0.1 collective-permute-start
  5.2 0.9 broadcast_multiply_fusion
  6.1 0.0 copy-start
  6.1 1.6 %copy-done = bf16[4096,256]{1,0:T(8,128)(2,1)S(1)} copy-done((bf16[4096,256]{1,0:T(8,128)(2,1)S(1)}, bf16[4096,256]{1,0:T(8,128)(2,1)}, u32[]{:S(2)}) %copy-start) | copy-done | bytes 2097176
  7.7 0.4 window_rows.1.refs_3_
  8.1 3.6 %collective-permute-done.1.outer = bf16[512,256]{1,0:T(8,128)(2,1)S(1)} collective-permute-done((bf16[512,256]{1,0:T(8,128)(2,1)S(1)}, bf16[512,256]{1,0:T(8,128)(2,1)S(1)}, u32[]{:S(2)}, u32[]{:S(2)}) %collective-permute-start.1) | collective-permute-done | bytes 262176 | tf_op jit(solution)/shard_map/ppermute | solution.py:457
  11.7 0.0 copy-start.2
  11.7 0.0 copy-start.3
  11.7 0.0 copy-start.5
  11.7 2.8 %conf_rows.1 = (bf16[128,256]{1,0:T(8,128)(2,1)S(1)}, f32[10240,128]{1,0:T(8,128)S(1)}) custom-call(s32[1]{0:T(128)} %bitcast.flip, s32[16384]{0:T(1024)S(1)} %bitcast.35, s32[128]{0:T(128)S(1)} %copy-done.7, bf16[512,256]{1,0:T(8,128)(2,1)S(1)} %collective-permute-done.inner, ...), custom_call_target="tpu_custom_call", output_to_operand_aliasing={{1}: (8, {})} | custom-call | flops 33554432 | bytes 6291456 | tf_op jit(solution)/shard_map/conf_rows/pallas_call | solution.py:121
  14.5 0.7 reshape.74
  15.2 13.5 %all-to-all-start = ((bf16[32,4,256]{2,1,0:T(4,128)(2,1)}), bf16[32,4,256]{2,1,0:T(4,128)(2,1)S(1)}, u32[]{:S(2)}, u32[]{:S(2)}) async-start(bf16[32,4,256]{2,1,0:T(4,128)(2,1)} %reshape.74), calls=%async_computation | async-start | bytes 131072 | tf_op jit(solution)/shard_map/all_to_all | solution.py:490
  28.7 0.0 copy-start.4
  28.7 0.0 copy-start.9
  28.7 0.0 copy-start.10
  28.8 0.0 copy-start.12
  28.8 0.0 copy-start.13
  28.8 6.0 %graph_layer.3.refs_0_ = bf16[4096,256]{1,0:T(8,128)(2,1)} custom-call(s32[1]{0:T(128)} %bitcast.flip, s32[16384]{0:T(1024)S(1)} %bitcast.36, bf16[512,256]{1,0:T(8,128)(2,1)S(1)} %collective-permute-done.inner, bf16[512,256]{1,0:T(8,128)(2,1)S(1)} %collective-permute-done.1.outer, bf16[4096,256]{1,0:T(8,128)(2,1)S(1)} %copy-done.1, ...), custom_call_target="tpu_custom_call" | custom-call | flops 268435456 | bytes 8388608 | tf_op jit(solution)/shard_map/graph_layer/pallas_call | solution.py:185
  34.7 2.7 %all-to-all-done = bf16[32,4,256]{2,1,0:T(4,128)(2,1)S(1)} async-done(((bf16[32,4,256]{2,1,0:T(4,128)(2,1)}), bf16[32,4,256]{2,1,0:T(4,128)(2,1)S(1)}, u32[]{:S(2)}, u32[]{:S(2)}) %all-to-all-start) | async-done | bytes 65568 | tf_op jit(solution)/shard_map/all_to_all | solution.py:490
  37.5 3.2 %collective-permute-start.4 = (bf16[128,256]{1,0:T(8,128)(2,1)S(1)}, bf16[128,256]{1,0:T(8,128)(2,1)S(1)}, u32[]{:S(2)}, u32[]{:S(2)}) collective-permute-start(bf16[128,256]{1,0:T(8,128)(2,1)S(1)} %reshape.75.refs_0_), channel_id=1, source_target_pairs={{0,192},{32,224},{64,128},{96,160},{128,64},{160,96},{192,0},{224,... | collective-permute-start | bytes 196616 | tf_op jit(solution)/shard_map/ppermute | solution.py:488
  40.7 0.9 collective-permute-start.3
  41.5 0.1 collective-permute-start.2
  41.7 1.7 %collective-permute-done.4.refs_3_ = bf16[128,256]{1,0:T(8,128)(2,1)S(1)} collective-permute-done((bf16[128,256]{1,0:T(8,128)(2,1)S(1)}, bf16[128,256]{1,0:T(8,128)(2,1)S(1)}, u32[]{:S(2)}, u32[]{:S(2)}) %collective-permute-start.4) | collective-permute-done | bytes 65568 | tf_op jit(solution)/shard_map/ppermute | solution.py:488
  43.4 3.0 %collective-permute-done.3.refs_2_ = bf16[128,256]{1,0:T(8,128)(2,1)S(1)} collective-permute-done((bf16[128,256]{1,0:T(8,128)(2,1)S(1)}, bf16[128,256]{1,0:T(8,128)(2,1)S(1)}, u32[]{:S(2)}, u32[]{:S(2)}) %collective-permute-start.3) | collective-permute-done | bytes 65568 | tf_op jit(solution)/shard_map/ppermute | solution.py:488
  46.4 0.5 collective-permute-start.6
  46.9 0.9 collective-permute-done.7.refs_6_
  47.8 0.4 collective-permute-done.6.refs_5_
  48.2 14.8 %scorer.1 = (bf16[8,16,128,256]{3,2,1,0:T(8,128)(2,1)}, f32[256,128]{1,0:T(8,128)}) custom-call(s32[1]{0:T(128)} %bitcast.6.where, bf16[128,256]{1,0:T(8,128)(2,1)S(1)} %reshape.75.refs_0_, bf16[128,256]{1,0:T(8,128)(2,1)} %collective-permute-done.2.refs_1_, bf16[128,256]{1,0:T(8,128)(2,1)S(1)} %collective-permute-done.3.refs_2_, ...), custom_call_target="tpu_custom_call" | custom-call | flops 6442450944 | bytes 10485760 | tf_op jit(solution)/shard_map/scorer/pallas_call | solution.py:296
  63.1 9.1 %all-to-all-start.1 = ((f32[256,1,128]{2,1,0:T(1,128)}), f32[256,1,128]{2,1,0:T(1,128)S(1)}, u32[]{:S(2)}, u32[]{:S(2)}) async-start(f32[256,1,128]{2,1,0:T(1,128)} %bitcast.14), calls=%async_computation.1 | async-start | bytes 262144 | tf_op jit(solution)/shard_map/all_to_all | solution.py:513
  72.2 6.0 %graph_layer.4.refs_0_ = bf16[4096,256]{1,0:T(8,128)(2,1)} custom-call(s32[1]{0:T(128)} %bitcast.flip, s32[16384]{0:T(1024)S(1)} %bitcast.37, bf16[512,256]{1,0:T(8,128)(2,1)S(1)} %collective-permute-done.inner, bf16[512,256]{1,0:T(8,128)(2,1)S(1)} %collective-permute-done.1.outer, bf16[4096,256]{1,0:T(8,128)(2,1)S(1)} %copy-done.1, ...), custom_call_target="tpu_custom_call", output_to_operand_aliasing={{}: (9, {})} | custom-call | flops 268435456 | bytes 8388608 | tf_op jit(solution)/shard_map/graph_layer/pallas_call | solution.py:185
  78.2 5.5 %all-to-all-done.1 = f32[256,1,128]{2,1,0:T(1,128)S(1)} async-done(((f32[256,1,128]{2,1,0:T(1,128)}), f32[256,1,128]{2,1,0:T(1,128)S(1)}, u32[]{:S(2)}, u32[]{:S(2)}) %all-to-all-start.1) | async-done | bytes 131104 | tf_op jit(solution)/shard_map/all_to_all | solution.py:513
  83.6 2.7 %ranking.1 = (f32[1,1]{1,0:T(1,128)}, f32[16,256]{1,0:T(8,128)S(1)}, bf16[4,128,256]{2,1,0:T(8,128)(2,1)S(1)}) custom-call(s32[1]{0:T(128)} %bitcast.6.where, f32[256,128]{1,0:T(8,128)S(1)} %bitcast.39, s32[2,512]{1,0:T(2,128)S(1)} %bitcast.44, bf16[8,16,128,256]{3,2,1,0:T(8,128)(2,1)} %get-tuple-element.24.grads_hbm), custom_call_target="tpu_custom_call" | custom-call | flops 16777216 | bytes 6291456 | tf_op jit(solution)/shard_map/ranking/pallas_call | solution.py:376
  86.4 0.3 collective-permute-start.9
  86.6 2.4 %rest.1 = bf16[4,128,256]{2,1,0:T(8,128)(2,1)S(1)} custom-call(f32[16,256]{1,0:T(8,128)S(1)} %get-tuple-element.25.coef, bf16[8,16,128,256]{3,2,1,0:T(8,128)(2,1)} %get-tuple-element.24.grads_hbm), custom_call_target="tpu_custom_call" | custom-call | flops 16777216 | bytes 6291456 | tf_op jit(solution)/shard_map/rest/pallas_call | solution.py:408
  89.1 0.1 fusion.3
  89.1 0.7 collective-permute-start.10
  89.8 1.8 %collective-permute-start.12 = (bf16[128,256]{1,0:T(8,128)(2,1)S(1)}, bf16[128,256]{1,0:T(8,128)(2,1)S(1)}, u32[]{:S(2)}, u32[]{:S(2)}) collective-permute-start(bf16[128,256]{1,0:T(8,128)(2,1)S(1)} %get-tuple-element.34), channel_id=1, source_target_pairs={{0,192},{32,224},{64,128},{96,160},{128,64},{160,96},{192,0},{224,... | collective-permute-start | bytes 196616 | tf_op jit(solution)/shard_map/ppermute | solution.py:488
  91.7 1.7 %collective-permute-start.11 = (bf16[128,256]{1,0:T(8,128)(2,1)S(1)}, bf16[128,256]{1,0:T(8,128)(2,1)S(1)}, u32[]{:S(2)}, u32[]{:S(2)}) collective-permute-start(bf16[128,256]{1,0:T(8,128)(2,1)S(1)} %get-tuple-element.35), channel_id=1, source_target_pairs={{0,128},{32,160},{64,192},{96,224},{128,0},{160,32},{192,64},{224,... | collective-permute-start | bytes 196616 | tf_op jit(solution)/shard_map/ppermute | solution.py:488
  93.3 0.2 collective-permute-done.10
  93.5 1.8 %collective-permute-done.12 = bf16[128,256]{1,0:T(8,128)(2,1)S(1)} collective-permute-done((bf16[128,256]{1,0:T(8,128)(2,1)S(1)}, bf16[128,256]{1,0:T(8,128)(2,1)S(1)}, u32[]{:S(2)}, u32[]{:S(2)}) %collective-permute-start.12) | collective-permute-done | bytes 65568 | tf_op jit(solution)/shard_map/ppermute | solution.py:488
  95.3 2.1 %collective-permute-done.11 = bf16[128,256]{1,0:T(8,128)(2,1)S(1)} collective-permute-done((bf16[128,256]{1,0:T(8,128)(2,1)S(1)}, bf16[128,256]{1,0:T(8,128)(2,1)S(1)}, u32[]{:S(2)}, u32[]{:S(2)}) %collective-permute-start.11) | collective-permute-done | bytes 65568 | tf_op jit(solution)/shard_map/ppermute | solution.py:488
  97.4 0.2 convolution_convert_fusion
  97.6 0.7 reshape.82
  98.3 6.5 %all-to-all-start.2 = ((bf16[32,4,256]{2,1,0:T(4,128)(2,1)}), bf16[32,4,256]{2,1,0:T(4,128)(2,1)S(1)}, u32[]{:S(2)}, u32[]{:S(2)}) async-start(bf16[32,4,256]{2,1,0:T(4,128)(2,1)} %reshape.82), calls=%async_computation.2 | async-start | bytes 131072 | tf_op jit(solution)/shard_map/all_to_all | solution.py:531
  104.8 10.0 %graph_layer.5 = bf16[4096,256]{1,0:T(8,128)(2,1)} custom-call(s32[1]{0:T(128)} %bitcast.flip, s32[16384]{0:T(1024)S(1)} %bitcast.38, bf16[512,256]{1,0:T(8,128)(2,1)S(1)} %collective-permute-done.inner, bf16[512,256]{1,0:T(8,128)(2,1)S(1)} %collective-permute-done.1.outer, bf16[4096,256]{1,0:T(8,128)(2,1)S(1)} %copy-done.1, ...), custom_call_target="tpu_custom_call", output_to_operand_aliasing={{}: (9, {})} | custom-call | flops 536870912 | bytes 16777216 | tf_op jit(solution)/shard_map/graph_layer/pallas_call | solution.py:185
  114.8 0.7 reshape.86
  (28 shorter events, 0.1 us)
Async XLA Ops:
  1.7 9.9 %collective-permute-start.1 = (bf16[512,256]{1,0:T(8,128)(2,1)S(1)}, bf16[512,256]{1,0:T(8,128)(2,1)S(1)}, u32[]{:S(2)}, u32[]{:S(2)}) collective-permute-start(bf16[512,256]{1,0:T(8,128)(2,1)S(1)} %get-tuple-element.31), channel_id=1, source_target_pairs={{1,2},{2,1},{3,4},{4,3},{5,6},{6,5},{7,8},{8,7},{9,10},{10,9},{11,... | collective-permute-start | bytes 786440 | tf_op jit(solution)/shard_map/ppermute | solution.py:457
  5.1 6.5 %collective-permute-start = (bf16[512,256]{1,0:T(8,128)(2,1)S(1)}, bf16[512,256]{1,0:T(8,128)(2,1)S(1)}, u32[]{:S(2)}, u32[]{:S(2)}) collective-permute-start(bf16[512,256]{1,0:T(8,128)(2,1)S(1)} %get-tuple-element.32), channel_id=1, source_target_pairs={{0,1},{1,0},{2,3},{3,2},{4,5},{5,4},{6,7},{7,6},{8,9},{9,8},{10,11... | collective-permute-start | bytes 786440 | tf_op jit(solution)/shard_map/ppermute | solution.py:457
  6.1 1.6 %copy-start = (bf16[4096,256]{1,0:T(8,128)(2,1)S(1)}, bf16[4096,256]{1,0:T(8,128)(2,1)}, u32[]{:S(2)}) copy-start(bf16[4096,256]{1,0:T(8,128)(2,1)} %own.5) | copy-start | bytes 6291460
  7.7 4.0 %copy-start.7 = (s32[128]{0:T(128)S(1)}, s32[128]{0:T(128)}, u32[]{:S(2)}) copy-start(s32[128]{0:T(128)} %picks.1) | copy-start | bytes 1540
  11.7 17.0 %copy-start.1 = (bf16[4096,256]{1,0:T(8,128)(2,1)S(1)}, bf16[4096,256]{1,0:T(8,128)(2,1)}, u32[]{:S(2)}) copy-start(bf16[4096,256]{1,0:T(8,128)(2,1)} %own.5) | copy-start | bytes 6291460
  11.7 17.0 %copy-start.2 = (bf16[256,256]{1,0:T(8,128)(2,1)S(1)}, bf16[256,256]{1,0:T(8,128)(2,1)}, u32[]{:S(2)}) copy-start(bf16[256,256]{1,0:T(8,128)(2,1)} %sw.5) | copy-start | bytes 393220
  11.7 17.0 %copy-start.3 = (bf16[256,256]{1,0:T(8,128)(2,1)S(1)}, bf16[256,256]{1,0:T(8,128)(2,1)}, u32[]{:S(2)}) copy-start(bf16[256,256]{1,0:T(8,128)(2,1)} %nw.5) | copy-start | bytes 393220
  11.7 17.0 %copy-start.5 = (f32[256]{0:T(256)S(1)}, f32[256]{0:T(256)}, u32[]{:S(2)}) copy-start(f32[256]{0:T(256)} %param.18) | copy-start | bytes 3076
  15.2 22.3 %all-to-all-start = ((bf16[32,4,256]{2,1,0:T(4,128)(2,1)}), bf16[32,4,256]{2,1,0:T(4,128)(2,1)S(1)}, u32[]{:S(2)}, u32[]{:S(2)}) async-start(bf16[32,4,256]{2,1,0:T(4,128)(2,1)} %reshape.74), calls=%async_computation | async-start | bytes 131072 | tf_op jit(solution)/shard_map/all_to_all | solution.py:490
  28.7 19.5 %copy-start.4 = (bf16[256,256]{1,0:T(8,128)(2,1)S(1)}, bf16[256,256]{1,0:T(8,128)(2,1)}, u32[]{:S(2)}) copy-start(bf16[256,256]{1,0:T(8,128)(2,1)} %refs_9_.1) | copy-start | bytes 393220
  28.7 19.5 %copy-start.8 = (bf16[256,256]{1,0:T(8,128)(2,1)S(1)}, bf16[256,256]{1,0:T(8,128)(2,1)}, u32[]{:S(2)}) copy-start(bf16[256,256]{1,0:T(8,128)(2,1)} %refs_12_.1) | copy-start | bytes 393220
  28.7 19.5 %copy-start.9 = (s32[16,1024]{1,0:T(8,128)S(1)}, s32[16,1024]{1,0:T(8,128)}, u32[]{:S(2)}) copy-start(s32[16,1024]{1,0:T(8,128)} %refs_8_.1) | copy-start | bytes 196612
  28.7 19.5 %copy-start.10 = (bf16[128,256]{1,0:T(8,128)(2,1)S(1)}, bf16[128,256]{1,0:T(8,128)(2,1)}, u32[]{:S(2)}) copy-start(bf16[128,256]{1,0:T(8,128)(2,1)} %refs_10_.1) | copy-start | bytes 196612
  28.7 19.5 %copy-start.11 = (f32[256]{0:T(256)S(1)}, f32[256]{0:T(256)}, u32[]{:S(2)}) copy-start(f32[256]{0:T(256)} %param.23) | copy-start | bytes 3076
  28.8 19.5 %copy-start.12 = (f32[256]{0:T(256)S(1)}, f32[256]{0:T(256)}, u32[]{:S(2)}) copy-start(f32[256]{0:T(256)} %param.25) | copy-start | bytes 3076
  28.8 19.5 %copy-start.13 = (f32[256]{0:T(256)S(1)}, f32[256]{0:T(256)}, u32[]{:S(2)}) copy-start(f32[256]{0:T(256)} %param.26) | copy-start | bytes 3076
  37.5 5.9 %collective-permute-start.4 = (bf16[128,256]{1,0:T(8,128)(2,1)S(1)}, bf16[128,256]{1,0:T(8,128)(2,1)S(1)}, u32[]{:S(2)}, u32[]{:S(2)}) collective-permute-start(bf16[128,256]{1,0:T(8,128)(2,1)S(1)} %reshape.75.refs_0_), channel_id=1, source_target_pairs={{0,192},{32,224},{64,128},{96,160},{128,64},{160,96},{192,0},{224,... | collective-permute-start | bytes 196616 | tf_op jit(solution)/shard_map/ppermute | solution.py:488
  40.7 5.8 %collective-permute-start.3 = (bf16[128,256]{1,0:T(8,128)(2,1)S(1)}, bf16[128,256]{1,0:T(8,128)(2,1)S(1)}, u32[]{:S(2)}, u32[]{:S(2)}) collective-permute-start(bf16[128,256]{1,0:T(8,128)(2,1)S(1)} %reshape.75.refs_0_), channel_id=1, source_target_pairs={{0,128},{32,160},{64,192},{96,224},{128,0},{160,32},{192,64},{224,... | collective-permute-start | bytes 196616 | tf_op jit(solution)/shard_map/ppermute | solution.py:488
  41.5 4.9 %collective-permute-start.2 = (bf16[128,256]{1,0:T(8,128)(2,1)S(1)}, bf16[128,256]{1,0:T(8,128)(2,1)}, u32[]{:S(2)}, u32[]{:S(2)}) collective-permute-start(bf16[128,256]{1,0:T(8,128)(2,1)S(1)} %reshape.75.refs_0_), channel_id=1, source_target_pairs={{0,64},{32,96},{64,0},{96,32},{128,192},{160,224},{192,128},{224,1... | collective-permute-start | bytes 196616 | tf_op jit(solution)/shard_map/ppermute | solution.py:488
  41.7 5.3 %collective-permute-start.5 = (bf16[128,256]{1,0:T(8,128)(2,1)S(1)}, bf16[128,256]{1,0:T(8,128)(2,1)}, u32[]{:S(2)}, u32[]{:S(2)}) collective-permute-start(bf16[128,256]{1,0:T(8,128)(2,1)S(1)} %reshape.75.refs_0_), channel_id=1, source_target_pairs={{0,32},{32,0},{64,96},{96,64},{128,160},{160,128},{192,224},{224,1... | collective-permute-start | bytes 196616 | tf_op jit(solution)/shard_map/ppermute | solution.py:497
  43.4 3.5 %collective-permute-start.8 = (bf16[128,256]{1,0:T(8,128)(2,1)S(1)}, bf16[128,256]{1,0:T(8,128)(2,1)}, u32[]{:S(2)}, u32[]{:S(2)}) collective-permute-start(bf16[128,256]{1,0:T(8,128)(2,1)S(1)} %collective-permute-done.4.refs_3_), channel_id=1, source_target_pairs={{0,32},{32,0},{64,96},{96,64},{128,160},{160,128},{192,224},{224,1... | collective-permute-start | bytes 196616 | tf_op jit(solution)/shard_map/ppermute | solution.py:497
  46.4 1.4 %collective-permute-start.7 = (bf16[128,256]{1,0:T(8,128)(2,1)S(1)}, bf16[128,256]{1,0:T(8,128)(2,1)}, u32[]{:S(2)}, u32[]{:S(2)}) collective-permute-start(bf16[128,256]{1,0:T(8,128)(2,1)S(1)} %collective-permute-done.3.refs_2_), channel_id=1, source_target_pairs={{0,32},{32,0},{64,96},{96,64},{128,160},{160,128},{192,224},{224,1... | collective-permute-start | bytes 196616 | tf_op jit(solution)/shard_map/ppermute | solution.py:497
  46.4 1.8 %collective-permute-start.6 = (bf16[128,256]{1,0:T(8,128)(2,1)}, bf16[128,256]{1,0:T(8,128)(2,1)}, u32[]{:S(2)}, u32[]{:S(2)}) collective-permute-start(bf16[128,256]{1,0:T(8,128)(2,1)} %collective-permute-done.2.refs_1_), channel_id=1, source_target_pairs={{0,32},{32,0},{64,96},{96,64},{128,160},{160,128},{192,224},{224,1... | collective-permute-start | bytes 196616 | tf_op jit(solution)/shard_map/ppermute | solution.py:497
  63.1 20.5 %all-to-all-start.1 = ((f32[256,1,128]{2,1,0:T(1,128)}), f32[256,1,128]{2,1,0:T(1,128)S(1)}, u32[]{:S(2)}, u32[]{:S(2)}) async-start(f32[256,1,128]{2,1,0:T(1,128)} %bitcast.14), calls=%async_computation.1 | async-start | bytes 262144 | tf_op jit(solution)/shard_map/all_to_all | solution.py:513
  72.2 11.4 %copy-start.6 = (s32[512,2]{0,1:T(2,128)S(1)}, s32[512,2]{0,1:T(2,128)}, u32[]{:S(2)}) copy-start(s32[512,2]{0,1:T(2,128)} %param.27) | copy-start | bytes 12292
  86.4 2.7 %collective-permute-start.9 = (bf16[4,128,256]{2,1,0:T(8,128)(2,1)S(1)}, bf16[4,128,256]{2,1,0:T(8,128)(2,1)S(1)}, u32[]{:S(2)}, u32[]{:S(2)}) collective-permute-start(bf16[4,128,256]{2,1,0:T(8,128)(2,1)S(1)} %get-tuple-element.26), channel_id=1, source_target_pairs={{0,32},{32,0},{64,96},{96,64},{128,160},{160,128},{192,224},{224,1... | collective-permute-start | bytes 786440 | tf_op jit(solution)/shard_map/ppermute | solution.py:517
  89.1 4.4 %collective-permute-start.10 = (bf16[128,256]{1,0:T(8,128)(2,1)S(1)}, bf16[128,256]{1,0:T(8,128)(2,1)S(1)}, u32[]{:S(2)}, u32[]{:S(2)}) collective-permute-start(bf16[128,256]{1,0:T(8,128)(2,1)S(1)} %get-tuple-element.33), channel_id=1, source_target_pairs={{0,64},{32,96},{64,0},{96,32},{128,192},{160,224},{192,128},{224,1... | collective-permute-start | bytes 196616 | tf_op jit(solution)/shard_map/ppermute | solution.py:488
  89.8 5.5 %collective-permute-start.12 = (bf16[128,256]{1,0:T(8,128)(2,1)S(1)}, bf16[128,256]{1,0:T(8,128)(2,1)S(1)}, u32[]{:S(2)}, u32[]{:S(2)}) collective-permute-start(bf16[128,256]{1,0:T(8,128)(2,1)S(1)} %get-tuple-element.34), channel_id=1, source_target_pairs={{0,192},{32,224},{64,128},{96,160},{128,64},{160,96},{192,0},{224,... | collective-permute-start | bytes 196616 | tf_op jit(solution)/shard_map/ppermute | solution.py:488
  91.7 5.8 %collective-permute-start.11 = (bf16[128,256]{1,0:T(8,128)(2,1)S(1)}, bf16[128,256]{1,0:T(8,128)(2,1)S(1)}, u32[]{:S(2)}, u32[]{:S(2)}) collective-permute-start(bf16[128,256]{1,0:T(8,128)(2,1)S(1)} %get-tuple-element.35), channel_id=1, source_target_pairs={{0,128},{32,160},{64,192},{96,224},{128,0},{160,32},{192,64},{224,... | collective-permute-start | bytes 196616 | tf_op jit(solution)/shard_map/ppermute | solution.py:488
  98.3 16.5 %all-to-all-start.2 = ((bf16[32,4,256]{2,1,0:T(4,128)(2,1)}), bf16[32,4,256]{2,1,0:T(4,128)(2,1)S(1)}, u32[]{:S(2)}, u32[]{:S(2)}) async-start(bf16[32,4,256]{2,1,0:T(4,128)(2,1)} %reshape.82), calls=%async_computation.2 | async-start | bytes 131072 | tf_op jit(solution)/shard_map/all_to_all | solution.py:531

commit v5 on v4

--- a/solution.py
+++ b/solution.py
@@ -68,15 +68,15 @@
     )(feats)
 
 
-def layer_rows(own_left, own_right, left, right, sw, nw, bias):
+def layer_rows(own_left, own_right, left, right, sw, nw, bias, kind=bf16):
     pre = jnp.dot(own_left, sw[:128, :], preferred_element_type=f32)
     pre += jnp.dot(own_right, sw[128:, :], preferred_element_type=f32)
     pre += jnp.dot(left, nw[:128, :], preferred_element_type=f32)
     pre += jnp.dot(right, nw[128:, :], preferred_element_type=f32)
-    return half_silu(0.5 * (pre + bias[...]))[0].astype(bf16)
-
-
-def conf_kernel(flip, nbrs, picks, inner, outer, *refs):
+    return half_silu(0.5 * (pre + bias[...]))[0].astype(kind)
+
+
+def conf_kernel(flip, nbrs, picks, outer, inner, *refs):
     sw_hbm, nw_hbm, bias_hbm, given, out, table, own, acc, sw, nw, bias, sems = refs
     copies = [
         pltpu.make_async_copy(source, target, sems.at[i])
@@ -104,7 +104,7 @@
     halves = [ref[pl.ds(side, count, stride=2), :] for ref in (own, acc) for side in (0, 1)]
     for copy in copies:
         copy.wait()
-    out[...] = layer_rows(
+    value = layer_rows(
         halves[0].astype(bf16),
         halves[1].astype(bf16),
         (halves[2] * 0.25).astype(bf16),
@@ -112,16 +112,20 @@
         sw,
         nw,
         bias,
-    )
-
-
-def conf_rows_of(flip, nbrs, picks, inner, outer, sw, nw, bias, table):
+        f32,
+    )
+    share = out.shape[1]
+    for peer in range(out.shape[0]):
+        out[peer] = value[peer * share : (peer + 1) * share, :].astype(bf16)
+
+
+def conf_rows_of(peers, flip, nbrs, picks, inner, outer, sw, nw, bias, table):
     count = picks.shape[0]
     width = sw.shape[0]
     return pl.pallas_call(
         conf_kernel,
         out_shape=(
-            jax.ShapeDtypeStruct((count, width), bf16),
+            jax.ShapeDtypeStruct((peers, count // peers, width), bf16),
             jax.ShapeDtypeStruct(table.shape, f32),
         ),
         in_specs=[SMEM] * 3 + [VMEM] * 2 + [HBM] * 3 + [VMEM],
@@ -140,10 +144,10 @@
         ),
         compiler_params=pltpu.CompilerParams(vmem_limit_bytes=16 << 20),
         name="conf_rows",
-    )(flip, nbrs, picks, inner, outer, in_hbm(sw), in_hbm(nw), in_hbm(bias), table)
-
-
-def layer_kernel(flip, nbrs, inner, outer, feats, own, sw, nw, bias, *refs):
+    )(flip, nbrs, picks, outer, inner, in_hbm(sw), in_hbm(nw), in_hbm(bias), table)
+
+
+def layer_kernel(flip, nbrs, outer, inner, feats, own, sw, nw, bias, *refs):
     out, table, acc = refs[-3:]
     tile = own.shape[0]
     nodes = feats.shape[0]
@@ -180,7 +184,7 @@
 
 def layer_of(first, steps, flip, nbrs, inner, outer, feats, sw, nw, bias, given):
     nodes, width = feats.shape
-    tile = 1024
+    tile = 512
     ahead = [] if given is None else [given]
     return pl.pallas_call(
         layer_kernel,
@@ -209,22 +213,41 @@
         ),
         compiler_params=pltpu.CompilerParams(vmem_limit_bytes=24 << 20),
         name="graph_layer",
-    )(flip, nbrs, inner, outer, feats, feats, sw, nw, bias, *ahead)
+    )(flip, nbrs, outer, inner, feats, feats, sw, nw, bias, *ahead)
 
 
 def place_of(group, turn):
     return group ^ (2 * (turn & 3) + (turn >> 2))
 
 
-def scorer_kernel(groups, where, *refs):
+def prepare_kernel(table, mid, weight, tabh, midh, back):
+    tabh[...] = (table[...].astype(f32) * 0.5).astype(bf16)
+    middle = mid[...].astype(f32)
+    midh[...] = (middle * 0.5).astype(bf16)
+    back[...] = jnp.transpose(middle * (weight[...] * 0.25)).astype(bf16)
+
+
+def prepared(table, mid, weight):
+    return pl.pallas_call(
+        prepare_kernel,
+        out_shape=tuple(jax.ShapeDtypeStruct(x.shape, bf16) for x in (table, mid, mid)),
+        in_specs=[VMEM] * 3,
+        out_specs=(VMEM,) * 3,
+        cost_estimate=pl.CostEstimate(flops=1 << 20, transcendentals=0, bytes_accessed=1 << 19),
+        compiler_params=pltpu.CompilerParams(vmem_limit_bytes=8 << 20),
+        name="prepare",
+    )(table, mid, weight)
+
+
+def scorer_kernel(groups, final, where, *refs):
     xs, refs = refs[:groups], refs[groups:]
-    ids, join, table, jbias, mid, mbias, weight, grads_hbm, sent = refs[:9]
-    base, tabh, midh, back, total, grads, sems = refs[9:]
+    ids, join, jbias, tabh, midh, back, mbias, weight = refs[:8]
+    given, (grads_hbm, sent, base, total, grads, sems) = refs[8:-6], refs[-6:]
     step = pl.program_id(0)
     slot = step & 1
     chunk = xs[0].shape[0]
     configs = ids.shape[0]
-    layouts = table.shape[0]
+    layouts = tabh.shape[0]
     one = jnp.asarray(1.0, bf16)
 
     @pl.when(step == 0)
@@ -233,11 +256,7 @@
             base[i] = 0.5 * (
                 jnp.dot(xs[i][...], join[...], preferred_element_type=f32) + jbias[...]
             )
-        tabh[...] = (table[...].astype(f32) * 0.5).astype(bf16)
-        middle = mid[...].astype(f32)
-        midh[...] = (middle * 0.5).astype(bf16)
-        back[...] = jnp.transpose(middle * (weight[...] * 0.25)).astype(bf16)
-        total[...] = jnp.zeros_like(total)
+        total[...] = given[0][...] if given else jnp.zeros_like(total)
 
     def copy_of(turn, place):
         return pltpu.make_async_copy(grads.at[place], grads_hbm.at[turn], sems.at[place])
@@ -261,13 +280,14 @@
         half = jnp.dot(picks, tabh[...], preferred_element_type=f32)
         half = (half + jnp.concatenate([rows] * some, axis=0)).astype(bf16)
         tanh = jnp.tanh(half)
-        act = half + half * tanh
-        slope = (one + tanh) * (one + half * (one - tanh))
-        outer = jnp.dot(act, midh[...], preferred_element_type=f32)
+        above = one + tanh
+        slope = above * (one + half * (one - tanh))
+        outer = jnp.dot(half * above, midh[...], preferred_element_type=f32)
         outer = (outer + 0.5 * mbias[...]).astype(bf16)
         tanh2 = jnp.tanh(outer)
-        act2 = (outer + outer * tanh2).astype(f32)
-        slope2 = (one + tanh2) * (one + outer * (one - tanh2))
+        above2 = one + tanh2
+        act2 = (outer * above2).astype(f32)
+        slope2 = above2 * (one + outer * (one - tanh2))
         for q in range(some):
             part = act2[q * chunk : (q + 1) * chunk, :]
             total[first + q : first + q + 1, :] += jnp.sum(part, axis=0, keepdims=True)
@@ -279,38 +299,44 @@
 
     @pl.when(step == groups - 1)
     def _():
-        scores = jnp.sum(total[...] * weight[...], axis=1, keepdims=True)
-        lane = lax.broadcasted_iota(jnp.int32, (configs, 128), 1)
-        sub = lax.broadcasted_iota(jnp.int32, (configs, 128), 0)
-        spread = jnp.where(lane == sub + where[0] * configs, scores, 0.0)
-        sent[...] = jnp.broadcast_to(jnp.sum(spread, axis=0, keepdims=True), sent.shape)
+        if final:
+            scores = jnp.sum(total[...] * weight[...], axis=1, keepdims=True)
+            lane = lax.broadcasted_iota(jnp.int32, (configs, 128), 1)
+            sub = lax.broadcasted_iota(jnp.int32, (configs, 128), 0)
+            spread = jnp.where(lane == sub + where[0] * configs, scores, 0.0)
+            sent[...] = jnp.broadcast_to(jnp.sum(spread, axis=0, keepdims=True), sent.shape)
+        else:
+            sent[...] = total[...]
         copy_of(step - 1, 1 - slot).wait()
         copy_of(step, slot).wait()
 
 
-def scorer_of(where, xs, ids, join, table, jbias, mid, mbias, weight, devices):
+def scorer_of(final, turns, where, xs, ids, join, jbias, weights, mbias, weight, given):
     groups = len(xs)
     configs = ids.shape[0]
     chunk, width = xs[0].shape
     hidden = join.shape[1]
-    return pl.pallas_call(
-        functools.partial(scorer_kernel, groups),
+    start, stride = turns
+    summed = final if final else (configs, hidden)
+    return pl.pallas_call(
+        functools.partial(scorer_kernel, groups, final),
         out_shape=(
             pltpu.HBM((groups, configs, chunk, hidden), bf16),
-            jax.ShapeDtypeStruct((devices, 128), f32),
+            jax.ShapeDtypeStruct(summed, f32),
         ),
         grid_spec=pltpu.PrefetchScalarGridSpec(
             num_scalar_prefetch=1,
             grid=(groups,),
             in_specs=[VMEM] * groups
-            + [pl.BlockSpec((configs, chunk), lambda i, where: (0, place_of(where[0], i)))]
-            + [VMEM] * 6,
+            + [
+                pl.BlockSpec(
+                    (configs, chunk), lambda i, where: (0, place_of(where[0], start + stride * i))
+                )
+            ]
+            + [VMEM] * (7 + len(given)),
             out_specs=(HBM, VMEM),
             scratch_shapes=[
                 pltpu.VMEM((groups, chunk, hidden), f32),
-                pltpu.VMEM(table.shape, bf16),
-                pltpu.VMEM(mid.shape, bf16),
-                pltpu.VMEM(mid.shape, bf16),
                 pltpu.VMEM((configs, hidden), f32),
                 pltpu.VMEM((2, configs, chunk, hidden), bf16),
                 pltpu.SemaphoreType.DMA((2,)),
@@ -319,11 +345,11 @@
         cost_estimate=pl.CostEstimate(
             flops=6 * groups * configs * chunk * width * width,
             transcendentals=2 * groups * configs * chunk * width,
-            bytes_accessed=10 << 20,
-        ),
-        compiler_params=pltpu.CompilerParams(vmem_limit_bytes=30 << 20),
+            bytes_accessed=groups << 20,
+        ),
+        compiler_params=pltpu.CompilerParams(vmem_limit_bytes=24 << 20),
         name="scorer",
-    )(where, *xs, ids, join, table, jbias, mid, mbias, weight)
+    )(where, *xs, ids, join, jbias, *weights, mbias, weight, *given)
 
 
 def weighted(coef, grads, out):
@@ -336,17 +362,16 @@
         out[start : start + some, :] = rows.astype(bf16)
 
 
-def fetches(grads_hbm, grads, sems, first):
-    half = grads.shape[0]
+def fetches(pair, later, which, grads, sems):
+    sources = [pair.at[which]] + [later.at[d] for d in range(grads.shape[0] - 1)]
     return [
-        pltpu.make_async_copy(grads_hbm.at[first + d], grads.at[d], sems.at[d])
-        for d in range(half)
+        pltpu.make_async_copy(source, grads.at[d], sems.at[d]) for d, source in enumerate(sources)
     ]
 
 
-def ranking_kernel(scale, where, got, pairs, grads_hbm, loss, coef, out, column, grads, sems):
+def ranking_kernel(scale, where, got, pairs, pair, later, loss, coef, out, column, grads, sems):
     half, configs, chunk, hidden = grads.shape
-    copies = fetches(grads_hbm, grads, sems, half)
+    copies = fetches(pair, later, 1, grads, sems)
     for copy in copies:
         copy.start()
     score = jnp.sum(got[...], axis=0, keepdims=True) * scale
@@ -370,9 +395,9 @@
         weighted(coef, grads.at[d], out.at[d])
 
 
-def ranking_of(scale, where, got, pairs, grads):
-    groups, configs, chunk, hidden = grads.shape
-    half = groups // 2
+def ranking_of(scale, where, got, pairs, pair, later):
+    half, configs, chunk, hidden = later.shape
+    half += 1
     return pl.pallas_call(
         functools.partial(ranking_kernel, scale),
         out_shape=(
@@ -380,7 +405,7 @@
             jax.ShapeDtypeStruct((configs, hidden), f32),
             jax.ShapeDtypeStruct((half, chunk, hidden), bf16),
         ),
-        in_specs=[SMEM, VMEM, VMEM, HBM],
+        in_specs=[SMEM, VMEM, VMEM, HBM, HBM],
         out_specs=(VMEM, VMEM, VMEM),
         scratch_shapes=[
             pltpu.VMEM((128, hidden), f32),
@@ -390,11 +415,11 @@
         cost_estimate=pl.CostEstimate(flops=1 << 24, transcendentals=0, bytes_accessed=6 << 20),
         compiler_params=pltpu.CompilerParams(vmem_limit_bytes=16 << 20),
         name="ranking",
-    )(where, got, pairs, in_hbm(grads))
-
-
-def rest_kernel(coef, grads_hbm, out, grads, sems):
-    copies = fetches(grads_hbm, grads, sems, 0)
+    )(where, got, pairs, in_hbm(pair), in_hbm(later))
+
+
+def rest_kernel(coef, pair, later, out, grads, sems):
+    copies = fetches(pair, later, 0, grads, sems)
     for copy in copies:
         copy.start()
     for d, copy in enumerate(copies):
@@ -402,13 +427,13 @@
         weighted(coef, grads.at[d], out.at[d])
 
 
-def rest_of(coef, grads):
-    groups, configs, chunk, hidden = grads.shape
-    half = groups // 2
+def rest_of(coef, pair, later):
+    half, configs, chunk, hidden = later.shape
+    half += 1
     return pl.pallas_call(
         rest_kernel,
         out_shape=jax.ShapeDtypeStruct((half, chunk, hidden), bf16),
-        in_specs=[VMEM, HBM],
+        in_specs=[VMEM, HBM, HBM],
         out_specs=VMEM,
         scratch_shapes=[
             pltpu.VMEM((half, configs, chunk, hidden), bf16),
@@ -417,7 +442,7 @@
         cost_estimate=pl.CostEstimate(flops=1 << 24, transcendentals=0, bytes_accessed=6 << 20),
         compiler_params=pltpu.CompilerParams(vmem_limit_bytes=16 << 20),
         name="rest",
-    )(coef, in_hbm(grads))
+    )(coef, in_hbm(pair), in_hbm(later))
 
 
 def shards(
@@ -451,20 +476,31 @@
     spot = lax.axis_index("node")
     flip = (spot & 1).reshape(1)
 
-    def trade(odd, partner):
-        rows = lax.dynamic_slice_in_dim(node_feats, odd * (nodes - HALO), HALO, 0)
+    def trade(rows, partner):
         pairs = [(i, partner(i)) for i in range(devices) if 0 <= partner(i) < devices]
         return lax.ppermute(rows, both, pairs)
 
-    outer = trade(spot & 1, lambda i: i + 1 if i % 2 else i - 1)
-    inner = trade(1 - (spot & 1), lambda i: i ^ 1)
+    def rim(feats, odd):
+        return lax.dynamic_slice_in_dim(feats, odd * (nodes - HALO), HALO, 0)
+
+    outer = trade(rim(node_feats, spot & 1), lambda i: i + 1 if i % 2 else i - 1)
+    inner = trade(rim(node_feats, 1 - (spot & 1)), lambda i: i ^ 1)
     nbrs = (2 * neighbors).T.reshape(near, nodes // 128, 128).transpose(1, 0, 2).reshape(-1)
     bias = sage_bias.reshape(1, -1)
     hold = lax.optimization_barrier
 
     table = table_of(node_feats)
     conf_src, _ = conf_rows_of(
-        flip, nbrs, conf_index, inner, outer, self_weight, neighbor_weight, bias, table
+        node_count,
+        flip,
+        nbrs,
+        conf_index,
+        inner,
+        outer,
+        self_weight,
+        neighbor_weight,
+        bias,
+        table,
     )
 
     def layer(first, steps, given):
@@ -487,35 +523,47 @@
     def shift(value, by):
         return lax.ppermute(value, "cfg", [(i, i ^ (2 * by)) for i in range(group_count)])
 
-    mine = lax.all_to_all(
-        conf_src.reshape(node_count, per_peer, width), "node", 0, 0, tiled=True
-    )
-    embed = layer(0, 1, None)
-    mine, embed = hold((mine, embed))
+    mine = lax.all_to_all(conf_src, "node", 0, 0, tiled=True)
+    embed = layer(0, 2, None)
+    weight = score_weight.reshape(1, -1)
+    weights = prepared(layout_table, mid_weight, weight)
+    mine, embed, *weights = hold((mine, embed, *weights))
     mine = mine.reshape(local_conf, width)
-    xs = [mine] + [shift(mine, by) for by in range(1, rings)]
-    xs = xs + [lax.ppermute(x, "cfg", swap) for x in xs]
+    others = [shift(mine, by) for by in range(1, rings)]
     where = group.reshape(1)
 
-    grads, sent = scorer_of(
-        where,
-        xs,
-        layout_ids,
-        join_weight,
-        layout_table,
-        join_bias.reshape(1, -1),
-        mid_weight,
-        mid_bias.reshape(1, -1),
-        score_weight.reshape(1, -1),
-        devices,
-    )
+    def scorer(final, turns, xs, given):
+        return scorer_of(
+            final,
+            turns,
+            where,
+            xs,
+            layout_ids,
+            join_weight,
+            join_bias.reshape(1, -1),
+            weights,
+            mid_bias.reshape(1, -1),
+            weight,
+            given,
+        )
+
+    pair, total = scorer(None, (0, rings), [mine, lax.ppermute(mine, "cfg", swap)], [])
+    others = list(hold((*others, total)))
+    total = others.pop()
+    swapped = [lax.ppermute(x, "cfg", swap) for x in others]
+    own, total = scorer(None, (1, 1), others, [total])
+    swapped = list(hold((*swapped, total)))
+    total = swapped.pop()
+    other, sent = scorer((devices, 128), (rings + 1, 1), swapped, [total])
     sent, embed = hold((sent, embed))
     got = lax.all_to_all(sent.reshape(devices, 1, 128), both, 0, 0, tiled=True)
-    embed = layer(1, 1, embed)
+    embed = layer(2, 3, embed)
     got, embed = hold((got, embed))
-    loss, coef, away = ranking_of(scale, where, got.reshape(devices, 128), config_pairs.T, grads)
+    loss, coef, away = ranking_of(
+        scale, where, got.reshape(devices, 128), config_pairs.T, pair, other
+    )
     came = lax.ppermute(away, "cfg", swap)
-    kept = rest_of(coef, grads)
+    kept = rest_of(coef, pair, own)
     sums = [kept[d].astype(f32) + came[d].astype(f32) for d in range(rings)]
     arrived = [shift(sums[d].astype(bf16), d) for d in range(1, rings)]
     row_grad = sums[0]
@@ -531,7 +579,7 @@
     conf_grad = lax.all_to_all(
         local_grad.reshape(node_count, per_peer, width), "node", 0, 0, tiled=True
     )
-    embed = layer(2, 2, embed)
+    embed = layer(5, 3, embed)
     conf_grad = conf_grad.astype(f32).reshape(local_conf, width)
     return (embed, loss.reshape(()), conf_grad)
 

time: 116 us -> 116 us (level)
  waiting for transfers between devices: 21.9 us -> 14 us
  starting transfers between devices: 41.7 us -> 46.1 us
  Pallas kernels: 45.1 us -> 48 us
    ppermute x6, waiting for transfers between devices: 8.86 us -> 3.66 us  [shift(): lax.ppermute(value, 'cfg', [(i, i ^ 2 * by) for i in range(group_count)])]
    pallas_call x2 -> x5, Pallas kernels: 17.7 us -> 20.4 us  [the longest x3 16.8 us: scorer_of(): pl.pallas_call(functools.partial(scorer_kernel, groups, final), out_shape...]
    all_to_all x1, starting transfers between devices: 6.47 us -> 9 us  [shards(): lax.all_to_all(local_grad.reshape(node_count, per_peer, width), 'node', 0...]
    all_to_all x1, waiting for transfers between devices: 5.46 us -> 3.35 us  [shards(): got = lax.all_to_all(sent.reshape(devices, 1, 128), both, 0, 0, tiled=True)]
    ppermute x4, waiting for transfers between devices: 1.24 us -> 0.01 us  [the longest x3 0.01 us: shards(): swapped = [lax.ppermute(x, 'cfg', swap) for x in others]]
  transfers between devices with their start and end apart: 16 -> 16, of which waited for: 10 -> 8; matrix products, arithmetic and copies ran while one was open for 1% -> 1% of each run, Pallas kernels for 21% -> 31%
where the time goes in v5:
time: 116 us; the launch traced here: 115 us
  Pallas kernels  48 us (41%)
  starting transfers between devices  46.1 us (40%)
  waiting for transfers between devices  14 us (12%)
  local copies, waits for them, and re-layouts  4.92 us (4%)
    pallas_call x3, Pallas kernels, layer_of(): pl.pallas_call(layer_kernel, out_shape=jax.ShapeDtypeStruct((nodes, width...  22.1 us
    pallas_call x3, Pallas kernels, scorer_of(): pl.pallas_call(functools.partial(scorer_kernel, groups, final), out_shape...  16.8 us
    all_to_all x1, starting transfers between devices, shards(): mine = lax.all_to_all(conf_src, 'node', 0, 0, tiled=True)  13.5 us
    all_to_all x1, starting transfers between devices, shards(): got = lax.all_to_all(sent.reshape(devices, 1, 128), both, 0, 0, tiled=True)  10.2 us
    all_to_all x1, starting transfers between devices, shards(): lax.all_to_all(local_grad.reshape(node_count, per_peer, width), 'node', 0...  9 us
    ppermute x6, starting transfers between devices, shift(): lax.ppermute(value, 'cfg', [(i, i ^ 2 * by) for i in range(group_count)])  8.97 us
    ppermute x6, waiting for transfers between devices, shift(): lax.ppermute(value, 'cfg', [(i, i ^ 2 * by) for i in range(group_count)])  3.66 us
    ppermute x2, waiting for transfers between devices, trade(): return lax.ppermute(rows, both, pairs)  3.6 us
  transfers between devices with their start and end apart: 16, of which 8 were waited for; matrix products, arithmetic and copies ran while one was open for 1% of the time, Pallas kernels for 31%

profile of v5, /device:TPU:2, one launch (start us, length us, event | category | flops | bytes accessed | tf_op | source)
XLA Modules:
  0.0 115.1 jit_solution(3292590131001984692)
XLA Ops:
  0.6 1.1 constant_dynamic-slice_fusion
  1.7 3.4 %collective-permute-start = (bf16[512,256]{1,0:T(8,128)(2,1)S(1)}, bf16[512,256]{1,0:T(8,128)(2,1)S(1)}, u32[]{:S(2)}, u32[]{:S(2)}) collective-permute-start(bf16[512,256]{1,0:T(8,128)(2,1)S(1)} %get-tuple-element.68), channel_id=1, source_target_pairs={{1,2},{2,1},{3,4},{4,3},{5,6},{6,5},{7,8},{8,7},{9,10},{10,9},{11,... | collective-permute-start | bytes 786440 | tf_op jit(solution)/shard_map/ppermute | solution.py:481
  5.1 0.1 collective-permute-start.1
  5.2 0.9 broadcast_multiply_fusion
  6.1 0.0 copy-start
  6.1 1.6 %copy-done = bf16[4096,256]{1,0:T(8,128)(2,1)S(1)} copy-done((bf16[4096,256]{1,0:T(8,128)(2,1)S(1)}, bf16[4096,256]{1,0:T(8,128)(2,1)}, u32[]{:S(2)}) %copy-start) | copy-done | bytes 2097176
  7.7 0.4 window_rows.1.refs_3_
  8.1 3.6 %collective-permute-done.outer = bf16[512,256]{1,0:T(8,128)(2,1)S(1)} collective-permute-done((bf16[512,256]{1,0:T(8,128)(2,1)S(1)}, bf16[512,256]{1,0:T(8,128)(2,1)S(1)}, u32[]{:S(2)}, u32[]{:S(2)}) %collective-permute-start) | collective-permute-done | bytes 262176 | tf_op jit(solution)/shard_map/ppermute | solution.py:481
  11.7 0.0 copy-start.9
  11.7 0.0 copy-start.1
  11.7 0.0 copy-start.7
  11.7 3.5 %conf_rows.1 = (bf16[32,4,256]{2,1,0:T(4,128)(2,1)}, f32[10240,128]{1,0:T(8,128)S(1)}) custom-call(s32[1]{0:T(128)} %bitcast.flip, s32[16384]{0:T(1024)S(1)} %bitcast.35, s32[128]{0:T(128)S(1)} %copy-done.10, bf16[512,256]{1,0:T(8,128)(2,1)S(1)} %collective-permute-done.outer, ...), custom_call_target="tpu_custom_call", output_to_operand_aliasing={{1}: (8, {})} | custom-call | flops 33554432 | bytes 6291456 | tf_op jit(solution)/shard_map/conf_rows/pallas_call | solution.py:125
  15.2 13.5 %all-to-all-start = ((bf16[32,4,256]{2,1,0:T(4,128)(2,1)}), bf16[32,4,256]{2,1,0:T(4,128)(2,1)}, u32[]{:S(2)}, u32[]{:S(2)}) async-start(bf16[32,4,256]{2,1,0:T(4,128)(2,1)} %get-tuple-element.35), calls=%async_computation | async-start | bytes 131072 | tf_op jit(solution)/shard_map/all_to_all | solution.py:526
  28.8 0.1 prepare.1
  28.9 0.0 copy-start.11
  28.9 0.0 copy-start.12
  29.0 5.9 %graph_layer.3.refs_0_ = bf16[4096,256]{1,0:T(8,128)(2,1)} custom-call(s32[1]{0:T(128)} %bitcast.flip, s32[16384]{0:T(1024)S(1)} %bitcast.36, bf16[512,256]{1,0:T(8,128)(2,1)S(1)} %collective-permute-done.outer, bf16[512,256]{1,0:T(8,128)(2,1)S(1)} %collective-permute-done.1.inner, bf16[4096,256]{1,0:T(8,128)(2,1)S(1)} %copy-done.1, ...), custom_call_target="tpu_custom_call" | custom-call | flops 268435456 | bytes 16777216 | tf_op jit(solution)/shard_map/graph_layer/pallas_call | solution.py:189
  34.9 2.7 %all-to-all-done = bf16[32,4,256]{2,1,0:T(4,128)(2,1)} async-done(((bf16[32,4,256]{2,1,0:T(4,128)(2,1)}), bf16[32,4,256]{2,1,0:T(4,128)(2,1)}, u32[]{:S(2)}, u32[]{:S(2)}) %all-to-all-start) | async-done | bytes 65568 | tf_op jit(solution)/shard_map/all_to_all | solution.py:526
  37.6 0.9 reshape.76.refs_0_
  38.5 0.1 collective-permute-start.5
  38.6 2.0 %collective-permute-start.2 = (bf16[128,256]{1,0:T(8,128)(2,1)S(1)}, bf16[128,256]{1,0:T(8,128)(2,1)S(1)}, u32[]{:S(2)}, u32[]{:S(2)}) collective-permute-start(bf16[128,256]{1,0:T(8,128)(2,1)S(1)} %reshape.76.refs_0_), channel_id=1, source_target_pairs={{0,64},{32,96},{64,0},{96,32},{128,192},{160,224},{192,128},{224,1... | collective-permute-start | bytes 196616 | tf_op jit(solution)/shard_map/ppermute | solution.py:524
  40.6 2.7 %collective-permute-start.3 = (bf16[128,256]{1,0:T(8,128)(2,1)S(1)}, bf16[128,256]{1,0:T(8,128)(2,1)S(1)}, u32[]{:S(2)}, u32[]{:S(2)}) collective-permute-start(bf16[128,256]{1,0:T(8,128)(2,1)S(1)} %reshape.76.refs_0_), channel_id=1, source_target_pairs={{0,128},{32,160},{64,192},{96,224},{128,0},{160,32},{192,64},{224,... | collective-permute-start | bytes 196616 | tf_op jit(solution)/shard_map/ppermute | solution.py:524
  43.3 0.1 collective-permute-start.4
  43.4 5.0 %scorer.3 = (bf16[2,16,128,256]{3,2,1,0:T(8,128)(2,1)}, f32[16,256]{1,0:T(8,128)S(1)}) custom-call(s32[1]{0:T(128)} %bitcast.6.where, bf16[128,256]{1,0:T(8,128)(2,1)S(1)} %reshape.76.refs_0_, bf16[128,256]{1,0:T(8,128)(2,1)} %collective-permute-done.5.refs_1_, s32[16,1024]{1,0:T(8,128)S(1)} %copy-done.11, bf16[256,256]{1,0:T(8,128)(2,1)S(1)} %copy-done.5, ...), custom_call_target="tpu_custom_call" | custom-call | flops 1610612736 | bytes 2097152 | tf_op jit(solution)/shard_map/scorer/pallas_call | solution.py:321
  48.5 0.3 collective-permute-done.4.refs_2_
  48.7 0.5 collective-permute-start.7
  49.2 5.5 %scorer.4 = (bf16[3,16,128,256]{3,2,1,0:T(8,128)(2,1)}, f32[16,256]{1,0:T(8,128)S(1)}) custom-call(s32[1]{0:T(128)} %bitcast.6.where, bf16[128,256]{1,0:T(8,128)(2,1)S(1)} %collective-permute-done.2.refs_0_, bf16[128,256]{1,0:T(8,128)(2,1)S(1)} %collective-permute-done.3.refs_1_, bf16[128,256]{1,0:T(8,128)(2,1)S(1)} %collective-permute-done.4.refs_2_, ...), custom_call_target="tpu_custom_call" | custom-call | flops 2415919104 | bytes 3145728 | tf_op jit(solution)/shard_map/scorer/pallas_call | solution.py:321
  54.8 6.3 %scorer.5 = (bf16[3,16,128,256]{3,2,1,0:T(8,128)(2,1)}, f32[256,128]{1,0:T(8,128)}) custom-call(s32[1]{0:T(128)} %bitcast.6.where, bf16[128,256]{1,0:T(8,128)(2,1)S(1)} %collective-permute-done.6.refs_0_, bf16[128,256]{1,0:T(8,128)(2,1)S(1)} %collective-permute-done.7.refs_1_, bf16[128,256]{1,0:T(8,128)(2,1)S(1)} %collective-permute-done.8.refs_2_, ...), custom_call_target="tpu_custom_call" | custom-call | flops 2415919104 | bytes 3145728 | tf_op jit(solution)/shard_map/scorer/pallas_call | solution.py:321
  61.1 10.2 %all-to-all-start.1 = ((f32[256,1,128]{2,1,0:T(1,128)}), f32[256,1,128]{2,1,0:T(1,128)S(1)}, u32[]{:S(2)}, u32[]{:S(2)}) async-start(f32[256,1,128]{2,1,0:T(1,128)} %bitcast.14), calls=%async_computation.1 | async-start | bytes 262144 | tf_op jit(solution)/shard_map/all_to_all | solution.py:559
  71.3 0.0 copy-start.8
  71.3 8.1 %graph_layer.4.refs_0_ = bf16[4096,256]{1,0:T(8,128)(2,1)} custom-call(s32[1]{0:T(128)} %bitcast.flip, s32[16384]{0:T(1024)S(1)} %bitcast.37, bf16[512,256]{1,0:T(8,128)(2,1)S(1)} %collective-permute-done.outer, bf16[512,256]{1,0:T(8,128)(2,1)S(1)} %collective-permute-done.1.inner, bf16[4096,256]{1,0:T(8,128)(2,1)S(1)} %copy-done.1, ...), custom_call_target="tpu_custom_call", output_to_operand_aliasing={{}: (9, {})} | custom-call | flops 402653184 | bytes 25165824 | tf_op jit(solution)/shard_map/graph_layer/pallas_call | solution.py:189
  79.4 3.4 %all-to-all-done.1 = f32[256,1,128]{2,1,0:T(1,128)S(1)} async-done(((f32[256,1,128]{2,1,0:T(1,128)}), f32[256,1,128]{2,1,0:T(1,128)S(1)}, u32[]{:S(2)}, u32[]{:S(2)}) %all-to-all-start.1) | async-done | bytes 131104 | tf_op jit(solution)/shard_map/all_to_all | solution.py:559
  82.7 2.7 %ranking.1 = (f32[1,1]{1,0:T(1,128)}, f32[16,256]{1,0:T(8,128)S(1)}, bf16[4,128,256]{2,1,0:T(8,128)(2,1)S(1)}) custom-call(s32[1]{0:T(128)} %bitcast.6.where, f32[256,128]{1,0:T(8,128)S(1)} %bitcast.39, s32[2,512]{1,0:T(2,128)S(1)} %bitcast.44, bf16[2,16,128,256]{3,2,1,0:T(8,128)(2,1)} %get-tuple-element.58.pair, ...), custom_call_target="tpu_custom_call" | custom-call | flops 16777216 | bytes 6291456 | tf_op jit(solution)/shard_map/ranking/pallas_call | solution.py:401
  85.4 0.3 collective-permute-start.9
  85.7 2.4 %rest.1 = bf16[4,128,256]{2,1,0:T(8,128)(2,1)S(1)} custom-call(f32[16,256]{1,0:T(8,128)S(1)} %get-tuple-element.60.coef, bf16[2,16,128,256]{3,2,1,0:T(8,128)(2,1)} %get-tuple-element.58.pair, bf16[3,16,128,256]{3,2,1,0:T(8,128)(2,1)} %get-tuple-element.61.later), custom_call_target="tpu_custom_call" | custom-call | flops 16777216 | bytes 6291456 | tf_op jit(solution)/shard_map/rest/pallas_call | solution.py:433
  88.2 0.1 fusion.3
  88.2 1.0 collective-permute-start.12
  89.2 1.8 %collective-permute-start.11 = (bf16[128,256]{1,0:T(8,128)(2,1)S(1)}, bf16[128,256]{1,0:T(8,128)(2,1)S(1)}, u32[]{:S(2)}, u32[]{:S(2)}) collective-permute-start(bf16[128,256]{1,0:T(8,128)(2,1)S(1)} %get-tuple-element.71), channel_id=1, source_target_pairs={{0,128},{32,160},{64,192},{96,224},{128,0},{160,32},{192,64},{224,... | collective-permute-start | bytes 196616 | tf_op jit(solution)/shard_map/ppermute | solution.py:524
  91.0 1.4 %collective-permute-start.10 = (bf16[128,256]{1,0:T(8,128)(2,1)S(1)}, bf16[128,256]{1,0:T(8,128)(2,1)S(1)}, u32[]{:S(2)}, u32[]{:S(2)}) collective-permute-start(bf16[128,256]{1,0:T(8,128)(2,1)S(1)} %get-tuple-element.69), channel_id=1, source_target_pairs={{0,64},{32,96},{64,0},{96,32},{128,192},{160,224},{192,128},{224,1... | collective-permute-start | bytes 196616 | tf_op jit(solution)/shard_map/ppermute | solution.py:524
  92.4 2.8 %collective-permute-done.12 = bf16[128,256]{1,0:T(8,128)(2,1)S(1)} collective-permute-done((bf16[128,256]{1,0:T(8,128)(2,1)S(1)}, bf16[128,256]{1,0:T(8,128)(2,1)S(1)}, u32[]{:S(2)}, u32[]{:S(2)}) %collective-permute-start.12) | collective-permute-done | bytes 65568 | tf_op jit(solution)/shard_map/ppermute | solution.py:524
  95.2 0.1 collective-permute-done.11
  95.3 0.5 collective-permute-done.10
  95.8 0.2 convolution_convert_fusion
  96.0 0.7 reshape.82
  96.7 9.0 %all-to-all-start.2 = ((bf16[32,4,256]{2,1,0:T(4,128)(2,1)}), bf16[32,4,256]{2,1,0:T(4,128)(2,1)S(1)}, u32[]{:S(2)}, u32[]{:S(2)}) async-start(bf16[32,4,256]{2,1,0:T(4,128)(2,1)} %reshape.82), calls=%async_computation.2 | async-start | bytes 131072 | tf_op jit(solution)/shard_map/all_to_all | solution.py:579
  105.7 8.1 %graph_layer.5 = bf16[4096,256]{1,0:T(8,128)(2,1)} custom-call(s32[1]{0:T(128)} %bitcast.flip, s32[16384]{0:T(1024)S(1)} %bitcast.38, bf16[512,256]{1,0:T(8,128)(2,1)S(1)} %collective-permute-done.outer, bf16[512,256]{1,0:T(8,128)(2,1)S(1)} %collective-permute-done.1.inner, bf16[4096,256]{1,0:T(8,128)(2,1)S(1)} %copy-done.1, ...), custom_call_target="tpu_custom_call", output_to_operand_aliasing={{}: (9, {})} | custom-call | flops 402653184 | bytes 25165824 | tf_op jit(solution)/shard_map/graph_layer/pallas_call | solution.py:189
  113.8 0.6 all-to-all-done.2
  114.4 0.7 reshape.86
  (30 shorter events, 0.1 us)
Async XLA Ops:
  1.7 9.9 %collective-permute-start = (bf16[512,256]{1,0:T(8,128)(2,1)S(1)}, bf16[512,256]{1,0:T(8,128)(2,1)S(1)}, u32[]{:S(2)}, u32[]{:S(2)}) collective-permute-start(bf16[512,256]{1,0:T(8,128)(2,1)S(1)} %get-tuple-element.68), channel_id=1, source_target_pairs={{1,2},{2,1},{3,4},{4,3},{5,6},{6,5},{7,8},{8,7},{9,10},{10,9},{11,... | collective-permute-start | bytes 786440 | tf_op jit(solution)/shard_map/ppermute | solution.py:481
  5.1 6.5 %collective-permute-start.1 = (bf16[512,256]{1,0:T(8,128)(2,1)S(1)}, bf16[512,256]{1,0:T(8,128)(2,1)S(1)}, u32[]{:S(2)}, u32[]{:S(2)}) collective-permute-start(bf16[512,256]{1,0:T(8,128)(2,1)S(1)} %get-tuple-element.67), channel_id=1, source_target_pairs={{0,1},{1,0},{2,3},{3,2},{4,5},{5,4},{6,7},{7,6},{8,9},{9,8},{10,11... | collective-permute-start | bytes 786440 | tf_op jit(solution)/shard_map/ppermute | solution.py:481
  6.1 1.6 %copy-start = (bf16[4096,256]{1,0:T(8,128)(2,1)S(1)}, bf16[4096,256]{1,0:T(8,128)(2,1)}, u32[]{:S(2)}) copy-start(bf16[4096,256]{1,0:T(8,128)(2,1)} %own.5) | copy-start | bytes 6291460
  7.7 4.0 %copy-start.10 = (s32[128]{0:T(128)S(1)}, s32[128]{0:T(128)}, u32[]{:S(2)}) copy-start(s32[128]{0:T(128)} %picks.1) | copy-start | bytes 1540
  11.7 17.1 %copy-start.4 = (bf16[256,256]{1,0:T(8,128)(2,1)S(1)}, bf16[256,256]{1,0:T(8,128)(2,1)}, u32[]{:S(2)}) copy-start(bf16[256,256]{1,0:T(8,128)(2,1)} %mid.1) | copy-start | bytes 393220
  11.7 17.1 %copy-start.6 = (bf16[128,256]{1,0:T(8,128)(2,1)S(1)}, bf16[128,256]{1,0:T(8,128)(2,1)}, u32[]{:S(2)}) copy-start(bf16[128,256]{1,0:T(8,128)(2,1)} %table.1) | copy-start | bytes 196612
  11.7 17.1 %copy-start.9 = (f32[256]{0:T(256)S(1)}, f32[256]{0:T(256)}, u32[]{:S(2)}) copy-start(f32[256]{0:T(256)} %param.26) | copy-start | bytes 3076
  11.7 17.2 %copy-start.1 = (bf16[4096,256]{1,0:T(8,128)(2,1)S(1)}, bf16[4096,256]{1,0:T(8,128)(2,1)}, u32[]{:S(2)}) copy-start(bf16[4096,256]{1,0:T(8,128)(2,1)} %own.5) | copy-start | bytes 6291460
  11.7 17.2 %copy-start.2 = (bf16[256,256]{1,0:T(8,128)(2,1)S(1)}, bf16[256,256]{1,0:T(8,128)(2,1)}, u32[]{:S(2)}) copy-start(bf16[256,256]{1,0:T(8,128)(2,1)} %sw.5) | copy-start | bytes 393220
  11.7 17.2 %copy-start.3 = (bf16[256,256]{1,0:T(8,128)(2,1)S(1)}, bf16[256,256]{1,0:T(8,128)(2,1)}, u32[]{:S(2)}) copy-start(bf16[256,256]{1,0:T(8,128)(2,1)} %nw.5) | copy-start | bytes 393220
  11.7 17.2 %copy-start.7 = (f32[256]{0:T(256)S(1)}, f32[256]{0:T(256)}, u32[]{:S(2)}) copy-start(f32[256]{0:T(256)} %param.18) | copy-start | bytes 3076
  15.2 22.4 %all-to-all-start = ((bf16[32,4,256]{2,1,0:T(4,128)(2,1)}), bf16[32,4,256]{2,1,0:T(4,128)(2,1)}, u32[]{:S(2)}, u32[]{:S(2)}) async-start(bf16[32,4,256]{2,1,0:T(4,128)(2,1)} %get-tuple-element.35), calls=%async_computation | async-start | bytes 131072 | tf_op jit(solution)/shard_map/all_to_all | solution.py:526
  28.9 14.5 %copy-start.5 = (bf16[256,256]{1,0:T(8,128)(2,1)S(1)}, bf16[256,256]{1,0:T(8,128)(2,1)}, u32[]{:S(2)}) copy-start(bf16[256,256]{1,0:T(8,128)(2,1)} %refs_4_.3) | copy-start | bytes 393220
  28.9 14.4 %copy-start.11 = (s32[16,1024]{1,0:T(8,128)S(1)}, s32[16,1024]{1,0:T(8,128)}, u32[]{:S(2)}) copy-start(s32[16,1024]{1,0:T(8,128)} %refs_3_.5) | copy-start | bytes 196612
  28.9 14.4 %copy-start.12 = (f32[256]{0:T(256)S(1)}, f32[256]{0:T(256)}, u32[]{:S(2)}) copy-start(f32[256]{0:T(256)} %param.23) | copy-start | bytes 3076
  29.0 14.4 %copy-start.13 = (f32[256]{0:T(256)S(1)}, f32[256]{0:T(256)}, u32[]{:S(2)}) copy-start(f32[256]{0:T(256)} %param.25) | copy-start | bytes 3076
  38.5 4.9 %collective-permute-start.5 = (bf16[128,256]{1,0:T(8,128)(2,1)S(1)}, bf16[128,256]{1,0:T(8,128)(2,1)}, u32[]{:S(2)}, u32[]{:S(2)}) collective-permute-start(bf16[128,256]{1,0:T(8,128)(2,1)S(1)} %reshape.76.refs_0_), channel_id=1, source_target_pairs={{0,32},{32,0},{64,96},{96,64},{128,160},{160,128},{192,224},{224,1... | collective-permute-start | bytes 196616 | tf_op jit(solution)/shard_map/ppermute | solution.py:550
  38.6 9.9 %collective-permute-start.2 = (bf16[128,256]{1,0:T(8,128)(2,1)S(1)}, bf16[128,256]{1,0:T(8,128)(2,1)S(1)}, u32[]{:S(2)}, u32[]{:S(2)}) collective-permute-start(bf16[128,256]{1,0:T(8,128)(2,1)S(1)} %reshape.76.refs_0_), channel_id=1, source_target_pairs={{0,64},{32,96},{64,0},{96,32},{128,192},{160,224},{192,128},{224,1... | collective-permute-start | bytes 196616 | tf_op jit(solution)/shard_map/ppermute | solution.py:524
  40.6 7.9 %collective-permute-start.3 = (bf16[128,256]{1,0:T(8,128)(2,1)S(1)}, bf16[128,256]{1,0:T(8,128)(2,1)S(1)}, u32[]{:S(2)}, u32[]{:S(2)}) collective-permute-start(bf16[128,256]{1,0:T(8,128)(2,1)S(1)} %reshape.76.refs_0_), channel_id=1, source_target_pairs={{0,128},{32,160},{64,192},{96,224},{128,0},{160,32},{192,64},{224,... | collective-permute-start | bytes 196616 | tf_op jit(solution)/shard_map/ppermute | solution.py:524
  43.3 5.5 %collective-permute-start.4 = (bf16[128,256]{1,0:T(8,128)(2,1)S(1)}, bf16[128,256]{1,0:T(8,128)(2,1)S(1)}, u32[]{:S(2)}, u32[]{:S(2)}) collective-permute-start(bf16[128,256]{1,0:T(8,128)(2,1)S(1)} %reshape.76.refs_0_), channel_id=1, source_target_pairs={{0,192},{32,224},{64,128},{96,160},{128,64},{160,96},{192,0},{224,... | collective-permute-start | bytes 196616 | tf_op jit(solution)/shard_map/ppermute | solution.py:524
  48.7 6.1 %collective-permute-start.6 = (bf16[128,256]{1,0:T(8,128)(2,1)S(1)}, bf16[128,256]{1,0:T(8,128)(2,1)S(1)}, u32[]{:S(2)}, u32[]{:S(2)}) collective-permute-start(bf16[128,256]{1,0:T(8,128)(2,1)S(1)} %collective-permute-done.2.refs_0_), channel_id=1, source_target_pairs={{0,32},{32,0},{64,96},{96,64},{128,160},{160,128},{192,224},{224,1... | collective-permute-start | bytes 196616 | tf_op jit(solution)/shard_map/ppermute | solution.py:553
  48.7 6.1 %collective-permute-start.7 = (bf16[128,256]{1,0:T(8,128)(2,1)S(1)}, bf16[128,256]{1,0:T(8,128)(2,1)S(1)}, u32[]{:S(2)}, u32[]{:S(2)}) collective-permute-start(bf16[128,256]{1,0:T(8,128)(2,1)S(1)} %collective-permute-done.3.refs_1_), channel_id=1, source_target_pairs={{0,32},{32,0},{64,96},{96,64},{128,160},{160,128},{192,224},{224,1... | collective-permute-start | bytes 196616 | tf_op jit(solution)/shard_map/ppermute | solution.py:553
  49.2 5.6 %collective-permute-start.8 = (bf16[128,256]{1,0:T(8,128)(2,1)S(1)}, bf16[128,256]{1,0:T(8,128)(2,1)S(1)}, u32[]{:S(2)}, u32[]{:S(2)}) collective-permute-start(bf16[128,256]{1,0:T(8,128)(2,1)S(1)} %collective-permute-done.4.refs_2_), channel_id=1, source_target_pairs={{0,32},{32,0},{64,96},{96,64},{128,160},{160,128},{192,224},{224,1... | collective-permute-start | bytes 196616 | tf_op jit(solution)/shard_map/ppermute | solution.py:553
  61.1 21.6 %all-to-all-start.1 = ((f32[256,1,128]{2,1,0:T(1,128)}), f32[256,1,128]{2,1,0:T(1,128)S(1)}, u32[]{:S(2)}, u32[]{:S(2)}) async-start(f32[256,1,128]{2,1,0:T(1,128)} %bitcast.14), calls=%async_computation.1 | async-start | bytes 262144 | tf_op jit(solution)/shard_map/all_to_all | solution.py:559
  71.3 11.4 %copy-start.8 = (s32[512,2]{0,1:T(2,128)S(1)}, s32[512,2]{0,1:T(2,128)}, u32[]{:S(2)}) copy-start(s32[512,2]{0,1:T(2,128)} %param.27) | copy-start | bytes 12292
  85.4 2.7 %collective-permute-start.9 = (bf16[4,128,256]{2,1,0:T(8,128)(2,1)S(1)}, bf16[4,128,256]{2,1,0:T(8,128)(2,1)S(1)}, u32[]{:S(2)}, u32[]{:S(2)}) collective-permute-start(bf16[4,128,256]{2,1,0:T(8,128)(2,1)S(1)} %get-tuple-element.62), channel_id=1, source_target_pairs={{0,32},{32,0},{64,96},{96,64},{128,160},{160,128},{192,224},{224,1... | collective-permute-start | bytes 786440 | tf_op jit(solution)/shard_map/ppermute | solution.py:565
  88.2 7.0 %collective-permute-start.12 = (bf16[128,256]{1,0:T(8,128)(2,1)S(1)}, bf16[128,256]{1,0:T(8,128)(2,1)S(1)}, u32[]{:S(2)}, u32[]{:S(2)}) collective-permute-start(bf16[128,256]{1,0:T(8,128)(2,1)S(1)} %get-tuple-element.70), channel_id=1, source_target_pairs={{0,192},{32,224},{64,128},{96,160},{128,64},{160,96},{192,0},{224,... | collective-permute-start | bytes 196616 | tf_op jit(solution)/shard_map/ppermute | solution.py:524
  89.2 6.0 %collective-permute-start.11 = (bf16[128,256]{1,0:T(8,128)(2,1)S(1)}, bf16[128,256]{1,0:T(8,128)(2,1)S(1)}, u32[]{:S(2)}, u32[]{:S(2)}) collective-permute-start(bf16[128,256]{1,0:T(8,128)(2,1)S(1)} %get-tuple-element.71), channel_id=1, source_target_pairs={{0,128},{32,160},{64,192},{96,224},{128,0},{160,32},{192,64},{224,... | collective-permute-start | bytes 196616 | tf_op jit(solution)/shard_map/ppermute | solution.py:524
  91.0 4.8 %collective-permute-start.10 = (bf16[128,256]{1,0:T(8,128)(2,1)S(1)}, bf16[128,256]{1,0:T(8,128)(2,1)S(1)}, u32[]{:S(2)}, u32[]{:S(2)}) collective-permute-start(bf16[128,256]{1,0:T(8,128)(2,1)S(1)} %get-tuple-element.69), channel_id=1, source_target_pairs={{0,64},{32,96},{64,0},{96,32},{128,192},{160,224},{192,128},{224,1... | collective-permute-start | bytes 196616 | tf_op jit(solution)/shard_map/ppermute | solution.py:524
  96.7 17.7 %all-to-all-start.2 = ((bf16[32,4,256]{2,1,0:T(4,128)(2,1)}), bf16[32,4,256]{2,1,0:T(4,128)(2,1)S(1)}, u32[]{:S(2)}, u32[]{:S(2)}) async-start(bf16[32,4,256]{2,1,0:T(4,128)(2,1)} %reshape.82), calls=%async_computation.2 | async-start | bytes 131072 | tf_op jit(solution)/shard_map/all_to_all | solution.py:579

commit v6 on v5

--- a/solution.py
+++ b/solution.py
@@ -48,106 +48,116 @@
     return table[pl.ds(pl.multiple_of(at, 2), 2), :]
 
 
-def table_kernel(feats, table):
+def table_kernel(nbrs, picks, feats, sw, bias, table, spots, base, own):
     rows = feats.shape[0]
-    put_rows(table, HALO + pl.multiple_of(pl.program_id(0) * rows, rows), feats)
-
-
-def table_of(feats):
+    step = pl.program_id(0)
+    put_rows(table, HALO + pl.multiple_of(step * rows, rows), feats)
+
+    @pl.when(step == pl.num_programs(0) - 1)
+    def _():
+        count = picks.shape[0]
+        own3 = own.reshape(count, 2, 128)
+
+        def body(block, carry):
+            values = []
+            for j in range(8):
+                g = picks[block * 8 + j]
+                at = (g >> 7) * 512 + (g & 127)
+                for k in range(4):
+                    spots[k * count + block * 8 + j] = nbrs[at + 128 * k]
+                values.append(pair_at(table, 2 * (HALO + g)))
+            for j in range(8):
+                own3[block * 8 + j] = values[j]
+            return carry
+
+        lax.fori_loop(0, count // 8, body, 0)
+        left, right = [own[pl.ds(side, count, stride=2), :].astype(bf16) for side in (0, 1)]
+        pre = jnp.dot(left, sw[:128, :], preferred_element_type=f32)
+        pre += jnp.dot(right, sw[128:, :], preferred_element_type=f32)
+        base[...] = pre + bias[...]
+
+
+def table_of(nbrs, picks, feats, sw, bias):
     nodes, width = feats.shape
+    count = picks.shape[0]
     tile = 512
     return pl.pallas_call(
         table_kernel,
-        out_shape=jax.ShapeDtypeStruct((2 * (nodes + 2 * HALO), 128), f32),
+        out_shape=(
+            jax.ShapeDtypeStruct((2 * (nodes + 2 * HALO), 128), f32),
+            jax.ShapeDtypeStruct((4 * count,), jnp.int32),
+            jax.ShapeDtypeStruct((count, width), f32),
+        ),
         grid=(nodes // tile,),
-        in_specs=[pl.BlockSpec((tile, width), lambda i: (i, 0))],
-        out_specs=VMEM,
-        cost_estimate=pl.CostEstimate(flops=1 << 20, transcendentals=0, bytes_accessed=6 << 20),
+        in_specs=[SMEM, SMEM, pl.BlockSpec((tile, width), lambda i: (i, 0)), VMEM, VMEM],
+        out_specs=(VMEM, SMEM, VMEM),
+        scratch_shapes=[pltpu.VMEM((2 * count, 128), f32)],
+        cost_estimate=pl.CostEstimate(flops=1 << 24, transcendentals=0, bytes_accessed=6 << 20),
         compiler_params=pltpu.CompilerParams(vmem_limit_bytes=16 << 20),
         name="window_rows",
-    )(feats)
-
-
-def layer_rows(own_left, own_right, left, right, sw, nw, bias, kind=bf16):
-    pre = jnp.dot(own_left, sw[:128, :], preferred_element_type=f32)
-    pre += jnp.dot(own_right, sw[128:, :], preferred_element_type=f32)
+    )(nbrs, picks, feats, sw, bias)
+
+
+def layer_rows(own, left, right, sw, nw, bias):
+    pre = jnp.dot(own, sw[...], preferred_element_type=f32) + bias[...]
     pre += jnp.dot(left, nw[:128, :], preferred_element_type=f32)
     pre += jnp.dot(right, nw[128:, :], preferred_element_type=f32)
-    return half_silu(0.5 * (pre + bias[...]))[0].astype(kind)
-
-
-def conf_kernel(flip, nbrs, picks, outer, inner, *refs):
-    sw_hbm, nw_hbm, bias_hbm, given, out, table, own, acc, sw, nw, bias, sems = refs
-    copies = [
-        pltpu.make_async_copy(source, target, sems.at[i])
-        for i, (source, target) in enumerate(((sw_hbm, sw), (nw_hbm, nw), (bias_hbm, bias)))
-    ]
-    for copy in copies:
-        copy.start()
+    return half_silu(0.5 * pre)[0].astype(bf16)
+
+
+def conf_kernel(flip, spots, outer, inner, nw_hbm, base, given, out, table, acc, nw, sem):
+    weights = pltpu.make_async_copy(nw_hbm, nw, sem)
+    weights.start()
     put_rims(table, flip, inner, outer)
-    count = picks.shape[0]
-    own3 = own.reshape(count, 2, 128)
+    count = base.shape[0]
     acc3 = acc.reshape(count, 2, 128)
+    some = 16
 
     def body(block, carry):
         values = []
-        for j in range(8):
-            g = picks[block * 8 + j]
-            at = (g >> 7) * 512 + (g & 127)
-            near = [pair_at(table, nbrs[at + 128 * k]) for k in range(4)]
-            values.append((pair_at(table, 2 * (HALO + g)), (near[0] + near[1]) + (near[2] + near[3])))
-        for j in range(8):
-            own3[block * 8 + j], acc3[block * 8 + j] = values[j]
+        for j in range(some):
+            near = [pair_at(table, spots[k * count + block * some + j]) for k in range(4)]
+            values.append((near[0] + near[1]) + (near[2] + near[3]))
+        for j in range(some):
+            acc3[block * some + j] = values[j]
         return carry
 
-    lax.fori_loop(0, count // 8, body, 0)
-    halves = [ref[pl.ds(side, count, stride=2), :] for ref in (own, acc) for side in (0, 1)]
-    for copy in copies:
-        copy.wait()
-    value = layer_rows(
-        halves[0].astype(bf16),
-        halves[1].astype(bf16),
-        (halves[2] * 0.25).astype(bf16),
-        (halves[3] * 0.25).astype(bf16),
-        sw,
-        nw,
-        bias,
-        f32,
-    )
+    lax.fori_loop(0, count // some, body, 0)
+    left, right = [(acc[pl.ds(side, count, stride=2), :] * 0.25).astype(bf16) for side in (0, 1)]
+    weights.wait()
+    pre = base[...] + jnp.dot(left, nw[:128, :], preferred_element_type=f32)
+    pre += jnp.dot(right, nw[128:, :], preferred_element_type=f32)
+    value = half_silu(0.5 * pre)[0]
     share = out.shape[1]
     for peer in range(out.shape[0]):
         out[peer] = value[peer * share : (peer + 1) * share, :].astype(bf16)
 
 
-def conf_rows_of(peers, flip, nbrs, picks, inner, outer, sw, nw, bias, table):
-    count = picks.shape[0]
-    width = sw.shape[0]
+def conf_rows_of(peers, flip, spots, inner, outer, nw, base, table):
+    count, width = base.shape
     return pl.pallas_call(
         conf_kernel,
         out_shape=(
             jax.ShapeDtypeStruct((peers, count // peers, width), bf16),
             jax.ShapeDtypeStruct(table.shape, f32),
         ),
-        in_specs=[SMEM] * 3 + [VMEM] * 2 + [HBM] * 3 + [VMEM],
+        in_specs=[SMEM] * 2 + [VMEM] * 2 + [HBM] + [VMEM] * 2,
         out_specs=(VMEM, VMEM),
-        input_output_aliases={8: 1},
+        input_output_aliases={6: 1},
         scratch_shapes=[
             pltpu.VMEM((2 * count, 128), f32),
-            pltpu.VMEM((2 * count, 128), f32),
-            pltpu.VMEM(sw.shape, bf16),
             pltpu.VMEM(nw.shape, bf16),
-            pltpu.VMEM(bias.shape, f32),
-            pltpu.SemaphoreType.DMA((3,)),
+            pltpu.SemaphoreType.DMA,
         ],
         cost_estimate=pl.CostEstimate(
             flops=4 * count * width * width, transcendentals=0, bytes_accessed=6 << 20
         ),
         compiler_params=pltpu.CompilerParams(vmem_limit_bytes=16 << 20),
         name="conf_rows",
-    )(flip, nbrs, picks, outer, inner, in_hbm(sw), in_hbm(nw), in_hbm(bias), table)
-
-
-def layer_kernel(flip, nbrs, outer, inner, feats, own, sw, nw, bias, *refs):
+    )(flip, spots, outer, inner, in_hbm(nw), base, table)
+
+
+def layer_kernel(flip, nbrs, inner, outer, feats, own, sw, nw, bias, *refs):
     out, table, acc = refs[-3:]
     tile = own.shape[0]
     nodes = feats.shape[0]
@@ -170,10 +180,8 @@
         return carry
 
     lax.fori_loop(0, tile // 128, body, 0)
-    rows = own[...]
     out[...] = layer_rows(
-        rows[:, :128],
-        rows[:, 128:],
+        own[...],
         (acc[pl.ds(0, tile, stride=2), :] * 0.25).astype(bf16),
         (acc[pl.ds(1, tile, stride=2), :] * 0.25).astype(bf16),
         sw,
@@ -213,7 +221,7 @@
         ),
         compiler_params=pltpu.CompilerParams(vmem_limit_bytes=24 << 20),
         name="graph_layer",
-    )(flip, nbrs, outer, inner, feats, feats, sw, nw, bias, *ahead)
+    )(flip, nbrs, inner, outer, feats, feats, sw, nw, bias, *ahead)
 
 
 def place_of(group, turn):
@@ -489,18 +497,9 @@
     bias = sage_bias.reshape(1, -1)
     hold = lax.optimization_barrier
 
-    table = table_of(node_feats)
+    table, spots, base = table_of(nbrs, conf_index, node_feats, self_weight, bias)
     conf_src, _ = conf_rows_of(
-        node_count,
-        flip,
-        nbrs,
-        conf_index,
-        inner,
-        outer,
-        self_weight,
-        neighbor_weight,
-        bias,
-        table,
+        node_count, flip, spots, inner, outer, neighbor_weight, base, table
     )
 
     def layer(first, steps, given):
@@ -557,7 +556,7 @@
     other, sent = scorer((devices, 128), (rings + 1, 1), swapped, [total])
     sent, embed = hold((sent, embed))
     got = lax.all_to_all(sent.reshape(devices, 1, 128), both, 0, 0, tiled=True)
-    embed = layer(2, 3, embed)
+    embed = layer(2, 4, embed)
     got, embed = hold((got, embed))
     loss, coef, away = ranking_of(
         scale, where, got.reshape(devices, 128), config_pairs.T, pair, other
@@ -579,7 +578,7 @@
     conf_grad = lax.all_to_all(
         local_grad.reshape(node_count, per_peer, width), "node", 0, 0, tiled=True
     )
-    embed = layer(5, 3, embed)
+    embed = layer(6, 2, embed)
     conf_grad = conf_grad.astype(f32).reshape(local_conf, width)
     return (embed, loss.reshape(()), conf_grad)
 

time: 116 us -> 117 us (level)
  waiting for transfers between devices: 14 us -> 10.9 us
  local copies, waits for them, and re-layouts: 4.92 us -> 7.15 us
  Pallas kernels: 48 us -> 49.9 us
    ppermute x2, waiting for transfers between devices: 3.6 us -> 0.01 us  [trade(): return lax.ppermute(rows, both, pairs)]
    pallas_call x1, Pallas kernels: 0.37 us -> 3.84 us  [table_of(): pl.pallas_call(table_kernel, out_shape=(jax.ShapeDtypeStruct((2 * (nodes...]
    all_to_all x1, starting transfers between devices: 13.5 us -> 11.2 us  [shards(): mine = lax.all_to_all(conf_src, 'node', 0, 0, tiled=True)]
    all_to_all x1, waiting for transfers between devices: 0.63 us -> 2.88 us  [shards(): lax.all_to_all(local_grad.reshape(node_count, per_peer, width), 'node', 0...]
    unnamed x28 -> x32, local copies, waits for them, and re-layouts: 1.66 us -> 3.9 us
    all_to_all x1, starting transfers between devices: 9 us -> 10.8 us  [shards(): lax.all_to_all(local_grad.reshape(node_count, per_peer, width), 'node', 0...]
    all_to_all x1, waiting for transfers between devices: 3.35 us -> 1.53 us  [shards(): got = lax.all_to_all(sent.reshape(devices, 1, 128), both, 0, 0, tiled=True)]
    ppermute x2, starting transfers between devices: 3.49 us -> 4.67 us  [trade(): return lax.ppermute(rows, both, pairs)]
  transfers between devices with their start and end apart: 16 -> 16, of which waited for: 8 -> 7; matrix products, arithmetic and copies ran while one was open for 1% -> 1% of each run, Pallas kernels for 31% -> 33%
where the time goes in v6:
time: 117 us
  Pallas kernels  49.9 us (43%)
  starting transfers between devices  46.6 us (40%)
  waiting for transfers between devices  10.9 us (9%)
  local copies, waits for them, and re-layouts  7.15 us (6%)
    pallas_call x3, Pallas kernels, layer_of(): pl.pallas_call(layer_kernel, out_shape=jax.ShapeDtypeStruct((nodes, width...  21.5 us
    pallas_call x3, Pallas kernels, scorer_of(): pl.pallas_call(functools.partial(scorer_kernel, groups, final), out_shape...  16.8 us
    all_to_all x1, starting transfers between devices, shards(): mine = lax.all_to_all(conf_src, 'node', 0, 0, tiled=True)  11.2 us
    all_to_all x1, starting transfers between devices, shards(): lax.all_to_all(local_grad.reshape(node_count, per_peer, width), 'node', 0...  10.8 us
    all_to_all x1, starting transfers between devices, shards(): got = lax.all_to_all(sent.reshape(devices, 1, 128), both, 0, 0, tiled=True)  10 us
    ppermute x6, starting transfers between devices, shift(): lax.ppermute(value, 'cfg', [(i, i ^ 2 * by) for i in range(group_count)])  9.05 us
    ppermute x2, starting transfers between devices, trade(): return lax.ppermute(rows, both, pairs)  4.67 us
    unnamed x32, local copies, waits for them, and re-layouts  3.9 us
  transfers between devices with their start and end apart: 16, of which 7 were waited for; matrix products, arithmetic and copies ran while one was open for 1% of the time, Pallas kernels for 33%

profile of v6, /device:TPU:2, one launch (start us, length us, event | category | flops | bytes accessed | tf_op | source)
XLA Modules:
  0.0 116.8 jit_solution(9012083585491554480)
XLA Ops:
  0.6 1.1 constant_dynamic-slice_fusion
  1.7 2.4 %collective-permute-start = (bf16[512,256]{1,0:T(8,128)(2,1)S(1)}, bf16[512,256]{1,0:T(8,128)(2,1)S(1)}, u32[]{:S(2)}, u32[]{:S(2)}) collective-permute-start(bf16[512,256]{1,0:T(8,128)(2,1)S(1)} %get-tuple-element.74), channel_id=1, source_target_pairs={{0,1},{1,0},{2,3},{3,2},{4,5},{5,4},{6,7},{7,6},{8,9},{9,8},{10,11... | collective-permute-start | bytes 786440 | tf_op jit(solution)/shard_map/ppermute | solution.py:489
  4.1 2.3 %collective-permute-start.1 = (bf16[512,256]{1,0:T(8,128)(2,1)S(1)}, bf16[512,256]{1,0:T(8,128)(2,1)S(1)}, u32[]{:S(2)}, u32[]{:S(2)}) collective-permute-start(bf16[512,256]{1,0:T(8,128)(2,1)S(1)} %get-tuple-element.73), channel_id=1, source_target_pairs={{1,2},{2,1},{3,4},{4,3},{5,6},{6,5},{7,8},{8,7},{9,10},{10,9},{11,... | collective-permute-start | bytes 786440 | tf_op jit(solution)/shard_map/ppermute | solution.py:489
  6.4 0.9 broadcast_multiply_fusion
  7.2 0.0 copy-start
  7.3 1.6 %copy-done = bf16[4096,256]{1,0:T(8,128)(2,1)S(1)} copy-done((bf16[4096,256]{1,0:T(8,128)(2,1)S(1)}, bf16[4096,256]{1,0:T(8,128)(2,1)}, u32[]{:S(2)}) %copy-start) | copy-done | bytes 2097176
  8.8 0.9 copy-done.2
  9.8 0.7 copy-done.8
  10.4 0.7 copy-done.12
  11.1 3.8 %window_rows.1 = (f32[10240,128]{1,0:T(8,128)S(1)}, s32[512]{0:T(512)S(1)}, f32[128,256]{1,0:T(8,128)S(1)}) custom-call(s32[16384]{0:T(1024)S(1)} %bitcast.35, s32[128]{0:T(128)S(1)} %copy-done.12, bf16[4096,256]{1,0:T(8,128)(2,1)S(1)} %copy-done, bf16[256,256]{1,0:T(8,128)(2,1)S(1)} %copy-done.2, f32[1,256]{1,0:T(1,128)S(1)} %bitcast.40), custom_call_target="tpu_custom_call" | custom-call | flops 16777216 | bytes 6291456 | tf_op jit(solution)/shard_map/window_rows/pallas_call | solution.py:84
  15.0 0.0 copy-start.7
  15.0 0.0 copy-start.11
  15.0 0.0 copy-start.4
  15.0 2.5 %conf_rows.1 = (bf16[32,4,256]{2,1,0:T(4,128)(2,1)}, f32[10240,128]{1,0:T(8,128)S(1)}) custom-call(s32[1]{0:T(128)} %bitcast.flip, s32[512]{0:T(512)S(1)} %get-tuple-element.38.spots, bf16[512,256]{1,0:T(8,128)(2,1)S(1)} %collective-permute-done.1.outer, bf16[512,256]{1,0:T(8,128)(2,1)S(1)} %collective-permute-done.inner, ...), custom_call_target="tpu_custom_call", output_to_operand_aliasing={{1}: (6, {})} | custom-call | flops 33554432 | bytes 6291456 | tf_op jit(solution)/shard_map/conf_rows/pallas_call | solution.py:138
  17.5 11.2 %all-to-all-start = ((bf16[32,4,256]{2,1,0:T(4,128)(2,1)}), bf16[32,4,256]{2,1,0:T(4,128)(2,1)}, u32[]{:S(2)}, u32[]{:S(2)}) async-start(bf16[32,4,256]{2,1,0:T(4,128)(2,1)} %get-tuple-element.41), calls=%async_computation | async-start | bytes 131072 | tf_op jit(solution)/shard_map/all_to_all | solution.py:525
  28.7 0.1 prepare.1
  28.9 0.0 copy-start.6
  28.9 0.0 copy-start.15
  28.9 5.8 %graph_layer.3.refs_0_ = bf16[4096,256]{1,0:T(8,128)(2,1)} custom-call(s32[1]{0:T(128)} %bitcast.flip, s32[16384]{0:T(1024)S(1)} %bitcast.36, bf16[512,256]{1,0:T(8,128)(2,1)S(1)} %collective-permute-done.inner, bf16[512,256]{1,0:T(8,128)(2,1)S(1)} %collective-permute-done.1.outer, bf16[4096,256]{1,0:T(8,128)(2,1)S(1)} %copy-done.1, ...), custom_call_target="tpu_custom_call" | custom-call | flops 268435456 | bytes 16777216 | tf_op jit(solution)/shard_map/graph_layer/pallas_call | solution.py:197
  34.7 2.7 %all-to-all-done = bf16[32,4,256]{2,1,0:T(4,128)(2,1)} async-done(((bf16[32,4,256]{2,1,0:T(4,128)(2,1)}), bf16[32,4,256]{2,1,0:T(4,128)(2,1)}, u32[]{:S(2)}, u32[]{:S(2)}) %all-to-all-start) | async-done | bytes 65568 | tf_op jit(solution)/shard_map/all_to_all | solution.py:525
  37.4 0.9 reshape.76.refs_0_
  38.3 0.1 collective-permute-start.5
  38.4 1.7 %collective-permute-start.2 = (bf16[128,256]{1,0:T(8,128)(2,1)S(1)}, bf16[128,256]{1,0:T(8,128)(2,1)S(1)}, u32[]{:S(2)}, u32[]{:S(2)}) collective-permute-start(bf16[128,256]{1,0:T(8,128)(2,1)S(1)} %reshape.76.refs_0_), channel_id=1, source_target_pairs={{0,64},{32,96},{64,0},{96,32},{128,192},{160,224},{192,128},{224,1... | collective-permute-start | bytes 196616 | tf_op jit(solution)/shard_map/ppermute | solution.py:523
  40.1 3.2 %collective-permute-start.3 = (bf16[128,256]{1,0:T(8,128)(2,1)S(1)}, bf16[128,256]{1,0:T(8,128)(2,1)S(1)}, u32[]{:S(2)}, u32[]{:S(2)}) collective-permute-start(bf16[128,256]{1,0:T(8,128)(2,1)S(1)} %reshape.76.refs_0_), channel_id=1, source_target_pairs={{0,128},{32,160},{64,192},{96,224},{128,0},{160,32},{192,64},{224,... | collective-permute-start | bytes 196616 | tf_op jit(solution)/shard_map/ppermute | solution.py:523
  43.3 5.0 %scorer.3 = (bf16[2,16,128,256]{3,2,1,0:T(8,128)(2,1)}, f32[16,256]{1,0:T(8,128)S(1)}) custom-call(s32[1]{0:T(128)} %bitcast.6.where, bf16[128,256]{1,0:T(8,128)(2,1)S(1)} %reshape.76.refs_0_, bf16[128,256]{1,0:T(8,128)(2,1)} %collective-permute-done.5.refs_1_, s32[16,1024]{1,0:T(8,128)S(1)} %copy-done.13, bf16[256,256]{1,0:T(8,128)(2,1)S(1)} %copy-done.6, ...), custom_call_target="tpu_custom_call" | custom-call | flops 1610612736 | bytes 2097152 | tf_op jit(solution)/shard_map/scorer/pallas_call | solution.py:329
  48.4 0.4 collective-permute-done.4.refs_2_
  48.8 0.5 collective-permute-start.7
  49.3 5.6 %scorer.4 = (bf16[3,16,128,256]{3,2,1,0:T(8,128)(2,1)}, f32[16,256]{1,0:T(8,128)S(1)}) custom-call(s32[1]{0:T(128)} %bitcast.6.where, bf16[128,256]{1,0:T(8,128)(2,1)S(1)} %collective-permute-done.2.refs_0_, bf16[128,256]{1,0:T(8,128)(2,1)S(1)} %collective-permute-done.3.refs_1_, bf16[128,256]{1,0:T(8,128)(2,1)S(1)} %collective-permute-done.4.refs_2_, ...), custom_call_target="tpu_custom_call" | custom-call | flops 2415919104 | bytes 3145728 | tf_op jit(solution)/shard_map/scorer/pallas_call | solution.py:329
  54.9 6.3 %scorer.5 = (bf16[3,16,128,256]{3,2,1,0:T(8,128)(2,1)}, f32[256,128]{1,0:T(8,128)}) custom-call(s32[1]{0:T(128)} %bitcast.6.where, bf16[128,256]{1,0:T(8,128)(2,1)S(1)} %collective-permute-done.6.refs_0_, bf16[128,256]{1,0:T(8,128)(2,1)S(1)} %collective-permute-done.7.refs_1_, bf16[128,256]{1,0:T(8,128)(2,1)S(1)} %collective-permute-done.8.refs_2_, ...), custom_call_target="tpu_custom_call" | custom-call | flops 2415919104 | bytes 3145728 | tf_op jit(solution)/shard_map/scorer/pallas_call | solution.py:329
  61.1 10.0 %all-to-all-start.1 = ((f32[256,1,128]{2,1,0:T(1,128)}), f32[256,1,128]{2,1,0:T(1,128)S(1)}, u32[]{:S(2)}, u32[]{:S(2)}) async-start(f32[256,1,128]{2,1,0:T(1,128)} %bitcast.14), calls=%async_computation.1 | async-start | bytes 262144 | tf_op jit(solution)/shard_map/all_to_all | solution.py:558
  71.2 9.9 %graph_layer.4.refs_0_ = bf16[4096,256]{1,0:T(8,128)(2,1)} custom-call(s32[1]{0:T(128)} %bitcast.flip, s32[16384]{0:T(1024)S(1)} %bitcast.37, bf16[512,256]{1,0:T(8,128)(2,1)S(1)} %collective-permute-done.inner, bf16[512,256]{1,0:T(8,128)(2,1)S(1)} %collective-permute-done.1.outer, bf16[4096,256]{1,0:T(8,128)(2,1)S(1)} %copy-done.1, ...), custom_call_target="tpu_custom_call", output_to_operand_aliasing={{}: (9, {})} | custom-call | flops 536870912 | bytes 33554432 | tf_op jit(solution)/shard_map/graph_layer/pallas_call | solution.py:197
  81.1 1.5 %all-to-all-done.1 = f32[256,1,128]{2,1,0:T(1,128)S(1)} async-done(((f32[256,1,128]{2,1,0:T(1,128)}), f32[256,1,128]{2,1,0:T(1,128)S(1)}, u32[]{:S(2)}, u32[]{:S(2)}) %all-to-all-start.1) | async-done | bytes 131104 | tf_op jit(solution)/shard_map/all_to_all | solution.py:558
  82.6 2.7 %ranking.1 = (f32[1,1]{1,0:T(1,128)}, f32[16,256]{1,0:T(8,128)S(1)}, bf16[4,128,256]{2,1,0:T(8,128)(2,1)S(1)}) custom-call(s32[1]{0:T(128)} %bitcast.6.where, f32[256,128]{1,0:T(8,128)S(1)} %bitcast.39, s32[2,512]{1,0:T(2,128)S(1)} %bitcast.44, bf16[2,16,128,256]{3,2,1,0:T(8,128)(2,1)} %get-tuple-element.64.pair, ...), custom_call_target="tpu_custom_call" | custom-call | flops 16777216 | bytes 6291456 | tf_op jit(solution)/shard_map/ranking/pallas_call | solution.py:409
  85.3 0.3 collective-permute-start.9
  85.6 2.4 %rest.1 = bf16[4,128,256]{2,1,0:T(8,128)(2,1)S(1)} custom-call(f32[16,256]{1,0:T(8,128)S(1)} %get-tuple-element.66.coef, bf16[2,16,128,256]{3,2,1,0:T(8,128)(2,1)} %get-tuple-element.64.pair, bf16[3,16,128,256]{3,2,1,0:T(8,128)(2,1)} %get-tuple-element.67.later), custom_call_target="tpu_custom_call" | custom-call | flops 16777216 | bytes 6291456 | tf_op jit(solution)/shard_map/rest/pallas_call | solution.py:441
  88.1 0.1 fusion.3
  88.1 1.3 %collective-permute-start.12 = (bf16[128,256]{1,0:T(8,128)(2,1)S(1)}, bf16[128,256]{1,0:T(8,128)(2,1)S(1)}, u32[]{:S(2)}, u32[]{:S(2)}) collective-permute-start(bf16[128,256]{1,0:T(8,128)(2,1)S(1)} %get-tuple-element.76), channel_id=1, source_target_pairs={{0,192},{32,224},{64,128},{96,160},{128,64},{160,96},{192,0},{224,... | collective-permute-start | bytes 196616 | tf_op jit(solution)/shard_map/ppermute | solution.py:523
  89.4 1.5 %collective-permute-start.11 = (bf16[128,256]{1,0:T(8,128)(2,1)S(1)}, bf16[128,256]{1,0:T(8,128)(2,1)S(1)}, u32[]{:S(2)}, u32[]{:S(2)}) collective-permute-start(bf16[128,256]{1,0:T(8,128)(2,1)S(1)} %get-tuple-element.77), channel_id=1, source_target_pairs={{0,128},{32,160},{64,192},{96,224},{128,0},{160,32},{192,64},{224,... | collective-permute-start | bytes 196616 | tf_op jit(solution)/shard_map/ppermute | solution.py:523
  90.9 1.4 %collective-permute-start.10 = (bf16[128,256]{1,0:T(8,128)(2,1)S(1)}, bf16[128,256]{1,0:T(8,128)(2,1)S(1)}, u32[]{:S(2)}, u32[]{:S(2)}) collective-permute-start(bf16[128,256]{1,0:T(8,128)(2,1)S(1)} %get-tuple-element.75), channel_id=1, source_target_pairs={{0,64},{32,96},{64,0},{96,32},{128,192},{160,224},{192,128},{224,1... | collective-permute-start | bytes 196616 | tf_op jit(solution)/shard_map/ppermute | solution.py:523
  92.3 2.1 %collective-permute-done.12 = bf16[128,256]{1,0:T(8,128)(2,1)S(1)} collective-permute-done((bf16[128,256]{1,0:T(8,128)(2,1)S(1)}, bf16[128,256]{1,0:T(8,128)(2,1)S(1)}, u32[]{:S(2)}, u32[]{:S(2)}) %collective-permute-start.12) | collective-permute-done | bytes 65568 | tf_op jit(solution)/shard_map/ppermute | solution.py:523
  94.4 1.2 %collective-permute-done.11 = bf16[128,256]{1,0:T(8,128)(2,1)S(1)} collective-permute-done((bf16[128,256]{1,0:T(8,128)(2,1)S(1)}, bf16[128,256]{1,0:T(8,128)(2,1)S(1)}, u32[]{:S(2)}, u32[]{:S(2)}) %collective-permute-start.11) | collective-permute-done | bytes 65568 | tf_op jit(solution)/shard_map/ppermute | solution.py:523
  95.6 0.1 collective-permute-done.10
  95.7 0.2 convolution_convert_fusion
  95.9 0.7 reshape.82
  96.6 10.8 %all-to-all-start.2 = ((bf16[32,4,256]{2,1,0:T(4,128)(2,1)}), bf16[32,4,256]{2,1,0:T(4,128)(2,1)S(1)}, u32[]{:S(2)}, u32[]{:S(2)}) async-start(bf16[32,4,256]{2,1,0:T(4,128)(2,1)} %reshape.82), calls=%async_computation.2 | async-start | bytes 131072 | tf_op jit(solution)/shard_map/all_to_all | solution.py:578
  107.4 5.8 %graph_layer.5 = bf16[4096,256]{1,0:T(8,128)(2,1)} custom-call(s32[1]{0:T(128)} %bitcast.flip, s32[16384]{0:T(1024)S(1)} %bitcast.38, bf16[512,256]{1,0:T(8,128)(2,1)S(1)} %collective-permute-done.inner, bf16[512,256]{1,0:T(8,128)(2,1)S(1)} %collective-permute-done.1.outer, bf16[4096,256]{1,0:T(8,128)(2,1)S(1)} %copy-done.1, ...), custom_call_target="tpu_custom_call", output_to_operand_aliasing={{}: (9, {})} | custom-call | flops 268435456 | bytes 16777216 | tf_op jit(solution)/shard_map/graph_layer/pallas_call | solution.py:197
  113.2 2.9 %all-to-all-done.2 = bf16[32,4,256]{2,1,0:T(4,128)(2,1)S(1)} async-done(((bf16[32,4,256]{2,1,0:T(4,128)(2,1)}), bf16[32,4,256]{2,1,0:T(4,128)(2,1)S(1)}, u32[]{:S(2)}, u32[]{:S(2)}) %all-to-all-start.2) | async-done | bytes 65568 | tf_op jit(solution)/shard_map/all_to_all | solution.py:578
  116.1 0.7 reshape.86
  (34 shorter events, 0.1 us)
Async XLA Ops:
  1.7 13.2 %collective-permute-start = (bf16[512,256]{1,0:T(8,128)(2,1)S(1)}, bf16[512,256]{1,0:T(8,128)(2,1)S(1)}, u32[]{:S(2)}, u32[]{:S(2)}) collective-permute-start(bf16[512,256]{1,0:T(8,128)(2,1)S(1)} %get-tuple-element.74), channel_id=1, source_target_pairs={{0,1},{1,0},{2,3},{3,2},{4,5},{5,4},{6,7},{7,6},{8,9},{9,8},{10,11... | collective-permute-start | bytes 786440 | tf_op jit(solution)/shard_map/ppermute | solution.py:489
  4.1 10.9 %collective-permute-start.1 = (bf16[512,256]{1,0:T(8,128)(2,1)S(1)}, bf16[512,256]{1,0:T(8,128)(2,1)S(1)}, u32[]{:S(2)}, u32[]{:S(2)}) collective-permute-start(bf16[512,256]{1,0:T(8,128)(2,1)S(1)} %get-tuple-element.73), channel_id=1, source_target_pairs={{1,2},{2,1},{3,4},{4,3},{5,6},{6,5},{7,8},{8,7},{9,10},{10,9},{11,... | collective-permute-start | bytes 786440 | tf_op jit(solution)/shard_map/ppermute | solution.py:489
  7.2 1.6 %copy-start = (bf16[4096,256]{1,0:T(8,128)(2,1)S(1)}, bf16[4096,256]{1,0:T(8,128)(2,1)}, u32[]{:S(2)}) copy-start(bf16[4096,256]{1,0:T(8,128)(2,1)} %own.5) | copy-start | bytes 6291460
  8.8 0.9 copy-start.2
  9.7 0.7 copy-start.8
  10.4 0.7 copy-start.12
  15.0 13.7 %copy-start.5 = (bf16[256,256]{1,0:T(8,128)(2,1)S(1)}, bf16[256,256]{1,0:T(8,128)(2,1)}, u32[]{:S(2)}) copy-start(bf16[256,256]{1,0:T(8,128)(2,1)} %mid.1) | copy-start | bytes 393220
  15.0 13.7 %copy-start.7 = (bf16[128,256]{1,0:T(8,128)(2,1)S(1)}, bf16[128,256]{1,0:T(8,128)(2,1)}, u32[]{:S(2)}) copy-start(bf16[128,256]{1,0:T(8,128)(2,1)} %table.1) | copy-start | bytes 196612
  15.0 13.7 %copy-start.11 = (f32[256]{0:T(256)S(1)}, f32[256]{0:T(256)}, u32[]{:S(2)}) copy-start(f32[256]{0:T(256)} %param.26) | copy-start | bytes 3076
  15.0 13.8 %copy-start.1 = (bf16[4096,256]{1,0:T(8,128)(2,1)S(1)}, bf16[4096,256]{1,0:T(8,128)(2,1)}, u32[]{:S(2)}) copy-start(bf16[4096,256]{1,0:T(8,128)(2,1)} %own.5) | copy-start | bytes 6291460
  15.0 13.8 %copy-start.3 = (bf16[256,256]{1,0:T(8,128)(2,1)S(1)}, bf16[256,256]{1,0:T(8,128)(2,1)}, u32[]{:S(2)}) copy-start(bf16[256,256]{1,0:T(8,128)(2,1)} %sw.7) | copy-start | bytes 393220
  15.0 13.8 %copy-start.4 = (bf16[256,256]{1,0:T(8,128)(2,1)S(1)}, bf16[256,256]{1,0:T(8,128)(2,1)}, u32[]{:S(2)}) copy-start(bf16[256,256]{1,0:T(8,128)(2,1)} %nw.5) | copy-start | bytes 393220
  15.0 13.8 %copy-start.9 = (f32[256]{0:T(256)S(1)}, f32[256]{0:T(256)}, u32[]{:S(2)}) copy-start(f32[256]{0:T(256)} %param.18) | copy-start | bytes 3076
  17.5 19.9 %all-to-all-start = ((bf16[32,4,256]{2,1,0:T(4,128)(2,1)}), bf16[32,4,256]{2,1,0:T(4,128)(2,1)}, u32[]{:S(2)}, u32[]{:S(2)}) async-start(bf16[32,4,256]{2,1,0:T(4,128)(2,1)} %get-tuple-element.41), calls=%async_computation | async-start | bytes 131072 | tf_op jit(solution)/shard_map/all_to_all | solution.py:525
  28.9 14.4 %copy-start.6 = (bf16[256,256]{1,0:T(8,128)(2,1)S(1)}, bf16[256,256]{1,0:T(8,128)(2,1)}, u32[]{:S(2)}) copy-start(bf16[256,256]{1,0:T(8,128)(2,1)} %refs_4_.3) | copy-start | bytes 393220
  28.9 14.4 %copy-start.13 = (s32[16,1024]{1,0:T(8,128)S(1)}, s32[16,1024]{1,0:T(8,128)}, u32[]{:S(2)}) copy-start(s32[16,1024]{1,0:T(8,128)} %refs_3_.5) | copy-start | bytes 196612
  28.9 14.4 %copy-start.14 = (f32[256]{0:T(256)S(1)}, f32[256]{0:T(256)}, u32[]{:S(2)}) copy-start(f32[256]{0:T(256)} %param.23) | copy-start | bytes 3076
  28.9 14.4 %copy-start.15 = (f32[256]{0:T(256)S(1)}, f32[256]{0:T(256)}, u32[]{:S(2)}) copy-start(f32[256]{0:T(256)} %param.25) | copy-start | bytes 3076
  38.3 5.0 %collective-permute-start.5 = (bf16[128,256]{1,0:T(8,128)(2,1)S(1)}, bf16[128,256]{1,0:T(8,128)(2,1)}, u32[]{:S(2)}, u32[]{:S(2)}) collective-permute-start(bf16[128,256]{1,0:T(8,128)(2,1)S(1)} %reshape.76.refs_0_), channel_id=1, source_target_pairs={{0,32},{32,0},{64,96},{96,64},{128,160},{160,128},{192,224},{224,1... | collective-permute-start | bytes 196616 | tf_op jit(solution)/shard_map/ppermute | solution.py:549
  38.4 9.9 %collective-permute-start.2 = (bf16[128,256]{1,0:T(8,128)(2,1)S(1)}, bf16[128,256]{1,0:T(8,128)(2,1)S(1)}, u32[]{:S(2)}, u32[]{:S(2)}) collective-permute-start(bf16[128,256]{1,0:T(8,128)(2,1)S(1)} %reshape.76.refs_0_), channel_id=1, source_target_pairs={{0,64},{32,96},{64,0},{96,32},{128,192},{160,224},{192,128},{224,1... | collective-permute-start | bytes 196616 | tf_op jit(solution)/shard_map/ppermute | solution.py:523
  40.1 8.3 %collective-permute-start.3 = (bf16[128,256]{1,0:T(8,128)(2,1)S(1)}, bf16[128,256]{1,0:T(8,128)(2,1)S(1)}, u32[]{:S(2)}, u32[]{:S(2)}) collective-permute-start(bf16[128,256]{1,0:T(8,128)(2,1)S(1)} %reshape.76.refs_0_), channel_id=1, source_target_pairs={{0,128},{32,160},{64,192},{96,224},{128,0},{160,32},{192,64},{224,... | collective-permute-start | bytes 196616 | tf_op jit(solution)/shard_map/ppermute | solution.py:523
  43.3 5.5 %collective-permute-start.4 = (bf16[128,256]{1,0:T(8,128)(2,1)S(1)}, bf16[128,256]{1,0:T(8,128)(2,1)S(1)}, u32[]{:S(2)}, u32[]{:S(2)}) collective-permute-start(bf16[128,256]{1,0:T(8,128)(2,1)S(1)} %reshape.76.refs_0_), channel_id=1, source_target_pairs={{0,192},{32,224},{64,128},{96,160},{128,64},{160,96},{192,0},{224,... | collective-permute-start | bytes 196616 | tf_op jit(solution)/shard_map/ppermute | solution.py:523
  48.7 6.1 %collective-permute-start.6 = (bf16[128,256]{1,0:T(8,128)(2,1)S(1)}, bf16[128,256]{1,0:T(8,128)(2,1)S(1)}, u32[]{:S(2)}, u32[]{:S(2)}) collective-permute-start(bf16[128,256]{1,0:T(8,128)(2,1)S(1)} %collective-permute-done.2.refs_0_), channel_id=1, source_target_pairs={{0,32},{32,0},{64,96},{96,64},{128,160},{160,128},{192,224},{224,1... | collective-permute-start | bytes 196616 | tf_op jit(solution)/shard_map/ppermute | solution.py:552
  48.8 6.1 %collective-permute-start.7 = (bf16[128,256]{1,0:T(8,128)(2,1)S(1)}, bf16[128,256]{1,0:T(8,128)(2,1)S(1)}, u32[]{:S(2)}, u32[]{:S(2)}) collective-permute-start(bf16[128,256]{1,0:T(8,128)(2,1)S(1)} %collective-permute-done.3.refs_1_), channel_id=1, source_target_pairs={{0,32},{32,0},{64,96},{96,64},{128,160},{160,128},{192,224},{224,1... | collective-permute-start | bytes 196616 | tf_op jit(solution)/shard_map/ppermute | solution.py:552
  49.3 5.6 %collective-permute-start.8 = (bf16[128,256]{1,0:T(8,128)(2,1)S(1)}, bf16[128,256]{1,0:T(8,128)(2,1)S(1)}, u32[]{:S(2)}, u32[]{:S(2)}) collective-permute-start(bf16[128,256]{1,0:T(8,128)(2,1)S(1)} %collective-permute-done.4.refs_2_), channel_id=1, source_target_pairs={{0,32},{32,0},{64,96},{96,64},{128,160},{160,128},{192,224},{224,1... | collective-permute-start | bytes 196616 | tf_op jit(solution)/shard_map/ppermute | solution.py:552
  61.1 21.5 %all-to-all-start.1 = ((f32[256,1,128]{2,1,0:T(1,128)}), f32[256,1,128]{2,1,0:T(1,128)S(1)}, u32[]{:S(2)}, u32[]{:S(2)}) async-start(f32[256,1,128]{2,1,0:T(1,128)} %bitcast.14), calls=%async_computation.1 | async-start | bytes 262144 | tf_op jit(solution)/shard_map/all_to_all | solution.py:558
  71.2 11.4 %copy-start.10 = (s32[512,2]{0,1:T(2,128)S(1)}, s32[512,2]{0,1:T(2,128)}, u32[]{:S(2)}) copy-start(s32[512,2]{0,1:T(2,128)} %param.27) | copy-start | bytes 12292
  85.3 2.7 %collective-permute-start.9 = (bf16[4,128,256]{2,1,0:T(8,128)(2,1)S(1)}, bf16[4,128,256]{2,1,0:T(8,128)(2,1)S(1)}, u32[]{:S(2)}, u32[]{:S(2)}) collective-permute-start(bf16[4,128,256]{2,1,0:T(8,128)(2,1)S(1)} %get-tuple-element.68), channel_id=1, source_target_pairs={{0,32},{32,0},{64,96},{96,64},{128,160},{160,128},{192,224},{224,1... | collective-permute-start | bytes 786440 | tf_op jit(solution)/shard_map/ppermute | solution.py:564
  88.1 6.3 %collective-permute-start.12 = (bf16[128,256]{1,0:T(8,128)(2,1)S(1)}, bf16[128,256]{1,0:T(8,128)(2,1)S(1)}, u32[]{:S(2)}, u32[]{:S(2)}) collective-permute-start(bf16[128,256]{1,0:T(8,128)(2,1)S(1)} %get-tuple-element.76), channel_id=1, source_target_pairs={{0,192},{32,224},{64,128},{96,160},{128,64},{160,96},{192,0},{224,... | collective-permute-start | bytes 196616 | tf_op jit(solution)/shard_map/ppermute | solution.py:523
  89.4 6.2 %collective-permute-start.11 = (bf16[128,256]{1,0:T(8,128)(2,1)S(1)}, bf16[128,256]{1,0:T(8,128)(2,1)S(1)}, u32[]{:S(2)}, u32[]{:S(2)}) collective-permute-start(bf16[128,256]{1,0:T(8,128)(2,1)S(1)} %get-tuple-element.77), channel_id=1, source_target_pairs={{0,128},{32,160},{64,192},{96,224},{128,0},{160,32},{192,64},{224,... | collective-permute-start | bytes 196616 | tf_op jit(solution)/shard_map/ppermute | solution.py:523
  90.9 4.8 %collective-permute-start.10 = (bf16[128,256]{1,0:T(8,128)(2,1)S(1)}, bf16[128,256]{1,0:T(8,128)(2,1)S(1)}, u32[]{:S(2)}, u32[]{:S(2)}) collective-permute-start(bf16[128,256]{1,0:T(8,128)(2,1)S(1)} %get-tuple-element.75), channel_id=1, source_target_pairs={{0,64},{32,96},{64,0},{96,32},{128,192},{160,224},{192,128},{224,1... | collective-permute-start | bytes 196616 | tf_op jit(solution)/shard_map/ppermute | solution.py:523
  96.6 19.5 %all-to-all-start.2 = ((bf16[32,4,256]{2,1,0:T(4,128)(2,1)}), bf16[32,4,256]{2,1,0:T(4,128)(2,1)S(1)}, u32[]{:S(2)}, u32[]{:S(2)}) async-start(bf16[32,4,256]{2,1,0:T(4,128)(2,1)} %reshape.82), calls=%async_computation.2 | async-start | bytes 131072 | tf_op jit(solution)/shard_map/all_to_all | solution.py:578

commit v7 on v5

--- a/solution.py
+++ b/solution.py
@@ -29,6 +29,27 @@
 def twice_slope(half, tanh, scaled):
     inner = 1.0 + half - scaled
     return inner + tanh * inner
+
+
+def halves_swapped(first, second):
+    low = lax.broadcasted_iota(jnp.int32, first.shape, 1) < 4
+    upper = jnp.where(low, first, pltpu.roll(second, 4, 1))
+    lower = jnp.where(low, pltpu.roll(first, 4, 1), second)
+    return upper, lower
+
+
+def pack(value):
+    rows = value.shape[0]
+    sides = [value[:, at : at + 128].reshape(rows // 8, 8, 128) for at in (0, 128)]
+    even, odd = halves_swapped(*sides)
+    return jnp.stack([even, odd], axis=1).reshape(rows // 4, 8, 128)
+
+
+def unpack(value):
+    groups = value.shape[0]
+    pairs = value.reshape(groups // 2, 2, 8, 128)
+    left, right = halves_swapped(pairs[:, 0], pairs[:, 1])
+    return jnp.concatenate([x.reshape(groups * 4, 128) for x in (left, right)], axis=1)
 
 
 def put_rows(table, first, source):
@@ -114,18 +135,16 @@
         bias,
         f32,
     )
-    share = out.shape[1]
-    for peer in range(out.shape[0]):
-        out[peer] = value[peer * share : (peer + 1) * share, :].astype(bf16)
-
-
-def conf_rows_of(peers, flip, nbrs, picks, inner, outer, sw, nw, bias, table):
+    out[...] = pack(value).astype(bf16)
+
+
+def conf_rows_of(flip, nbrs, picks, inner, outer, sw, nw, bias, table):
     count = picks.shape[0]
     width = sw.shape[0]
     return pl.pallas_call(
         conf_kernel,
         out_shape=(
-            jax.ShapeDtypeStruct((peers, count // peers, width), bf16),
+            jax.ShapeDtypeStruct((count // 4, 8, width // 2), bf16),
             jax.ShapeDtypeStruct(table.shape, f32),
         ),
         in_specs=[SMEM] * 3 + [VMEM] * 2 + [HBM] * 3 + [VMEM],
@@ -147,7 +166,7 @@
     )(flip, nbrs, picks, outer, inner, in_hbm(sw), in_hbm(nw), in_hbm(bias), table)
 
 
-def layer_kernel(flip, nbrs, outer, inner, feats, own, sw, nw, bias, *refs):
+def layer_kernel(flip, nbrs, inner, outer, feats, own, sw, nw, bias, *refs):
     out, table, acc = refs[-3:]
     tile = own.shape[0]
     nodes = feats.shape[0]
@@ -213,7 +232,7 @@
         ),
         compiler_params=pltpu.CompilerParams(vmem_limit_bytes=24 << 20),
         name="graph_layer",
-    )(flip, nbrs, outer, inner, feats, feats, sw, nw, bias, *ahead)
+    )(flip, nbrs, inner, outer, feats, feats, sw, nw, bias, *ahead)
 
 
 def place_of(group, turn):
@@ -245,7 +264,7 @@
     given, (grads_hbm, sent, base, total, grads, sems) = refs[8:-6], refs[-6:]
     step = pl.program_id(0)
     slot = step & 1
-    chunk = xs[0].shape[0]
+    chunk = base.shape[1]
     configs = ids.shape[0]
     layouts = tabh.shape[0]
     one = jnp.asarray(1.0, bf16)
@@ -254,7 +273,12 @@
     def _():
         for i in range(groups):
             base[i] = 0.5 * (
-                jnp.dot(xs[i][...], join[...], preferred_element_type=f32) + jbias[...]
+                jnp.dot(
+                    unpack(xs[i][...].astype(f32)).astype(bf16),
+                    join[...],
+                    preferred_element_type=f32,
+                )
+                + jbias[...]
             )
         total[...] = given[0][...] if given else jnp.zeros_like(total)
 
@@ -314,8 +338,8 @@
 def scorer_of(final, turns, where, xs, ids, join, jbias, weights, mbias, weight, given):
     groups = len(xs)
     configs = ids.shape[0]
-    chunk, width = xs[0].shape
-    hidden = join.shape[1]
+    chunk = xs[0].shape[0] * 4
+    width, hidden = join.shape
     start, stride = turns
     summed = final if final else (configs, hidden)
     return pl.pallas_call(
@@ -445,6 +469,47 @@
     )(coef, in_hbm(pair), in_hbm(later))
 
 
+def finish_kernel(kept, came, *refs):
+    arrived, (join, out) = refs[:-2], refs[-2:]
+    rows = kept[0].astype(f32) + came[0].astype(f32)
+    for part in arrived:
+        rows = rows + part[...].astype(f32)
+    value = lax.dot_general(
+        rows.astype(bf16), join[...], (((1,), (1,)), ((), ())), preferred_element_type=f32
+    )
+    out[...] = pack(value).astype(bf16)
+
+
+def finish_of(kept, came, arrived, join):
+    rows, width = kept.shape[1], join.shape[0]
+    return pl.pallas_call(
+        finish_kernel,
+        out_shape=jax.ShapeDtypeStruct((rows // 4, 8, width // 2), bf16),
+        in_specs=[VMEM] * (3 + len(arrived)),
+        out_specs=VMEM,
+        cost_estimate=pl.CostEstimate(flops=1 << 24, transcendentals=0, bytes_accessed=1 << 19),
+        compiler_params=pltpu.CompilerParams(vmem_limit_bytes=8 << 20),
+        name="finish",
+    )(kept, came, *arrived, join)
+
+
+def returned_kernel(value, out):
+    out[...] = unpack(value[...].astype(f32))
+
+
+def returned_of(value):
+    groups = value.shape[0]
+    return pl.pallas_call(
+        returned_kernel,
+        out_shape=jax.ShapeDtypeStruct((groups * 4, 256), f32),
+        in_specs=[VMEM],
+        out_specs=VMEM,
+        cost_estimate=pl.CostEstimate(flops=1 << 16, transcendentals=0, bytes_accessed=1 << 18),
+        compiler_params=pltpu.CompilerParams(vmem_limit_bytes=8 << 20),
+        name="returned",
+    )(value)
+
+
 def shards(
     node_feats,
     neighbors,
@@ -466,9 +531,6 @@
     node_count = lax.axis_size("node")
     group_count = lax.axis_size("cfg")
     rings = group_count // 2
-    local_conf = conf_index.shape[0]
-    width = node_feats.shape[1]
-    per_peer = local_conf // node_count
     scale = 1.0 / math.sqrt(layout_ids.shape[1] * node_count)
     group = lax.axis_index("cfg")
 
@@ -491,7 +553,6 @@
 
     table = table_of(node_feats)
     conf_src, _ = conf_rows_of(
-        node_count,
         flip,
         nbrs,
         conf_index,
@@ -528,7 +589,6 @@
     weight = score_weight.reshape(1, -1)
     weights = prepared(layout_table, mid_weight, weight)
     mine, embed, *weights = hold((mine, embed, *weights))
-    mine = mine.reshape(local_conf, width)
     others = [shift(mine, by) for by in range(1, rings)]
     where = group.reshape(1)
 
@@ -557,30 +617,19 @@
     other, sent = scorer((devices, 128), (rings + 1, 1), swapped, [total])
     sent, embed = hold((sent, embed))
     got = lax.all_to_all(sent.reshape(devices, 1, 128), both, 0, 0, tiled=True)
-    embed = layer(2, 3, embed)
+    embed = layer(2, 4, embed)
     got, embed = hold((got, embed))
     loss, coef, away = ranking_of(
         scale, where, got.reshape(devices, 128), config_pairs.T, pair, other
     )
     came = lax.ppermute(away, "cfg", swap)
     kept = rest_of(coef, pair, own)
-    sums = [kept[d].astype(f32) + came[d].astype(f32) for d in range(rings)]
-    arrived = [shift(sums[d].astype(bf16), d) for d in range(1, rings)]
-    row_grad = sums[0]
-    for part in arrived:
-        row_grad = row_grad + part.astype(f32)
-    local_grad = lax.dot_general(
-        row_grad.astype(bf16),
-        join_weight,
-        (((1,), (1,)), ((), ())),
-        preferred_element_type=f32,
-    )
-    local_grad, embed = hold((local_grad.astype(bf16), embed))
-    conf_grad = lax.all_to_all(
-        local_grad.reshape(node_count, per_peer, width), "node", 0, 0, tiled=True
-    )
-    embed = layer(5, 3, embed)
-    conf_grad = conf_grad.astype(f32).reshape(local_conf, width)
+    sums = [(kept[d].astype(f32) + came[d].astype(f32)).astype(bf16) for d in range(1, rings)]
+    arrived = [shift(part, by) for by, part in enumerate(sums, 1)]
+    local_grad, embed = hold((finish_of(kept, came, arrived, join_weight), embed))
+    conf_grad = lax.all_to_all(local_grad, "node", 0, 0, tiled=True)
+    embed = layer(6, 2, embed)
+    conf_grad = returned_of(conf_grad)
     return (embed, loss.reshape(()), conf_grad)
 
 

time: 116 us -> 120 us (1.034)
  starting transfers between devices: 46.1 us -> 50.7 us
  Pallas kernels: 48 us -> 49.5 us
    reshape x3 -> x0, local copies, waits for them, and re-layouts: 2.18 us -> none  [the longest x1 0.86 us: shards(): mine = mine.reshape(local_conf, width)]
    all_to_all x1, waiting for transfers between devices: 3.35 us -> 1.25 us  [shards(): got = lax.all_to_all(sent.reshape(devices, 1, 128), both, 0, 0, tiled=True)]
    all_to_all x1, waiting for transfers between devices: 0.63 us -> 2.73 us  [shards(): conf_grad = lax.all_to_all(local_grad, 'node', 0, 0, tiled=True)]
    all_to_all x1, starting transfers between devices: 9 us -> 10.9 us  [shards(): conf_grad = lax.all_to_all(local_grad, 'node', 0, 0, tiled=True)]
    pallas_call x1 -> x3, Pallas kernels: 3.46 us -> 4.97 us  [the longest x1 3.47 us: conf_rows_of(): pl.pallas_call(conf_kernel, out_shape=(jax.ShapeDtypeStruct((count // 4,...]
    unnamed x28 -> x32, local copies, waits for them, and re-layouts: 1.66 us -> 3.1 us
  transfers between devices with their start and end apart: 16 -> 16, of which waited for: 8 -> 7; matrix products, arithmetic and copies ran while one was open for 1% -> 1% of each run, Pallas kernels for 31% -> 30%
where the time goes in v7:
time: 120 us; the launch traced here: 119 us
  starting transfers between devices  50.7 us (42%)
  Pallas kernels  49.5 us (41%)
  waiting for transfers between devices  12.9 us (11%)
  local copies, waits for them, and re-layouts  4.17 us (3%)
    pallas_call x3, Pallas kernels, layer_of(): pl.pallas_call(layer_kernel, out_shape=jax.ShapeDtypeStruct((nodes, width...  22.1 us
    pallas_call x3, Pallas kernels, scorer_of(): pl.pallas_call(functools.partial(scorer_kernel, groups, final), out_shape...  16.8 us
    all_to_all x1, starting transfers between devices, shards(): mine = lax.all_to_all(conf_src, 'node', 0, 0, tiled=True)  13.3 us
    all_to_all x1, starting transfers between devices, shards(): got = lax.all_to_all(sent.reshape(devices, 1, 128), both, 0, 0, tiled=True)  11.1 us
    all_to_all x1, starting transfers between devices, shards(): conf_grad = lax.all_to_all(local_grad, 'node', 0, 0, tiled=True)  10.9 us
    ppermute x6, starting transfers between devices, shift(): lax.ppermute(value, 'cfg', [(i, i ^ 2 * by) for i in range(group_count)])  9.79 us
    ppermute x2, starting transfers between devices, trade(): return lax.ppermute(rows, both, pairs)  4.67 us
    ppermute x6, waiting for transfers between devices, shift(): lax.ppermute(value, 'cfg', [(i, i ^ 2 * by) for i in range(group_count)])  3.7 us
  transfers between devices with their start and end apart: 16, of which 7 were waited for; matrix products, arithmetic and copies ran while one was open for 1% of the time, Pallas kernels for 30%

profile of v7, /device:TPU:2, one launch (start us, length us, event | category | flops | bytes accessed | tf_op | source)
XLA Modules:
  0.0 119.2 jit_solution(1118887767719879925)
XLA Ops:
  0.6 1.1 constant_dynamic-slice_fusion
  1.7 2.4 %collective-permute-start = (bf16[512,256]{1,0:T(8,128)(2,1)S(1)}, bf16[512,256]{1,0:T(8,128)(2,1)S(1)}, u32[]{:S(2)}, u32[]{:S(2)}) collective-permute-start(bf16[512,256]{1,0:T(8,128)(2,1)S(1)} %get-tuple-element.68), channel_id=1, source_target_pairs={{0,1},{1,0},{2,3},{3,2},{4,5},{5,4},{6,7},{7,6},{8,9},{9,8},{10,11... | collective-permute-start | bytes 786440 | tf_op jit(solution)/shard_map/ppermute | solution.py:543
  4.1 2.3 %collective-permute-start.1 = (bf16[512,256]{1,0:T(8,128)(2,1)S(1)}, bf16[512,256]{1,0:T(8,128)(2,1)S(1)}, u32[]{:S(2)}, u32[]{:S(2)}) collective-permute-start(bf16[512,256]{1,0:T(8,128)(2,1)S(1)} %get-tuple-element.67), channel_id=1, source_target_pairs={{1,2},{2,1},{3,4},{4,3},{5,6},{6,5},{7,8},{8,7},{9,10},{10,9},{11,... | collective-permute-start | bytes 786440 | tf_op jit(solution)/shard_map/ppermute | solution.py:543
  6.4 0.9 broadcast_multiply_fusion
  7.2 0.0 copy-start
  7.3 1.6 %copy-done = bf16[4096,256]{1,0:T(8,128)(2,1)S(1)} copy-done((bf16[4096,256]{1,0:T(8,128)(2,1)S(1)}, bf16[4096,256]{1,0:T(8,128)(2,1)}, u32[]{:S(2)}) %copy-start) | copy-done | bytes 2097176
  8.8 0.4 window_rows.1.refs_3_
  9.2 0.6 collective-permute-done.inner
  9.8 2.6 %collective-permute-done.1.outer = bf16[512,256]{1,0:T(8,128)(2,1)S(1)} collective-permute-done((bf16[512,256]{1,0:T(8,128)(2,1)S(1)}, bf16[512,256]{1,0:T(8,128)(2,1)S(1)}, u32[]{:S(2)}, u32[]{:S(2)}) %collective-permute-start.1) | collective-permute-done | bytes 262176 | tf_op jit(solution)/shard_map/ppermute | solution.py:543
  12.4 0.0 copy-start.1
  12.4 0.0 copy-start.2
  12.4 0.0 copy-start.3
  12.4 0.0 copy-start.7
  12.5 3.5 %conf_rows.1 = (bf16[32,8,128]{2,1,0:T(8,128)(2,1)}, f32[10240,128]{1,0:T(8,128)S(1)}) custom-call(s32[1]{0:T(128)} %bitcast.flip, s32[16384]{0:T(1024)S(1)} %bitcast.25, s32[128]{0:T(128)S(1)} %copy-done.10, bf16[512,256]{1,0:T(8,128)(2,1)S(1)} %collective-permute-done.1.outer, ...), custom_call_target="tpu_custom_call", output_to_operand_aliasing={{1}: (8, {})} | custom-call | flops 33554432 | bytes 6291456 | tf_op jit(solution)/shard_map/conf_rows/pallas_call | solution.py:144
  15.9 13.3 %all-to-all-start = ((bf16[32,8,128]{2,1,0:T(8,128)(2,1)}), bf16[32,8,128]{2,1,0:T(8,128)(2,1)S(1)}, u32[]{:S(2)}, u32[]{:S(2)}) async-start(bf16[32,8,128]{2,1,0:T(8,128)(2,1)} %get-tuple-element.35), calls=%async_computation | async-start | bytes 131072 | tf_op jit(solution)/shard_map/all_to_all | solution.py:587
  29.3 0.1 prepare.1
  29.4 0.6 copy-done.12
  30.1 0.0 copy-start.4
  30.1 0.0 copy-start.14
  30.1 0.0 copy-start.15
  30.1 5.9 %graph_layer.3.refs_0_ = bf16[4096,256]{1,0:T(8,128)(2,1)} custom-call(s32[1]{0:T(128)} %bitcast.flip, s32[16384]{0:T(1024)S(1)} %bitcast.26, bf16[512,256]{1,0:T(8,128)(2,1)S(1)} %collective-permute-done.inner, bf16[512,256]{1,0:T(8,128)(2,1)S(1)} %collective-permute-done.1.outer, bf16[4096,256]{1,0:T(8,128)(2,1)S(1)} %copy-done.1, ...), custom_call_target="tpu_custom_call" | custom-call | flops 268435456 | bytes 16777216 | tf_op jit(solution)/shard_map/graph_layer/pallas_call | solution.py:208
  36.1 2.0 %all-to-all-done.refs_0_ = bf16[32,8,128]{2,1,0:T(8,128)(2,1)S(1)} async-done(((bf16[32,8,128]{2,1,0:T(8,128)(2,1)}), bf16[32,8,128]{2,1,0:T(8,128)(2,1)S(1)}, u32[]{:S(2)}, u32[]{:S(2)}) %all-to-all-start) | async-done | bytes 65568 | tf_op jit(solution)/shard_map/all_to_all | solution.py:587
  38.1 1.8 %collective-permute-start.2 = (bf16[32,8,128]{2,1,0:T(8,128)(2,1)S(1)}, bf16[32,8,128]{2,1,0:T(8,128)(2,1)S(1)}, u32[]{:S(2)}, u32[]{:S(2)}) collective-permute-start(bf16[32,8,128]{2,1,0:T(8,128)(2,1)S(1)} %all-to-all-done.refs_0_), channel_id=1, source_target_pairs={{0,64},{32,96},{64,0},{96,32},{128,192},{160,224},{192,128},{224,1... | collective-permute-start | bytes 196616 | tf_op jit(solution)/shard_map/ppermute | solution.py:585
  39.9 3.2 %collective-permute-start.3 = (bf16[32,8,128]{2,1,0:T(8,128)(2,1)S(1)}, bf16[32,8,128]{2,1,0:T(8,128)(2,1)S(1)}, u32[]{:S(2)}, u32[]{:S(2)}) collective-permute-start(bf16[32,8,128]{2,1,0:T(8,128)(2,1)S(1)} %all-to-all-done.refs_0_), channel_id=1, source_target_pairs={{0,128},{32,160},{64,192},{96,224},{128,0},{160,32},{192,64},{224,... | collective-permute-start | bytes 196616 | tf_op jit(solution)/shard_map/ppermute | solution.py:585
  43.1 0.8 copy-done.13
  44.0 5.0 %scorer.3 = (bf16[2,16,128,256]{3,2,1,0:T(8,128)(2,1)}, f32[16,256]{1,0:T(8,128)S(1)}) custom-call(s32[1]{0:T(128)} %bitcast.6.where, bf16[32,8,128]{2,1,0:T(8,128)(2,1)S(1)} %all-to-all-done.refs_0_, bf16[32,8,128]{2,1,0:T(8,128)(2,1)} %collective-permute-done.5.refs_1_, s32[16,1024]{1,0:T(8,128)S(1)} %copy-done.11, bf16[256,256]{1,0:T(8,128)(2,1)S(1)} %copy-done.4, ...), custom_call_target="tpu_custom_call" | custom-call | flops 1610612736 | bytes 2097152 | tf_op jit(solution)/shard_map/scorer/pallas_call | solution.py:345
  49.0 0.1 collective-permute-start.6
  49.1 0.5 collective-permute-start.7
  49.6 0.1 collective-permute-start.8
  49.7 5.6 %scorer.4 = (bf16[3,16,128,256]{3,2,1,0:T(8,128)(2,1)}, f32[16,256]{1,0:T(8,128)S(1)}) custom-call(s32[1]{0:T(128)} %bitcast.6.where, bf16[32,8,128]{2,1,0:T(8,128)(2,1)S(1)} %collective-permute-done.2.refs_0_, bf16[32,8,128]{2,1,0:T(8,128)(2,1)S(1)} %collective-permute-done.3.refs_1_, bf16[32,8,128]{2,1,0:T(8,128)(2,1)S(1)} %collective-permute-done.4.refs_2_, ...), custom_call_target="tpu_custom_call" | custom-call | flops 2415919104 | bytes 3145728 | tf_op jit(solution)/shard_map/scorer/pallas_call | solution.py:345
  55.3 6.3 %scorer.5 = (bf16[3,16,128,256]{3,2,1,0:T(8,128)(2,1)}, f32[256,128]{1,0:T(8,128)}) custom-call(s32[1]{0:T(128)} %bitcast.6.where, bf16[32,8,128]{2,1,0:T(8,128)(2,1)S(1)} %collective-permute-done.6.refs_0_, bf16[32,8,128]{2,1,0:T(8,128)(2,1)S(1)} %collective-permute-done.7.refs_1_, bf16[32,8,128]{2,1,0:T(8,128)(2,1)S(1)} %collective-permute-done.8.refs_2_, ...), custom_call_target="tpu_custom_call" | custom-call | flops 2415919104 | bytes 3145728 | tf_op jit(solution)/shard_map/scorer/pallas_call | solution.py:345
  61.6 11.1 %all-to-all-start.1 = ((f32[256,1,128]{2,1,0:T(1,128)}), f32[256,1,128]{2,1,0:T(1,128)S(1)}, u32[]{:S(2)}, u32[]{:S(2)}) async-start(f32[256,1,128]{2,1,0:T(1,128)} %bitcast.14), calls=%async_computation.1 | async-start | bytes 262144 | tf_op jit(solution)/shard_map/all_to_all | solution.py:619
  72.7 0.0 copy-start.8
  72.7 10.2 %graph_layer.4.refs_0_ = bf16[4096,256]{1,0:T(8,128)(2,1)} custom-call(s32[1]{0:T(128)} %bitcast.flip, s32[16384]{0:T(1024)S(1)} %bitcast.27, bf16[512,256]{1,0:T(8,128)(2,1)S(1)} %collective-permute-done.inner, bf16[512,256]{1,0:T(8,128)(2,1)S(1)} %collective-permute-done.1.outer, bf16[4096,256]{1,0:T(8,128)(2,1)S(1)} %copy-done.1, ...), custom_call_target="tpu_custom_call", output_to_operand_aliasing={{}: (9, {})} | custom-call | flops 536870912 | bytes 33554432 | tf_op jit(solution)/shard_map/graph_layer/pallas_call | solution.py:208
  82.9 1.2 %all-to-all-done.1 = f32[256,1,128]{2,1,0:T(1,128)S(1)} async-done(((f32[256,1,128]{2,1,0:T(1,128)}), f32[256,1,128]{2,1,0:T(1,128)S(1)}, u32[]{:S(2)}, u32[]{:S(2)}) %all-to-all-start.1) | async-done | bytes 131104 | tf_op jit(solution)/shard_map/all_to_all | solution.py:619
  84.1 2.7 %ranking.1 = (f32[1,1]{1,0:T(1,128)}, f32[16,256]{1,0:T(8,128)S(1)}, bf16[4,128,256]{2,1,0:T(8,128)(2,1)S(1)}) custom-call(s32[1]{0:T(128)} %bitcast.6.where, f32[256,128]{1,0:T(8,128)S(1)} %bitcast.29, s32[2,512]{1,0:T(2,128)S(1)} %bitcast.34, bf16[2,16,128,256]{3,2,1,0:T(8,128)(2,1)} %get-tuple-element.58.pair, ...), custom_call_target="tpu_custom_call" | custom-call | flops 16777216 | bytes 6291456 | tf_op jit(solution)/shard_map/ranking/pallas_call | solution.py:425
  86.8 0.3 collective-permute-start.9
  87.1 2.4 %rest.1.kept = bf16[4,128,256]{2,1,0:T(8,128)(2,1)S(1)} custom-call(f32[16,256]{1,0:T(8,128)S(1)} %get-tuple-element.60.coef, bf16[2,16,128,256]{3,2,1,0:T(8,128)(2,1)} %get-tuple-element.58.pair, bf16[3,16,128,256]{3,2,1,0:T(8,128)(2,1)} %get-tuple-element.61.later), custom_call_target="tpu_custom_call" | custom-call | flops 16777216 | bytes 6291456 | tf_op jit(solution)/shard_map/rest/pallas_call | solution.py:457
  89.6 0.7 collective-permute-start.10
  90.3 2.3 %collective-permute-start.11 = (bf16[128,256]{1,0:T(8,128)(2,1)S(1)}, bf16[128,256]{1,0:T(8,128)(2,1)S(1)}, u32[]{:S(2)}, u32[]{:S(2)}) collective-permute-start(bf16[128,256]{1,0:T(8,128)(2,1)S(1)} %get-tuple-element.70), channel_id=1, source_target_pairs={{0,128},{32,160},{64,192},{96,224},{128,0},{160,32},{192,64},{224,... | collective-permute-start | bytes 196616 | tf_op jit(solution)/shard_map/ppermute | solution.py:585
  92.6 1.8 %collective-permute-start.12 = (bf16[128,256]{1,0:T(8,128)(2,1)S(1)}, bf16[128,256]{1,0:T(8,128)(2,1)S(1)}, u32[]{:S(2)}, u32[]{:S(2)}) collective-permute-start(bf16[128,256]{1,0:T(8,128)(2,1)S(1)} %get-tuple-element.69), channel_id=1, source_target_pairs={{0,192},{32,224},{64,128},{96,160},{128,64},{160,96},{192,0},{224,... | collective-permute-start | bytes 196616 | tf_op jit(solution)/shard_map/ppermute | solution.py:585
  94.4 1.9 %collective-permute-done.11.refs_1_ = bf16[128,256]{1,0:T(8,128)(2,1)S(1)} collective-permute-done((bf16[128,256]{1,0:T(8,128)(2,1)S(1)}, bf16[128,256]{1,0:T(8,128)(2,1)S(1)}, u32[]{:S(2)}, u32[]{:S(2)}) %collective-permute-start.11) | collective-permute-done | bytes 65568 | tf_op jit(solution)/shard_map/ppermute | solution.py:585
  96.4 1.7 %collective-permute-done.12.refs_2_ = bf16[128,256]{1,0:T(8,128)(2,1)S(1)} collective-permute-done((bf16[128,256]{1,0:T(8,128)(2,1)S(1)}, bf16[128,256]{1,0:T(8,128)(2,1)S(1)}, u32[]{:S(2)}, u32[]{:S(2)}) %collective-permute-start.12) | collective-permute-done | bytes 65568 | tf_op jit(solution)/shard_map/ppermute | solution.py:585
  98.1 0.8 finish.1
  98.9 10.9 %all-to-all-start.2 = ((bf16[32,8,128]{2,1,0:T(8,128)(2,1)}), bf16[32,8,128]{2,1,0:T(8,128)(2,1)S(1)}, u32[]{:S(2)}, u32[]{:S(2)}) async-start(bf16[32,8,128]{2,1,0:T(8,128)(2,1)} %finish.1), calls=%async_computation.2 | async-start | bytes 131072 | tf_op jit(solution)/shard_map/all_to_all | solution.py:630
  109.8 6.0 %graph_layer.5 = bf16[4096,256]{1,0:T(8,128)(2,1)} custom-call(s32[1]{0:T(128)} %bitcast.flip, s32[16384]{0:T(1024)S(1)} %bitcast.28, bf16[512,256]{1,0:T(8,128)(2,1)S(1)} %collective-permute-done.inner, bf16[512,256]{1,0:T(8,128)(2,1)S(1)} %collective-permute-done.1.outer, bf16[4096,256]{1,0:T(8,128)(2,1)S(1)} %copy-done.1, ...), custom_call_target="tpu_custom_call", output_to_operand_aliasing={{}: (9, {})} | custom-call | flops 268435456 | bytes 16777216 | tf_op jit(solution)/shard_map/graph_layer/pallas_call | solution.py:208
  115.8 2.7 %all-to-all-done.2.value = bf16[32,8,128]{2,1,0:T(8,128)(2,1)S(1)} async-done(((bf16[32,8,128]{2,1,0:T(8,128)(2,1)}), bf16[32,8,128]{2,1,0:T(8,128)(2,1)S(1)}, u32[]{:S(2)}, u32[]{:S(2)}) %all-to-all-start.2) | async-done | bytes 65568 | tf_op jit(solution)/shard_map/all_to_all | solution.py:630
  118.5 0.7 returned.1
  (32 shorter events, 0.1 us)
Async XLA Ops:
  1.7 8.1 %collective-permute-start = (bf16[512,256]{1,0:T(8,128)(2,1)S(1)}, bf16[512,256]{1,0:T(8,128)(2,1)S(1)}, u32[]{:S(2)}, u32[]{:S(2)}) collective-permute-start(bf16[512,256]{1,0:T(8,128)(2,1)S(1)} %get-tuple-element.68), channel_id=1, source_target_pairs={{0,1},{1,0},{2,3},{3,2},{4,5},{5,4},{6,7},{7,6},{8,9},{9,8},{10,11... | collective-permute-start | bytes 786440 | tf_op jit(solution)/shard_map/ppermute | solution.py:543
  4.1 8.3 %collective-permute-start.1 = (bf16[512,256]{1,0:T(8,128)(2,1)S(1)}, bf16[512,256]{1,0:T(8,128)(2,1)S(1)}, u32[]{:S(2)}, u32[]{:S(2)}) collective-permute-start(bf16[512,256]{1,0:T(8,128)(2,1)S(1)} %get-tuple-element.67), channel_id=1, source_target_pairs={{1,2},{2,1},{3,4},{4,3},{5,6},{6,5},{7,8},{8,7},{9,10},{10,9},{11,... | collective-permute-start | bytes 786440 | tf_op jit(solution)/shard_map/ppermute | solution.py:543
  7.2 1.6 %copy-start = (bf16[4096,256]{1,0:T(8,128)(2,1)S(1)}, bf16[4096,256]{1,0:T(8,128)(2,1)}, u32[]{:S(2)}) copy-start(bf16[4096,256]{1,0:T(8,128)(2,1)} %own.5) | copy-start | bytes 6291460
  8.8 3.6 %copy-start.10 = (s32[128]{0:T(128)S(1)}, s32[128]{0:T(128)}, u32[]{:S(2)}) copy-start(s32[128]{0:T(128)} %picks.1) | copy-start | bytes 1540
  12.4 16.9 %copy-start.5 = (bf16[256,256]{1,0:T(8,128)(2,1)S(1)}, bf16[256,256]{1,0:T(8,128)(2,1)}, u32[]{:S(2)}) copy-start(bf16[256,256]{1,0:T(8,128)(2,1)} %mid.1) | copy-start | bytes 393220
  12.4 16.9 %copy-start.6 = (bf16[128,256]{1,0:T(8,128)(2,1)S(1)}, bf16[128,256]{1,0:T(8,128)(2,1)}, u32[]{:S(2)}) copy-start(bf16[128,256]{1,0:T(8,128)(2,1)} %table.1) | copy-start | bytes 196612
  12.4 16.9 %copy-start.9 = (f32[256]{0:T(256)S(1)}, f32[256]{0:T(256)}, u32[]{:S(2)}) copy-start(f32[256]{0:T(256)} %param.26) | copy-start | bytes 3076
  12.4 17.6 %copy-start.1 = (bf16[4096,256]{1,0:T(8,128)(2,1)S(1)}, bf16[4096,256]{1,0:T(8,128)(2,1)}, u32[]{:S(2)}) copy-start(bf16[4096,256]{1,0:T(8,128)(2,1)} %own.5) | copy-start | bytes 6291460
  12.4 17.6 %copy-start.2 = (bf16[256,256]{1,0:T(8,128)(2,1)S(1)}, bf16[256,256]{1,0:T(8,128)(2,1)}, u32[]{:S(2)}) copy-start(bf16[256,256]{1,0:T(8,128)(2,1)} %sw.5) | copy-start | bytes 393220
  12.4 17.6 %copy-start.3 = (bf16[256,256]{1,0:T(8,128)(2,1)S(1)}, bf16[256,256]{1,0:T(8,128)(2,1)}, u32[]{:S(2)}) copy-start(bf16[256,256]{1,0:T(8,128)(2,1)} %nw.5) | copy-start | bytes 393220
  12.4 17.6 %copy-start.7 = (f32[256]{0:T(256)S(1)}, f32[256]{0:T(256)}, u32[]{:S(2)}) copy-start(f32[256]{0:T(256)} %param.18) | copy-start | bytes 3076
  15.9 22.1 %all-to-all-start = ((bf16[32,8,128]{2,1,0:T(8,128)(2,1)}), bf16[32,8,128]{2,1,0:T(8,128)(2,1)S(1)}, u32[]{:S(2)}, u32[]{:S(2)}) async-start(bf16[32,8,128]{2,1,0:T(8,128)(2,1)} %get-tuple-element.35), calls=%async_computation | async-start | bytes 131072 | tf_op jit(solution)/shard_map/all_to_all | solution.py:587
  29.4 0.6 copy-start.12
  30.1 13.0 %copy-start.4 = (bf16[256,256]{1,0:T(8,128)(2,1)S(1)}, bf16[256,256]{1,0:T(8,128)(2,1)}, u32[]{:S(2)}) copy-start(bf16[256,256]{1,0:T(8,128)(2,1)} %refs_3_.7) | copy-start | bytes 393220
  30.1 13.0 %copy-start.11 = (s32[16,1024]{1,0:T(8,128)S(1)}, s32[16,1024]{1,0:T(8,128)}, u32[]{:S(2)}) copy-start(s32[16,1024]{1,0:T(8,128)} %refs_3_.6) | copy-start | bytes 196612
  30.1 13.0 %copy-start.14 = (f32[256]{0:T(256)S(1)}, f32[256]{0:T(256)}, u32[]{:S(2)}) copy-start(f32[256]{0:T(256)} %param.23) | copy-start | bytes 3076
  30.1 13.0 %copy-start.15 = (f32[256]{0:T(256)S(1)}, f32[256]{0:T(256)}, u32[]{:S(2)}) copy-start(f32[256]{0:T(256)} %param.25) | copy-start | bytes 3076
  38.1 5.0 %collective-permute-start.5 = (bf16[32,8,128]{2,1,0:T(8,128)(2,1)S(1)}, bf16[32,8,128]{2,1,0:T(8,128)(2,1)}, u32[]{:S(2)}, u32[]{:S(2)}) collective-permute-start(bf16[32,8,128]{2,1,0:T(8,128)(2,1)S(1)} %all-to-all-done.refs_0_), channel_id=1, source_target_pairs={{0,32},{32,0},{64,96},{96,64},{128,160},{160,128},{192,224},{224,1... | collective-permute-start | bytes 196616 | tf_op jit(solution)/shard_map/ppermute | solution.py:610
  38.1 10.9 %collective-permute-start.2 = (bf16[32,8,128]{2,1,0:T(8,128)(2,1)S(1)}, bf16[32,8,128]{2,1,0:T(8,128)(2,1)S(1)}, u32[]{:S(2)}, u32[]{:S(2)}) collective-permute-start(bf16[32,8,128]{2,1,0:T(8,128)(2,1)S(1)} %all-to-all-done.refs_0_), channel_id=1, source_target_pairs={{0,64},{32,96},{64,0},{96,32},{128,192},{160,224},{192,128},{224,1... | collective-permute-start | bytes 196616 | tf_op jit(solution)/shard_map/ppermute | solution.py:585
  39.9 9.1 %collective-permute-start.3 = (bf16[32,8,128]{2,1,0:T(8,128)(2,1)S(1)}, bf16[32,8,128]{2,1,0:T(8,128)(2,1)S(1)}, u32[]{:S(2)}, u32[]{:S(2)}) collective-permute-start(bf16[32,8,128]{2,1,0:T(8,128)(2,1)S(1)} %all-to-all-done.refs_0_), channel_id=1, source_target_pairs={{0,128},{32,160},{64,192},{96,224},{128,0},{160,32},{192,64},{224,... | collective-permute-start | bytes 196616 | tf_op jit(solution)/shard_map/ppermute | solution.py:585
  43.1 5.9 %collective-permute-start.4 = (bf16[32,8,128]{2,1,0:T(8,128)(2,1)S(1)}, bf16[32,8,128]{2,1,0:T(8,128)(2,1)S(1)}, u32[]{:S(2)}, u32[]{:S(2)}) collective-permute-start(bf16[32,8,128]{2,1,0:T(8,128)(2,1)S(1)} %all-to-all-done.refs_0_), channel_id=1, source_target_pairs={{0,192},{32,224},{64,128},{96,160},{128,64},{160,96},{192,0},{224,... | collective-permute-start | bytes 196616 | tf_op jit(solution)/shard_map/ppermute | solution.py:585
  43.1 0.8 copy-start.13
  49.0 6.3 %collective-permute-start.6 = (bf16[32,8,128]{2,1,0:T(8,128)(2,1)S(1)}, bf16[32,8,128]{2,1,0:T(8,128)(2,1)S(1)}, u32[]{:S(2)}, u32[]{:S(2)}) collective-permute-start(bf16[32,8,128]{2,1,0:T(8,128)(2,1)S(1)} %collective-permute-done.2.refs_0_), channel_id=1, source_target_pairs={{0,32},{32,0},{64,96},{96,64},{128,160},{160,128},{192,224},{224,1... | collective-permute-start | bytes 196616 | tf_op jit(solution)/shard_map/ppermute | solution.py:613
  49.1 6.2 %collective-permute-start.7 = (bf16[32,8,128]{2,1,0:T(8,128)(2,1)S(1)}, bf16[32,8,128]{2,1,0:T(8,128)(2,1)S(1)}, u32[]{:S(2)}, u32[]{:S(2)}) collective-permute-start(bf16[32,8,128]{2,1,0:T(8,128)(2,1)S(1)} %collective-permute-done.3.refs_1_), channel_id=1, source_target_pairs={{0,32},{32,0},{64,96},{96,64},{128,160},{160,128},{192,224},{224,1... | collective-permute-start | bytes 196616 | tf_op jit(solution)/shard_map/ppermute | solution.py:613
  49.6 5.7 %collective-permute-start.8 = (bf16[32,8,128]{2,1,0:T(8,128)(2,1)S(1)}, bf16[32,8,128]{2,1,0:T(8,128)(2,1)S(1)}, u32[]{:S(2)}, u32[]{:S(2)}) collective-permute-start(bf16[32,8,128]{2,1,0:T(8,128)(2,1)S(1)} %collective-permute-done.4.refs_2_), channel_id=1, source_target_pairs={{0,32},{32,0},{64,96},{96,64},{128,160},{160,128},{192,224},{224,1... | collective-permute-start | bytes 196616 | tf_op jit(solution)/shard_map/ppermute | solution.py:613
  61.6 22.5 %all-to-all-start.1 = ((f32[256,1,128]{2,1,0:T(1,128)}), f32[256,1,128]{2,1,0:T(1,128)S(1)}, u32[]{:S(2)}, u32[]{:S(2)}) async-start(f32[256,1,128]{2,1,0:T(1,128)} %bitcast.14), calls=%async_computation.1 | async-start | bytes 262144 | tf_op jit(solution)/shard_map/all_to_all | solution.py:619
  72.7 11.4 %copy-start.8 = (s32[512,2]{0,1:T(2,128)S(1)}, s32[512,2]{0,1:T(2,128)}, u32[]{:S(2)}) copy-start(s32[512,2]{0,1:T(2,128)} %param.27) | copy-start | bytes 12292
  86.8 2.7 %collective-permute-start.9 = (bf16[4,128,256]{2,1,0:T(8,128)(2,1)S(1)}, bf16[4,128,256]{2,1,0:T(8,128)(2,1)S(1)}, u32[]{:S(2)}, u32[]{:S(2)}) collective-permute-start(bf16[4,128,256]{2,1,0:T(8,128)(2,1)S(1)} %get-tuple-element.62), channel_id=1, source_target_pairs={{0,32},{32,0},{64,96},{96,64},{128,160},{160,128},{192,224},{224,1... | collective-permute-start | bytes 786440 | tf_op jit(solution)/shard_map/ppermute | solution.py:625
  89.6 4.8 %collective-permute-start.10 = (bf16[128,256]{1,0:T(8,128)(2,1)S(1)}, bf16[128,256]{1,0:T(8,128)(2,1)S(1)}, u32[]{:S(2)}, u32[]{:S(2)}) collective-permute-start(bf16[128,256]{1,0:T(8,128)(2,1)S(1)} %get-tuple-element.71), channel_id=1, source_target_pairs={{0,64},{32,96},{64,0},{96,32},{128,192},{160,224},{192,128},{224,1... | collective-permute-start | bytes 196616 | tf_op jit(solution)/shard_map/ppermute | solution.py:585
  90.3 6.1 %collective-permute-start.11 = (bf16[128,256]{1,0:T(8,128)(2,1)S(1)}, bf16[128,256]{1,0:T(8,128)(2,1)S(1)}, u32[]{:S(2)}, u32[]{:S(2)}) collective-permute-start(bf16[128,256]{1,0:T(8,128)(2,1)S(1)} %get-tuple-element.70), channel_id=1, source_target_pairs={{0,128},{32,160},{64,192},{96,224},{128,0},{160,32},{192,64},{224,... | collective-permute-start | bytes 196616 | tf_op jit(solution)/shard_map/ppermute | solution.py:585
  92.6 5.5 %collective-permute-start.12 = (bf16[128,256]{1,0:T(8,128)(2,1)S(1)}, bf16[128,256]{1,0:T(8,128)(2,1)S(1)}, u32[]{:S(2)}, u32[]{:S(2)}) collective-permute-start(bf16[128,256]{1,0:T(8,128)(2,1)S(1)} %get-tuple-element.69), channel_id=1, source_target_pairs={{0,192},{32,224},{64,128},{96,160},{128,64},{160,96},{192,0},{224,... | collective-permute-start | bytes 196616 | tf_op jit(solution)/shard_map/ppermute | solution.py:585
  98.9 19.6 %all-to-all-start.2 = ((bf16[32,8,128]{2,1,0:T(8,128)(2,1)}), bf16[32,8,128]{2,1,0:T(8,128)(2,1)S(1)}, u32[]{:S(2)}, u32[]{:S(2)}) async-start(bf16[32,8,128]{2,1,0:T(8,128)(2,1)} %finish.1), calls=%async_computation.2 | async-start | bytes 131072 | tf_op jit(solution)/shard_map/all_to_all | solution.py:630

commit v8 on v7

--- a/solution.py
+++ b/solution.py
@@ -239,34 +239,32 @@
     return group ^ (2 * (turn & 3) + (turn >> 2))
 
 
-def prepare_kernel(table, mid, weight, tabh, midh, back):
-    tabh[...] = (table[...].astype(f32) * 0.5).astype(bf16)
-    middle = mid[...].astype(f32)
-    midh[...] = (middle * 0.5).astype(bf16)
-    back[...] = jnp.transpose(middle * (weight[...] * 0.25)).astype(bf16)
-
-
-def prepared(table, mid, weight):
+def prepare_kernel(mid, weight, back):
+    back[...] = jnp.transpose(mid[...].astype(f32) * (weight[...] * 0.25)).astype(bf16)
+
+
+def prepared(mid, weight):
     return pl.pallas_call(
         prepare_kernel,
-        out_shape=tuple(jax.ShapeDtypeStruct(x.shape, bf16) for x in (table, mid, mid)),
-        in_specs=[VMEM] * 3,
-        out_specs=(VMEM,) * 3,
+        out_shape=jax.ShapeDtypeStruct(mid.shape, bf16),
+        in_specs=[VMEM] * 2,
+        out_specs=VMEM,
         cost_estimate=pl.CostEstimate(flops=1 << 20, transcendentals=0, bytes_accessed=1 << 19),
         compiler_params=pltpu.CompilerParams(vmem_limit_bytes=8 << 20),
         name="prepare",
-    )(table, mid, weight)
+    )(mid, weight)
 
 
 def scorer_kernel(groups, final, where, *refs):
     xs, refs = refs[:groups], refs[groups:]
-    ids, join, jbias, tabh, midh, back, mbias, weight = refs[:8]
-    given, (grads_hbm, sent, base, total, grads, sems) = refs[8:-6], refs[-6:]
+    ids, join, jbias, table, mid, back, mbias, weight = refs[:8]
+    given, refs = refs[8:-8], refs[-8:]
+    grads_hbm, sent, base, tabh, midh, total, grads, sems = refs
     step = pl.program_id(0)
     slot = step & 1
     chunk = base.shape[1]
     configs = ids.shape[0]
-    layouts = tabh.shape[0]
+    layouts = table.shape[0]
     one = jnp.asarray(1.0, bf16)
 
     @pl.when(step == 0)
@@ -280,19 +278,29 @@
                 )
                 + jbias[...]
             )
+        tabh[...] = (table[...].astype(f32) * 0.5).astype(bf16)
+        midh[...] = (mid[...].astype(f32) * 0.5).astype(bf16)
         total[...] = given[0][...] if given else jnp.zeros_like(total)
 
-    def copy_of(turn, place):
-        return pltpu.make_async_copy(grads.at[place], grads_hbm.at[turn], sems.at[place])
+    some = 8
+
+    def copy_of(turn, place, first):
+        part = pl.ds(first, some)
+        return pltpu.make_async_copy(
+            grads.at[place, part], grads_hbm.at[turn, part], sems.at[place, first // some]
+        )
+
+    def wait_for(turn, place):
+        for first in range(0, configs, some):
+            copy_of(turn, place, first).wait()
 
     @pl.when(step >= 2)
     def _():
-        copy_of(step - 2, slot).wait()
+        wait_for(step - 2, slot)
 
     columns = jnp.transpose(ids[...].astype(f32))
     lanes = lax.broadcasted_iota(jnp.int32, (chunk, layouts), 1).astype(f32)
     rows = base[step]
-    some = 8
     for first in range(0, configs, some):
         picks = jnp.concatenate(
             [
@@ -318,8 +326,7 @@
         grad = jnp.dot(slope2, back[...], preferred_element_type=f32).astype(bf16) * slope
         for q in range(some):
             grads[slot, first + q] = grad[q * chunk : (q + 1) * chunk, :]
-
-    copy_of(step, slot).start()
+        copy_of(step, slot, first).start()
 
     @pl.when(step == groups - 1)
     def _():
@@ -331,8 +338,8 @@
             sent[...] = jnp.broadcast_to(jnp.sum(spread, axis=0, keepdims=True), sent.shape)
         else:
             sent[...] = total[...]
-        copy_of(step - 1, 1 - slot).wait()
-        copy_of(step, slot).wait()
+        wait_for(step - 1, 1 - slot)
+        wait_for(step, slot)
 
 
 def scorer_of(final, turns, where, xs, ids, join, jbias, weights, mbias, weight, given):
@@ -361,9 +368,11 @@
             out_specs=(HBM, VMEM),
             scratch_shapes=[
                 pltpu.VMEM((groups, chunk, hidden), f32),
+                pltpu.VMEM(weights[0].shape, bf16),
+                pltpu.VMEM(weights[1].shape, bf16),
                 pltpu.VMEM((configs, hidden), f32),
                 pltpu.VMEM((2, configs, chunk, hidden), bf16),
-                pltpu.SemaphoreType.DMA((2,)),
+                pltpu.SemaphoreType.DMA((2, 2)),
             ],
         ),
         cost_estimate=pl.CostEstimate(
@@ -587,8 +596,8 @@
     mine = lax.all_to_all(conf_src, "node", 0, 0, tiled=True)
     embed = layer(0, 2, None)
     weight = score_weight.reshape(1, -1)
-    weights = prepared(layout_table, mid_weight, weight)
-    mine, embed, *weights = hold((mine, embed, *weights))
+    mine, embed, back = hold((mine, embed, prepared(mid_weight, weight)))
+    weights = (layout_table, mid_weight, back)
     others = [shift(mine, by) for by in range(1, rings)]
     where = group.reshape(1)
 
@@ -617,7 +626,7 @@
     other, sent = scorer((devices, 128), (rings + 1, 1), swapped, [total])
     sent, embed = hold((sent, embed))
     got = lax.all_to_all(sent.reshape(devices, 1, 128), both, 0, 0, tiled=True)
-    embed = layer(2, 4, embed)
+    embed = layer(2, 3, embed)
     got, embed = hold((got, embed))
     loss, coef, away = ranking_of(
         scale, where, got.reshape(devices, 128), config_pairs.T, pair, other
@@ -628,7 +637,7 @@
     arrived = [shift(part, by) for by, part in enumerate(sums, 1)]
     local_grad, embed = hold((finish_of(kept, came, arrived, join_weight), embed))
     conf_grad = lax.all_to_all(local_grad, "node", 0, 0, tiled=True)
-    embed = layer(6, 2, embed)
+    embed = layer(5, 3, embed)
     conf_grad = returned_of(conf_grad)
     return (embed, loss.reshape(()), conf_grad)
 

time: 120 us -> 115 us (0.958)
  starting transfers between devices: 50.7 us -> 48 us
  local copies, waits for them, and re-layouts: 4.17 us -> 2.73 us
    all_to_all x1, waiting for transfers between devices: 1.25 us -> 3.35 us  [shards(): got = lax.all_to_all(sent.reshape(devices, 1, 128), both, 0, 0, tiled=True)]
    all_to_all x1, waiting for transfers between devices: 2.73 us -> 0.63 us  [shards(): conf_grad = lax.all_to_all(local_grad, 'node', 0, 0, tiled=True)]
    all_to_all x1, starting transfers between devices: 10.9 us -> 9.3 us  [shards(): conf_grad = lax.all_to_all(local_grad, 'node', 0, 0, tiled=True)]
    unnamed x32 -> x28, local copies, waits for them, and re-layouts: 3.1 us -> 1.66 us
  transfers between devices with their start and end apart: 16 -> 16, of which waited for: 7 -> 8; matrix products, arithmetic and copies ran while one was open for 1% -> 1% of each run, Pallas kernels for 30% -> 31%
where the time goes in v8:
time: 115 us
  Pallas kernels  48.8 us (42%)
  starting transfers between devices  48 us (42%)
  waiting for transfers between devices  13.6 us (12%)
  local copies, waits for them, and re-layouts  2.73 us (2%)
    pallas_call x3, Pallas kernels, layer_of(): pl.pallas_call(layer_kernel, out_shape=jax.ShapeDtypeStruct((nodes, width...  22.1 us
    pallas_call x3, Pallas kernels, scorer_of(): pl.pallas_call(functools.partial(scorer_kernel, groups, final), out_shape...  16.1 us
    all_to_all x1, starting transfers between devices, shards(): mine = lax.all_to_all(conf_src, 'node', 0, 0, tiled=True)  13.3 us
    all_to_all x1, starting transfers between devices, shards(): got = lax.all_to_all(sent.reshape(devices, 1, 128), both, 0, 0, tiled=True)  10.1 us
    ppermute x6, starting transfers between devices, shift(): lax.ppermute(value, 'cfg', [(i, i ^ 2 * by) for i in range(group_count)])  9.79 us
    all_to_all x1, starting transfers between devices, shards(): conf_grad = lax.all_to_all(local_grad, 'node', 0, 0, tiled=True)  9.3 us
    ppermute x2, starting transfers between devices, trade(): return lax.ppermute(rows, both, pairs)  4.67 us
    ppermute x6, waiting for transfers between devices, shift(): lax.ppermute(value, 'cfg', [(i, i ^ 2 * by) for i in range(group_count)])  3.77 us
  transfers between devices with their start and end apart: 16, of which 8 were waited for; matrix products, arithmetic and copies ran while one was open for 1% of the time, Pallas kernels for 31%

profile of v8, /device:TPU:2, one launch (start us, length us, event | category | flops | bytes accessed | tf_op | source)
XLA Modules:
  0.0 114.9 jit_solution(3309575122034661083)
XLA Ops:
  0.6 1.1 constant_dynamic-slice_fusion
  1.7 2.4 %collective-permute-start = (bf16[512,256]{1,0:T(8,128)(2,1)S(1)}, bf16[512,256]{1,0:T(8,128)(2,1)S(1)}, u32[]{:S(2)}, u32[]{:S(2)}) collective-permute-start(bf16[512,256]{1,0:T(8,128)(2,1)S(1)} %get-tuple-element.58), channel_id=1, source_target_pairs={{0,1},{1,0},{2,3},{3,2},{4,5},{5,4},{6,7},{7,6},{8,9},{9,8},{10,11... | collective-permute-start | bytes 786440 | tf_op jit(solution)/shard_map/ppermute | solution.py:552
  4.1 2.3 %collective-permute-start.1 = (bf16[512,256]{1,0:T(8,128)(2,1)S(1)}, bf16[512,256]{1,0:T(8,128)(2,1)S(1)}, u32[]{:S(2)}, u32[]{:S(2)}) collective-permute-start(bf16[512,256]{1,0:T(8,128)(2,1)S(1)} %get-tuple-element.57), channel_id=1, source_target_pairs={{1,2},{2,1},{3,4},{4,3},{5,6},{6,5},{7,8},{8,7},{9,10},{10,9},{11,... | collective-permute-start | bytes 786440 | tf_op jit(solution)/shard_map/ppermute | solution.py:552
  6.4 0.9 broadcast_multiply_fusion
  7.2 0.0 copy-start
  7.3 1.6 %copy-done = bf16[4096,256]{1,0:T(8,128)(2,1)S(1)} copy-done((bf16[4096,256]{1,0:T(8,128)(2,1)S(1)}, bf16[4096,256]{1,0:T(8,128)(2,1)}, u32[]{:S(2)}) %copy-start) | copy-done | bytes 2097176
  8.8 0.4 window_rows.1.refs_3_
  9.2 0.6 collective-permute-done.inner
  9.8 2.6 %collective-permute-done.1.outer = bf16[512,256]{1,0:T(8,128)(2,1)S(1)} collective-permute-done((bf16[512,256]{1,0:T(8,128)(2,1)S(1)}, bf16[512,256]{1,0:T(8,128)(2,1)S(1)}, u32[]{:S(2)}, u32[]{:S(2)}) %collective-permute-start.1) | collective-permute-done | bytes 262176 | tf_op jit(solution)/shard_map/ppermute | solution.py:552
  12.4 0.0 copy-start.2
  12.4 0.0 copy-start.3
  12.4 0.0 copy-start.6
  12.4 3.5 %conf_rows.1 = (bf16[32,8,128]{2,1,0:T(8,128)(2,1)}, f32[10240,128]{1,0:T(8,128)S(1)}) custom-call(s32[1]{0:T(128)} %bitcast.flip, s32[16384]{0:T(1024)S(1)} %bitcast.25, s32[128]{0:T(128)S(1)} %copy-done.9, bf16[512,256]{1,0:T(8,128)(2,1)S(1)} %collective-permute-done.1.outer, ...), custom_call_target="tpu_custom_call", output_to_operand_aliasing={{1}: (8, {})} | custom-call | flops 33554432 | bytes 6291456 | tf_op jit(solution)/shard_map/conf_rows/pallas_call | solution.py:144
  15.9 13.3 %all-to-all-start = ((bf16[32,8,128]{2,1,0:T(8,128)(2,1)}), bf16[32,8,128]{2,1,0:T(8,128)(2,1)S(1)}, u32[]{:S(2)}, u32[]{:S(2)}) async-start(bf16[32,8,128]{2,1,0:T(8,128)(2,1)} %get-tuple-element.30), calls=%async_computation | async-start | bytes 131072 | tf_op jit(solution)/shard_map/all_to_all | solution.py:596
  29.3 0.1 prepare.1.refs_7_.refs_8_
  29.4 0.0 copy-start.4
  29.5 0.0 copy-start.10
  29.5 0.0 copy-start.11
  29.5 0.0 copy-start.12
  29.5 0.0 copy-start.13
  29.5 5.9 %graph_layer.3.refs_0_ = bf16[4096,256]{1,0:T(8,128)(2,1)} custom-call(s32[1]{0:T(128)} %bitcast.flip, s32[16384]{0:T(1024)S(1)} %bitcast.26, bf16[512,256]{1,0:T(8,128)(2,1)S(1)} %collective-permute-done.inner, bf16[512,256]{1,0:T(8,128)(2,1)S(1)} %collective-permute-done.1.outer, bf16[4096,256]{1,0:T(8,128)(2,1)S(1)} %copy-done.1, ...), custom_call_target="tpu_custom_call" | custom-call | flops 268435456 | bytes 16777216 | tf_op jit(solution)/shard_map/graph_layer/pallas_call | solution.py:208
  35.5 2.6 %all-to-all-done.refs_0_ = bf16[32,8,128]{2,1,0:T(8,128)(2,1)S(1)} async-done(((bf16[32,8,128]{2,1,0:T(8,128)(2,1)}), bf16[32,8,128]{2,1,0:T(8,128)(2,1)S(1)}, u32[]{:S(2)}, u32[]{:S(2)}) %all-to-all-start) | async-done | bytes 65568 | tf_op jit(solution)/shard_map/all_to_all | solution.py:596
  38.1 1.8 %collective-permute-start.2 = (bf16[32,8,128]{2,1,0:T(8,128)(2,1)S(1)}, bf16[32,8,128]{2,1,0:T(8,128)(2,1)S(1)}, u32[]{:S(2)}, u32[]{:S(2)}) collective-permute-start(bf16[32,8,128]{2,1,0:T(8,128)(2,1)S(1)} %all-to-all-done.refs_0_), channel_id=1, source_target_pairs={{0,64},{32,96},{64,0},{96,32},{128,192},{160,224},{192,128},{224,1... | collective-permute-start | bytes 196616 | tf_op jit(solution)/shard_map/ppermute | solution.py:594
  39.9 3.2 %collective-permute-start.3 = (bf16[32,8,128]{2,1,0:T(8,128)(2,1)S(1)}, bf16[32,8,128]{2,1,0:T(8,128)(2,1)S(1)}, u32[]{:S(2)}, u32[]{:S(2)}) collective-permute-start(bf16[32,8,128]{2,1,0:T(8,128)(2,1)S(1)} %all-to-all-done.refs_0_), channel_id=1, source_target_pairs={{0,128},{32,160},{64,192},{96,224},{128,0},{160,32},{192,64},{224,... | collective-permute-start | bytes 196616 | tf_op jit(solution)/shard_map/ppermute | solution.py:594
  43.1 0.0 collective-permute-start.4
  43.1 4.8 %scorer.3 = (bf16[2,16,128,256]{3,2,1,0:T(8,128)(2,1)}, f32[16,256]{1,0:T(8,128)S(1)}) custom-call(s32[1]{0:T(128)} %bitcast.6.where, bf16[32,8,128]{2,1,0:T(8,128)(2,1)S(1)} %all-to-all-done.refs_0_, bf16[32,8,128]{2,1,0:T(8,128)(2,1)} %collective-permute-done.5.refs_1_, s32[16,1024]{1,0:T(8,128)S(1)} %copy-done.10, bf16[256,256]{1,0:T(8,128)(2,1)S(1)} %copy-done.4, ...), custom_call_target="tpu_custom_call" | custom-call | flops 1610612736 | bytes 2097152 | tf_op jit(solution)/shard_map/scorer/pallas_call | solution.py:352
  47.9 0.6 collective-permute-done.4.refs_2_
  48.6 0.5 collective-permute-start.7
  49.1 0.0 collective-permute-start.8
  49.1 5.3 %scorer.4 = (bf16[3,16,128,256]{3,2,1,0:T(8,128)(2,1)}, f32[16,256]{1,0:T(8,128)S(1)}) custom-call(s32[1]{0:T(128)} %bitcast.6.where, bf16[32,8,128]{2,1,0:T(8,128)(2,1)S(1)} %collective-permute-done.2.refs_0_, bf16[32,8,128]{2,1,0:T(8,128)(2,1)S(1)} %collective-permute-done.3.refs_1_, bf16[32,8,128]{2,1,0:T(8,128)(2,1)S(1)} %collective-permute-done.4.refs_2_, ...), custom_call_target="tpu_custom_call" | custom-call | flops 2415919104 | bytes 3145728 | tf_op jit(solution)/shard_map/scorer/pallas_call | solution.py:352
  54.4 6.0 %scorer.5 = (bf16[3,16,128,256]{3,2,1,0:T(8,128)(2,1)}, f32[256,128]{1,0:T(8,128)}) custom-call(s32[1]{0:T(128)} %bitcast.6.where, bf16[32,8,128]{2,1,0:T(8,128)(2,1)S(1)} %collective-permute-done.6.refs_0_, bf16[32,8,128]{2,1,0:T(8,128)(2,1)S(1)} %collective-permute-done.7.refs_1_, bf16[32,8,128]{2,1,0:T(8,128)(2,1)S(1)} %collective-permute-done.8.refs_2_, ...), custom_call_target="tpu_custom_call" | custom-call | flops 2415919104 | bytes 3145728 | tf_op jit(solution)/shard_map/scorer/pallas_call | solution.py:352
  60.5 10.1 %all-to-all-start.1 = ((f32[256,1,128]{2,1,0:T(1,128)}), f32[256,1,128]{2,1,0:T(1,128)S(1)}, u32[]{:S(2)}, u32[]{:S(2)}) async-start(f32[256,1,128]{2,1,0:T(1,128)} %bitcast.14), calls=%async_computation.1 | async-start | bytes 262144 | tf_op jit(solution)/shard_map/all_to_all | solution.py:628
  70.6 0.0 copy-start.7
  70.6 8.1 %graph_layer.4.refs_0_ = bf16[4096,256]{1,0:T(8,128)(2,1)} custom-call(s32[1]{0:T(128)} %bitcast.flip, s32[16384]{0:T(1024)S(1)} %bitcast.27, bf16[512,256]{1,0:T(8,128)(2,1)S(1)} %collective-permute-done.inner, bf16[512,256]{1,0:T(8,128)(2,1)S(1)} %collective-permute-done.1.outer, bf16[4096,256]{1,0:T(8,128)(2,1)S(1)} %copy-done.1, ...), custom_call_target="tpu_custom_call", output_to_operand_aliasing={{}: (9, {})} | custom-call | flops 402653184 | bytes 25165824 | tf_op jit(solution)/shard_map/graph_layer/pallas_call | solution.py:208
  78.6 3.3 %all-to-all-done.1 = f32[256,1,128]{2,1,0:T(1,128)S(1)} async-done(((f32[256,1,128]{2,1,0:T(1,128)}), f32[256,1,128]{2,1,0:T(1,128)S(1)}, u32[]{:S(2)}, u32[]{:S(2)}) %all-to-all-start.1) | async-done | bytes 131104 | tf_op jit(solution)/shard_map/all_to_all | solution.py:628
  82.0 2.7 %ranking.1 = (f32[1,1]{1,0:T(1,128)}, f32[16,256]{1,0:T(8,128)S(1)}, bf16[4,128,256]{2,1,0:T(8,128)(2,1)S(1)}) custom-call(s32[1]{0:T(128)} %bitcast.6.where, f32[256,128]{1,0:T(8,128)S(1)} %bitcast.29, s32[2,512]{1,0:T(2,128)S(1)} %bitcast.34, bf16[2,16,128,256]{3,2,1,0:T(8,128)(2,1)} %get-tuple-element.48.pair, ...), custom_call_target="tpu_custom_call" | custom-call | flops 16777216 | bytes 6291456 | tf_op jit(solution)/shard_map/ranking/pallas_call | solution.py:434
  84.7 0.3 collective-permute-start.9
  85.0 2.4 %rest.1.kept = bf16[4,128,256]{2,1,0:T(8,128)(2,1)S(1)} custom-call(f32[16,256]{1,0:T(8,128)S(1)} %get-tuple-element.50.coef, bf16[2,16,128,256]{3,2,1,0:T(8,128)(2,1)} %get-tuple-element.48.pair, bf16[3,16,128,256]{3,2,1,0:T(8,128)(2,1)} %get-tuple-element.51.later), custom_call_target="tpu_custom_call" | custom-call | flops 16777216 | bytes 6291456 | tf_op jit(solution)/shard_map/rest/pallas_call | solution.py:466
  87.5 0.7 collective-permute-start.10
  88.2 1.8 %collective-permute-start.11 = (bf16[128,256]{1,0:T(8,128)(2,1)S(1)}, bf16[128,256]{1,0:T(8,128)(2,1)S(1)}, u32[]{:S(2)}, u32[]{:S(2)}) collective-permute-start(bf16[128,256]{1,0:T(8,128)(2,1)S(1)} %get-tuple-element.60), channel_id=1, source_target_pairs={{0,128},{32,160},{64,192},{96,224},{128,0},{160,32},{192,64},{224,... | collective-permute-start | bytes 196616 | tf_op jit(solution)/shard_map/ppermute | solution.py:594
  90.0 2.3 %collective-permute-start.12 = (bf16[128,256]{1,0:T(8,128)(2,1)S(1)}, bf16[128,256]{1,0:T(8,128)(2,1)S(1)}, u32[]{:S(2)}, u32[]{:S(2)}) collective-permute-start(bf16[128,256]{1,0:T(8,128)(2,1)S(1)} %get-tuple-element.59), channel_id=1, source_target_pairs={{0,192},{32,224},{64,128},{96,160},{128,64},{160,96},{192,0},{224,... | collective-permute-start | bytes 196616 | tf_op jit(solution)/shard_map/ppermute | solution.py:594
  92.3 1.7 %collective-permute-done.11.refs_1_ = bf16[128,256]{1,0:T(8,128)(2,1)S(1)} collective-permute-done((bf16[128,256]{1,0:T(8,128)(2,1)S(1)}, bf16[128,256]{1,0:T(8,128)(2,1)S(1)}, u32[]{:S(2)}, u32[]{:S(2)}) %collective-permute-start.11) | collective-permute-done | bytes 65568 | tf_op jit(solution)/shard_map/ppermute | solution.py:594
  94.0 1.5 %collective-permute-done.12.refs_2_ = bf16[128,256]{1,0:T(8,128)(2,1)S(1)} collective-permute-done((bf16[128,256]{1,0:T(8,128)(2,1)S(1)}, bf16[128,256]{1,0:T(8,128)(2,1)S(1)}, u32[]{:S(2)}, u32[]{:S(2)}) %collective-permute-start.12) | collective-permute-done | bytes 65568 | tf_op jit(solution)/shard_map/ppermute | solution.py:594
  95.4 0.8 finish.1
  96.3 9.3 %all-to-all-start.2 = ((bf16[32,8,128]{2,1,0:T(8,128)(2,1)}), bf16[32,8,128]{2,1,0:T(8,128)(2,1)S(1)}, u32[]{:S(2)}, u32[]{:S(2)}) async-start(bf16[32,8,128]{2,1,0:T(8,128)(2,1)} %finish.1), calls=%async_computation.2 | async-start | bytes 131072 | tf_op jit(solution)/shard_map/all_to_all | solution.py:639
  105.6 8.1 %graph_layer.5 = bf16[4096,256]{1,0:T(8,128)(2,1)} custom-call(s32[1]{0:T(128)} %bitcast.flip, s32[16384]{0:T(1024)S(1)} %bitcast.28, bf16[512,256]{1,0:T(8,128)(2,1)S(1)} %collective-permute-done.inner, bf16[512,256]{1,0:T(8,128)(2,1)S(1)} %collective-permute-done.1.outer, bf16[4096,256]{1,0:T(8,128)(2,1)S(1)} %copy-done.1, ...), custom_call_target="tpu_custom_call", output_to_operand_aliasing={{}: (9, {})} | custom-call | flops 402653184 | bytes 25165824 | tf_op jit(solution)/shard_map/graph_layer/pallas_call | solution.py:208
  113.6 0.6 all-to-all-done.2.value
  114.3 0.7 returned.1
  (28 shorter events, 0.1 us)
Async XLA Ops:
  1.7 8.1 %collective-permute-start = (bf16[512,256]{1,0:T(8,128)(2,1)S(1)}, bf16[512,256]{1,0:T(8,128)(2,1)S(1)}, u32[]{:S(2)}, u32[]{:S(2)}) collective-permute-start(bf16[512,256]{1,0:T(8,128)(2,1)S(1)} %get-tuple-element.58), channel_id=1, source_target_pairs={{0,1},{1,0},{2,3},{3,2},{4,5},{5,4},{6,7},{7,6},{8,9},{9,8},{10,11... | collective-permute-start | bytes 786440 | tf_op jit(solution)/shard_map/ppermute | solution.py:552
  4.1 8.3 %collective-permute-start.1 = (bf16[512,256]{1,0:T(8,128)(2,1)S(1)}, bf16[512,256]{1,0:T(8,128)(2,1)S(1)}, u32[]{:S(2)}, u32[]{:S(2)}) collective-permute-start(bf16[512,256]{1,0:T(8,128)(2,1)S(1)} %get-tuple-element.57), channel_id=1, source_target_pairs={{1,2},{2,1},{3,4},{4,3},{5,6},{6,5},{7,8},{8,7},{9,10},{10,9},{11,... | collective-permute-start | bytes 786440 | tf_op jit(solution)/shard_map/ppermute | solution.py:552
  7.2 1.6 %copy-start = (bf16[4096,256]{1,0:T(8,128)(2,1)S(1)}, bf16[4096,256]{1,0:T(8,128)(2,1)}, u32[]{:S(2)}) copy-start(bf16[4096,256]{1,0:T(8,128)(2,1)} %own.5) | copy-start | bytes 6291460
  8.8 3.6 %copy-start.9 = (s32[128]{0:T(128)S(1)}, s32[128]{0:T(128)}, u32[]{:S(2)}) copy-start(s32[128]{0:T(128)} %picks.1) | copy-start | bytes 1540
  12.4 16.9 %copy-start.5 = (bf16[256,256]{1,0:T(8,128)(2,1)S(1)}, bf16[256,256]{1,0:T(8,128)(2,1)}, u32[]{:S(2)}) copy-start(bf16[256,256]{1,0:T(8,128)(2,1)} %refs_7_.3) | copy-start | bytes 393220
  12.4 16.9 %copy-start.8 = (f32[256]{0:T(256)S(1)}, f32[256]{0:T(256)}, u32[]{:S(2)}) copy-start(f32[256]{0:T(256)} %param.26) | copy-start | bytes 3076
  12.4 17.0 %copy-start.1 = (bf16[4096,256]{1,0:T(8,128)(2,1)S(1)}, bf16[4096,256]{1,0:T(8,128)(2,1)}, u32[]{:S(2)}) copy-start(bf16[4096,256]{1,0:T(8,128)(2,1)} %own.5) | copy-start | bytes 6291460
  12.4 17.0 %copy-start.2 = (bf16[256,256]{1,0:T(8,128)(2,1)S(1)}, bf16[256,256]{1,0:T(8,128)(2,1)}, u32[]{:S(2)}) copy-start(bf16[256,256]{1,0:T(8,128)(2,1)} %sw.5) | copy-start | bytes 393220
  12.4 17.0 %copy-start.3 = (bf16[256,256]{1,0:T(8,128)(2,1)S(1)}, bf16[256,256]{1,0:T(8,128)(2,1)}, u32[]{:S(2)}) copy-start(bf16[256,256]{1,0:T(8,128)(2,1)} %nw.5) | copy-start | bytes 393220
  12.4 17.0 %copy-start.6 = (f32[256]{0:T(256)S(1)}, f32[256]{0:T(256)}, u32[]{:S(2)}) copy-start(f32[256]{0:T(256)} %param.18) | copy-start | bytes 3076
  15.9 22.2 %all-to-all-start = ((bf16[32,8,128]{2,1,0:T(8,128)(2,1)}), bf16[32,8,128]{2,1,0:T(8,128)(2,1)S(1)}, u32[]{:S(2)}, u32[]{:S(2)}) async-start(bf16[32,8,128]{2,1,0:T(8,128)(2,1)} %get-tuple-element.30), calls=%async_computation | async-start | bytes 131072 | tf_op jit(solution)/shard_map/all_to_all | solution.py:596
  29.4 13.7 %copy-start.4 = (bf16[256,256]{1,0:T(8,128)(2,1)S(1)}, bf16[256,256]{1,0:T(8,128)(2,1)}, u32[]{:S(2)}) copy-start(bf16[256,256]{1,0:T(8,128)(2,1)} %refs_3_.7) | copy-start | bytes 393220
  29.5 13.6 %copy-start.10 = (s32[16,1024]{1,0:T(8,128)S(1)}, s32[16,1024]{1,0:T(8,128)}, u32[]{:S(2)}) copy-start(s32[16,1024]{1,0:T(8,128)} %refs_3_.6) | copy-start | bytes 196612
  29.5 13.6 %copy-start.11 = (bf16[128,256]{1,0:T(8,128)(2,1)S(1)}, bf16[128,256]{1,0:T(8,128)(2,1)}, u32[]{:S(2)}) copy-start(bf16[128,256]{1,0:T(8,128)(2,1)} %refs_6_.5) | copy-start | bytes 196612
  29.5 13.6 %copy-start.12 = (f32[256]{0:T(256)S(1)}, f32[256]{0:T(256)}, u32[]{:S(2)}) copy-start(f32[256]{0:T(256)} %param.23) | copy-start | bytes 3076
  29.5 13.6 %copy-start.13 = (f32[256]{0:T(256)S(1)}, f32[256]{0:T(256)}, u32[]{:S(2)}) copy-start(f32[256]{0:T(256)} %param.25) | copy-start | bytes 3076
  38.1 5.0 %collective-permute-start.5 = (bf16[32,8,128]{2,1,0:T(8,128)(2,1)S(1)}, bf16[32,8,128]{2,1,0:T(8,128)(2,1)}, u32[]{:S(2)}, u32[]{:S(2)}) collective-permute-start(bf16[32,8,128]{2,1,0:T(8,128)(2,1)S(1)} %all-to-all-done.refs_0_), channel_id=1, source_target_pairs={{0,32},{32,0},{64,96},{96,64},{128,160},{160,128},{192,224},{224,1... | collective-permute-start | bytes 196616 | tf_op jit(solution)/shard_map/ppermute | solution.py:619
  38.1 9.8 %collective-permute-start.2 = (bf16[32,8,128]{2,1,0:T(8,128)(2,1)S(1)}, bf16[32,8,128]{2,1,0:T(8,128)(2,1)S(1)}, u32[]{:S(2)}, u32[]{:S(2)}) collective-permute-start(bf16[32,8,128]{2,1,0:T(8,128)(2,1)S(1)} %all-to-all-done.refs_0_), channel_id=1, source_target_pairs={{0,64},{32,96},{64,0},{96,32},{128,192},{160,224},{192,128},{224,1... | collective-permute-start | bytes 196616 | tf_op jit(solution)/shard_map/ppermute | solution.py:594
  39.9 8.1 %collective-permute-start.3 = (bf16[32,8,128]{2,1,0:T(8,128)(2,1)S(1)}, bf16[32,8,128]{2,1,0:T(8,128)(2,1)S(1)}, u32[]{:S(2)}, u32[]{:S(2)}) collective-permute-start(bf16[32,8,128]{2,1,0:T(8,128)(2,1)S(1)} %all-to-all-done.refs_0_), channel_id=1, source_target_pairs={{0,128},{32,160},{64,192},{96,224},{128,0},{160,32},{192,64},{224,... | collective-permute-start | bytes 196616 | tf_op jit(solution)/shard_map/ppermute | solution.py:594
  43.1 5.5 %collective-permute-start.4 = (bf16[32,8,128]{2,1,0:T(8,128)(2,1)S(1)}, bf16[32,8,128]{2,1,0:T(8,128)(2,1)S(1)}, u32[]{:S(2)}, u32[]{:S(2)}) collective-permute-start(bf16[32,8,128]{2,1,0:T(8,128)(2,1)S(1)} %all-to-all-done.refs_0_), channel_id=1, source_target_pairs={{0,192},{32,224},{64,128},{96,160},{128,64},{160,96},{192,0},{224,... | collective-permute-start | bytes 196616 | tf_op jit(solution)/shard_map/ppermute | solution.py:594
  48.6 5.8 %collective-permute-start.6 = (bf16[32,8,128]{2,1,0:T(8,128)(2,1)S(1)}, bf16[32,8,128]{2,1,0:T(8,128)(2,1)S(1)}, u32[]{:S(2)}, u32[]{:S(2)}) collective-permute-start(bf16[32,8,128]{2,1,0:T(8,128)(2,1)S(1)} %collective-permute-done.2.refs_0_), channel_id=1, source_target_pairs={{0,32},{32,0},{64,96},{96,64},{128,160},{160,128},{192,224},{224,1... | collective-permute-start | bytes 196616 | tf_op jit(solution)/shard_map/ppermute | solution.py:622
  48.6 5.8 %collective-permute-start.7 = (bf16[32,8,128]{2,1,0:T(8,128)(2,1)S(1)}, bf16[32,8,128]{2,1,0:T(8,128)(2,1)S(1)}, u32[]{:S(2)}, u32[]{:S(2)}) collective-permute-start(bf16[32,8,128]{2,1,0:T(8,128)(2,1)S(1)} %collective-permute-done.3.refs_1_), channel_id=1, source_target_pairs={{0,32},{32,0},{64,96},{96,64},{128,160},{160,128},{192,224},{224,1... | collective-permute-start | bytes 196616 | tf_op jit(solution)/shard_map/ppermute | solution.py:622
  49.1 5.3 %collective-permute-start.8 = (bf16[32,8,128]{2,1,0:T(8,128)(2,1)S(1)}, bf16[32,8,128]{2,1,0:T(8,128)(2,1)S(1)}, u32[]{:S(2)}, u32[]{:S(2)}) collective-permute-start(bf16[32,8,128]{2,1,0:T(8,128)(2,1)S(1)} %collective-permute-done.4.refs_2_), channel_id=1, source_target_pairs={{0,32},{32,0},{64,96},{96,64},{128,160},{160,128},{192,224},{224,1... | collective-permute-start | bytes 196616 | tf_op jit(solution)/shard_map/ppermute | solution.py:622
  60.5 21.5 %all-to-all-start.1 = ((f32[256,1,128]{2,1,0:T(1,128)}), f32[256,1,128]{2,1,0:T(1,128)S(1)}, u32[]{:S(2)}, u32[]{:S(2)}) async-start(f32[256,1,128]{2,1,0:T(1,128)} %bitcast.14), calls=%async_computation.1 | async-start | bytes 262144 | tf_op jit(solution)/shard_map/all_to_all | solution.py:628
  70.6 11.4 %copy-start.7 = (s32[512,2]{0,1:T(2,128)S(1)}, s32[512,2]{0,1:T(2,128)}, u32[]{:S(2)}) copy-start(s32[512,2]{0,1:T(2,128)} %param.27) | copy-start | bytes 12292
  84.7 2.7 %collective-permute-start.9 = (bf16[4,128,256]{2,1,0:T(8,128)(2,1)S(1)}, bf16[4,128,256]{2,1,0:T(8,128)(2,1)S(1)}, u32[]{:S(2)}, u32[]{:S(2)}) collective-permute-start(bf16[4,128,256]{2,1,0:T(8,128)(2,1)S(1)} %get-tuple-element.52), channel_id=1, source_target_pairs={{0,32},{32,0},{64,96},{96,64},{128,160},{160,128},{192,224},{224,1... | collective-permute-start | bytes 786440 | tf_op jit(solution)/shard_map/ppermute | solution.py:634
  87.5 4.8 %collective-permute-start.10 = (bf16[128,256]{1,0:T(8,128)(2,1)S(1)}, bf16[128,256]{1,0:T(8,128)(2,1)S(1)}, u32[]{:S(2)}, u32[]{:S(2)}) collective-permute-start(bf16[128,256]{1,0:T(8,128)(2,1)S(1)} %get-tuple-element.61), channel_id=1, source_target_pairs={{0,64},{32,96},{64,0},{96,32},{128,192},{160,224},{192,128},{224,1... | collective-permute-start | bytes 196616 | tf_op jit(solution)/shard_map/ppermute | solution.py:594
  88.2 5.8 %collective-permute-start.11 = (bf16[128,256]{1,0:T(8,128)(2,1)S(1)}, bf16[128,256]{1,0:T(8,128)(2,1)S(1)}, u32[]{:S(2)}, u32[]{:S(2)}) collective-permute-start(bf16[128,256]{1,0:T(8,128)(2,1)S(1)} %get-tuple-element.60), channel_id=1, source_target_pairs={{0,128},{32,160},{64,192},{96,224},{128,0},{160,32},{192,64},{224,... | collective-permute-start | bytes 196616 | tf_op jit(solution)/shard_map/ppermute | solution.py:594
  90.0 5.5 %collective-permute-start.12 = (bf16[128,256]{1,0:T(8,128)(2,1)S(1)}, bf16[128,256]{1,0:T(8,128)(2,1)S(1)}, u32[]{:S(2)}, u32[]{:S(2)}) collective-permute-start(bf16[128,256]{1,0:T(8,128)(2,1)S(1)} %get-tuple-element.59), channel_id=1, source_target_pairs={{0,192},{32,224},{64,128},{96,160},{128,64},{160,96},{192,0},{224,... | collective-permute-start | bytes 196616 | tf_op jit(solution)/shard_map/ppermute | solution.py:594
  96.3 18.0 %all-to-all-start.2 = ((bf16[32,8,128]{2,1,0:T(8,128)(2,1)}), bf16[32,8,128]{2,1,0:T(8,128)(2,1)S(1)}, u32[]{:S(2)}, u32[]{:S(2)}) async-start(bf16[32,8,128]{2,1,0:T(8,128)(2,1)} %finish.1), calls=%async_computation.2 | async-start | bytes 131072 | tf_op jit(solution)/shard_map/all_to_all | solution.py:639

commit v9 on v8

--- a/solution.py
+++ b/solution.py
@@ -178,27 +178,38 @@
             put_rows(table, HALO + start, feats.at[start : start + 512, :])
 
     acc3 = acc.reshape(tile, 2, 128)
-
-    def body(block, carry):
+    some = 128
+
+    part = 32
+
+    def gather(block, first):
         values = []
-        for j in range(128):
+        for j in range(first, first + part):
             near = [pair_at(table, nbrs[block * 512 + (128 * k + j)]) for k in range(4)]
             values.append((near[0] + near[1]) + (near[2] + near[3]))
-        for j in range(128):
-            acc3[block * 128 + j] = values[j]
-        return carry
-
-    lax.fori_loop(0, tile // 128, body, 0)
-    rows = own[...]
-    out[...] = layer_rows(
-        rows[:, :128],
-        rows[:, 128:],
-        (acc[pl.ds(0, tile, stride=2), :] * 0.25).astype(bf16),
-        (acc[pl.ds(1, tile, stride=2), :] * 0.25).astype(bf16),
-        sw,
-        nw,
-        bias,
-    )
+        for j, value in enumerate(values, first):
+            acc3[block * some + j] = value
+
+    def products(block):
+        start = block * some
+        sides = [
+            (acc[pl.ds(2 * start + side, some, stride=2), :] * 0.25).astype(bf16)
+            for side in (0, 1)
+        ]
+        pre = jnp.dot(own[start : start + some, :], sw[...], preferred_element_type=f32)
+        pre += jnp.dot(sides[0], nw[:128, :], preferred_element_type=f32)
+        return pre + jnp.dot(sides[1], nw[128:, :], preferred_element_type=f32)
+
+    blocks = tile // some
+    for block in range(blocks + 1):
+        pre = products(block - 1) if block > 0 else None
+        for first in range(0, some, part):
+            if block < blocks:
+                gather(block, first)
+            if block > 0:
+                start = (block - 1) * some + first
+                half = 0.5 * (pre[first : first + part, :] + bias[...])
+                out[start : start + part, :] = half_silu(half)[0].astype(bf16)
 
 
 def layer_of(first, steps, flip, nbrs, inner, outer, feats, sw, nw, bias, given):

time: 115 us -> 115 us (level)
  transfers between devices with their start and end apart: 16 -> 16, of which waited for: 8 -> 8; matrix products, arithmetic and copies ran while one was open for 1% -> 1% of each run, Pallas kernels for 31% -> 30%
where the time goes in v9:
time: 115 us; the launch traced here: 114 us
  Pallas kernels  47.8 us (42%)
  starting transfers between devices  47.3 us (41%)
  waiting for transfers between devices  14.6 us (13%)
  local copies, waits for them, and re-layouts  2.73 us (2%)
    pallas_call x3, Pallas kernels, layer_of(): pl.pallas_call(layer_kernel, out_shape=jax.ShapeDtypeStruct((nodes, width...  21 us
    pallas_call x3, Pallas kernels, scorer_of(): pl.pallas_call(functools.partial(scorer_kernel, groups, final), out_shape...  16.1 us
    all_to_all x1, starting transfers between devices, shards(): mine = lax.all_to_all(conf_src, 'node', 0, 0, tiled=True)  13.3 us
    all_to_all x1, starting transfers between devices, shards(): got = lax.all_to_all(sent.reshape(devices, 1, 128), both, 0, 0, tiled=True)  9.82 us
    ppermute x6, starting transfers between devices, shift(): lax.ppermute(value, 'cfg', [(i, i ^ 2 * by) for i in range(group_count)])  9.79 us
    all_to_all x1, starting transfers between devices, shards(): conf_grad = lax.all_to_all(local_grad, 'node', 0, 0, tiled=True)  8.91 us
    ppermute x2, starting transfers between devices, trade(): return lax.ppermute(rows, both, pairs)  4.67 us
    ppermute x6, waiting for transfers between devices, shift(): lax.ppermute(value, 'cfg', [(i, i ^ 2 * by) for i in range(group_count)])  3.77 us
  transfers between devices with their start and end apart: 16, of which 8 were waited for; matrix products, arithmetic and copies ran while one was open for 1% of the time, Pallas kernels for 30%

profile of v9, /device:TPU:2, one launch (start us, length us, event | category | flops | bytes accessed | tf_op | source)
XLA Modules:
  0.0 114.3 jit_solution(8831856330261006856)
XLA Ops:
  0.6 1.1 constant_dynamic-slice_fusion
  1.7 2.4 %collective-permute-start = (bf16[512,256]{1,0:T(8,128)(2,1)S(1)}, bf16[512,256]{1,0:T(8,128)(2,1)S(1)}, u32[]{:S(2)}, u32[]{:S(2)}) collective-permute-start(bf16[512,256]{1,0:T(8,128)(2,1)S(1)} %get-tuple-element.58), channel_id=1, source_target_pairs={{0,1},{1,0},{2,3},{3,2},{4,5},{5,4},{6,7},{7,6},{8,9},{9,8},{10,11... | collective-permute-start | bytes 786440 | tf_op jit(solution)/shard_map/ppermute | solution.py:563
  4.1 2.3 %collective-permute-start.1 = (bf16[512,256]{1,0:T(8,128)(2,1)S(1)}, bf16[512,256]{1,0:T(8,128)(2,1)S(1)}, u32[]{:S(2)}, u32[]{:S(2)}) collective-permute-start(bf16[512,256]{1,0:T(8,128)(2,1)S(1)} %get-tuple-element.57), channel_id=1, source_target_pairs={{1,2},{2,1},{3,4},{4,3},{5,6},{6,5},{7,8},{8,7},{9,10},{10,9},{11,... | collective-permute-start | bytes 786440 | tf_op jit(solution)/shard_map/ppermute | solution.py:563
  6.4 0.9 broadcast_multiply_fusion
  7.2 0.0 copy-start
  7.3 1.6 %copy-done = bf16[4096,256]{1,0:T(8,128)(2,1)S(1)} copy-done((bf16[4096,256]{1,0:T(8,128)(2,1)S(1)}, bf16[4096,256]{1,0:T(8,128)(2,1)}, u32[]{:S(2)}) %copy-start) | copy-done | bytes 2097176
  8.8 0.4 window_rows.1.refs_3_
  9.2 0.6 collective-permute-done.inner
  9.8 2.6 %collective-permute-done.1.outer = bf16[512,256]{1,0:T(8,128)(2,1)S(1)} collective-permute-done((bf16[512,256]{1,0:T(8,128)(2,1)S(1)}, bf16[512,256]{1,0:T(8,128)(2,1)S(1)}, u32[]{:S(2)}, u32[]{:S(2)}) %collective-permute-start.1) | collective-permute-done | bytes 262176 | tf_op jit(solution)/shard_map/ppermute | solution.py:563
  12.4 0.0 copy-start.2
  12.4 0.0 copy-start.3
  12.4 0.0 copy-start.6
  12.4 3.5 %conf_rows.1 = (bf16[32,8,128]{2,1,0:T(8,128)(2,1)}, f32[10240,128]{1,0:T(8,128)S(1)}) custom-call(s32[1]{0:T(128)} %bitcast.flip, s32[16384]{0:T(1024)S(1)} %bitcast.25, s32[128]{0:T(128)S(1)} %copy-done.9, bf16[512,256]{1,0:T(8,128)(2,1)S(1)} %collective-permute-done.1.outer, ...), custom_call_target="tpu_custom_call", output_to_operand_aliasing={{1}: (8, {})} | custom-call | flops 33554432 | bytes 6291456 | tf_op jit(solution)/shard_map/conf_rows/pallas_call | solution.py:144
  15.9 13.3 %all-to-all-start = ((bf16[32,8,128]{2,1,0:T(8,128)(2,1)}), bf16[32,8,128]{2,1,0:T(8,128)(2,1)S(1)}, u32[]{:S(2)}, u32[]{:S(2)}) async-start(bf16[32,8,128]{2,1,0:T(8,128)(2,1)} %get-tuple-element.30), calls=%async_computation | async-start | bytes 131072 | tf_op jit(solution)/shard_map/all_to_all | solution.py:607
  29.3 0.1 prepare.1.refs_7_.refs_8_
  29.4 0.0 copy-start.4
  29.5 0.0 copy-start.10
  29.5 0.0 copy-start.11
  29.5 0.0 copy-start.12
  29.5 0.0 copy-start.13
  29.5 5.7 %graph_layer.3.refs_0_ = bf16[4096,256]{1,0:T(8,128)(2,1)} custom-call(s32[1]{0:T(128)} %bitcast.flip, s32[16384]{0:T(1024)S(1)} %bitcast.26, bf16[512,256]{1,0:T(8,128)(2,1)S(1)} %collective-permute-done.inner, bf16[512,256]{1,0:T(8,128)(2,1)S(1)} %collective-permute-done.1.outer, bf16[4096,256]{1,0:T(8,128)(2,1)S(1)} %copy-done.1, ...), custom_call_target="tpu_custom_call" | custom-call | flops 268435456 | bytes 16777216 | tf_op jit(solution)/shard_map/graph_layer/pallas_call | solution.py:219
  35.2 2.9 %all-to-all-done.refs_0_ = bf16[32,8,128]{2,1,0:T(8,128)(2,1)S(1)} async-done(((bf16[32,8,128]{2,1,0:T(8,128)(2,1)}), bf16[32,8,128]{2,1,0:T(8,128)(2,1)S(1)}, u32[]{:S(2)}, u32[]{:S(2)}) %all-to-all-start) | async-done | bytes 65568 | tf_op jit(solution)/shard_map/all_to_all | solution.py:607
  38.1 1.8 %collective-permute-start.2 = (bf16[32,8,128]{2,1,0:T(8,128)(2,1)S(1)}, bf16[32,8,128]{2,1,0:T(8,128)(2,1)S(1)}, u32[]{:S(2)}, u32[]{:S(2)}) collective-permute-start(bf16[32,8,128]{2,1,0:T(8,128)(2,1)S(1)} %all-to-all-done.refs_0_), channel_id=1, source_target_pairs={{0,64},{32,96},{64,0},{96,32},{128,192},{160,224},{192,128},{224,1... | collective-permute-start | bytes 196616 | tf_op jit(solution)/shard_map/ppermute | solution.py:605
  39.9 3.2 %collective-permute-start.3 = (bf16[32,8,128]{2,1,0:T(8,128)(2,1)S(1)}, bf16[32,8,128]{2,1,0:T(8,128)(2,1)S(1)}, u32[]{:S(2)}, u32[]{:S(2)}) collective-permute-start(bf16[32,8,128]{2,1,0:T(8,128)(2,1)S(1)} %all-to-all-done.refs_0_), channel_id=1, source_target_pairs={{0,128},{32,160},{64,192},{96,224},{128,0},{160,32},{192,64},{224,... | collective-permute-start | bytes 196616 | tf_op jit(solution)/shard_map/ppermute | solution.py:605
  43.1 0.0 collective-permute-start.4
  43.1 4.8 %scorer.3 = (bf16[2,16,128,256]{3,2,1,0:T(8,128)(2,1)}, f32[16,256]{1,0:T(8,128)S(1)}) custom-call(s32[1]{0:T(128)} %bitcast.6.where, bf16[32,8,128]{2,1,0:T(8,128)(2,1)S(1)} %all-to-all-done.refs_0_, bf16[32,8,128]{2,1,0:T(8,128)(2,1)} %collective-permute-done.5.refs_1_, s32[16,1024]{1,0:T(8,128)S(1)} %copy-done.10, bf16[256,256]{1,0:T(8,128)(2,1)S(1)} %copy-done.4, ...), custom_call_target="tpu_custom_call" | custom-call | flops 1610612736 | bytes 2097152 | tf_op jit(solution)/shard_map/scorer/pallas_call | solution.py:363
  47.9 0.6 collective-permute-done.4.refs_2_
  48.6 0.5 collective-permute-start.7
  49.1 0.0 collective-permute-start.8
  49.1 5.3 %scorer.4 = (bf16[3,16,128,256]{3,2,1,0:T(8,128)(2,1)}, f32[16,256]{1,0:T(8,128)S(1)}) custom-call(s32[1]{0:T(128)} %bitcast.6.where, bf16[32,8,128]{2,1,0:T(8,128)(2,1)S(1)} %collective-permute-done.2.refs_0_, bf16[32,8,128]{2,1,0:T(8,128)(2,1)S(1)} %collective-permute-done.3.refs_1_, bf16[32,8,128]{2,1,0:T(8,128)(2,1)S(1)} %collective-permute-done.4.refs_2_, ...), custom_call_target="tpu_custom_call" | custom-call | flops 2415919104 | bytes 3145728 | tf_op jit(solution)/shard_map/scorer/pallas_call | solution.py:363
  54.4 6.0 %scorer.5 = (bf16[3,16,128,256]{3,2,1,0:T(8,128)(2,1)}, f32[256,128]{1,0:T(8,128)}) custom-call(s32[1]{0:T(128)} %bitcast.6.where, bf16[32,8,128]{2,1,0:T(8,128)(2,1)S(1)} %collective-permute-done.6.refs_0_, bf16[32,8,128]{2,1,0:T(8,128)(2,1)S(1)} %collective-permute-done.7.refs_1_, bf16[32,8,128]{2,1,0:T(8,128)(2,1)S(1)} %collective-permute-done.8.refs_2_, ...), custom_call_target="tpu_custom_call" | custom-call | flops 2415919104 | bytes 3145728 | tf_op jit(solution)/shard_map/scorer/pallas_call | solution.py:363
  60.5 9.8 %all-to-all-start.1 = ((f32[256,1,128]{2,1,0:T(1,128)}), f32[256,1,128]{2,1,0:T(1,128)S(1)}, u32[]{:S(2)}, u32[]{:S(2)}) async-start(f32[256,1,128]{2,1,0:T(1,128)} %bitcast.14), calls=%async_computation.1 | async-start | bytes 262144 | tf_op jit(solution)/shard_map/all_to_all | solution.py:639
  70.3 0.0 copy-start.7
  70.3 7.7 %graph_layer.4.refs_0_ = bf16[4096,256]{1,0:T(8,128)(2,1)} custom-call(s32[1]{0:T(128)} %bitcast.flip, s32[16384]{0:T(1024)S(1)} %bitcast.27, bf16[512,256]{1,0:T(8,128)(2,1)S(1)} %collective-permute-done.inner, bf16[512,256]{1,0:T(8,128)(2,1)S(1)} %collective-permute-done.1.outer, bf16[4096,256]{1,0:T(8,128)(2,1)S(1)} %copy-done.1, ...), custom_call_target="tpu_custom_call", output_to_operand_aliasing={{}: (9, {})} | custom-call | flops 402653184 | bytes 25165824 | tf_op jit(solution)/shard_map/graph_layer/pallas_call | solution.py:219
  78.0 3.7 %all-to-all-done.1 = f32[256,1,128]{2,1,0:T(1,128)S(1)} async-done(((f32[256,1,128]{2,1,0:T(1,128)}), f32[256,1,128]{2,1,0:T(1,128)S(1)}, u32[]{:S(2)}, u32[]{:S(2)}) %all-to-all-start.1) | async-done | bytes 131104 | tf_op jit(solution)/shard_map/all_to_all | solution.py:639
  81.7 2.7 %ranking.1 = (f32[1,1]{1,0:T(1,128)}, f32[16,256]{1,0:T(8,128)S(1)}, bf16[4,128,256]{2,1,0:T(8,128)(2,1)S(1)}) custom-call(s32[1]{0:T(128)} %bitcast.6.where, f32[256,128]{1,0:T(8,128)S(1)} %bitcast.29, s32[2,512]{1,0:T(2,128)S(1)} %bitcast.34, bf16[2,16,128,256]{3,2,1,0:T(8,128)(2,1)} %get-tuple-element.48.pair, ...), custom_call_target="tpu_custom_call" | custom-call | flops 16777216 | bytes 6291456 | tf_op jit(solution)/shard_map/ranking/pallas_call | solution.py:445
  84.5 0.3 collective-permute-start.9
  84.8 2.4 %rest.1.kept = bf16[4,128,256]{2,1,0:T(8,128)(2,1)S(1)} custom-call(f32[16,256]{1,0:T(8,128)S(1)} %get-tuple-element.50.coef, bf16[2,16,128,256]{3,2,1,0:T(8,128)(2,1)} %get-tuple-element.48.pair, bf16[3,16,128,256]{3,2,1,0:T(8,128)(2,1)} %get-tuple-element.51.later), custom_call_target="tpu_custom_call" | custom-call | flops 16777216 | bytes 6291456 | tf_op jit(solution)/shard_map/rest/pallas_call | solution.py:477
  87.3 0.7 collective-permute-start.10
  87.9 1.8 %collective-permute-start.11 = (bf16[128,256]{1,0:T(8,128)(2,1)S(1)}, bf16[128,256]{1,0:T(8,128)(2,1)S(1)}, u32[]{:S(2)}, u32[]{:S(2)}) collective-permute-start(bf16[128,256]{1,0:T(8,128)(2,1)S(1)} %get-tuple-element.60), channel_id=1, source_target_pairs={{0,128},{32,160},{64,192},{96,224},{128,0},{160,32},{192,64},{224,... | collective-permute-start | bytes 196616 | tf_op jit(solution)/shard_map/ppermute | solution.py:605
  89.7 2.3 %collective-permute-start.12 = (bf16[128,256]{1,0:T(8,128)(2,1)S(1)}, bf16[128,256]{1,0:T(8,128)(2,1)S(1)}, u32[]{:S(2)}, u32[]{:S(2)}) collective-permute-start(bf16[128,256]{1,0:T(8,128)(2,1)S(1)} %get-tuple-element.59), channel_id=1, source_target_pairs={{0,192},{32,224},{64,128},{96,160},{128,64},{160,96},{192,0},{224,... | collective-permute-start | bytes 196616 | tf_op jit(solution)/shard_map/ppermute | solution.py:605
  92.0 1.7 %collective-permute-done.11.refs_1_ = bf16[128,256]{1,0:T(8,128)(2,1)S(1)} collective-permute-done((bf16[128,256]{1,0:T(8,128)(2,1)S(1)}, bf16[128,256]{1,0:T(8,128)(2,1)S(1)}, u32[]{:S(2)}, u32[]{:S(2)}) %collective-permute-start.11) | collective-permute-done | bytes 65568 | tf_op jit(solution)/shard_map/ppermute | solution.py:605
  93.7 1.5 %collective-permute-done.12.refs_2_ = bf16[128,256]{1,0:T(8,128)(2,1)S(1)} collective-permute-done((bf16[128,256]{1,0:T(8,128)(2,1)S(1)}, bf16[128,256]{1,0:T(8,128)(2,1)S(1)}, u32[]{:S(2)}, u32[]{:S(2)}) %collective-permute-start.12) | collective-permute-done | bytes 65568 | tf_op jit(solution)/shard_map/ppermute | solution.py:605
  95.2 0.8 finish.1
  96.0 8.9 %all-to-all-start.2 = ((bf16[32,8,128]{2,1,0:T(8,128)(2,1)}), bf16[32,8,128]{2,1,0:T(8,128)(2,1)S(1)}, u32[]{:S(2)}, u32[]{:S(2)}) async-start(bf16[32,8,128]{2,1,0:T(8,128)(2,1)} %finish.1), calls=%async_computation.2 | async-start | bytes 131072 | tf_op jit(solution)/shard_map/all_to_all | solution.py:650
  104.9 7.7 %graph_layer.5 = bf16[4096,256]{1,0:T(8,128)(2,1)} custom-call(s32[1]{0:T(128)} %bitcast.flip, s32[16384]{0:T(1024)S(1)} %bitcast.28, bf16[512,256]{1,0:T(8,128)(2,1)S(1)} %collective-permute-done.inner, bf16[512,256]{1,0:T(8,128)(2,1)S(1)} %collective-permute-done.1.outer, bf16[4096,256]{1,0:T(8,128)(2,1)S(1)} %copy-done.1, ...), custom_call_target="tpu_custom_call", output_to_operand_aliasing={{}: (9, {})} | custom-call | flops 402653184 | bytes 25165824 | tf_op jit(solution)/shard_map/graph_layer/pallas_call | solution.py:219
  112.6 1.0 all-to-all-done.2.value
  113.6 0.7 returned.1
  (28 shorter events, 0.1 us)
Async XLA Ops:
  1.7 8.1 %collective-permute-start = (bf16[512,256]{1,0:T(8,128)(2,1)S(1)}, bf16[512,256]{1,0:T(8,128)(2,1)S(1)}, u32[]{:S(2)}, u32[]{:S(2)}) collective-permute-start(bf16[512,256]{1,0:T(8,128)(2,1)S(1)} %get-tuple-element.58), channel_id=1, source_target_pairs={{0,1},{1,0},{2,3},{3,2},{4,5},{5,4},{6,7},{7,6},{8,9},{9,8},{10,11... | collective-permute-start | bytes 786440 | tf_op jit(solution)/shard_map/ppermute | solution.py:563
  4.1 8.3 %collective-permute-start.1 = (bf16[512,256]{1,0:T(8,128)(2,1)S(1)}, bf16[512,256]{1,0:T(8,128)(2,1)S(1)}, u32[]{:S(2)}, u32[]{:S(2)}) collective-permute-start(bf16[512,256]{1,0:T(8,128)(2,1)S(1)} %get-tuple-element.57), channel_id=1, source_target_pairs={{1,2},{2,1},{3,4},{4,3},{5,6},{6,5},{7,8},{8,7},{9,10},{10,9},{11,... | collective-permute-start | bytes 786440 | tf_op jit(solution)/shard_map/ppermute | solution.py:563
  7.2 1.6 %copy-start = (bf16[4096,256]{1,0:T(8,128)(2,1)S(1)}, bf16[4096,256]{1,0:T(8,128)(2,1)}, u32[]{:S(2)}) copy-start(bf16[4096,256]{1,0:T(8,128)(2,1)} %own.5) | copy-start | bytes 6291460
  8.8 3.6 %copy-start.9 = (s32[128]{0:T(128)S(1)}, s32[128]{0:T(128)}, u32[]{:S(2)}) copy-start(s32[128]{0:T(128)} %picks.1) | copy-start | bytes 1540
  12.4 16.9 %copy-start.5 = (bf16[256,256]{1,0:T(8,128)(2,1)S(1)}, bf16[256,256]{1,0:T(8,128)(2,1)}, u32[]{:S(2)}) copy-start(bf16[256,256]{1,0:T(8,128)(2,1)} %refs_7_.3) | copy-start | bytes 393220
  12.4 16.9 %copy-start.8 = (f32[256]{0:T(256)S(1)}, f32[256]{0:T(256)}, u32[]{:S(2)}) copy-start(f32[256]{0:T(256)} %param.26) | copy-start | bytes 3076
  12.4 17.0 %copy-start.1 = (bf16[4096,256]{1,0:T(8,128)(2,1)S(1)}, bf16[4096,256]{1,0:T(8,128)(2,1)}, u32[]{:S(2)}) copy-start(bf16[4096,256]{1,0:T(8,128)(2,1)} %own.5) | copy-start | bytes 6291460
  12.4 17.0 %copy-start.2 = (bf16[256,256]{1,0:T(8,128)(2,1)S(1)}, bf16[256,256]{1,0:T(8,128)(2,1)}, u32[]{:S(2)}) copy-start(bf16[256,256]{1,0:T(8,128)(2,1)} %sw.5) | copy-start | bytes 393220
  12.4 17.0 %copy-start.3 = (bf16[256,256]{1,0:T(8,128)(2,1)S(1)}, bf16[256,256]{1,0:T(8,128)(2,1)}, u32[]{:S(2)}) copy-start(bf16[256,256]{1,0:T(8,128)(2,1)} %nw.5) | copy-start | bytes 393220
  12.4 17.0 %copy-start.6 = (f32[256]{0:T(256)S(1)}, f32[256]{0:T(256)}, u32[]{:S(2)}) copy-start(f32[256]{0:T(256)} %param.18) | copy-start | bytes 3076
  15.9 22.2 %all-to-all-start = ((bf16[32,8,128]{2,1,0:T(8,128)(2,1)}), bf16[32,8,128]{2,1,0:T(8,128)(2,1)S(1)}, u32[]{:S(2)}, u32[]{:S(2)}) async-start(bf16[32,8,128]{2,1,0:T(8,128)(2,1)} %get-tuple-element.30), calls=%async_computation | async-start | bytes 131072 | tf_op jit(solution)/shard_map/all_to_all | solution.py:607
  29.4 13.7 %copy-start.4 = (bf16[256,256]{1,0:T(8,128)(2,1)S(1)}, bf16[256,256]{1,0:T(8,128)(2,1)}, u32[]{:S(2)}) copy-start(bf16[256,256]{1,0:T(8,128)(2,1)} %refs_3_.7) | copy-start | bytes 393220
  29.5 13.6 %copy-start.10 = (s32[16,1024]{1,0:T(8,128)S(1)}, s32[16,1024]{1,0:T(8,128)}, u32[]{:S(2)}) copy-start(s32[16,1024]{1,0:T(8,128)} %refs_3_.6) | copy-start | bytes 196612
  29.5 13.6 %copy-start.11 = (bf16[128,256]{1,0:T(8,128)(2,1)S(1)}, bf16[128,256]{1,0:T(8,128)(2,1)}, u32[]{:S(2)}) copy-start(bf16[128,256]{1,0:T(8,128)(2,1)} %refs_6_.5) | copy-start | bytes 196612
  29.5 13.6 %copy-start.12 = (f32[256]{0:T(256)S(1)}, f32[256]{0:T(256)}, u32[]{:S(2)}) copy-start(f32[256]{0:T(256)} %param.23) | copy-start | bytes 3076
  29.5 13.6 %copy-start.13 = (f32[256]{0:T(256)S(1)}, f32[256]{0:T(256)}, u32[]{:S(2)}) copy-start(f32[256]{0:T(256)} %param.25) | copy-start | bytes 3076
  38.1 5.0 %collective-permute-start.5 = (bf16[32,8,128]{2,1,0:T(8,128)(2,1)S(1)}, bf16[32,8,128]{2,1,0:T(8,128)(2,1)}, u32[]{:S(2)}, u32[]{:S(2)}) collective-permute-start(bf16[32,8,128]{2,1,0:T(8,128)(2,1)S(1)} %all-to-all-done.refs_0_), channel_id=1, source_target_pairs={{0,32},{32,0},{64,96},{96,64},{128,160},{160,128},{192,224},{224,1... | collective-permute-start | bytes 196616 | tf_op jit(solution)/shard_map/ppermute | solution.py:630
  38.1 9.8 %collective-permute-start.2 = (bf16[32,8,128]{2,1,0:T(8,128)(2,1)S(1)}, bf16[32,8,128]{2,1,0:T(8,128)(2,1)S(1)}, u32[]{:S(2)}, u32[]{:S(2)}) collective-permute-start(bf16[32,8,128]{2,1,0:T(8,128)(2,1)S(1)} %all-to-all-done.refs_0_), channel_id=1, source_target_pairs={{0,64},{32,96},{64,0},{96,32},{128,192},{160,224},{192,128},{224,1... | collective-permute-start | bytes 196616 | tf_op jit(solution)/shard_map/ppermute | solution.py:605
  39.9 8.1 %collective-permute-start.3 = (bf16[32,8,128]{2,1,0:T(8,128)(2,1)S(1)}, bf16[32,8,128]{2,1,0:T(8,128)(2,1)S(1)}, u32[]{:S(2)}, u32[]{:S(2)}) collective-permute-start(bf16[32,8,128]{2,1,0:T(8,128)(2,1)S(1)} %all-to-all-done.refs_0_), channel_id=1, source_target_pairs={{0,128},{32,160},{64,192},{96,224},{128,0},{160,32},{192,64},{224,... | collective-permute-start | bytes 196616 | tf_op jit(solution)/shard_map/ppermute | solution.py:605
  43.1 5.5 %collective-permute-start.4 = (bf16[32,8,128]{2,1,0:T(8,128)(2,1)S(1)}, bf16[32,8,128]{2,1,0:T(8,128)(2,1)S(1)}, u32[]{:S(2)}, u32[]{:S(2)}) collective-permute-start(bf16[32,8,128]{2,1,0:T(8,128)(2,1)S(1)} %all-to-all-done.refs_0_), channel_id=1, source_target_pairs={{0,192},{32,224},{64,128},{96,160},{128,64},{160,96},{192,0},{224,... | collective-permute-start | bytes 196616 | tf_op jit(solution)/shard_map/ppermute | solution.py:605
  48.6 5.8 %collective-permute-start.6 = (bf16[32,8,128]{2,1,0:T(8,128)(2,1)S(1)}, bf16[32,8,128]{2,1,0:T(8,128)(2,1)S(1)}, u32[]{:S(2)}, u32[]{:S(2)}) collective-permute-start(bf16[32,8,128]{2,1,0:T(8,128)(2,1)S(1)} %collective-permute-done.2.refs_0_), channel_id=1, source_target_pairs={{0,32},{32,0},{64,96},{96,64},{128,160},{160,128},{192,224},{224,1... | collective-permute-start | bytes 196616 | tf_op jit(solution)/shard_map/ppermute | solution.py:633
  48.6 5.8 %collective-permute-start.7 = (bf16[32,8,128]{2,1,0:T(8,128)(2,1)S(1)}, bf16[32,8,128]{2,1,0:T(8,128)(2,1)S(1)}, u32[]{:S(2)}, u32[]{:S(2)}) collective-permute-start(bf16[32,8,128]{2,1,0:T(8,128)(2,1)S(1)} %collective-permute-done.3.refs_1_), channel_id=1, source_target_pairs={{0,32},{32,0},{64,96},{96,64},{128,160},{160,128},{192,224},{224,1... | collective-permute-start | bytes 196616 | tf_op jit(solution)/shard_map/ppermute | solution.py:633
  49.1 5.3 %collective-permute-start.8 = (bf16[32,8,128]{2,1,0:T(8,128)(2,1)S(1)}, bf16[32,8,128]{2,1,0:T(8,128)(2,1)S(1)}, u32[]{:S(2)}, u32[]{:S(2)}) collective-permute-start(bf16[32,8,128]{2,1,0:T(8,128)(2,1)S(1)} %collective-permute-done.4.refs_2_), channel_id=1, source_target_pairs={{0,32},{32,0},{64,96},{96,64},{128,160},{160,128},{192,224},{224,1... | collective-permute-start | bytes 196616 | tf_op jit(solution)/shard_map/ppermute | solution.py:633
  60.5 21.3 %all-to-all-start.1 = ((f32[256,1,128]{2,1,0:T(1,128)}), f32[256,1,128]{2,1,0:T(1,128)S(1)}, u32[]{:S(2)}, u32[]{:S(2)}) async-start(f32[256,1,128]{2,1,0:T(1,128)} %bitcast.14), calls=%async_computation.1 | async-start | bytes 262144 | tf_op jit(solution)/shard_map/all_to_all | solution.py:639
  70.3 11.4 %copy-start.7 = (s32[512,2]{0,1:T(2,128)S(1)}, s32[512,2]{0,1:T(2,128)}, u32[]{:S(2)}) copy-start(s32[512,2]{0,1:T(2,128)} %param.27) | copy-start | bytes 12292
  84.5 2.7 %collective-permute-start.9 = (bf16[4,128,256]{2,1,0:T(8,128)(2,1)S(1)}, bf16[4,128,256]{2,1,0:T(8,128)(2,1)S(1)}, u32[]{:S(2)}, u32[]{:S(2)}) collective-permute-start(bf16[4,128,256]{2,1,0:T(8,128)(2,1)S(1)} %get-tuple-element.52), channel_id=1, source_target_pairs={{0,32},{32,0},{64,96},{96,64},{128,160},{160,128},{192,224},{224,1... | collective-permute-start | bytes 786440 | tf_op jit(solution)/shard_map/ppermute | solution.py:645
  87.3 4.8 %collective-permute-start.10 = (bf16[128,256]{1,0:T(8,128)(2,1)S(1)}, bf16[128,256]{1,0:T(8,128)(2,1)S(1)}, u32[]{:S(2)}, u32[]{:S(2)}) collective-permute-start(bf16[128,256]{1,0:T(8,128)(2,1)S(1)} %get-tuple-element.61), channel_id=1, source_target_pairs={{0,64},{32,96},{64,0},{96,32},{128,192},{160,224},{192,128},{224,1... | collective-permute-start | bytes 196616 | tf_op jit(solution)/shard_map/ppermute | solution.py:605
  87.9 5.8 %collective-permute-start.11 = (bf16[128,256]{1,0:T(8,128)(2,1)S(1)}, bf16[128,256]{1,0:T(8,128)(2,1)S(1)}, u32[]{:S(2)}, u32[]{:S(2)}) collective-permute-start(bf16[128,256]{1,0:T(8,128)(2,1)S(1)} %get-tuple-element.60), channel_id=1, source_target_pairs={{0,128},{32,160},{64,192},{96,224},{128,0},{160,32},{192,64},{224,... | collective-permute-start | bytes 196616 | tf_op jit(solution)/shard_map/ppermute | solution.py:605
  89.7 5.5 %collective-permute-start.12 = (bf16[128,256]{1,0:T(8,128)(2,1)S(1)}, bf16[128,256]{1,0:T(8,128)(2,1)S(1)}, u32[]{:S(2)}, u32[]{:S(2)}) collective-permute-start(bf16[128,256]{1,0:T(8,128)(2,1)S(1)} %get-tuple-element.59), channel_id=1, source_target_pairs={{0,192},{32,224},{64,128},{96,160},{128,64},{160,96},{192,0},{224,... | collective-permute-start | bytes 196616 | tf_op jit(solution)/shard_map/ppermute | solution.py:605
  96.0 17.6 %all-to-all-start.2 = ((bf16[32,8,128]{2,1,0:T(8,128)(2,1)}), bf16[32,8,128]{2,1,0:T(8,128)(2,1)S(1)}, u32[]{:S(2)}, u32[]{:S(2)}) async-start(bf16[32,8,128]{2,1,0:T(8,128)(2,1)} %finish.1), calls=%async_computation.2 | async-start | bytes 131072 | tf_op jit(solution)/shard_map/all_to_all | solution.py:650

commit v10 on v9

--- a/solution.py
+++ b/solution.py
@@ -636,7 +636,7 @@
     total = swapped.pop()
     other, sent = scorer((devices, 128), (rings + 1, 1), swapped, [total])
     sent, embed = hold((sent, embed))
-    got = lax.all_to_all(sent.reshape(devices, 1, 128), both, 0, 0, tiled=True)
+    got = lax.all_to_all(sent.reshape(devices, 1, 128), both[::-1], 0, 0, tiled=True)
     embed = layer(2, 3, embed)
     got, embed = hold((got, embed))
     loss, coef, away = ranking_of(

time: 115 us -> 115 us (level)
  transfers between devices with their start and end apart: 16 -> 16, of which waited for: 8 -> 9; matrix products, arithmetic and copies ran while one was open for 1% -> 1% of each run, Pallas kernels for 30% -> 30%
where the time goes in v10:
time: 115 us; the launch traced here: 114 us
  Pallas kernels  47.8 us (42%)
  starting transfers between devices  46.2 us (40%)
  waiting for transfers between devices  15.7 us (14%)
  local copies, waits for them, and re-layouts  2.73 us (2%)
    pallas_call x3, Pallas kernels, layer_of(): pl.pallas_call(layer_kernel, out_shape=jax.ShapeDtypeStruct((nodes, width...  21 us
    pallas_call x3, Pallas kernels, scorer_of(): pl.pallas_call(functools.partial(scorer_kernel, groups, final), out_shape...  16.1 us
    all_to_all x1, starting transfers between devices, shards(): mine = lax.all_to_all(conf_src, 'node', 0, 0, tiled=True)  13.3 us
    all_to_all x1, starting transfers between devices, shards(): lax.all_to_all(sent.reshape(devices, 1, 128), both[::-1], 0, 0, tiled=True)  9.81 us
    ppermute x6, starting transfers between devices, shift(): lax.ppermute(value, 'cfg', [(i, i ^ 2 * by) for i in range(group_count)])  9.79 us
    all_to_all x1, starting transfers between devices, shards(): conf_grad = lax.all_to_all(local_grad, 'node', 0, 0, tiled=True)  7.98 us
    ppermute x2, starting transfers between devices, trade(): return lax.ppermute(rows, both, pairs)  4.67 us
    ppermute x6, waiting for transfers between devices, shift(): lax.ppermute(value, 'cfg', [(i, i ^ 2 * by) for i in range(group_count)])  4.36 us
  transfers between devices with their start and end apart: 16, of which 9 were waited for; matrix products, arithmetic and copies ran while one was open for 1% of the time, Pallas kernels for 30%

profile of v10, /device:TPU:2, one launch (start us, length us, event | category | flops | bytes accessed | tf_op | source)
XLA Modules:
  0.0 114.3 jit_solution(11537063123127926654)
XLA Ops:
  0.6 1.1 constant_dynamic-slice_fusion
  1.7 2.4 %collective-permute-start = (bf16[512,256]{1,0:T(8,128)(2,1)S(1)}, bf16[512,256]{1,0:T(8,128)(2,1)S(1)}, u32[]{:S(2)}, u32[]{:S(2)}) collective-permute-start(bf16[512,256]{1,0:T(8,128)(2,1)S(1)} %get-tuple-element.58), channel_id=1, source_target_pairs={{0,1},{1,0},{2,3},{3,2},{4,5},{5,4},{6,7},{7,6},{8,9},{9,8},{10,11... | collective-permute-start | bytes 786440 | tf_op jit(solution)/shard_map/ppermute | solution.py:563
  4.1 2.3 %collective-permute-start.1 = (bf16[512,256]{1,0:T(8,128)(2,1)S(1)}, bf16[512,256]{1,0:T(8,128)(2,1)S(1)}, u32[]{:S(2)}, u32[]{:S(2)}) collective-permute-start(bf16[512,256]{1,0:T(8,128)(2,1)S(1)} %get-tuple-element.57), channel_id=1, source_target_pairs={{1,2},{2,1},{3,4},{4,3},{5,6},{6,5},{7,8},{8,7},{9,10},{10,9},{11,... | collective-permute-start | bytes 786440 | tf_op jit(solution)/shard_map/ppermute | solution.py:563
  6.4 0.9 broadcast_multiply_fusion
  7.2 0.0 copy-start
  7.3 1.6 %copy-done = bf16[4096,256]{1,0:T(8,128)(2,1)S(1)} copy-done((bf16[4096,256]{1,0:T(8,128)(2,1)S(1)}, bf16[4096,256]{1,0:T(8,128)(2,1)}, u32[]{:S(2)}) %copy-start) | copy-done | bytes 2097176
  8.8 0.4 window_rows.1.refs_3_
  9.2 0.6 collective-permute-done.inner
  9.8 2.6 %collective-permute-done.1.outer = bf16[512,256]{1,0:T(8,128)(2,1)S(1)} collective-permute-done((bf16[512,256]{1,0:T(8,128)(2,1)S(1)}, bf16[512,256]{1,0:T(8,128)(2,1)S(1)}, u32[]{:S(2)}, u32[]{:S(2)}) %collective-permute-start.1) | collective-permute-done | bytes 262176 | tf_op jit(solution)/shard_map/ppermute | solution.py:563
  12.4 0.0 copy-start.2
  12.4 0.0 copy-start.3
  12.4 0.0 copy-start.6
  12.4 3.5 %conf_rows.1 = (bf16[32,8,128]{2,1,0:T(8,128)(2,1)}, f32[10240,128]{1,0:T(8,128)S(1)}) custom-call(s32[1]{0:T(128)} %bitcast.flip, s32[16384]{0:T(1024)S(1)} %bitcast.25, s32[128]{0:T(128)S(1)} %copy-done.9, bf16[512,256]{1,0:T(8,128)(2,1)S(1)} %collective-permute-done.1.outer, ...), custom_call_target="tpu_custom_call", output_to_operand_aliasing={{1}: (8, {})} | custom-call | flops 33554432 | bytes 6291456 | tf_op jit(solution)/shard_map/conf_rows/pallas_call | solution.py:144
  15.9 13.3 %all-to-all-start = ((bf16[32,8,128]{2,1,0:T(8,128)(2,1)}), bf16[32,8,128]{2,1,0:T(8,128)(2,1)S(1)}, u32[]{:S(2)}, u32[]{:S(2)}) async-start(bf16[32,8,128]{2,1,0:T(8,128)(2,1)} %get-tuple-element.30), calls=%async_computation | async-start | bytes 131072 | tf_op jit(solution)/shard_map/all_to_all | solution.py:607
  29.3 0.1 prepare.1.refs_7_.refs_8_
  29.4 0.0 copy-start.4
  29.5 0.0 copy-start.10
  29.5 0.0 copy-start.11
  29.5 0.0 copy-start.12
  29.5 0.0 copy-start.13
  29.5 5.7 %graph_layer.3.refs_0_ = bf16[4096,256]{1,0:T(8,128)(2,1)} custom-call(s32[1]{0:T(128)} %bitcast.flip, s32[16384]{0:T(1024)S(1)} %bitcast.26, bf16[512,256]{1,0:T(8,128)(2,1)S(1)} %collective-permute-done.inner, bf16[512,256]{1,0:T(8,128)(2,1)S(1)} %collective-permute-done.1.outer, bf16[4096,256]{1,0:T(8,128)(2,1)S(1)} %copy-done.1, ...), custom_call_target="tpu_custom_call" | custom-call | flops 268435456 | bytes 16777216 | tf_op jit(solution)/shard_map/graph_layer/pallas_call | solution.py:219
  35.2 2.9 %all-to-all-done.refs_0_ = bf16[32,8,128]{2,1,0:T(8,128)(2,1)S(1)} async-done(((bf16[32,8,128]{2,1,0:T(8,128)(2,1)}), bf16[32,8,128]{2,1,0:T(8,128)(2,1)S(1)}, u32[]{:S(2)}, u32[]{:S(2)}) %all-to-all-start) | async-done | bytes 65568 | tf_op jit(solution)/shard_map/all_to_all | solution.py:607
  38.1 1.8 %collective-permute-start.2 = (bf16[32,8,128]{2,1,0:T(8,128)(2,1)S(1)}, bf16[32,8,128]{2,1,0:T(8,128)(2,1)S(1)}, u32[]{:S(2)}, u32[]{:S(2)}) collective-permute-start(bf16[32,8,128]{2,1,0:T(8,128)(2,1)S(1)} %all-to-all-done.refs_0_), channel_id=1, source_target_pairs={{0,64},{32,96},{64,0},{96,32},{128,192},{160,224},{192,128},{224,1... | collective-permute-start | bytes 196616 | tf_op jit(solution)/shard_map/ppermute | solution.py:605
  39.9 3.2 %collective-permute-start.3 = (bf16[32,8,128]{2,1,0:T(8,128)(2,1)S(1)}, bf16[32,8,128]{2,1,0:T(8,128)(2,1)S(1)}, u32[]{:S(2)}, u32[]{:S(2)}) collective-permute-start(bf16[32,8,128]{2,1,0:T(8,128)(2,1)S(1)} %all-to-all-done.refs_0_), channel_id=1, source_target_pairs={{0,128},{32,160},{64,192},{96,224},{128,0},{160,32},{192,64},{224,... | collective-permute-start | bytes 196616 | tf_op jit(solution)/shard_map/ppermute | solution.py:605
  43.1 4.8 %scorer.3 = (bf16[2,16,128,256]{3,2,1,0:T(8,128)(2,1)}, f32[16,256]{1,0:T(8,128)S(1)}) custom-call(s32[1]{0:T(128)} %bitcast.6.where, bf16[32,8,128]{2,1,0:T(8,128)(2,1)S(1)} %all-to-all-done.refs_0_, bf16[32,8,128]{2,1,0:T(8,128)(2,1)} %collective-permute-done.5.refs_1_, s32[16,1024]{1,0:T(8,128)S(1)} %copy-done.10, bf16[256,256]{1,0:T(8,128)(2,1)S(1)} %copy-done.4, ...), custom_call_target="tpu_custom_call" | custom-call | flops 1610612736 | bytes 2097152 | tf_op jit(solution)/shard_map/scorer/pallas_call | solution.py:363
  47.9 0.6 collective-permute-done.4.refs_2_
  48.6 0.5 collective-permute-start.7
  49.1 0.0 collective-permute-start.8
  49.1 5.3 %scorer.4 = (bf16[3,16,128,256]{3,2,1,0:T(8,128)(2,1)}, f32[16,256]{1,0:T(8,128)S(1)}) custom-call(s32[1]{0:T(128)} %bitcast.6.where, bf16[32,8,128]{2,1,0:T(8,128)(2,1)S(1)} %collective-permute-done.2.refs_0_, bf16[32,8,128]{2,1,0:T(8,128)(2,1)S(1)} %collective-permute-done.3.refs_1_, bf16[32,8,128]{2,1,0:T(8,128)(2,1)S(1)} %collective-permute-done.4.refs_2_, ...), custom_call_target="tpu_custom_call" | custom-call | flops 2415919104 | bytes 3145728 | tf_op jit(solution)/shard_map/scorer/pallas_call | solution.py:363
  54.4 6.0 %scorer.5 = (bf16[3,16,128,256]{3,2,1,0:T(8,128)(2,1)}, f32[256,128]{1,0:T(8,128)}) custom-call(s32[1]{0:T(128)} %bitcast.6.where, bf16[32,8,128]{2,1,0:T(8,128)(2,1)S(1)} %collective-permute-done.6.refs_0_, bf16[32,8,128]{2,1,0:T(8,128)(2,1)S(1)} %collective-permute-done.7.refs_1_, bf16[32,8,128]{2,1,0:T(8,128)(2,1)S(1)} %collective-permute-done.8.refs_2_, ...), custom_call_target="tpu_custom_call" | custom-call | flops 2415919104 | bytes 3145728 | tf_op jit(solution)/shard_map/scorer/pallas_call | solution.py:363
  60.5 9.8 %all-to-all-start.1 = ((f32[256,1,128]{2,1,0:T(1,128)}), f32[256,1,128]{2,1,0:T(1,128)S(1)}, u32[]{:S(2)}, u32[]{:S(2)}) async-start(f32[256,1,128]{2,1,0:T(1,128)} %bitcast.14), calls=%async_computation.1 | async-start | bytes 262144 | tf_op jit(solution)/shard_map/all_to_all | solution.py:639
  70.3 0.0 copy-start.7
  70.3 7.7 %graph_layer.4.refs_0_ = bf16[4096,256]{1,0:T(8,128)(2,1)} custom-call(s32[1]{0:T(128)} %bitcast.flip, s32[16384]{0:T(1024)S(1)} %bitcast.27, bf16[512,256]{1,0:T(8,128)(2,1)S(1)} %collective-permute-done.inner, bf16[512,256]{1,0:T(8,128)(2,1)S(1)} %collective-permute-done.1.outer, bf16[4096,256]{1,0:T(8,128)(2,1)S(1)} %copy-done.1, ...), custom_call_target="tpu_custom_call", output_to_operand_aliasing={{}: (9, {})} | custom-call | flops 402653184 | bytes 25165824 | tf_op jit(solution)/shard_map/graph_layer/pallas_call | solution.py:219
  78.0 4.3 %all-to-all-done.1 = f32[256,1,128]{2,1,0:T(1,128)S(1)} async-done(((f32[256,1,128]{2,1,0:T(1,128)}), f32[256,1,128]{2,1,0:T(1,128)S(1)}, u32[]{:S(2)}, u32[]{:S(2)}) %all-to-all-start.1) | async-done | bytes 131104 | tf_op jit(solution)/shard_map/all_to_all | solution.py:639
  82.2 2.7 %ranking.1 = (f32[1,1]{1,0:T(1,128)}, f32[16,256]{1,0:T(8,128)S(1)}, bf16[4,128,256]{2,1,0:T(8,128)(2,1)S(1)}) custom-call(s32[1]{0:T(128)} %bitcast.6.where, f32[256,128]{1,0:T(8,128)S(1)} %bitcast.29, s32[2,512]{1,0:T(2,128)S(1)} %bitcast.34, bf16[2,16,128,256]{3,2,1,0:T(8,128)(2,1)} %get-tuple-element.48.pair, ...), custom_call_target="tpu_custom_call" | custom-call | flops 16777216 | bytes 6291456 | tf_op jit(solution)/shard_map/ranking/pallas_call | solution.py:445
  85.0 0.1 collective-permute-start.9
  85.1 2.4 %rest.1.kept = bf16[4,128,256]{2,1,0:T(8,128)(2,1)S(1)} custom-call(f32[16,256]{1,0:T(8,128)S(1)} %get-tuple-element.50.coef, bf16[2,16,128,256]{3,2,1,0:T(8,128)(2,1)} %get-tuple-element.48.pair, bf16[3,16,128,256]{3,2,1,0:T(8,128)(2,1)} %get-tuple-element.51.later), custom_call_target="tpu_custom_call" | custom-call | flops 16777216 | bytes 6291456 | tf_op jit(solution)/shard_map/rest/pallas_call | solution.py:477
  87.6 0.7 collective-permute-start.10
  88.3 2.3 %collective-permute-start.11 = (bf16[128,256]{1,0:T(8,128)(2,1)S(1)}, bf16[128,256]{1,0:T(8,128)(2,1)S(1)}, u32[]{:S(2)}, u32[]{:S(2)}) collective-permute-start(bf16[128,256]{1,0:T(8,128)(2,1)S(1)} %get-tuple-element.60), channel_id=1, source_target_pairs={{0,128},{32,160},{64,192},{96,224},{128,0},{160,32},{192,64},{224,... | collective-permute-start | bytes 196616 | tf_op jit(solution)/shard_map/ppermute | solution.py:605
  90.6 1.7 %collective-permute-start.12 = (bf16[128,256]{1,0:T(8,128)(2,1)S(1)}, bf16[128,256]{1,0:T(8,128)(2,1)S(1)}, u32[]{:S(2)}, u32[]{:S(2)}) collective-permute-start(bf16[128,256]{1,0:T(8,128)(2,1)S(1)} %get-tuple-element.59), channel_id=1, source_target_pairs={{0,192},{32,224},{64,128},{96,160},{128,64},{160,96},{192,0},{224,... | collective-permute-start | bytes 196616 | tf_op jit(solution)/shard_map/ppermute | solution.py:605
  92.4 0.2 collective-permute-done.10.refs_0_
  92.6 2.0 %collective-permute-done.11.refs_1_ = bf16[128,256]{1,0:T(8,128)(2,1)S(1)} collective-permute-done((bf16[128,256]{1,0:T(8,128)(2,1)S(1)}, bf16[128,256]{1,0:T(8,128)(2,1)S(1)}, u32[]{:S(2)}, u32[]{:S(2)}) %collective-permute-start.11) | collective-permute-done | bytes 65568 | tf_op jit(solution)/shard_map/ppermute | solution.py:605
  94.5 1.6 %collective-permute-done.12.refs_2_ = bf16[128,256]{1,0:T(8,128)(2,1)S(1)} collective-permute-done((bf16[128,256]{1,0:T(8,128)(2,1)S(1)}, bf16[128,256]{1,0:T(8,128)(2,1)S(1)}, u32[]{:S(2)}, u32[]{:S(2)}) %collective-permute-start.12) | collective-permute-done | bytes 65568 | tf_op jit(solution)/shard_map/ppermute | solution.py:605
  96.1 0.8 finish.1
  97.0 8.0 %all-to-all-start.2 = ((bf16[32,8,128]{2,1,0:T(8,128)(2,1)}), bf16[32,8,128]{2,1,0:T(8,128)(2,1)S(1)}, u32[]{:S(2)}, u32[]{:S(2)}) async-start(bf16[32,8,128]{2,1,0:T(8,128)(2,1)} %finish.1), calls=%async_computation.2 | async-start | bytes 131072 | tf_op jit(solution)/shard_map/all_to_all | solution.py:650
  104.9 7.7 %graph_layer.5 = bf16[4096,256]{1,0:T(8,128)(2,1)} custom-call(s32[1]{0:T(128)} %bitcast.flip, s32[16384]{0:T(1024)S(1)} %bitcast.28, bf16[512,256]{1,0:T(8,128)(2,1)S(1)} %collective-permute-done.inner, bf16[512,256]{1,0:T(8,128)(2,1)S(1)} %collective-permute-done.1.outer, bf16[4096,256]{1,0:T(8,128)(2,1)S(1)} %copy-done.1, ...), custom_call_target="tpu_custom_call", output_to_operand_aliasing={{}: (9, {})} | custom-call | flops 402653184 | bytes 25165824 | tf_op jit(solution)/shard_map/graph_layer/pallas_call | solution.py:219
  112.6 1.0 all-to-all-done.2.value
  113.6 0.7 returned.1
  (28 shorter events, 0.1 us)
Async XLA Ops:
  1.7 8.1 %collective-permute-start = (bf16[512,256]{1,0:T(8,128)(2,1)S(1)}, bf16[512,256]{1,0:T(8,128)(2,1)S(1)}, u32[]{:S(2)}, u32[]{:S(2)}) collective-permute-start(bf16[512,256]{1,0:T(8,128)(2,1)S(1)} %get-tuple-element.58), channel_id=1, source_target_pairs={{0,1},{1,0},{2,3},{3,2},{4,5},{5,4},{6,7},{7,6},{8,9},{9,8},{10,11... | collective-permute-start | bytes 786440 | tf_op jit(solution)/shard_map/ppermute | solution.py:563
  4.1 8.3 %collective-permute-start.1 = (bf16[512,256]{1,0:T(8,128)(2,1)S(1)}, bf16[512,256]{1,0:T(8,128)(2,1)S(1)}, u32[]{:S(2)}, u32[]{:S(2)}) collective-permute-start(bf16[512,256]{1,0:T(8,128)(2,1)S(1)} %get-tuple-element.57), channel_id=1, source_target_pairs={{1,2},{2,1},{3,4},{4,3},{5,6},{6,5},{7,8},{8,7},{9,10},{10,9},{11,... | collective-permute-start | bytes 786440 | tf_op jit(solution)/shard_map/ppermute | solution.py:563
  7.2 1.6 %copy-start = (bf16[4096,256]{1,0:T(8,128)(2,1)S(1)}, bf16[4096,256]{1,0:T(8,128)(2,1)}, u32[]{:S(2)}) copy-start(bf16[4096,256]{1,0:T(8,128)(2,1)} %own.5) | copy-start | bytes 6291460
  8.8 3.6 %copy-start.9 = (s32[128]{0:T(128)S(1)}, s32[128]{0:T(128)}, u32[]{:S(2)}) copy-start(s32[128]{0:T(128)} %picks.1) | copy-start | bytes 1540
  12.4 16.9 %copy-start.5 = (bf16[256,256]{1,0:T(8,128)(2,1)S(1)}, bf16[256,256]{1,0:T(8,128)(2,1)}, u32[]{:S(2)}) copy-start(bf16[256,256]{1,0:T(8,128)(2,1)} %refs_7_.3) | copy-start | bytes 393220
  12.4 16.9 %copy-start.8 = (f32[256]{0:T(256)S(1)}, f32[256]{0:T(256)}, u32[]{:S(2)}) copy-start(f32[256]{0:T(256)} %param.26) | copy-start | bytes 3076
  12.4 17.0 %copy-start.1 = (bf16[4096,256]{1,0:T(8,128)(2,1)S(1)}, bf16[4096,256]{1,0:T(8,128)(2,1)}, u32[]{:S(2)}) copy-start(bf16[4096,256]{1,0:T(8,128)(2,1)} %own.5) | copy-start | bytes 6291460
  12.4 17.0 %copy-start.2 = (bf16[256,256]{1,0:T(8,128)(2,1)S(1)}, bf16[256,256]{1,0:T(8,128)(2,1)}, u32[]{:S(2)}) copy-start(bf16[256,256]{1,0:T(8,128)(2,1)} %sw.5) | copy-start | bytes 393220
  12.4 17.0 %copy-start.3 = (bf16[256,256]{1,0:T(8,128)(2,1)S(1)}, bf16[256,256]{1,0:T(8,128)(2,1)}, u32[]{:S(2)}) copy-start(bf16[256,256]{1,0:T(8,128)(2,1)} %nw.5) | copy-start | bytes 393220
  12.4 17.0 %copy-start.6 = (f32[256]{0:T(256)S(1)}, f32[256]{0:T(256)}, u32[]{:S(2)}) copy-start(f32[256]{0:T(256)} %param.18) | copy-start | bytes 3076
  15.9 22.2 %all-to-all-start = ((bf16[32,8,128]{2,1,0:T(8,128)(2,1)}), bf16[32,8,128]{2,1,0:T(8,128)(2,1)S(1)}, u32[]{:S(2)}, u32[]{:S(2)}) async-start(bf16[32,8,128]{2,1,0:T(8,128)(2,1)} %get-tuple-element.30), calls=%async_computation | async-start | bytes 131072 | tf_op jit(solution)/shard_map/all_to_all | solution.py:607
  29.4 13.7 %copy-start.4 = (bf16[256,256]{1,0:T(8,128)(2,1)S(1)}, bf16[256,256]{1,0:T(8,128)(2,1)}, u32[]{:S(2)}) copy-start(bf16[256,256]{1,0:T(8,128)(2,1)} %refs_3_.7) | copy-start | bytes 393220
  29.5 13.6 %copy-start.10 = (s32[16,1024]{1,0:T(8,128)S(1)}, s32[16,1024]{1,0:T(8,128)}, u32[]{:S(2)}) copy-start(s32[16,1024]{1,0:T(8,128)} %refs_3_.6) | copy-start | bytes 196612
  29.5 13.6 %copy-start.11 = (bf16[128,256]{1,0:T(8,128)(2,1)S(1)}, bf16[128,256]{1,0:T(8,128)(2,1)}, u32[]{:S(2)}) copy-start(bf16[128,256]{1,0:T(8,128)(2,1)} %refs_6_.5) | copy-start | bytes 196612
  29.5 13.6 %copy-start.12 = (f32[256]{0:T(256)S(1)}, f32[256]{0:T(256)}, u32[]{:S(2)}) copy-start(f32[256]{0:T(256)} %param.23) | copy-start | bytes 3076
  29.5 13.6 %copy-start.13 = (f32[256]{0:T(256)S(1)}, f32[256]{0:T(256)}, u32[]{:S(2)}) copy-start(f32[256]{0:T(256)} %param.25) | copy-start | bytes 3076
  38.1 5.0 %collective-permute-start.5 = (bf16[32,8,128]{2,1,0:T(8,128)(2,1)S(1)}, bf16[32,8,128]{2,1,0:T(8,128)(2,1)}, u32[]{:S(2)}, u32[]{:S(2)}) collective-permute-start(bf16[32,8,128]{2,1,0:T(8,128)(2,1)S(1)} %all-to-all-done.refs_0_), channel_id=1, source_target_pairs={{0,32},{32,0},{64,96},{96,64},{128,160},{160,128},{192,224},{224,1... | collective-permute-start | bytes 196616 | tf_op jit(solution)/shard_map/ppermute | solution.py:630
  38.1 9.8 %collective-permute-start.2 = (bf16[32,8,128]{2,1,0:T(8,128)(2,1)S(1)}, bf16[32,8,128]{2,1,0:T(8,128)(2,1)S(1)}, u32[]{:S(2)}, u32[]{:S(2)}) collective-permute-start(bf16[32,8,128]{2,1,0:T(8,128)(2,1)S(1)} %all-to-all-done.refs_0_), channel_id=1, source_target_pairs={{0,64},{32,96},{64,0},{96,32},{128,192},{160,224},{192,128},{224,1... | collective-permute-start | bytes 196616 | tf_op jit(solution)/shard_map/ppermute | solution.py:605
  39.9 8.1 %collective-permute-start.3 = (bf16[32,8,128]{2,1,0:T(8,128)(2,1)S(1)}, bf16[32,8,128]{2,1,0:T(8,128)(2,1)S(1)}, u32[]{:S(2)}, u32[]{:S(2)}) collective-permute-start(bf16[32,8,128]{2,1,0:T(8,128)(2,1)S(1)} %all-to-all-done.refs_0_), channel_id=1, source_target_pairs={{0,128},{32,160},{64,192},{96,224},{128,0},{160,32},{192,64},{224,... | collective-permute-start | bytes 196616 | tf_op jit(solution)/shard_map/ppermute | solution.py:605
  43.1 5.5 %collective-permute-start.4 = (bf16[32,8,128]{2,1,0:T(8,128)(2,1)S(1)}, bf16[32,8,128]{2,1,0:T(8,128)(2,1)S(1)}, u32[]{:S(2)}, u32[]{:S(2)}) collective-permute-start(bf16[32,8,128]{2,1,0:T(8,128)(2,1)S(1)} %all-to-all-done.refs_0_), channel_id=1, source_target_pairs={{0,192},{32,224},{64,128},{96,160},{128,64},{160,96},{192,0},{224,... | collective-permute-start | bytes 196616 | tf_op jit(solution)/shard_map/ppermute | solution.py:605
  48.6 5.8 %collective-permute-start.6 = (bf16[32,8,128]{2,1,0:T(8,128)(2,1)S(1)}, bf16[32,8,128]{2,1,0:T(8,128)(2,1)S(1)}, u32[]{:S(2)}, u32[]{:S(2)}) collective-permute-start(bf16[32,8,128]{2,1,0:T(8,128)(2,1)S(1)} %collective-permute-done.2.refs_0_), channel_id=1, source_target_pairs={{0,32},{32,0},{64,96},{96,64},{128,160},{160,128},{192,224},{224,1... | collective-permute-start | bytes 196616 | tf_op jit(solution)/shard_map/ppermute | solution.py:633
  48.6 5.8 %collective-permute-start.7 = (bf16[32,8,128]{2,1,0:T(8,128)(2,1)S(1)}, bf16[32,8,128]{2,1,0:T(8,128)(2,1)S(1)}, u32[]{:S(2)}, u32[]{:S(2)}) collective-permute-start(bf16[32,8,128]{2,1,0:T(8,128)(2,1)S(1)} %collective-permute-done.3.refs_1_), channel_id=1, source_target_pairs={{0,32},{32,0},{64,96},{96,64},{128,160},{160,128},{192,224},{224,1... | collective-permute-start | bytes 196616 | tf_op jit(solution)/shard_map/ppermute | solution.py:633
  49.1 5.3 %collective-permute-start.8 = (bf16[32,8,128]{2,1,0:T(8,128)(2,1)S(1)}, bf16[32,8,128]{2,1,0:T(8,128)(2,1)S(1)}, u32[]{:S(2)}, u32[]{:S(2)}) collective-permute-start(bf16[32,8,128]{2,1,0:T(8,128)(2,1)S(1)} %collective-permute-done.4.refs_2_), channel_id=1, source_target_pairs={{0,32},{32,0},{64,96},{96,64},{128,160},{160,128},{192,224},{224,1... | collective-permute-start | bytes 196616 | tf_op jit(solution)/shard_map/ppermute | solution.py:633
  60.5 21.8 %all-to-all-start.1 = ((f32[256,1,128]{2,1,0:T(1,128)}), f32[256,1,128]{2,1,0:T(1,128)S(1)}, u32[]{:S(2)}, u32[]{:S(2)}) async-start(f32[256,1,128]{2,1,0:T(1,128)} %bitcast.14), calls=%async_computation.1 | async-start | bytes 262144 | tf_op jit(solution)/shard_map/all_to_all | solution.py:639
  70.3 11.9 %copy-start.7 = (s32[512,2]{0,1:T(2,128)S(1)}, s32[512,2]{0,1:T(2,128)}, u32[]{:S(2)}) copy-start(s32[512,2]{0,1:T(2,128)} %param.27) | copy-start | bytes 12292
  85.0 2.5 %collective-permute-start.9 = (bf16[4,128,256]{2,1,0:T(8,128)(2,1)S(1)}, bf16[4,128,256]{2,1,0:T(8,128)(2,1)S(1)}, u32[]{:S(2)}, u32[]{:S(2)}) collective-permute-start(bf16[4,128,256]{2,1,0:T(8,128)(2,1)S(1)} %get-tuple-element.52), channel_id=1, source_target_pairs={{0,32},{32,0},{64,96},{96,64},{128,160},{160,128},{192,224},{224,1... | collective-permute-start | bytes 786440 | tf_op jit(solution)/shard_map/ppermute | solution.py:645
  87.6 5.0 %collective-permute-start.10 = (bf16[128,256]{1,0:T(8,128)(2,1)S(1)}, bf16[128,256]{1,0:T(8,128)(2,1)S(1)}, u32[]{:S(2)}, u32[]{:S(2)}) collective-permute-start(bf16[128,256]{1,0:T(8,128)(2,1)S(1)} %get-tuple-element.61), channel_id=1, source_target_pairs={{0,64},{32,96},{64,0},{96,32},{128,192},{160,224},{192,128},{224,1... | collective-permute-start | bytes 196616 | tf_op jit(solution)/shard_map/ppermute | solution.py:605
  88.3 6.2 %collective-permute-start.11 = (bf16[128,256]{1,0:T(8,128)(2,1)S(1)}, bf16[128,256]{1,0:T(8,128)(2,1)S(1)}, u32[]{:S(2)}, u32[]{:S(2)}) collective-permute-start(bf16[128,256]{1,0:T(8,128)(2,1)S(1)} %get-tuple-element.60), channel_id=1, source_target_pairs={{0,128},{32,160},{64,192},{96,224},{128,0},{160,32},{192,64},{224,... | collective-permute-start | bytes 196616 | tf_op jit(solution)/shard_map/ppermute | solution.py:605
  90.6 5.5 %collective-permute-start.12 = (bf16[128,256]{1,0:T(8,128)(2,1)S(1)}, bf16[128,256]{1,0:T(8,128)(2,1)S(1)}, u32[]{:S(2)}, u32[]{:S(2)}) collective-permute-start(bf16[128,256]{1,0:T(8,128)(2,1)S(1)} %get-tuple-element.59), channel_id=1, source_target_pairs={{0,192},{32,224},{64,128},{96,160},{128,64},{160,96},{192,0},{224,... | collective-permute-start | bytes 196616 | tf_op jit(solution)/shard_map/ppermute | solution.py:605
  97.0 16.7 %all-to-all-start.2 = ((bf16[32,8,128]{2,1,0:T(8,128)(2,1)}), bf16[32,8,128]{2,1,0:T(8,128)(2,1)S(1)}, u32[]{:S(2)}, u32[]{:S(2)}) async-start(bf16[32,8,128]{2,1,0:T(8,128)(2,1)} %finish.1), calls=%async_computation.2 | async-start | bytes 131072 | tf_op jit(solution)/shard_map/all_to_all | solution.py:650
